TPU v7x, 256 devices: a whole 4x4x8 slice. The times are simulated.
256 devices in a mesh: seq: 64 (over x_hi, y, z), head: 4 (over x_lo, core).
Axes of the slice: x: 4 (x_hi: 2, x_lo: 2; x = x_hi * 2 + x_lo), y: 4, z: 8, core: 2. Of those that a mesh axis runs over, the one named last changes fastest.
Arguments:
- queries: bfloat16 [32768, 2048], P('seq', 'head'), may hold values from -256 to 256
- keys_new: bfloat16 [32768, 2048], P('seq', 'head'), may hold values from -6 to 6
- values_new: bfloat16 [32768, 2048], P('seq', 'head'), may hold values from -6 to 6
- residual: bfloat16 [32768, 4096], P('seq', 'head'), may hold values from -6 to 6
- layer_scale: float32 [4096], P('head'), may hold values from 0.1 to 1.9
- out_weight: bfloat16 [2048, 4096], P('head'), may hold values from -0.125 to 0.125
- segment_ids: int32 [32768], P('seq'), may hold values from 0 to 203, never falling along the last dimension, each value on 1 to 201 neighbouring positions
- cache_keys: bfloat16 [8192, 2048], P('seq', 'head'), may hold values from -6 to 6
- cache_values: bfloat16 [8192, 2048], P('seq', 'head'), may hold values from -6 to 6
- block_live: int32 [512], P('seq'), may hold values from 0 to 1, as said below
- recompute_block: int32 [64], P('seq'), may hold values from 0 to 7
- recompute_hidden: bfloat16 [1024, 4096], P('seq'), may hold values from -6 to 6
- key_weight: bfloat16 [4096, 2048], P(None, 'head'), may hold values from -0.09375 to 0.09375
- owners: int32 [8192, 1], P('seq'), may hold values from 0 to 63; in each aligned block of 128 rows (0 to 127, 128 to 255, ...) at most 3 rows name the same one
Outputs:
- delivered: bfloat16 [12288, 16384], P('seq', 'head')
- refreshed_keys: bfloat16 [8192, 2048], P('seq', 'head')
Inputs may be any that keep to these rules, and one draw needn't show every extreme that they name: `block_live`: one index of seq has between 2 and 6 live blocks, and some index has exactly 6. `owners`: out of the merged rows of one index of seq (aligned blocks of 128 rows), at most 3 have the same owner.
All inputs are finite; a program needn't handle non-finite values.
Results may differ from a plain program's by a relative error of at most 0.014.
Values may be sent and summed in bfloat16 or wider, within the bound.
No kernel may reach another device: no remote copies, remote signals or barrier semaphores. Data moves between devices by JAX's collectives and lax.ppermute only.
A program may use at most 128 MiB of HBM per device.

v0:
```python
import math

import jax
import jax.numpy as jnp
from jax import lax
from jax.sharding import PartitionSpec as P

HD = 128
BLK = 16
SEG_MOST = 201


def padded(shard, sides, width):
    for axis, dim in sides:
        count, length = (lax.axis_size(axis), shard.shape[dim])
        up = [(i, (i + 1) % count) for i in range(count - 1)]
        down = [(j, i) for i, j in up]
        last = lax.slice_in_dim(shard, length - width, length, axis=dim)
        initial = lax.slice_in_dim(shard, 0, width, axis=dim)
        before = lax.ppermute(last, axis, up)
        after = lax.ppermute(initial, axis, down)
        shard = jnp.concatenate([before, shard, after], axis=dim)
    return shard


def rotate(vectors, positions):
    half_size = vectors.shape[-1] // 2
    freqs = 100.0 ** (-jnp.arange(half_size, dtype=jnp.float32) / half_size)
    angles = positions.astype(jnp.float32)[:, None] * freqs[None, :]
    cosine = jnp.cos(angles)[:, None, :]
    sine = jnp.sin(angles)[:, None, :]
    first_half = vectors[..., :half_size]
    second_half = vectors[..., half_size:]
    return jnp.concatenate(
        [first_half * cosine - second_half * sine, second_half * cosine + first_half * sine],
        axis=-1,
    )


def shards(
    queries,
    keys_new,
    values_new,
    residual,
    layer_scale,
    out_weight,
    segment_ids,
    cache_keys,
    cache_values,
    block_live,
    recompute_block,
    recompute_hidden,
    key_weight,
    owners,
):
    tok_rows = queries.shape[0]
    columns = queries.shape[1]
    head_count = columns // HD
    rim_rows = SEG_MOST - 1
    score_scale = 1.0 / math.sqrt(HD)
    cycle_size = lax.axis_size("seq")
    cycle_pos = lax.axis_index("seq")
    key_vals = jnp.concatenate([keys_new, values_new], axis=1)
    marks = segment_ids + 1
    wide_kv, wide_marks = (
        padded(key_vals, (("seq", 0),), rim_rows),
        padded(marks, (("seq", 0),), rim_rows),
    )
    ext_rows = wide_kv.shape[0]
    ext_index = jnp.arange(ext_rows, dtype=jnp.int32)
    same_frame = (wide_marks[:, None] == wide_marks[None, :]) & (wide_marks[None, :] > 0)
    frame_first = jnp.min(jnp.where(same_frame, ext_index[None, :], ext_rows), axis=1)
    ext_pos = ext_index - frame_first
    own_pos = ext_pos[rim_rows : rim_rows + tok_rows]
    q_rot = rotate(queries.astype(jnp.float32).reshape(tok_rows, head_count, HD), own_pos).astype(
        jnp.bfloat16
    )
    k_ext = rotate(
        wide_kv[:, :columns].astype(jnp.float32).reshape(ext_rows, head_count, HD), ext_pos
    ).astype(jnp.bfloat16)
    v_ext = wide_kv[:, columns:].reshape(ext_rows, head_count, HD)

    def absorb(running, keys3, values3, allowed):
        numer, top_score, weight_sum = running
        scores = (
            jnp.einsum("qhd,khd->hqk", q_rot, keys3, preferred_element_type=jnp.float32)
            * score_scale
        )
        scores = jnp.where(allowed, scores, -jnp.inf)
        new_top = jnp.maximum(top_score, jnp.max(scores, axis=-1))
        weights = jnp.exp(scores - new_top[..., None])
        decay = jnp.exp(top_score - new_top)
        weight_sum = weight_sum * decay + jnp.sum(weights, axis=-1)
        numer = numer * decay[..., None] + jnp.einsum(
            "hqk,khd->hqd",
            weights.astype(jnp.bfloat16),
            values3,
            preferred_element_type=jnp.float32,
        )
        return (numer, new_top, weight_sum)

    start_state = (
        jnp.zeros((head_count, tok_rows, HD), jnp.float32),
        jnp.full((head_count, tok_rows), -jnp.inf, jnp.float32),
        jnp.zeros((head_count, tok_rows), jnp.float32),
    )
    own_marks = marks[:, None] == wide_marks[None, :]
    running = absorb(start_state, k_ext, v_ext, own_marks[None])
    cache_rows = cache_keys.shape[0]
    block_index = recompute_block[0]
    fresh_keys = jnp.dot(recompute_hidden, key_weight, preferred_element_type=jnp.float32)
    fresh_rows = cycle_pos * cache_rows + block_index * BLK + jnp.arange(BLK, dtype=jnp.int32)
    fresh_keys = rotate(fresh_keys.reshape(BLK, head_count, HD), fresh_rows % SEG_MOST)
    fresh_keys = fresh_keys.reshape(BLK, columns).astype(jnp.bfloat16)
    refreshed = lax.dynamic_update_slice(cache_keys, fresh_keys, (block_index * BLK, 0))

    def absorb_rows(state_now, block_keys, block_values, block_marks):
        rows_here = block_keys.shape[0]
        return absorb(
            state_now,
            block_keys.reshape(rows_here, head_count, HD),
            block_values.reshape(rows_here, head_count, HD),
            (block_marks > 0)[None, None, :],
        )

    live_rows = jnp.repeat(block_live, BLK)
    state_now = running
    piece_keys = lax.all_gather(refreshed, "seq", axis=0, tiled=True)
    piece_values = lax.all_gather(cache_values, "seq", axis=0, tiled=True)
    piece_marks = lax.all_gather(live_rows, "seq", axis=0, tiled=True)
    piece_rows = piece_keys.shape[0]
    step_rows = math.gcd(piece_rows, 512)
    step_count = piece_rows // step_rows

    def visit(inner, parts):
        return (absorb_rows(inner, parts[0], parts[1], parts[2]), None)

    state_now, unused = lax.scan(
        visit,
        state_now,
        (
            piece_keys.reshape(step_count, step_rows, columns),
            piece_values.reshape(step_count, step_rows, columns),
            piece_marks.reshape(step_count, step_rows),
        ),
    )
    running = state_now
    numer, top_score, weight_sum = running
    attended = (
        jnp.transpose(numer / weight_sum[..., None], (1, 0, 2))
        .reshape(tok_rows, columns)
        .astype(jnp.bfloat16)
    )
    partial_proj = jnp.dot(attended, out_weight, preferred_element_type=jnp.float32)
    projected = lax.psum_scatter(
        partial_proj.astype(jnp.bfloat16), "head", scatter_dimension=1, tiled=True
    ).astype(jnp.float32)
    width_here = projected.shape[1]
    layer = (residual.astype(jnp.float32) + layer_scale[None, :] * projected).astype(jnp.bfloat16)
    merged_rows = tok_rows // 4
    merged = jnp.transpose(layer.reshape(merged_rows, 4, width_here), (0, 2, 1)).reshape(
        merged_rows, 4 * width_here
    )
    capacity = max(3, (merged_rows + cycle_size - 1) // cycle_size)
    owner_list = owners[:, 0]
    hits = (owner_list[:, None] == jnp.arange(cycle_size, dtype=jnp.int32)[None, :]).astype(
        jnp.int32
    )
    before = jnp.cumsum(hits, axis=0) - hits
    slot_index = jnp.sum(before * hits, axis=1)
    target = owner_list * capacity + slot_index
    outgoing = (
        jnp.zeros((cycle_size * capacity, 4 * width_here), jnp.bfloat16).at[target].set(merged)
    )
    incoming = lax.all_to_all(
        outgoing.reshape(cycle_size, capacity, 4 * width_here),
        "seq",
        split_axis=0,
        concat_axis=0,
        tiled=True,
    )
    delivered = incoming.reshape(cycle_size * capacity, 4 * width_here)
    return (delivered, refreshed)


def solution(mesh):
    in_specs = (
        P("seq", "head"),
        P("seq", "head"),
        P("seq", "head"),
        P("seq", "head"),
        P("head"),
        P("head", None),
        P("seq"),
        P("seq", "head"),
        P("seq", "head"),
        P("seq"),
        P("seq"),
        P("seq", None),
        P(None, "head"),
        P("seq", None),
    )
    out_specs = (P("seq", "head"), P("seq", "head"))
    return jax.shard_map(shards, mesh=mesh, in_specs=in_specs, out_specs=out_specs, check_vma=False)
```

profile of v0, /device:TPU:1, one launch (start us, length us, event | category | flops | bytes accessed | tf_op | source)
XLA Modules:
  0.0 621.5 jit_solution(10397541522404778360)
XLA Ops:
  12.9 4.4 collective-permute-start
  19.7 4.9 collective-permute-start.2
  27.2 156.1 %all-gather = s32[64,1,128]{2,1,0:T(1,128)S(1)} all-gather(s32[1,1,128]{2,1,0:T(1,128)S(1)} %reshape.317), channel_id=1, replica_groups=mesh['seq'=64,'head'=4] {'seq'}, dimensions={0}, use_global_device_ids=true | all-gather | bytes 33280 | tf_op jit(solution)/shard_map/all_gather | solution.py:130
  208.3 107.8 %all-gather.6.cloned.1.call-done = bf16[8192,512]{1,0:T(8,128)(2,1)} async-done(((bf16[128,512]{1,0:T(8,128)(2,1)}), bf16[8192,512]{1,0:T(8,128)(2,1)}) %all-gather.6.cloned.1.call-update) | async-done | bytes 8388624 | tf_op jit(solution)/shard_map/all_gather | solution.py:129
  316.1 166.8 %while.14 = (s32[]{:T(128)}, f32[4,512,128]{2,1,0:T(8,128)}, f32[4,512]{1,0:T(4,128)S(1)}, f32[4,512]{1,0:T(4,128)S(1)}, s32[16,512]{1,0:T(8,128)S(1)}, /*index=...) while((s32[]{:T(128)}, f32[4,512,128]{2,1,0:T(8,128)}, ...), condition=%wide.region_8.9_spmd, body=%wide.region_5.8_spmd.sunk | while | flops 548934144 | bytes 45748408 | solution.py:138
  321.9 3.7 fusion.63
  332.3 3.7 fusion.63
  342.7 3.7 fusion.63
  353.1 3.7 fusion.63
  363.6 3.7 fusion.63
  374.0 3.7 fusion.63
  384.4 3.7 fusion.63
  394.8 3.7 fusion.63
  405.3 3.7 fusion.63
  415.7 3.7 fusion.63
  426.1 3.7 fusion.63
  436.5 3.7 fusion.63
  447.0 3.7 fusion.63
  457.4 3.7 fusion.63
  467.8 3.7 fusion.63
  484.7 6.5 %convolution_convert_fusion = bf16[512,4096]{1,0:T(8,128)(2,1)} fusion(bf16[512,512]{0,1:T(8,128)(2,1)S(1)} %bitcast.68, bf16[512,4096]{1,0:T(8,128)(2,1)} %param.21), kind=kOutput, calls=%fused_computation.23 | convolution fusion | flops 2149580800 | bytes 8912896 | tf_op jit(solution)/shard_map/dot_general | solution.py:154
  492.3 46.5 %reduce-scatter.2.cloned.1.call-done = bf16[512,1024]{1,0:T(8,128)(2,1)} async-done(((bf16[512,4096]{1,0:T(8,128)(2,1)}), bf16[512,1024]{1,0:T(8,128)(2,1)}) %reduce-scatter.2.cloned.1.call-update) | async-done | bytes 1048592 | tf_op jit(solution)/shard_map/reduce_scatter | solution.py:155
  549.0 61.7 %all_to_all.5 = bf16[64,3,4096]{2,1,0:T(4,128)(2,1)} all-to-all(bf16[64,3,4096]{2,1,0:T(4,128)(2,1)S(1)} %reshape.303), channel_id=1, replica_groups=mesh['seq'=64,'head'=4] {'seq'}, dimensions={0} | all-to-all | bytes 3145728 | tf_op jit(solution)/shard_map/all_to_all | solution.py:175
  610.7 4.3 reshape.304
  (335 shorter events, 157.0 us)
Async XLA Ops:
  7.2 11.4 %copy-start.8 = (bf16[512,512]{1,0:T(8,128)(2,1)S(1)}, bf16[512,512]{1,0:T(8,128)(2,1)}, u32[]{:S(2)}) copy-start(bf16[512,512]{1,0:T(8,128)(2,1)} %param.17) | copy-start | bytes 1572868
  7.2 11.5 %copy-start.9 = (bf16[512,512]{1,0:T(8,128)(2,1)S(1)}, bf16[512,512]{1,0:T(8,128)(2,1)}, u32[]{:S(2)}) copy-start(bf16[512,512]{1,0:T(8,128)(2,1)} %param.18) | copy-start | bytes 1572868
  7.2 5.6 copy-start.15
  7.2 4.1 copy-start.12
  7.2 201.1 %all-gather.4.cloned.1.call-start = ((), (), s32[]{:S(2)}) async-start(), calls=%async_computation.2 | async-start | bytes 8519680 | tf_op jit(solution)/shard_map/all_gather | solution.py:128
  8.1 17.8 %copy-start.10 = (bf16[512,512]{1,0:T(8,128)(2,1)S(1)}, bf16[512,512]{1,0:T(8,128)(2,1)}, u32[]{:S(2)}) copy-start(bf16[512,512]{1,0:T(8,128)(2,1)} %param.16) | copy-start | bytes 1572868
  11.0 15.2 %copy-start.16 = (s32[8]{0:T(128)S(1)}, s32[8]{0:T(128)}, u32[]{:S(2)}) copy-start(s32[8]{0:T(128)} %param.25) | copy-start | bytes 100
  12.0 304.1 %all-gather.6.cloned.1.call-start = ((), (), s32[]{:S(2)}) async-start(), calls=%async_computation.3 | async-start | bytes 8519680 | tf_op jit(solution)/shard_map/all_gather | solution.py:129
  12.8 526.0 %reduce-scatter.2.cloned.1.call-start = ((), (), s32[]{:S(2)}) async-start(), calls=%async_computation.4 | async-start | bytes 5242880 | tf_op jit(solution)/shard_map/reduce_scatter | solution.py:155
  12.9 174.5 %collective-permute-start = (s32[200]{0:T(256)S(1)}, s32[200]{0:T(256)S(1)}, u32[]{:S(2)}, u32[]{:S(2)}) collective-permute-start(s32[200]{0:T(256)S(1)} %get-tuple-element.123), channel_id=1, source_target_pairs={{0,4},{4,8},{8,12},{12,16},{16,20},{20,24},{24,28},{28,32},{32,36}... | collective-permute-start | bytes 2408 | tf_op jit(solution)/shard_map/ppermute | solution.py:20
  17.3 170.1 %collective-permute-start.1 = (s32[200]{0:T(256)S(1)}, s32[200]{0:T(256)S(1)}, u32[]{:S(2)}, u32[]{:S(2)}) collective-permute-start(s32[200]{0:T(256)S(1)} %get-tuple-element.124), channel_id=1, source_target_pairs={{4,0},{8,4},{12,8},{16,12},{20,16},{24,20},{28,24},{32,28},{36,32}... | collective-permute-start | bytes 2408 | tf_op jit(solution)/shard_map/ppermute | solution.py:21
  19.7 175.0 %collective-permute-start.2 = (bf16[200,1024]{1,0:T(8,128)(2,1)}, bf16[200,1024]{1,0:T(8,128)(2,1)}, u32[]{:S(2)}, u32[]{:S(2)}) collective-permute-start(bf16[200,1024]{1,0:T(8,128)(2,1)} %get-tuple-element.109), channel_id=1, source_target_pairs={{0,4},{4,8},{8,12},{12,16},{16,20},{20,24},{24,28},{28,32},{32,36}... | collective-permute-start | bytes 1228808 | tf_op jit(solution)/shard_map/ppermute | solution.py:20
  24.6 170.1 %collective-permute-start.3 = (bf16[200,1024]{1,0:T(8,128)(2,1)}, bf16[200,1024]{1,0:T(8,128)(2,1)}, u32[]{:S(2)}, u32[]{:S(2)}) collective-permute-start(bf16[200,1024]{1,0:T(8,128)(2,1)} %get-tuple-element.110), channel_id=1, source_target_pairs={{4,0},{8,4},{12,8},{16,12},{20,16},{24,20},{28,24},{32,28},{36,32}... | collective-permute-start | bytes 1228808 | tf_op jit(solution)/shard_map/ppermute | solution.py:21
  318.7 3.1 copy-start.5
  329.1 3.1 copy-start.5
  339.6 3.1 copy-start.5
  350.0 3.1 copy-start.5
  360.4 3.1 copy-start.5
  391.7 3.1 copy-start.5
  423.0 3.1 copy-start.5
  454.2 3.1 copy-start.5
  491.2 47.6 %copy-start.4 = (bf16[512,1024]{1,0:T(8,128)(2,1)S(1)}, bf16[512,1024]{1,0:T(8,128)(2,1)}, u32[]{:S(2)}) copy-start(bf16[512,1024]{1,0:T(8,128)(2,1)} %param.19) | copy-start | bytes 3145732
  491.2 47.6 %copy-start.13 = (f32[1024]{0:T(1024)S(1)}, f32[1024]{0:T(1024)}, u32[]{:S(2)}) copy-start(f32[1024]{0:T(1024)} %param.20) | copy-start | bytes 12292
  546.2 68.7 %copy-start.1 = (bf16[16,4096]{1,0:T(8,128)(2,1)S(1)}, bf16[16,4096]{1,0:T(8,128)(2,1)}, u32[]{:S(2)}) copy-start(bf16[16,4096]{1,0:T(8,128)(2,1)} %param.27) | copy-start | bytes 393220
  (45 other events, 76.9 us)
Sparse Core Ops, SparseCore 0:
  12.4 152.3 all-gather.3
  168.4 147.6 all-gather.5
  491.3 47.4 reduce-scatter.1
where the time goes:
time: 625 us; the launch traced here: 622 us
  blocking collectives  218 us (35%)
  waiting for transfers between devices  155 us (25%)
  local copies, waits for them, and re-layouts  97.7 us (16%)
  matrix products  91.2 us (15%)
  other arithmetic  31.5 us (5%)
  between operations  14.9 us (2%)
  starting transfers between devices  12 us (2%)
    all_gather x1, blocking collectives, shards(): piece_marks = lax.all_gather(live_rows, 'seq', axis=0, tiled=True)  156 us
    all_gather x1, waiting for transfers between devices, shards(): piece_values = lax.all_gather(cache_values, 'seq', axis=0, tiled=True)  108 us
    dot_general x17, matrix products, absorb(): jnp.einsum('hqk,khd->hqd', weights.astype(jnp.bfloat16), values3, preferr...  63.3 us
    all_to_all x1, blocking collectives, shards(): lax.all_to_all(outgoing.reshape(cycle_size, capacity, 4 * width_here), 's...  61.7 us
    reduce_scatter x1, waiting for transfers between devices, shards(): lax.psum_scatter(partial_proj.astype(jnp.bfloat16), 'head', scatter_dimen...  46.5 us
    while x112, local copies, waits for them, and re-layouts  46.2 us
    dynamic_slice x48, local copies, waits for them, and re-layouts, shards(): lax.scan(visit, state_now, (piece_keys.reshape(step_count, step_rows, col...  27.1 us
    dot_general x17, matrix products, absorb(): jnp.einsum('qhd,khd->hqk', q_rot, keys3, preferred_element_type=jnp.float32)  18.5 us
  transfers between devices with their start and end apart: 7, of which 2 were waited for; matrix products, arithmetic and copies ran while one was open for 4% of the time, Pallas kernels for 0%

commit v1 on v0

v1 whole, which is shorter than its diff:
```python
import math

import jax
import jax.numpy as jnp
import numpy as np
from jax import lax
from jax.experimental import pallas as pl
from jax.experimental.pallas import tpu as pltpu
from jax.sharding import Mesh, PartitionSpec as P

HD = 128
BLK = 16
SEG_MOST = 201
LIVE_MOST = 6
CAP = 3
HALO = 208
PAD = 256
TOK = 512
KT = 512
NEG = -1e30
SEQ = ("xh", "y", "zh", "zp")
HEAD = ("xl", "c")
bf16 = jnp.bfloat16
f32 = jnp.float32


def rope_parts(positions):
    half = HD // 2
    freqs = 100.0 ** (-jnp.arange(half, dtype=f32) / half)
    angles = positions.astype(f32)[:, None] * freqs[None, :]
    return jnp.cos(angles), jnp.sin(angles)


def rotate(vectors, cosine, sine):
    half = HD // 2
    a, b = vectors[..., :half], vectors[..., half:]
    c, s = cosine[:, None, :], sine[:, None, :]
    return jnp.concatenate([a * c - b * s, b * c + a * s], axis=-1)


def pack_kernel(idx, k_ref, v_ref, out_ref):
    heads = out_ref.shape[0]
    for j in range(LIVE_MOST):
        rows = pl.ds(pl.multiple_of(idx[j] * BLK, BLK), BLK)
        k = k_ref[rows, :]
        v = v_ref[rows, :]
        for p in range(heads):
            out_ref[p, j * BLK : (j + 1) * BLK, :HD] = k[:, p * HD : (p + 1) * HD]
            out_ref[p, j * BLK : (j + 1) * BLK, HD:] = v[:, p * HD : (p + 1) * HD]


def attention_kernel(
    off, tgt, zp, y0, y1, y2, y3, left, right, kvg, qid, kid, out, kc, vc, qs, kw, vw, ob, send
):
    i = pl.program_id(0)
    sources = off.shape[0] - 1
    slot_rows = LIVE_MOST * BLK
    coef = math.log2(math.e) / math.sqrt(HD)
    total = off[sources]

    @pl.when(i == 0)
    def _():
        def copy_source(s, carry):
            dst = pl.ds(pl.multiple_of(off[s], BLK), slot_rows)
            src = pl.ds(pl.multiple_of(s * slot_rows, BLK), slot_rows)
            kc[dst, :] = kvg[src, :HD]
            vc[dst, :HD] = kvg[src, HD:]
            return carry

        lax.fori_loop(0, sources, copy_source, 0)
        tail = pl.ds(pl.multiple_of(total, BLK), KT)
        kc[tail, :] = jnp.zeros((KT, HD), bf16)
        vc[tail, :HD] = jnp.zeros((KT, HD), bf16)
        vc[:, HD:] = jnp.ones((vc.shape[0], HD), bf16)
        vw[:, HD:] = jnp.ones((vw.shape[0], HD), bf16)
        for k, y in enumerate((y0, y1, y2, y3)):
            chunk = zp[0] ^ k
            dst = pl.ds(pl.multiple_of(chunk * TOK, TOK), TOK)
            qs[dst, :] = y[:, :HD]
            dst = pl.ds(pl.multiple_of(PAD + chunk * TOK, PAD), TOK)
            kw[dst, :] = y[:, HD : 2 * HD]
            vw[dst, :HD] = y[:, 2 * HD :]
        end = PAD + 4 * TOK
        gap = PAD - HALO
        kw[:gap, :] = jnp.zeros((gap, HD), bf16)
        vw[:gap, :HD] = jnp.zeros((gap, HD), bf16)
        kw[gap:PAD, :] = left[:, :HD]
        vw[gap:PAD, :HD] = left[:, HD:]
        kw[end : end + HALO, :] = right[:, :HD]
        vw[end : end + HALO, :HD] = right[:, HD:]
        kw[end + HALO :, :] = jnp.zeros((gap, HD), bf16)
        vw[end + HALO :, :HD] = jnp.zeros((gap, HD), bf16)
        send[...] = jnp.zeros(send.shape, f32)

    q = qs[pl.ds(pl.multiple_of(i * TOK, TOK), TOK), :]
    ids = qid[...]

    def scores(keys):
        return lax.dot_general(q, keys, (((1,), (1,)), ((), ())), preferred_element_type=f32)

    def step(s, values, state):
        m, acc = state
        new = jnp.max(s, axis=1, keepdims=True)
        if m is not None:
            new = jnp.maximum(m, new)
        w = jnp.exp2(s * coef - new * coef).astype(bf16)
        part = jnp.dot(w, values, preferred_element_type=f32)
        if m is not None:
            part = acc * jnp.exp2((m - new) * coef) + part
        return new, part

    window = TOK + 2 * PAD
    base = pl.multiple_of(i * TOK, TOK)
    s = scores(kw[pl.ds(base, window), :])
    s = jnp.where(ids == kid[0], s, NEG)
    state = step(s, vw[pl.ds(base, window), :], (None, None))

    def body(j, state):
        rows = pl.ds(pl.multiple_of(j * KT, KT), KT)
        return step(scores(kc[rows, :]), vc[rows, :], state)

    full = total // KT
    state = lax.fori_loop(0, full, body, state)
    rows = pl.ds(pl.multiple_of(full * KT, KT), KT)
    s = scores(kc[rows, :])
    col = lax.broadcasted_iota(jnp.int32, s.shape, 1)
    s = jnp.where(col < total - full * KT, s, NEG)
    m, acc = step(s, vc[rows, :], state)
    ob[...] = acc[:, :HD] / acc[:, HD:]

    def place(r, carry):
        dst = tgt[i * (TOK // 4) + r] * 4
        send[pl.ds(pl.multiple_of(dst, 4), 4), :] = ob[pl.ds(pl.multiple_of(r * 4, 4), 4), :]
        return carry

    lax.fori_loop(0, TOK // 4, place, 0, unroll=8)

    @pl.when(i == pl.num_programs(0) - 1)
    def _():
        out[...] = send[...].astype(bf16)


def attend(off, tgt, zp, ys, left, right, kvg, qid, kid, slots):
    chunks = len(ys)
    sources = off.shape[0] - 1
    cache_most = sources * LIVE_MOST * BLK
    whole = pl.BlockSpec(memory_space=pltpu.VMEM)
    window = TOK + 2 * PAD
    return pl.pallas_call(
        attention_kernel,
        out_shape=jax.ShapeDtypeStruct((slots * 4, HD), bf16),
        grid_spec=pltpu.PrefetchScalarGridSpec(
            num_scalar_prefetch=3,
            grid=(chunks,),
            in_specs=[whole] * 7
            + [
                pl.BlockSpec((TOK, 1), lambda i, *_: (i, 0)),
                pl.BlockSpec((1, 1, window), lambda i, *_: (i, 0, 0)),
            ],
            out_specs=whole,
            scratch_shapes=[
                pltpu.VMEM((cache_most + KT, HD), bf16),
                pltpu.VMEM((cache_most + KT, 2 * HD), bf16),
                pltpu.VMEM((chunks * TOK, HD), bf16),
                pltpu.VMEM((chunks * TOK + 2 * PAD, HD), bf16),
                pltpu.VMEM((chunks * TOK + 2 * PAD, 2 * HD), bf16),
                pltpu.VMEM((TOK, HD), f32),
                pltpu.VMEM((slots * 4, HD), f32),
            ],
        ),
        compiler_params=pltpu.CompilerParams(
            dimension_semantics=("arbitrary",), vmem_limit_bytes=48 << 20
        ),
        cost_estimate=pl.CostEstimate(
            flops=4 * 2048 * 7168 * 128, bytes_accessed=8 << 20, transcendentals=2048 * 7168
        ),
    )(off, tgt, zp, *ys, left, right, kvg, qid, kid)


def project_kernel(a0, a1, a2, a3, w0, w1, w2, w3, res, scale, mix, out, att, res32, proj):
    b = pl.program_id(0)
    groups = att.shape[0] // 48

    @pl.when(b == 0)
    def _():
        res32[...] = res[...].astype(f32)
        for k, a in enumerate((a0, a1, a2, a3)):
            for p in range(4):
                col = (k * 4 + p) * HD

                def move(g, carry):
                    src = pl.ds(pl.multiple_of(g * 192 + p * 48, 16), 48)
                    att[pl.ds(pl.multiple_of(g * 48, 16), 48), col : col + HD] = a[src, :]
                    return carry

                lax.fori_loop(0, groups, move, 0, unroll=4)

    total = None
    width = w0.shape[0]
    for k, w in enumerate((w0, w1, w2, w3)):
        part = jnp.dot(att[:, k * width : (k + 1) * width], w[...], preferred_element_type=f32)
        total = part if total is None else total + part
    total = total * scale[...]
    slots = out.shape[0]
    per = w0.shape[1] // HD
    for d in range(per):
        proj[d * 4 * slots : (d + 1) * 4 * slots, :] = total[:, d * HD : (d + 1) * HD]
    for d in range(per):
        parts = []
        for t in range(4):
            new = proj[pl.ds(d * 4 * slots + t, slots, stride=4), :]
            old = res32[pl.ds(t * 8 + b * per + d, slots, stride=32), :]
            parts.append((old + new).astype(bf16))
        rows = jnp.concatenate(parts, axis=1)
        out[:, d * 4 * HD : (d + 1) * 4 * HD] = jnp.dot(
            rows, mix[...], preferred_element_type=f32
        ).astype(bf16)


def project(atts, weights, res, scale, slots):
    width = weights[0].shape[1]
    part = 256
    whole = pl.BlockSpec(memory_space=pltpu.VMEM)
    source = np.arange(4 * HD)
    mix = np.zeros((4 * HD, 4 * HD), np.float32)
    mix[source, (source % HD) * 4 + source // HD] = 1.0
    return pl.pallas_call(
        project_kernel,
        out_shape=jax.ShapeDtypeStruct((slots, 4 * width), bf16),
        grid_spec=pltpu.PrefetchScalarGridSpec(
            num_scalar_prefetch=0,
            grid=(width // part,),
            in_specs=[whole] * 4
            + [pl.BlockSpec((weights[0].shape[0], part), lambda b: (0, b))] * 4
            + [whole, pl.BlockSpec((1, part), lambda b: (0, b)), whole],
            out_specs=pl.BlockSpec((slots, 4 * part), lambda b: (0, b)),
            scratch_shapes=[
                pltpu.VMEM((slots * 4, 16 * HD), bf16),
                pltpu.VMEM((slots * 32, HD), f32),
                pltpu.VMEM((slots * 4 * part // HD, HD), f32),
            ],
        ),
        compiler_params=pltpu.CompilerParams(
            dimension_semantics=("arbitrary",), vmem_limit_bytes=48 << 20
        ),
        cost_estimate=pl.CostEstimate(
            flops=2 * 768 * 2048 * 1024, bytes_accessed=16 << 20, transcendentals=0
        ),
    )(*atts, *weights, res, scale, jnp.asarray(mix, bf16))


def swap(x, axis, k):
    n = lax.axis_size(axis)
    return lax.ppermute(x, axis, [(i, i ^ k) for i in range(n)])


def tie(x, *others):
    return lax.optimization_barrier((x, *others))[0]


def shards(
    queries,
    keys_new,
    values_new,
    residual,
    layer_scale,
    out_weight,
    segment_ids,
    cache_keys,
    cache_values,
    block_live,
    recompute_block,
    recompute_hidden,
    key_weight,
    owners,
):
    tokens, columns = queries.shape
    heads = columns // HD
    n_seq = lax.axis_size(SEQ)
    seq = lax.axis_index(SEQ)
    zp = lax.axis_index("zp")
    head = lax.axis_index(HEAD)
    merged_rows = tokens // 4

    meta = jnp.concatenate(
        [segment_ids, owners[:, 0], block_live, jnp.zeros((128 - block_live.shape[0],), jnp.int32)]
    )
    meta = jnp.broadcast_to(meta[None, None, :], (n_seq, 1, meta.shape[0]))
    meta = lax.all_to_all(meta, SEQ, split_axis=0, concat_axis=0, tiled=True)[:, 0, :]
    ids_all = meta[:, :tokens].reshape(-1)
    owners_all = meta[:, tokens : tokens + merged_rows]
    live_all = meta[:, tokens + merged_rows : tokens + merged_rows + block_live.shape[0]]

    cache_rows = cache_keys.shape[0]
    block = recompute_block[0]
    fresh = jnp.dot(recompute_hidden, key_weight, preferred_element_type=f32)
    fresh_rows = seq * cache_rows + block * BLK + jnp.arange(BLK, dtype=jnp.int32)
    fresh = rotate(fresh.reshape(BLK, heads, HD), *rope_parts(fresh_rows % SEG_MOST))
    fresh = fresh.reshape(BLK, columns).astype(bf16)
    refreshed = lax.dynamic_update_slice(cache_keys, fresh, (block * BLK, 0))

    live = block_live > 0
    rank = jnp.cumsum(live.astype(jnp.int32)) - 1
    blocks = jnp.arange(block_live.shape[0], dtype=jnp.int32)
    hit = live[None, :] & (rank[None, :] == jnp.arange(LIVE_MOST, dtype=jnp.int32)[:, None])
    order = jnp.sum(jnp.where(hit, blocks[None, :], 0), axis=1)
    kv = pl.pallas_call(
        pack_kernel,
        out_shape=jax.ShapeDtypeStruct((heads, LIVE_MOST * BLK, 2 * HD), bf16),
        grid_spec=pltpu.PrefetchScalarGridSpec(
            num_scalar_prefetch=1,
            grid=(),
            in_specs=[pl.BlockSpec(memory_space=pltpu.VMEM)] * 2,
            out_specs=pl.BlockSpec(memory_space=pltpu.VMEM),
        ),
    )(order, refreshed, cache_values)
    kv = lax.all_to_all(kv, "zp", split_axis=0, concat_axis=0, tiled=True)
    kv = kv.reshape(heads * LIVE_MOST * BLK, 2 * HD)
    kv = lax.all_gather(kv, "zh", axis=0, tiled=True)
    kv = lax.all_gather(kv, "xh", axis=0, tiled=True)
    kvg = lax.all_gather(kv, "y", axis=0, tiled=True)
    counts = jnp.sum((live_all > 0).astype(jnp.int32), axis=1)
    sizes = tuple(lax.axis_size(a) for a in SEQ)
    counts = jnp.transpose(counts.reshape(sizes), (1, 0, 2, 3)).reshape(-1)
    upto = jnp.sum(
        jnp.where(
            jnp.arange(n_seq)[None, :] < jnp.arange(n_seq + 1)[:, None], counts[None, :], 0
        ),
        axis=1,
    )
    off = (upto * BLK).astype(jnp.int32)

    padded_ids = jnp.pad(ids_all, (PAD, PAD), constant_values=-1)
    near_ids = lax.dynamic_slice(padded_ids, (seq * tokens,), (PAD + tokens,))
    near_index = jnp.arange(PAD + tokens, dtype=jnp.int32)
    same = segment_ids[:, None] == near_ids[None, :]
    first = jnp.min(jnp.where(same, near_index[None, :], PAD + tokens), axis=1)
    own_pos = PAD + jnp.arange(tokens, dtype=jnp.int32) - first
    cosine, sine = rope_parts(own_pos)
    q = rotate(queries.astype(f32).reshape(tokens, heads, HD), cosine, sine).astype(bf16)
    k = rotate(keys_new.astype(f32).reshape(tokens, heads, HD), cosine, sine).astype(bf16)
    v = values_new.reshape(tokens, heads, HD)
    qkv = jnp.transpose(jnp.concatenate([q, k, v], axis=2), (1, 0, 2))
    ys = []
    for j in range(heads):
        part = lax.dynamic_index_in_dim(qkv, zp ^ j, 0, keepdims=False)
        ys.append(part if j == 0 else swap(part, "zp", j))
    tails = jnp.stack([y[tokens - HALO :, HD:] for y in ys])
    starts = jnp.stack([y[:HALO, HD:] for y in ys])
    up = [(i, i + heads) for i in range(n_seq - heads)]
    down = [(j, i) for i, j in up]
    left = lax.ppermute(
        lax.dynamic_index_in_dim(tails, zp ^ (heads - 1), 0, keepdims=False), SEQ, up
    )
    right = lax.ppermute(lax.dynamic_index_in_dim(starts, zp, 0, keepdims=False), SEQ, down)
    group = seq // heads
    span = heads * tokens
    group_ids = lax.dynamic_slice(padded_ids, (group * span,), (span + 2 * PAD,))
    qid = group_ids[PAD : PAD + span, None]
    kid = jnp.stack(
        [group_ids[j * tokens : j * tokens + tokens + 2 * PAD] for j in range(heads)]
    )[:, None, :]

    group_owners = lax.dynamic_slice(owners_all, (group * heads, 0), (heads, merged_rows))
    r = jnp.arange(merged_rows, dtype=jnp.int32)
    equal = group_owners[:, :, None] == group_owners[:, None, :]
    slot = jnp.sum((equal & (r[None, None, :] < r[None, :, None])).astype(jnp.int32), axis=2)
    peer = jnp.arange(heads, dtype=jnp.int32)[:, None]
    tgt = (group_owners * (heads * CAP) + peer * CAP + slot).reshape(-1)

    own_target = lax.dynamic_index_in_dim(group_owners * CAP + slot, zp, 0, keepdims=False)
    choose = (jnp.arange(n_seq * CAP, dtype=jnp.int32)[:, None] == own_target[None, :]).astype(bf16)
    width = residual.shape[1]
    res = jnp.dot(
        choose, residual.reshape(merged_rows, 4 * width), preferred_element_type=f32
    ).astype(bf16)
    res = res.reshape(n_seq, CAP * 4 * width // HD, HD)
    res = lax.all_to_all(res, SEQ, split_axis=0, concat_axis=0, tiled=True)
    res = res.reshape(n_seq * CAP * 4 * width // HD, HD)

    weights = []
    for j in range(lax.axis_size(HEAD)):
        part = lax.dynamic_slice(out_weight, (0, (head ^ j) * width), (columns, width))
        weights.append(part if j == 0 else swap(part, HEAD, j))

    sent = attend(off, tgt, zp[None].astype(jnp.int32), ys, left, right, kvg, qid, kid, n_seq * heads * CAP)
    got = lax.all_to_all(
        sent.reshape(n_seq, heads * CAP * 4, HD), SEQ, split_axis=0, concat_axis=0, tiled=True
    ).reshape(n_seq * heads * CAP * 4, HD)
    got_c = swap(got, HEAD, 1)
    got_x = swap(got, HEAD, 2)
    got_xc = swap(got_x, HEAD, 1)
    delivered = project(
        (got, got_c, got_x, got_xc), weights, res, layer_scale[None, :], n_seq * CAP
    )
    return (delivered, refreshed)


def solution(mesh):
    devices = np.asarray(mesh.devices).reshape(2, 4, 2, 4, 2, 2)
    fine = Mesh(devices, SEQ + HEAD)
    in_specs = (
        P(SEQ, HEAD),
        P(SEQ, HEAD),
        P(SEQ, HEAD),
        P(SEQ, HEAD),
        P(HEAD),
        P(HEAD, None),
        P(SEQ),
        P(SEQ, HEAD),
        P(SEQ, HEAD),
        P(SEQ),
        P(SEQ),
        P(SEQ, None),
        P(None, HEAD),
        P(SEQ, None),
    )
    out_specs = (P(SEQ, HEAD), P(SEQ, HEAD))
    return jax.shard_map(shards, mesh=fine, in_specs=in_specs, out_specs=out_specs, check_vma=False)
```

time: 625 us -> 313 us (0.50)
  blocking collectives: 218 us -> 21.4 us
  matrix products: 91.2 us -> 4.7 us
  local copies, waits for them, and re-layouts: 97.7 us -> 20.7 us
  starting transfers between devices: 12 us -> 87.4 us
  waiting for transfers between devices: 155 us -> 90.2 us
  Pallas kernels: 0 us -> 58.7 us
  other arithmetic: 31.5 us -> 9.57 us
    all_gather x1 -> x2, blocking collectives: 156 us -> 21.4 us  [the longest x1 12.4 us: shards(): kv = lax.all_gather(kv, 'zh', axis=0, tiled=True)]
    all_gather x2 -> x1, waiting for transfers between devices: 108 us -> 0.01 us  [shards(): kvg = lax.all_gather(kv, 'y', axis=0, tiled=True)]
    dot_general x36 -> x2, matrix products: 91.2 us -> 4.7 us  [the longest x1 2.92 us: shards(): fresh = jnp.dot(recompute_hidden, key_weight, preferred_element_type=f32)]
    ppermute x4 -> x11, waiting for transfers between devices: 0.01 us -> 73.4 us  [the longest x9 71.8 us: swap(): return lax.ppermute(x, axis, [(i, i ^ k) for i in range(n)])]
    all_to_all x1 -> x0, blocking collectives: 61.7 us -> none  [shards(): lax.all_to_all(outgoing.reshape(cycle_size, capacity, 4 * width_here), 's...]
    pallas_call x0 -> x3, Pallas kernels: none -> 58.7 us  [the longest x1 44 us: attend(): pl.pallas_call(attention_kernel, out_shape=jax.ShapeDtypeStruct((slots *...]
    while x113 -> x0, local copies, waits for them, and re-layouts: 47.8 us -> none
    reduce_scatter x1 -> x0, waiting for transfers between devices: 46.5 us -> none  [shards(): lax.psum_scatter(partial_proj.astype(jnp.bfloat16), 'head', scatter_dimen...]
  transfers between devices with their start and end apart: 7 -> 16, of which waited for: 2 -> 8; matrix products, arithmetic and copies ran while one was open for 4% -> 9% of each run, Pallas kernels for 0% -> 0%
where the time goes in v1:
time: 313 us; the launch traced here: 308 us
  waiting for transfers between devices  90.2 us (29%)
  starting transfers between devices  87.4 us (28%)
  Pallas kernels  58.7 us (19%)
  blocking collectives  21.4 us (7%)
  local copies, waits for them, and re-layouts  20.7 us (7%)
  between operations  15.1 us (5%)
  other arithmetic  9.57 us (3%)
  matrix products  4.7 us (2%)
    ppermute x9, waiting for transfers between devices, swap(): return lax.ppermute(x, axis, [(i, i ^ k) for i in range(n)])  71.8 us
    pallas_call x1, Pallas kernels, attend(): pl.pallas_call(attention_kernel, out_shape=jax.ShapeDtypeStruct((slots *...  44 us
    ppermute x9, starting transfers between devices, swap(): return lax.ppermute(x, axis, [(i, i ^ k) for i in range(n)])  37.7 us
    all_to_all x1, starting transfers between devices, shards(): lax.all_to_all(sent.reshape(n_seq, heads * CAP * 4, HD), SEQ, split_axis=...  14.2 us
    all_gather x1, blocking collectives, shards(): kv = lax.all_gather(kv, 'zh', axis=0, tiled=True)  12.4 us
    all_to_all x1, starting transfers between devices, shards(): lax.all_to_all(meta, SEQ, split_axis=0, concat_axis=0, tiled=True)[:, 0, :]  12.4 us
    pallas_call x1, Pallas kernels, project(): pl.pallas_call(project_kernel, out_shape=jax.ShapeDtypeStruct((slots, 4 *...  12.4 us
    all_to_all x1, waiting for transfers between devices, shards(): lax.all_to_all(sent.reshape(n_seq, heads * CAP * 4, HD), SEQ, split_axis=...  11.7 us
  transfers between devices with their start and end apart: 16, of which 8 were waited for; matrix products, arithmetic and copies ran while one was open for 9% of the time, Pallas kernels for 0%

profile of v1, /device:TPU:1, one launch (start us, length us, event | category | flops | bytes accessed | tf_op | source)
XLA Modules:
  0.0 307.9 jit_solution(10577232768791899415)
XLA Ops:
  8.9 2.9 fusion.14
  16.0 6.4 %all-to-all-start.1 = ((bf16[4,96,256]{2,1,0:T(8,128)(2,1)}), bf16[4,96,256]{2,1,0:T(8,128)(2,1)S(1)}, u32[]{:S(2)}, u32[]{:S(2)}) async-start(bf16[4,96,256]{2,1,0:T(8,128)(2,1)} %shard_map.158), calls=%async_computation.1 | async-start | bytes 393216 | tf_op jit(solution)/shard_map/all_to_all | solution.py:317
  22.5 5.1 %all-to-all-done.1 = bf16[4,96,256]{2,1,0:T(8,128)(2,1)S(1)} async-done(((bf16[4,96,256]{2,1,0:T(8,128)(2,1)}), bf16[4,96,256]{2,1,0:T(8,128)(2,1)S(1)}, u32[]{:S(2)}, u32[]{:S(2)}) %all-to-all-start.1) | async-done | bytes 196640 | tf_op jit(solution)/shard_map/all_to_all | solution.py:317
  28.4 12.4 %all-to-all-start = ((s32[64,1,768]{2,1,0:T(1,128)}), s32[64,1,768]{2,1,0:T(1,128)S(1)}, u32[]{:S(2)}, u32[]{:S(2)}) async-start(s32[64,1,768]{2,1,0:T(1,128)} %broadcast_in_dim.51), calls=%async_computation | async-start | bytes 393216 | tf_op jit(solution)/shard_map/all_to_all | solution.py:289
  40.9 12.4 %all_gather.9 = bf16[768,256]{1,0:T(8,128)(2,1)S(1)} all-gather(bf16[384,256]{1,0:T(8,128)(2,1)S(1)} %bitcast.77), channel_id=1, replica_groups=mesh['xh'=2,'y'=4,'zh'=2,'zp'=4,'xl'=2,'c'=2] {'zh'}, dimensions={0}, use_global_device_ids=true | all-gather | bytes 589824 | tf_op jit(solution)/shard_map/all_gather | solution.py:319
  53.2 9.0 %all_gather.10 = bf16[1536,256]{1,0:T(8,128)(2,1)} all-gather(bf16[768,256]{1,0:T(8,128)(2,1)S(1)} %all_gather.9), channel_id=1, replica_groups=mesh['xh'=2,'y'=4,'zh'=2,'zp'=4,'xl'=2,'c'=2] {'xh'}, dimensions={0}, use_global_device_ids=true | all-gather | bytes 1179648 | tf_op jit(solution)/shard_map/all_gather | solution.py:320
  64.7 3.2 %fusion.12 = (f32[512,4,64]{2,1,0:T(4,128)}, f32[512,4,64]{2,1,0:T(4,128)}, f32[512,4,64]{2,1,0:T(4,128)}, f32[512,4,64]{2,1,0:T(4,128)}) fusion(f32[512,4,128]{2,1,0:T(4,128)S(1)} %reshape.256, f32[512,4,128]{2,1,0:T(4,128)S(1)} %reshape.254), kind=kLoop, calls=%fused_computation.82 | loop fusion | bytes 4194304 | tf_op jit(solution)/shard_map/slice | solution.py:36
  70.9 3.6 %add_convert_fusion = (bf16[512,4,64]{2,0,1:T(8,128)(2,1)}, bf16[512,4,64]{2,0,1:T(8,128)(2,1)}, bf16[512,4,64]{2,0,1:T(8,128)(2,1)}, bf16[512,4,64]{2,0,1:T(8,128)(2,1)}) fusion(f32[512,4,64]{2,1,0:T(4,128)} %get-tuple-element.15, f32[512,4,64]{2,1,0:T(4,128)S(1)} %copy-done.3, f32[512,64]{1,0:T(8,128)S(1)} %get-tuple-element.37, ...), kind=kLoop, calls=%fused_computation.2 | loop fusion | flops 2097152 | bytes 3407872 | tf_op jit(solution)/shard_map/convert.6
  74.5 2.9 concatenate.16
  78.4 9.7 %collective-permute-start.2 = (bf16[512,384]{1,0:T(8,128)(2,1)}, bf16[512,384]{1,0:T(8,128)(2,1)S(1)}, u32[]{:S(2)}, u32[]{:S(2)}) collective-permute-start(bf16[512,384]{1,0:T(8,128)(2,1)} %get-tuple-element.10), channel_id=1, source_target_pairs={{0,12},{4,8},{8,4},{12,0},{1,13},{5,9},{9,5},{13,1},{2,14},{6,10},... | collective-permute-start | bytes 1179656 | tf_op jit(solution)/shard_map/ppermute | solution.py:254
  89.4 6.3 %collective-permute-done.2.y3 = bf16[512,384]{1,0:T(8,128)(2,1)S(1)} collective-permute-done((bf16[512,384]{1,0:T(8,128)(2,1)}, bf16[512,384]{1,0:T(8,128)(2,1)S(1)}, u32[]{:S(2)}, u32[]{:S(2)}) %collective-permute-start.2) | collective-permute-done | bytes 393248 | tf_op jit(solution)/shard_map/ppermute | solution.py:254
  95.8 21.8 %collective-permute-done.1.y2 = bf16[512,384]{1,0:T(8,128)(2,1)S(1)} collective-permute-done((bf16[512,384]{1,0:T(8,128)(2,1)}, bf16[512,384]{1,0:T(8,128)(2,1)S(1)}, u32[]{:S(2)}, u32[]{:S(2)}) %collective-permute-start.1) | collective-permute-done | bytes 393248 | tf_op jit(solution)/shard_map/ppermute | solution.py:254
  119.8 8.1 %collective-permute-start.3 = (bf16[208,256]{1,0:T(8,128)(2,1)}, bf16[208,256]{1,0:T(8,128)(2,1)S(1)}, u32[]{:S(2)}, u32[]{:S(2)}) collective-permute-start(bf16[208,256]{1,0:T(8,128)(2,1)} %fusion.7), channel_id=1, source_target_pairs={{0,16},{4,20},{8,24},{12,28},{16,32},{20,36},{24,40},{28,44},{32,4... | collective-permute-start | bytes 319496 | tf_op jit(solution)/shard_map/ppermute | solution.py:352
  129.9 44.0 %shard_map.159 = bf16[3072,128]{1,0:T(8,128)(2,1)} custom-call(s32[65]{0:T(128)S(1)} %broadcast_multiply_fusion.off, s32[512]{0:T(512)S(1)} %get-tuple-element.35.tgt, s32[1]{0:T(128)} %bitcast.3.zp, bf16[512,384]{1,0:T(8,128)(2,1)S(1)} %get-tuple-element.13.y0, bf16[512,384]{1,0:T(8,128)(2,1)S(1)} %collective-permute-done.y1, ...), custom_call_target="tpu_custom_call" | custom-call | flops 7516192768 | bytes 8388608 | tf_op jit(solution)/shard_map/pallas_call | solution.py:149
  173.9 14.2 %all-to-all-start.2 = ((bf16[64,48,128]{2,1,0:T(8,128)(2,1)}), bf16[64,48,128]{2,1,0:T(8,128)(2,1)S(1)}, u32[]{:S(2)}, u32[]{:S(2)}) async-start(bf16[64,48,128]{2,1,0:T(8,128)(2,1)} %bitcast.27), calls=%async_computation.2 | async-start | bytes 1572864 | tf_op jit(solution)/shard_map/all_to_all | solution.py:387
  193.5 11.7 %all-to-all-done.2 = bf16[64,48,128]{2,1,0:T(8,128)(2,1)S(1)} async-done(((bf16[64,48,128]{2,1,0:T(8,128)(2,1)}), bf16[64,48,128]{2,1,0:T(8,128)(2,1)S(1)}, u32[]{:S(2)}, u32[]{:S(2)}) %all-to-all-start.2) | async-done | bytes 786464 | tf_op jit(solution)/shard_map/all_to_all | solution.py:387
  205.2 7.3 %all-to-all-start.3 = ((bf16[64,96,128]{2,1,0:T(8,128)(2,1)}), bf16[64,96,128]{2,1,0:T(8,128)(2,1)}, u32[]{:S(2)}, u32[]{:S(2)}) async-start(bf16[64,96,128]{2,1,0:T(8,128)(2,1)} %reshape.251), calls=%async_computation.3 | async-start | bytes 3145728 | tf_op jit(solution)/shard_map/all_to_all | solution.py:378
  213.1 2.8 constant_dynamic-slice_fusion.1
  215.9 8.9 %collective-permute-start.10 = (bf16[512,1024]{1,0:T(8,128)(2,1)S(1)}, bf16[512,1024]{1,0:T(8,128)(2,1)S(1)}, u32[]{:S(2)}, u32[]{:S(2)}) collective-permute-start(bf16[512,1024]{1,0:T(8,128)(2,1)S(1)} %get-tuple-element.2), channel_id=1, source_target_pairs={{0,3},{1,2},{2,1},{3,0},{4,7},{5,6},{6,5},{7,4},{8,11},{9,10},{10,... | collective-permute-start | bytes 3145736 | tf_op jit(solution)/shard_map/ppermute | solution.py:254
  225.9 10.8 %collective-permute-done.6.a2 = bf16[3072,128]{1,0:T(8,128)(2,1)} collective-permute-done((bf16[3072,128]{1,0:T(8,128)(2,1)S(1)}, bf16[3072,128]{1,0:T(8,128)(2,1)}, u32[]{:S(2)}, u32[]{:S(2)}) %collective-permute-start.6) | collective-permute-done | bytes 786464 | tf_op jit(solution)/shard_map/ppermute | solution.py:254
  236.6 17.1 %collective-permute-start.7 = (bf16[3072,128]{1,0:T(8,128)(2,1)}, bf16[3072,128]{1,0:T(8,128)(2,1)}, u32[]{:S(2)}, u32[]{:S(2)}) collective-permute-start(bf16[3072,128]{1,0:T(8,128)(2,1)} %collective-permute-done.6.a2), channel_id=1, source_target_pairs={{0,1},{1,0},{2,3},{3,2},{4,5},{5,4},{6,7},{7,6},{8,9},{9,8},{10,11... | collective-permute-start | bytes 2359304 | tf_op jit(solution)/shard_map/ppermute | solution.py:254
  253.7 21.7 %collective-permute-done.10.w3 = bf16[512,1024]{1,0:T(8,128)(2,1)S(1)} collective-permute-done((bf16[512,1024]{1,0:T(8,128)(2,1)S(1)}, bf16[512,1024]{1,0:T(8,128)(2,1)S(1)}, u32[]{:S(2)}, u32[]{:S(2)}) %collective-permute-start.10) | collective-permute-done | bytes 1048608 | tf_op jit(solution)/shard_map/ppermute | solution.py:254
  276.4 11.2 %collective-permute-done.9.w2 = bf16[512,1024]{1,0:T(8,128)(2,1)} collective-permute-done((bf16[512,1024]{1,0:T(8,128)(2,1)S(1)}, bf16[512,1024]{1,0:T(8,128)(2,1)}, u32[]{:S(2)}, u32[]{:S(2)}) %collective-permute-start.9) | collective-permute-done | bytes 1048608 | tf_op jit(solution)/shard_map/ppermute | solution.py:254
  288.7 12.4 %shard_map.160 = bf16[192,4096]{1,0:T(8,128)(2,1)} custom-call(bf16[3072,128]{1,0:T(8,128)(2,1)S(1)} %bitcast.69, bf16[3072,128]{1,0:T(8,128)(2,1)} %collective-permute-done.5.a1, bf16[3072,128]{1,0:T(8,128)(2,1)} %collective-permute-done.6.a2, bf16[3072,128]{1,0:T(8,128)(2,1)} %collective-permute-done.7.a3, bf16[512,1024]{1,0:T(8,128)(2,1)S(1)} %get-tuple-element.4.w0, ...), custom_call_target="tpu_custom_call" | custom-call | flops 3221225472 | bytes 16777216 | tf_op jit(solution)/shard_map/pallas_call | solution.py:227
  (98 shorter events, 26.9 us)
Async XLA Ops:
  7.2 55.2 %copy-start = (bf16[512,512]{1,0:T(8,128)(2,1)S(1)}, bf16[512,512]{1,0:T(8,128)(2,1)}, u32[]{:S(2)}) copy-start(bf16[512,512]{1,0:T(8,128)(2,1)} %param.17) | copy-start | bytes 1572868
  8.2 3.9 %copy-start.8 = (f32[64]{0:T(128)}, f32[64]{0:T(128)S(1)}, u32[]{:S(2)}) copy-start(f32[64]{0:T(128)S(1)} %multiply_power_fusion) | copy-start | bytes 772
  8.9 13.6 %copy-start.7 = (s32[512]{0:T(512)S(1)}, s32[512]{0:T(512)}, u32[]{:S(2)}) copy-start(s32[512]{0:T(512)} %param.21) | copy-start | bytes 6148
  8.9 13.6 %copy-start.11 = (s32[128,1]{0,1:T(1,128)S(1)}, s32[128,1]{0,1:T(1,128)}, u32[]{:S(2)}) copy-start(s32[128,1]{0,1:T(1,128)} %param.28) | copy-start | bytes 1540
  16.0 11.6 %all-to-all-start.1 = ((bf16[4,96,256]{2,1,0:T(8,128)(2,1)}), bf16[4,96,256]{2,1,0:T(8,128)(2,1)S(1)}, u32[]{:S(2)}, u32[]{:S(2)}) async-start(bf16[4,96,256]{2,1,0:T(8,128)(2,1)} %shard_map.158), calls=%async_computation.1 | async-start | bytes 393216 | tf_op jit(solution)/shard_map/all_to_all | solution.py:317
  28.4 39.5 %all-to-all-start = ((s32[64,1,768]{2,1,0:T(1,128)}), s32[64,1,768]{2,1,0:T(1,128)S(1)}, u32[]{:S(2)}, u32[]{:S(2)}) async-start(s32[64,1,768]{2,1,0:T(1,128)} %broadcast_in_dim.51), calls=%async_computation | async-start | bytes 393216 | tf_op jit(solution)/shard_map/all_to_all | solution.py:289
  40.8 89.1 %all-gather.2.cloned.1.call-start = ((), (), s32[]{:S(2)}) async-start(), calls=%async_computation.4 | async-start | bytes 3932160 | tf_op jit(solution)/shard_map/all_gather | solution.py:321
  53.2 9.7 %copy-start.5 = (bf16[512,512]{1,0:T(8,128)(2,1)S(1)}, bf16[512,512]{1,0:T(8,128)(2,1)}, u32[]{:S(2)}) copy-start(bf16[512,512]{1,0:T(8,128)(2,1)} %param.15) | copy-start | bytes 1572868
  77.4 11.9 %copy-start.9 = (s32[4]{0:T(128)S(1)}, s32[4]{0:T(128)}, u32[]{:S(2)}) copy-start(s32[4]{0:T(128)} %iota_multiply_fusion) | copy-start | bytes 52
  78.4 17.3 %collective-permute-start.2 = (bf16[512,384]{1,0:T(8,128)(2,1)}, bf16[512,384]{1,0:T(8,128)(2,1)S(1)}, u32[]{:S(2)}, u32[]{:S(2)}) collective-permute-start(bf16[512,384]{1,0:T(8,128)(2,1)} %get-tuple-element.10), channel_id=1, source_target_pairs={{0,12},{4,8},{8,4},{12,0},{1,13},{5,9},{9,5},{13,1},{2,14},{6,10},... | collective-permute-start | bytes 1179656 | tf_op jit(solution)/shard_map/ppermute | solution.py:254
  88.2 29.4 %collective-permute-start.1 = (bf16[512,384]{1,0:T(8,128)(2,1)}, bf16[512,384]{1,0:T(8,128)(2,1)S(1)}, u32[]{:S(2)}, u32[]{:S(2)}) collective-permute-start(bf16[512,384]{1,0:T(8,128)(2,1)} %get-tuple-element.11), channel_id=1, source_target_pairs={{0,8},{4,12},{8,0},{12,4},{1,9},{5,13},{9,1},{13,5},{2,10},{6,14},... | collective-permute-start | bytes 1179656 | tf_op jit(solution)/shard_map/ppermute | solution.py:254
  88.2 29.4 %collective-permute-start = (bf16[512,384]{1,0:T(8,128)(2,1)S(1)}, bf16[512,384]{1,0:T(8,128)(2,1)S(1)}, u32[]{:S(2)}, u32[]{:S(2)}) collective-permute-start(bf16[512,384]{1,0:T(8,128)(2,1)S(1)} %get-tuple-element.12), channel_id=1, source_target_pairs={{0,4},{4,0},{8,12},{12,8},{1,5},{5,1},{9,13},{13,9},{2,6},{6,2},{1... | collective-permute-start | bytes 1179656 | tf_op jit(solution)/shard_map/ppermute | solution.py:254
  117.7 10.6 %collective-permute-start.4 = (bf16[208,256]{1,0:T(8,128)(2,1)S(1)}, bf16[208,256]{1,0:T(8,128)(2,1)S(1)}, u32[]{:S(2)}, u32[]{:S(2)}) collective-permute-start(bf16[208,256]{1,0:T(8,128)(2,1)S(1)} %fusion.3), channel_id=1, source_target_pairs={{16,0},{20,4},{24,8},{28,12},{32,16},{36,20},{40,24},{44,28},{48,3... | collective-permute-start | bytes 319496 | tf_op jit(solution)/shard_map/ppermute | solution.py:355
  119.8 10.1 %collective-permute-start.3 = (bf16[208,256]{1,0:T(8,128)(2,1)}, bf16[208,256]{1,0:T(8,128)(2,1)S(1)}, u32[]{:S(2)}, u32[]{:S(2)}) collective-permute-start(bf16[208,256]{1,0:T(8,128)(2,1)} %fusion.7), channel_id=1, source_target_pairs={{0,16},{4,20},{8,24},{12,28},{16,32},{20,36},{24,40},{28,44},{32,4... | collective-permute-start | bytes 319496 | tf_op jit(solution)/shard_map/ppermute | solution.py:352
  173.9 14.2 %copy-start.4 = (bf16[512,1024]{1,0:T(8,128)(2,1)S(1)}, bf16[512,1024]{1,0:T(8,128)(2,1)}, u32[]{:S(2)}) copy-start(bf16[512,1024]{1,0:T(8,128)(2,1)} %param.18) | copy-start | bytes 3145732
  173.9 31.3 %all-to-all-start.2 = ((bf16[64,48,128]{2,1,0:T(8,128)(2,1)}), bf16[64,48,128]{2,1,0:T(8,128)(2,1)S(1)}, u32[]{:S(2)}, u32[]{:S(2)}) async-start(bf16[64,48,128]{2,1,0:T(8,128)(2,1)} %bitcast.27), calls=%async_computation.2 | async-start | bytes 1572864 | tf_op jit(solution)/shard_map/all_to_all | solution.py:387
  205.2 82.5 %all-to-all-start.3 = ((bf16[64,96,128]{2,1,0:T(8,128)(2,1)}), bf16[64,96,128]{2,1,0:T(8,128)(2,1)}, u32[]{:S(2)}, u32[]{:S(2)}) async-start(bf16[64,96,128]{2,1,0:T(8,128)(2,1)} %reshape.251), calls=%async_computation.3 | async-start | bytes 3145728 | tf_op jit(solution)/shard_map/all_to_all | solution.py:378
  212.5 24.2 %collective-permute-start.6 = (bf16[3072,128]{1,0:T(8,128)(2,1)S(1)}, bf16[3072,128]{1,0:T(8,128)(2,1)}, u32[]{:S(2)}, u32[]{:S(2)}) collective-permute-start(bf16[3072,128]{1,0:T(8,128)(2,1)S(1)} %bitcast.67), channel_id=1, source_target_pairs={{0,2},{1,3},{2,0},{3,1},{4,6},{5,7},{6,4},{7,5},{8,10},{9,11},{10,... | collective-permute-start | bytes 2359304 | tf_op jit(solution)/shard_map/ppermute | solution.py:254
  213.1 74.5 %copy-start.1 = (f32[1024]{0:T(1024)S(1)}, f32[1024]{0:T(1024)}, u32[]{:S(2)}) copy-start(f32[1024]{0:T(1024)} %param.19) | copy-start | bytes 12292
  215.9 59.5 %collective-permute-start.10 = (bf16[512,1024]{1,0:T(8,128)(2,1)S(1)}, bf16[512,1024]{1,0:T(8,128)(2,1)S(1)}, u32[]{:S(2)}, u32[]{:S(2)}) collective-permute-start(bf16[512,1024]{1,0:T(8,128)(2,1)S(1)} %get-tuple-element.2), channel_id=1, source_target_pairs={{0,3},{1,2},{2,1},{3,0},{4,7},{5,6},{6,5},{7,4},{8,11},{9,10},{10,... | collective-permute-start | bytes 3145736 | tf_op jit(solution)/shard_map/ppermute | solution.py:254
  224.8 50.7 %collective-permute-start.8 = (bf16[512,1024]{1,0:T(8,128)(2,1)S(1)}, bf16[512,1024]{1,0:T(8,128)(2,1)S(1)}, u32[]{:S(2)}, u32[]{:S(2)}) collective-permute-start(bf16[512,1024]{1,0:T(8,128)(2,1)S(1)} %get-tuple-element.3), channel_id=1, source_target_pairs={{0,1},{1,0},{2,3},{3,2},{4,5},{5,4},{6,7},{7,6},{8,9},{9,8},{10,11... | collective-permute-start | bytes 3145736 | tf_op jit(solution)/shard_map/ppermute | solution.py:254
  224.8 62.9 %collective-permute-start.9 = (bf16[512,1024]{1,0:T(8,128)(2,1)S(1)}, bf16[512,1024]{1,0:T(8,128)(2,1)}, u32[]{:S(2)}, u32[]{:S(2)}) collective-permute-start(bf16[512,1024]{1,0:T(8,128)(2,1)S(1)} %get-tuple-element.5), channel_id=1, source_target_pairs={{0,2},{1,3},{2,0},{3,1},{4,6},{5,7},{6,4},{7,5},{8,10},{9,11},{10,... | collective-permute-start | bytes 3145736 | tf_op jit(solution)/shard_map/ppermute | solution.py:254
  225.1 62.5 %collective-permute-start.5 = (bf16[3072,128]{1,0:T(8,128)(2,1)S(1)}, bf16[3072,128]{1,0:T(8,128)(2,1)}, u32[]{:S(2)}, u32[]{:S(2)}) collective-permute-start(bf16[3072,128]{1,0:T(8,128)(2,1)S(1)} %bitcast.68), channel_id=1, source_target_pairs={{0,1},{1,0},{2,3},{3,2},{4,5},{5,4},{6,7},{7,6},{8,9},{9,8},{10,11... | collective-permute-start | bytes 2359304 | tf_op jit(solution)/shard_map/ppermute | solution.py:254
  236.6 51.0 %collective-permute-start.7 = (bf16[3072,128]{1,0:T(8,128)(2,1)}, bf16[3072,128]{1,0:T(8,128)(2,1)}, u32[]{:S(2)}, u32[]{:S(2)}) collective-permute-start(bf16[3072,128]{1,0:T(8,128)(2,1)} %collective-permute-done.6.a2), channel_id=1, source_target_pairs={{0,1},{1,0},{2,3},{3,2},{4,5},{5,4},{6,7},{7,6},{8,9},{9,8},{10,11... | collective-permute-start | bytes 2359304 | tf_op jit(solution)/shard_map/ppermute | solution.py:254
  (5 other events, 8.7 us)
Sparse Core Ops, SparseCore 0:
  62.4 49.4 all-gather.1

commit v2 on v1

v2 whole, which is shorter than its diff:
```python
import math

import jax
import jax.numpy as jnp
import numpy as np
from jax import lax
from jax.experimental import pallas as pl
from jax.experimental.pallas import tpu as pltpu
from jax.sharding import Mesh, PartitionSpec as P

HD = 128
BLK = 16
SEG_MOST = 201
LIVE_MOST = 6
CAP = 3
HALO = 208
PAD = 256
TOK = 512
KT = 2048
NEG = -1e30
SEQ = ("xh", "y", "zh", "zp")
HEAD = ("xl", "c")
bf16 = jnp.bfloat16
f32 = jnp.float32


def rope_parts(positions):
    half = HD // 2
    freqs = 100.0 ** (-jnp.arange(half, dtype=f32) / half)
    angles = positions.astype(f32)[:, None] * freqs[None, :]
    return jnp.cos(angles), jnp.sin(angles)


def rotate(vectors, cosine, sine):
    half = HD // 2
    a, b = vectors[..., :half], vectors[..., half:]
    c, s = cosine[:, None, :], sine[:, None, :]
    return jnp.concatenate([a * c - b * s, b * c + a * s], axis=-1)


def pack_kernel(idx, k_ref, v_ref, out_ref):
    heads = out_ref.shape[0]
    for j in range(LIVE_MOST):
        rows = pl.ds(pl.multiple_of(idx[j] * BLK, BLK), BLK)
        k = k_ref[rows, :]
        v = v_ref[rows, :]
        for p in range(heads):
            out_ref[p, j * BLK : (j + 1) * BLK, :HD] = k[:, p * HD : (p + 1) * HD]
            out_ref[p, j * BLK : (j + 1) * BLK, HD:] = v[:, p * HD : (p + 1) * HD]


def rope_kernel(q_ref, k_ref, v_ref, c_ref, s_ref, out_ref):
    c = c_ref[...]
    s = s_ref[...]
    for h in range(out_ref.shape[0]):
        cols = slice(h * HD, (h + 1) * HD)
        for j, ref in enumerate((q_ref, k_ref)):
            x = ref[:, cols].astype(f32)
            turned = x * c + pltpu.roll(x, HD // 2, 1) * s
            out_ref[h, :, j * HD : (j + 1) * HD] = turned.astype(bf16)
        out_ref[h, :, 2 * HD :] = v_ref[:, cols]


def attention_kernel(off, tgt, zp, *refs):
    chunks = 4
    ys = refs[:chunks]
    left, right, ids = refs[chunks : chunks + 3]
    pieces = refs[chunks + 3 : -13]
    out, kc, vc, qs, kw, vw, ob, send, mx, ac, idcol, gathered, sems = refs[-13:]
    i = pl.program_id(0)
    sources = off.shape[0] - 1
    slot_rows = LIVE_MOST * BLK
    coef = math.log2(math.e) / math.sqrt(HD)
    total = off[sources]

    @pl.when(i == 0)
    def _():
        copies = []
        row = 0
        for n, piece in enumerate(pieces):
            to = gathered.at[pl.ds(row, piece.shape[0])]
            copies.append(pltpu.make_async_copy(piece, to, sems.at[n]))
            row += piece.shape[0]
        for copy in copies:
            copy.start()
        vc[:, HD:] = jnp.ones((vc.shape[0], HD), bf16)
        vw[:, HD:] = jnp.ones((vw.shape[0], HD), bf16)
        for k, y in enumerate(ys):
            chunk = zp[0] ^ k
            dst = pl.ds(pl.multiple_of(chunk * TOK, TOK), TOK)
            qs[dst, :] = y[:, :HD]
            dst = pl.ds(pl.multiple_of(PAD + chunk * TOK, PAD), TOK)
            kw[dst, :] = y[:, HD : 2 * HD]
            vw[dst, :HD] = y[:, 2 * HD :]
        end = PAD + chunks * TOK
        gap = PAD - HALO
        kw[:gap, :] = jnp.zeros((gap, HD), bf16)
        vw[:gap, :HD] = jnp.zeros((gap, HD), bf16)
        kw[gap:PAD, :] = left[:, :HD]
        vw[gap:PAD, :HD] = left[:, HD:]
        kw[end : end + HALO, :] = right[:, :HD]
        vw[end : end + HALO, :HD] = right[:, HD:]
        kw[end + HALO :, :] = jnp.zeros((gap, HD), bf16)
        vw[end + HALO :, :HD] = jnp.zeros((gap, HD), bf16)
        send[...] = jnp.zeros(send.shape, f32)
        for copy in copies:
            copy.wait()

        def copy_source(s, carry):
            dst = pl.ds(pl.multiple_of(off[s], BLK), slot_rows)
            src = pl.ds(pl.multiple_of(s * slot_rows, BLK), slot_rows)
            kc[dst, :] = gathered[src, :HD]
            vc[dst, :HD] = gathered[src, HD:]
            return carry

        lax.fori_loop(0, sources, copy_source, 0, unroll=2)
        tail = pl.ds(pl.multiple_of(total, BLK), KT)
        kc[tail, :] = jnp.zeros((KT, HD), bf16)
        vc[tail, :HD] = jnp.zeros((KT, HD), bf16)

    base = pl.multiple_of(i * TOK, TOK)
    sub = 128
    parts = TOK // sub
    wide = sub + 2 * PAD
    for b in range(parts):
        line = ids[:, pl.ds(pl.multiple_of(base + PAD + b * sub, sub), sub)]
        idcol[b * sub : (b + 1) * sub, :] = jnp.transpose(jnp.broadcast_to(line, (sub, sub)))

    def scores(b, keys):
        q = qs[pl.ds(pl.multiple_of(base + b * sub, sub), sub), :]
        return lax.dot_general(q, keys, (((1,), (1,)), ((), ())), preferred_element_type=f32)

    def weigh(s, m):
        new = jnp.max(s, axis=1, keepdims=True)
        if m is not None:
            new = jnp.maximum(m, new)
        return new, jnp.exp2(s * coef - new * coef).astype(bf16)

    for b in range(parts):
        rows = pl.ds(pl.multiple_of(base + b * sub, sub), wide)
        s = scores(b, kw[rows, :])
        near = ids[:, rows]
        s = jnp.where(idcol[b * sub : (b + 1) * sub, :1] == near, s, NEG)
        new, w = weigh(s, None)
        mx[b * sub : (b + 1) * sub, :] = new
        ac[b * sub : (b + 1) * sub, :] = jnp.dot(w, vw[rows, :], preferred_element_type=f32)

    def visit(start, size, masked):
        rows = pl.ds(pl.multiple_of(start, size // 2), size)
        keys, values = kc[rows, :], vc[rows, :]

        def rows_of(b, carry):
            s = scores(b, keys)
            if masked:
                col = lax.broadcasted_iota(jnp.int32, s.shape, 1)
                s = jnp.where(col < total - start, s, NEG)
            here = pl.ds(pl.multiple_of(b * sub, sub), sub)
            m = mx[here, :]
            new, w = weigh(s, m)
            mx[here, :] = new
            part = jnp.dot(w, values, preferred_element_type=f32)
            ac[here, :] = ac[here, :] * jnp.exp2((m - new) * coef) + part
            return carry

        lax.fori_loop(0, parts, rows_of, 0, unroll=2 if masked else True)

    def loop(j, carry):
        visit(j * KT, KT, False)
        return carry

    full = total // KT
    rest = total - full * KT
    lax.fori_loop(0, full, loop, 0)

    @pl.when(rest > KT // 2)
    def _():
        visit(full * KT, KT, True)

    @pl.when((rest > 0) & (rest <= KT // 2))
    def _():
        visit(full * KT, KT // 2, True)

    ob[...] = ac[:, :HD] / ac[:, HD:]

    def place(r, carry):
        dst = tgt[i * (TOK // 4) + r] * 4
        send[pl.ds(pl.multiple_of(dst, 4), 4), :] = ob[pl.ds(pl.multiple_of(r * 4, 4), 4), :]
        return carry

    lax.fori_loop(0, TOK // 4, place, 0, unroll=8)

    @pl.when(i == pl.num_programs(0) - 1)
    def _():
        out[...] = send[...].astype(bf16)


def attend(off, tgt, zp, ys, left, right, ids, pieces, slots):
    chunks = len(ys)
    sources = off.shape[0] - 1
    cache_most = sources * LIVE_MOST * BLK
    whole = pl.BlockSpec(memory_space=pltpu.VMEM)
    return pl.pallas_call(
        attention_kernel,
        out_shape=jax.ShapeDtypeStruct((slots * 4, HD), bf16),
        grid_spec=pltpu.PrefetchScalarGridSpec(
            num_scalar_prefetch=3,
            grid=(chunks,),
            in_specs=[whole] * (chunks + 3)
            + [pl.BlockSpec(memory_space=pl.ANY)] * len(pieces),
            out_specs=whole,
            scratch_shapes=[
                pltpu.VMEM((cache_most + KT, HD), bf16),
                pltpu.VMEM((cache_most + KT, 2 * HD), bf16),
                pltpu.VMEM((chunks * TOK, HD), bf16),
                pltpu.VMEM((chunks * TOK + 2 * PAD, HD), bf16),
                pltpu.VMEM((chunks * TOK + 2 * PAD, 2 * HD), bf16),
                pltpu.VMEM((TOK, HD), f32),
                pltpu.VMEM((slots * 4, HD), f32),
                pltpu.VMEM((TOK, 1), f32),
                pltpu.VMEM((TOK, 2 * HD), f32),
                pltpu.VMEM((TOK, 128), f32),
                pltpu.VMEM((cache_most, 2 * HD), bf16),
                pltpu.SemaphoreType.DMA((len(pieces),)),
            ],
        ),
        compiler_params=pltpu.CompilerParams(
            dimension_semantics=("arbitrary",), vmem_limit_bytes=48 << 20
        ),
        cost_estimate=pl.CostEstimate(
            flops=4 * 2048 * 7168 * 128, bytes_accessed=8 << 20, transcendentals=2048 * 7168
        ),
    )(off, tgt, zp, *ys, left, right, ids, *pieces)


def project_kernel(core, a0, a1, a2, a3, weights, res, scale, mix, out, att, pick):
    b = pl.program_id(0)
    c = core[1]
    groups = a0.shape[0] // (8 * 48)

    @pl.when(b == 0)
    def _():
        slot = lax.broadcasted_iota(jnp.int32, pick.shape, 0)
        row = lax.broadcasted_iota(jnp.int32, pick.shape, 1)
        slots = out.shape[0]
        pick[...] = (row == (slot % slots) * 4 + slot // slots).astype(bf16)
        for k, a in enumerate((a0, a1, a2, a3)):

            def move(g, carry):
                to = pl.ds(pl.multiple_of((g * 2 + (c ^ (k % 2))) * 48, 16), 48)
                for p in range(8):
                    block = (core[0] ^ (k // 2)) * 2 + p // 4
                    src = pl.ds(pl.multiple_of(g * 384 + p * 48, 16), 48)
                    att[block, to, (p % 4) * HD : (p % 4 + 1) * HD] = a[src, :]
                return carry

            lax.fori_loop(0, groups, move, 0)

    total = None
    for k in range(4):
        part = jnp.dot(att[k], weights[k], preferred_element_type=f32)
        total = part if total is None else total + part
    layer = (res[...].astype(f32) + total * scale[...]).astype(bf16)
    turns = jnp.dot(pick[...], layer, preferred_element_type=f32).astype(bf16)
    slots = out.shape[0]
    for d in range(weights.shape[2] // HD):
        cols = slice(d * HD, (d + 1) * HD)
        rows = jnp.concatenate([turns[t * slots : (t + 1) * slots, cols] for t in range(4)], axis=1)
        out[:, d * 4 * HD : (d + 1) * 4 * HD] = jnp.dot(
            rows, mix[...], preferred_element_type=f32
        ).astype(bf16)


def project(core, atts, weights, res, scale, slots):
    width = weights.shape[2]
    part = 256
    whole = pl.BlockSpec(memory_space=pltpu.VMEM)
    source = np.arange(4 * HD)
    mix = np.zeros((4 * HD, 4 * HD), np.float32)
    mix[source, (source % HD) * 4 + source // HD] = 1.0
    return pl.pallas_call(
        project_kernel,
        out_shape=jax.ShapeDtypeStruct((slots, 4 * width), bf16),
        grid_spec=pltpu.PrefetchScalarGridSpec(
            num_scalar_prefetch=1,
            grid=(width // part,),
            in_specs=[whole] * 4
            + [pl.BlockSpec((*weights.shape[:2], part), lambda b, *_: (0, 0, b))]
            + [pl.BlockSpec((slots * 4, part), lambda b, *_: (0, b)), pl.BlockSpec((1, part), lambda b, *_: (0, b)), whole],
            out_specs=pl.BlockSpec((slots, 4 * part), lambda b, *_: (0, b)),
            scratch_shapes=[
                pltpu.VMEM((4, slots * 4, 4 * HD), bf16),
                pltpu.VMEM((slots * 4, slots * 4), bf16),
            ],
        ),
        compiler_params=pltpu.CompilerParams(
            dimension_semantics=("arbitrary",), vmem_limit_bytes=48 << 20
        ),
        cost_estimate=pl.CostEstimate(
            flops=2 * 768 * 2048 * 1024, bytes_accessed=16 << 20, transcendentals=0
        ),
    )(core, *atts, weights, res, scale, jnp.asarray(mix, bf16))


def swap(x, axis, k):
    n = lax.axis_size(axis)
    return lax.ppermute(x, axis, [(i, i ^ k) for i in range(n)])


def tie(x, *others):
    return lax.optimization_barrier((x, *others))[0]


def shards(
    queries,
    keys_new,
    values_new,
    residual,
    layer_scale,
    out_weight,
    segment_ids,
    cache_keys,
    cache_values,
    block_live,
    recompute_block,
    recompute_hidden,
    key_weight,
    owners,
):
    tokens, columns = queries.shape
    heads = columns // HD
    n_head = lax.axis_size(HEAD)
    n_seq = lax.axis_size(SEQ)
    seq = lax.axis_index(SEQ)
    xh, y, zp, xl, c = (lax.axis_index(n) for n in ("xh", "y", "zp", "xl", "c"))
    head = lax.axis_index(HEAD)
    merged_rows = tokens // 4
    group = (xh * 4 + y) * 2 + c
    n_group = n_seq // heads
    whole = pl.BlockSpec(memory_space=pltpu.VMEM)

    marks = segment_ids + 1
    n_blocks = block_live.shape[0]
    meta = jnp.concatenate(
        [marks, owners[:, 0], block_live, jnp.zeros((128 - n_blocks,), jnp.int32)]
    )
    meta = jnp.broadcast_to(meta[None, None, :], (n_seq, 1, meta.shape[0]))
    meta = lax.all_to_all(meta, SEQ, split_axis=0, concat_axis=0, tiled=True)[:, 0, :]
    marks_all = jnp.pad(meta[:, :tokens].reshape(-1), (PAD, PAD))

    near = lax.dynamic_slice(marks_all, (seq * tokens,), (PAD + tokens,))
    same = marks[:, None] == near[None, :]
    index = jnp.arange(PAD + tokens, dtype=jnp.int32)
    first = jnp.min(jnp.where(same, index[None, :], PAD + tokens), axis=1)
    cosine, sine = rope_parts(PAD + jnp.arange(tokens, dtype=jnp.int32) - first)

    qkv = pl.pallas_call(
        rope_kernel,
        out_shape=jax.ShapeDtypeStruct((heads, tokens, 3 * HD), bf16),
        in_specs=[whole] * 5,
        out_specs=whole,
    )(
        queries,
        keys_new,
        values_new,
        jnp.concatenate([cosine, cosine], axis=1),
        jnp.concatenate([-sine, sine], axis=1),
    )

    cache_rows = cache_keys.shape[0]
    block = recompute_block[0]
    fresh = jnp.dot(recompute_hidden, key_weight, preferred_element_type=f32)
    fresh_rows = seq * cache_rows + block * BLK + jnp.arange(BLK, dtype=jnp.int32)
    fresh = rotate(fresh.reshape(BLK, heads, HD), *rope_parts(fresh_rows % SEG_MOST))
    fresh = fresh.reshape(BLK, columns).astype(bf16)
    refreshed = lax.dynamic_update_slice(cache_keys, fresh, (block * BLK, 0))

    live = block_live > 0
    blocks = jnp.arange(n_blocks, dtype=jnp.int32)
    rank = jnp.sum(jnp.where(blocks[None, :] < blocks[:, None], live[None, :], False), axis=1)
    hit = live[None, :] & (rank[None, :] == jnp.arange(LIVE_MOST, dtype=jnp.int32)[:, None])
    order = jnp.sum(jnp.where(hit, blocks[None, :], 0), axis=1)
    kv = pl.pallas_call(
        pack_kernel,
        out_shape=jax.ShapeDtypeStruct((heads, LIVE_MOST * BLK, 2 * HD), bf16),
        grid_spec=pltpu.PrefetchScalarGridSpec(
            num_scalar_prefetch=1, grid=(), in_specs=[whole] * 2, out_specs=whole
        ),
    )(order, refreshed, cache_values)

    def spread(x, j):
        pairs = []
        for a in range(2):
            for b in range(heads):
                for d in range(2):
                    pairs.append(((a * heads + b) * 2 + d, (d * heads + (b ^ j)) * 2 + a))
        part = lax.dynamic_index_in_dim(x, zp ^ j, 0, keepdims=False)
        return lax.ppermute(part, ("zh", "zp", "c"), pairs)

    kv4 = jnp.concatenate([spread(kv, j) for j in range(heads)], axis=0)
    ys = [spread(qkv, j) for j in range(heads)]

    kv4 = tie(kv4, qkv)
    kv8 = jnp.concatenate([kv4, swap(kv4, "xh", 1)], axis=0)
    kv32 = lax.all_gather(kv8, "y", axis=0, tiled=True)
    pieces = [kv32, swap(kv32, "c", 1)]

    owners_all = meta[:, tokens : tokens + merged_rows]
    live_all = meta[:, tokens + merged_rows : tokens + merged_rows + n_blocks]
    counts = jnp.sum((live_all > 0).astype(jnp.int32), axis=1)
    j4 = jnp.arange(heads, dtype=jnp.int32) ^ zp
    x2 = jnp.arange(2, dtype=jnp.int32) ^ xh
    y4 = jnp.arange(4, dtype=jnp.int32)
    c2 = jnp.arange(2, dtype=jnp.int32) ^ c
    arrival = (
        (x2[None, None, :, None] * 4 + y4[None, :, None, None]) * 2 + c2[:, None, None, None]
    ) * heads + j4[None, None, None, :]
    arrival = arrival.reshape(-1)
    every = jnp.arange(n_seq, dtype=jnp.int32)
    counts = jnp.sum(jnp.where(arrival[:, None] == every[None, :], counts[None, :], 0), axis=1)
    ends = jnp.arange(n_seq + 1, dtype=jnp.int32)
    off = jnp.sum(jnp.where(every[None, :] < ends[:, None], counts[None, :] * BLK, 0), axis=1)

    tails = jnp.stack([t[tokens - HALO :, HD:] for t in ys])
    starts = jnp.stack([t[:HALO, HD:] for t in ys])
    ahead = [(i, i + 1) for i in range(n_group - 1)]
    left = lax.ppermute(
        lax.dynamic_index_in_dim(tails, zp ^ (heads - 1), 0, keepdims=False),
        ("xh", "y", "c"),
        ahead,
    )
    right = lax.ppermute(
        lax.dynamic_index_in_dim(starts, zp, 0, keepdims=False),
        ("xh", "y", "c"),
        [(j, i) for i, j in ahead],
    )
    span = heads * tokens
    ids = lax.dynamic_slice(
        marks_all, (group * span,), (span + 2 * PAD,)
    )
    ids = ids.astype(f32)[None, :]

    def slots_of(owner_rows):
        r = jnp.arange(merged_rows, dtype=jnp.int32)
        equal = owner_rows[:, :, None] == owner_rows[:, None, :]
        return jnp.sum((equal & (r[None, None, :] < r[None, :, None])).astype(jnp.int32), axis=2)

    group_owners = lax.dynamic_slice(owners_all, (group * heads, 0), (heads, merged_rows))
    peer = jnp.arange(heads, dtype=jnp.int32)[:, None]
    tgt = (group_owners * (heads * CAP) + peer * CAP + slots_of(group_owners)).reshape(-1)

    width = residual.shape[1]
    weights = out_weight.reshape(columns, n_head, width).transpose(1, 0, 2)
    weights = lax.all_to_all(tie(weights, kv4), HEAD, split_axis=0, concat_axis=0, tiled=True)

    own_target = owners[:, 0] * CAP + slots_of(owners[:, 0][None, :])[0]
    choose = (jnp.arange(n_seq * CAP, dtype=jnp.int32)[:, None] == own_target[None, :]).astype(bf16)
    width = residual.shape[1]
    res = jnp.dot(
        choose, residual.reshape(merged_rows, 4 * width), preferred_element_type=f32
    ).astype(bf16)
    res = res.reshape(n_seq, CAP * 4 * width // HD, HD)
    res = lax.all_to_all(tie(res, kv32, weights, *ys), SEQ, split_axis=0, concat_axis=0, tiled=True)
    res = res.reshape(n_seq * CAP * 4, width)

    one = zp[None].astype(jnp.int32)
    sent = attend(off, tgt, one, ys, left, right, ids, pieces, n_seq * heads * CAP)
    sent, res, weights = lax.optimization_barrier((sent, res, weights))
    got = lax.all_to_all(
        sent.reshape(n_seq, heads * CAP * 4, HD), SEQ, split_axis=0, concat_axis=0, tiled=True
    ).reshape(n_seq * heads * CAP * 4, HD)
    got_c = swap(got, HEAD, 1)
    got_x = swap(got, HEAD, 2)
    got_xc = swap(got_x, HEAD, 1)
    delivered = project(
        jnp.stack([xl, c]).astype(jnp.int32),
        (got, got_c, got_x, got_xc),
        weights,
        res,
        layer_scale[None, :],
        n_seq * CAP,
    )
    return (delivered, refreshed)


def solution(mesh):
    devices = np.asarray(mesh.devices).reshape(2, 4, 2, 4, 2, 2)
    fine = Mesh(devices, SEQ + HEAD)
    in_specs = (
        P(SEQ, HEAD),
        P(SEQ, HEAD),
        P(SEQ, HEAD),
        P(SEQ, HEAD),
        P(HEAD),
        P(HEAD, None),
        P(SEQ),
        P(SEQ, HEAD),
        P(SEQ, HEAD),
        P(SEQ),
        P(SEQ),
        P(SEQ, None),
        P(None, HEAD),
        P(SEQ, None),
    )
    out_specs = (P(SEQ, HEAD), P(SEQ, HEAD))
    return jax.shard_map(shards, mesh=fine, in_specs=in_specs, out_specs=out_specs, check_vma=False)
```

time: 313 us -> 301 us (0.962); the launches traced: 308 us -> 302 us
  blocking collectives: 21.4 us -> 31.9 us
  Pallas kernels: 58.7 us -> 50.1 us
  starting transfers between devices: 87.4 us -> 79 us
  local copies, waits for them, and re-layouts: 20.7 us -> 24.6 us
  waiting for transfers between devices: 90.2 us -> 86.9 us
    ppermute x1 -> x9, waiting for transfers between devices: 0.01 us -> 33.7 us  [the longest x8 31.8 us: spread(): return lax.ppermute(part, ('zh', 'zp', 'c'), pairs)]
    all_to_all x0 -> x1, blocking collectives: none -> 31.9 us  [shards(): lax.all_to_all(sent.reshape(n_seq, heads * CAP * 4, HD), SEQ, split_axis=...]
    ppermute x1 -> x9, starting transfers between devices: 1.29 us -> 27.3 us  [the longest x8 25.3 us: spread(): return lax.ppermute(part, ('zh', 'zp', 'c'), pairs)]
    all_gather x2 -> x0, blocking collectives: 21.4 us -> none  [the longest x1 12.4 us: shards(): kv = lax.all_gather(kv, 'zh', axis=0, tiled=True)]
    ppermute x9 -> x5, waiting for transfers between devices: 71.8 us -> 53 us  [swap(): return lax.ppermute(x, axis, [(i, i ^ k) for i in range(n)])]
    all_to_all x3 -> x2, waiting for transfers between devices: 16.8 us -> 0.01 us  [the longest x1 0.01 us: shards(): lax.all_to_all(tie(weights, kv4), HEAD, split_axis=0, concat_axis=0, tile...]
    all_to_all x3 -> x2, starting transfers between devices: 27.9 us -> 11.4 us  [the longest x1 6.54 us: shards(): lax.all_to_all(tie(res, kv32, weights, *ys), SEQ, split_axis=0, concat_ax...]
    ppermute x9 -> x5, starting transfers between devices: 37.7 us -> 21.5 us  [swap(): return lax.ppermute(x, axis, [(i, i ^ k) for i in range(n)])]
  transfers between devices with their start and end apart: 16 -> 19, of which waited for: 8 -> 8; matrix products, arithmetic and copies ran while one was open for 9% -> 10% of each run, Pallas kernels for 0% -> 11%
where the time goes in v2:
time: 301 us; the launch traced here: 302 us
  waiting for transfers between devices  86.9 us (29%)
  starting transfers between devices  79 us (26%)
  Pallas kernels  50.1 us (17%)
  blocking collectives  31.9 us (11%)
  local copies, waits for them, and re-layouts  24.6 us (8%)
  between operations  15.1 us (5%)
  other arithmetic  10.5 us (3%)
  matrix products  3.4 us (1%)
    ppermute x5, waiting for transfers between devices, swap(): return lax.ppermute(x, axis, [(i, i ^ k) for i in range(n)])  53 us
    all_to_all x1, blocking collectives, shards(): lax.all_to_all(sent.reshape(n_seq, heads * CAP * 4, HD), SEQ, split_axis=...  31.9 us
    ppermute x8, waiting for transfers between devices, spread(): return lax.ppermute(part, ('zh', 'zp', 'c'), pairs)  31.8 us
    pallas_call x1, Pallas kernels, attend(): pl.pallas_call(attention_kernel, out_shape=jax.ShapeDtypeStruct((slots *...  30.2 us
    ppermute x8, starting transfers between devices, spread(): return lax.ppermute(part, ('zh', 'zp', 'c'), pairs)  25.3 us
    ppermute x5, starting transfers between devices, swap(): return lax.ppermute(x, axis, [(i, i ^ k) for i in range(n)])  21.5 us
    all_to_all x1, starting transfers between devices, shards(): lax.all_to_all(meta, SEQ, split_axis=0, concat_axis=0, tiled=True)[:, 0, :]  15.1 us
    pallas_call x1, Pallas kernels, project(): pl.pallas_call(project_kernel, out_shape=jax.ShapeDtypeStruct((slots, 4 *...  14.4 us
  transfers between devices with their start and end apart: 19, of which 8 were waited for; matrix products, arithmetic and copies ran while one was open for 10% of the time, Pallas kernels for 11%

profile of v2, /device:TPU:1, one launch (start us, length us, event | category | flops | bytes accessed | tf_op | source)
XLA Modules:
  0.0 301.5 jit_solution(8177814850447816864)
XLA Ops:
  10.3 15.1 %all-to-all-start = ((s32[64,1,768]{2,1,0:T(1,128)}), s32[64,1,768]{2,1,0:T(1,128)S(1)}, u32[]{:S(2)}, u32[]{:S(2)}) async-start(s32[64,1,768]{2,1,0:T(1,128)} %broadcast_in_dim.71), calls=%async_computation | async-start | bytes 393216 | tf_op jit(solution)/shard_map/all_to_all | solution.py:347
  26.8 2.8 fusion.15
  34.0 7.9 %collective-permute-start.6 = (bf16[96,256]{1,0:T(8,128)(2,1)S(1)}, bf16[96,256]{1,0:T(8,128)(2,1)S(1)}, u32[]{:S(2)}, u32[]{:S(2)}) collective-permute-start(bf16[96,256]{1,0:T(8,128)(2,1)S(1)} %get-tuple-element.26), channel_id=1, source_target_pairs={{0,0},{1,16},{4,4},{5,20},{8,8},{9,24},{12,12},{13,28},{16,1},{17,... | collective-permute-start | bytes 147464 | tf_op jit(solution)/shard_map/ppermute | solution.py:397
  42.1 2.9 collective-permute-start.8
  45.1 6.4 %copy.37 = bf16[512,4096]{0,1:T(8,128)(2,1)} copy(bf16[512,4096]{1,0:T(8,128)(2,1)} %param.20) | data formatting | bytes 8388608 | tf_op args[5]
  51.6 6.3 %copy.38 = bf16[512,4,1024]{2,0,1:T(8,128)(2,1)} copy(bf16[512,4,1024]{0,2,1:T(8,128)(2,1)} %bitcast.64) | data formatting | bytes 8388608 | tf_op jit(solution)/shard_map/reshape | solution.py:452
  60.9 3.2 %shard_map.158 = bf16[4,512,384]{2,1,0:T(8,128)(2,1)} custom-call(bf16[512,512]{1,0:T(8,128)(2,1)} %q_ref.1, bf16[512,512]{1,0:T(8,128)(2,1)} %k_ref.1, bf16[512,512]{1,0:T(8,128)(2,1)} %v_ref.2, f32[512,128]{1,0:T(8,128)} %get-tuple-element.37.c_ref, f32[512,128]{1,0:T(8,128)} %get-tuple-element.38.s_ref), custom_call_target="tpu_custom_call" | custom-call | tf_op jit(solution)/shard_map/pallas_call | solution.py:356
  64.1 4.8 %all-to-all-start.1 = ((bf16[4,512,1024]{2,1,0:T(8,128)(2,1)}), bf16[4,512,1024]{2,1,0:T(8,128)(2,1)}, u32[]{:S(2)}, u32[]{:S(2)}) async-start(bf16[4,512,1024]{2,1,0:T(8,128)(2,1)} %bitcast.63), calls=%async_computation.1 | async-start | bytes 8388608 | tf_op jit(solution)/shard_map/all_to_all | solution.py:453
  69.0 2.9 collective-permute-start.10
  71.9 48.1 %collective-permute-done.10 = bf16[384,256]{1,0:T(8,128)(2,1)S(1)} collective-permute-done((bf16[384,256]{1,0:T(8,128)(2,1)S(1)}, bf16[384,256]{1,0:T(8,128)(2,1)S(1)}, u32[]{:S(2)}, u32[]{:S(2)}) %collective-permute-start.10) | collective-permute-done | bytes 196640 | tf_op jit(solution)/shard_map/ppermute | solution.py:306
  124.6 10.2 %collective-permute-start = (bf16[512,384]{1,0:T(8,128)(2,1)S(1)}, bf16[512,384]{1,0:T(8,128)(2,1)S(1)}, u32[]{:S(2)}, u32[]{:S(2)}) collective-permute-start(bf16[512,384]{1,0:T(8,128)(2,1)S(1)} %get-tuple-element.17), channel_id=1, source_target_pairs={{0,0},{1,16},{4,4},{5,20},{8,8},{9,24},{12,12},{13,28},{16,1},{17,... | collective-permute-start | bytes 1179656 | tf_op jit(solution)/shard_map/ppermute | solution.py:397
  134.9 3.0 collective-permute-start.2
  139.7 11.9 %collective-permute-done.refs_0_ = bf16[512,384]{1,0:T(8,128)(2,1)S(1)} collective-permute-done((bf16[512,384]{1,0:T(8,128)(2,1)S(1)}, bf16[512,384]{1,0:T(8,128)(2,1)S(1)}, u32[]{:S(2)}, u32[]{:S(2)}) %collective-permute-start) | collective-permute-done | bytes 393248 | tf_op jit(solution)/shard_map/ppermute | solution.py:397
  151.5 15.3 %collective-permute-done.1.refs_1_ = bf16[512,384]{1,0:T(8,128)(2,1)S(1)} collective-permute-done((bf16[512,384]{1,0:T(8,128)(2,1)S(1)}, bf16[512,384]{1,0:T(8,128)(2,1)S(1)}, u32[]{:S(2)}, u32[]{:S(2)}) %collective-permute-start.1) | collective-permute-done | bytes 393248 | tf_op jit(solution)/shard_map/ppermute | solution.py:397
  166.9 4.7 %collective-permute-done.3.refs_3_ = bf16[512,384]{1,0:T(8,128)(2,1)S(1)} collective-permute-done((bf16[512,384]{1,0:T(8,128)(2,1)S(1)}, bf16[512,384]{1,0:T(8,128)(2,1)S(1)}, u32[]{:S(2)}, u32[]{:S(2)}) %collective-permute-start.3) | collective-permute-done | bytes 393248 | tf_op jit(solution)/shard_map/ppermute | solution.py:397
  171.5 6.5 %all-to-all-start.2 = ((bf16[64,96,128]{2,1,0:T(8,128)(2,1)}), bf16[64,96,128]{2,1,0:T(8,128)(2,1)}, u32[]{:S(2)}, u32[]{:S(2)}) async-start(bf16[64,96,128]{2,1,0:T(8,128)(2,1)} %reshape.300), calls=%async_computation.2 | async-start | bytes 3145728 | tf_op jit(solution)/shard_map/all_to_all | solution.py:462
  186.7 3.6 %collective-permute-start.4 = (bf16[208,256]{1,0:T(8,128)(2,1)S(1)}, bf16[208,256]{1,0:T(8,128)(2,1)S(1)}, u32[]{:S(2)}, u32[]{:S(2)}) collective-permute-start(bf16[208,256]{1,0:T(8,128)(2,1)S(1)} %fusion.7), channel_id=1, source_target_pairs={{0,1},{1,32},{32,33},{33,64},{64,65},{65,96},{96,97},{97,128},{128... | collective-permute-start | bytes 319496 | tf_op jit(solution)/shard_map/ppermute | solution.py:426
  192.4 30.2 %shard_map.160 = bf16[3072,128]{1,0:T(8,128)(2,1)S(1)} custom-call(s32[65]{0:T(128)S(1)} %select_reduce_fusion.1.off, s32[512]{0:T(512)S(1)} %bitcast.61, s32[1]{0:T(128)} %bitcast.5.zp, bf16[512,384]{1,0:T(8,128)(2,1)S(1)} %collective-permute-done.refs_0_, bf16[512,384]{1,0:T(8,128)(2,1)S(1)} %collective-permute-done.1.refs_1_, ...), custom_call_target="tpu_custom_call" | custom-call | flops 7516192768 | bytes 8388608 | tf_op jit(solution)/shard_map/pallas_call | solution.py:202
  222.6 2.5 reshape.302.res
  225.2 31.9 %all_to_all.20 = bf16[64,48,128]{2,1,0:T(8,128)(2,1)S(1)} all-to-all(bf16[64,48,128]{2,1,0:T(8,128)(2,1)S(1)} %bitcast.60), channel_id=1, replica_groups=mesh['xh'=2,'y'=4,'zh'=2,'zp'=4,'xl'=2,'c'=2] {'xh','y','zh','zp'}, dimensions={0} | all-to-all | bytes 1572864 | tf_op jit(solution)/shard_map/all_to_all | solution.py:468
  258.5 7.6 %collective-permute-start.12 = (bf16[3072,128]{1,0:T(8,128)(2,1)S(1)}, bf16[3072,128]{1,0:T(8,128)(2,1)}, u32[]{:S(2)}, u32[]{:S(2)}) collective-permute-start(bf16[3072,128]{1,0:T(8,128)(2,1)S(1)} %bitcast.58), channel_id=1, source_target_pairs={{0,1},{1,0},{2,3},{3,2},{4,5},{5,4},{6,7},{7,6},{8,9},{9,8},{10,11... | collective-permute-start | bytes 2359304 | tf_op jit(solution)/shard_map/ppermute | solution.py:306
  266.1 3.0 collective-permute-done.13.a2
  269.0 8.1 %collective-permute-start.14 = (bf16[3072,128]{1,0:T(8,128)(2,1)S(1)}, bf16[3072,128]{1,0:T(8,128)(2,1)}, u32[]{:S(2)}, u32[]{:S(2)}) collective-permute-start(bf16[3072,128]{1,0:T(8,128)(2,1)S(1)} %collective-permute-done.13.a2), channel_id=1, source_target_pairs={{0,1},{1,0},{2,3},{3,2},{4,5},{5,4},{6,7},{7,6},{8,9},{9,8},{10,11... | collective-permute-start | bytes 2359304 | tf_op jit(solution)/shard_map/ppermute | solution.py:306
  280.2 14.4 %shard_map.161 = bf16[192,4096]{1,0:T(8,128)(2,1)} custom-call(s32[2]{0:T(128)S(1)} %pad_add_fusion.1.core, bf16[3072,128]{1,0:T(8,128)(2,1)S(1)} %bitcast.59, bf16[3072,128]{1,0:T(8,128)(2,1)} %collective-permute-done.12.a1, bf16[3072,128]{1,0:T(8,128)(2,1)S(1)} %collective-permute-done.13.a2, bf16[3072,128]{1,0:T(8,128)(2,1)} %collective-permute-done.14.a3, ...), custom_call_target="tpu_custom_call" | custom-call | flops 3221225472 | bytes 16777216 | tf_op jit(solution)/shard_map/pallas_call | solution.py:280
  (106 shorter events, 32.9 us)
Async XLA Ops:
  7.2 19.7 %copy-start = (bf16[16,4096]{1,0:T(8,128)(2,1)S(1)}, bf16[16,4096]{1,0:T(8,128)(2,1)}, u32[]{:S(2)}) copy-start(bf16[16,4096]{1,0:T(8,128)(2,1)} %param.26) | copy-start | bytes 393220
  10.3 47.6 %all-to-all-start = ((s32[64,1,768]{2,1,0:T(1,128)}), s32[64,1,768]{2,1,0:T(1,128)S(1)}, u32[]{:S(2)}, u32[]{:S(2)}) async-start(s32[64,1,768]{2,1,0:T(1,128)} %broadcast_in_dim.71), calls=%async_computation | async-start | bytes 393216 | tf_op jit(solution)/shard_map/all_to_all | solution.py:347
  34.0 23.9 %collective-permute-start.6 = (bf16[96,256]{1,0:T(8,128)(2,1)S(1)}, bf16[96,256]{1,0:T(8,128)(2,1)S(1)}, u32[]{:S(2)}, u32[]{:S(2)}) collective-permute-start(bf16[96,256]{1,0:T(8,128)(2,1)S(1)} %get-tuple-element.26), channel_id=1, source_target_pairs={{0,0},{1,16},{4,4},{5,20},{8,8},{9,24},{12,12},{13,28},{16,1},{17,... | collective-permute-start | bytes 147464 | tf_op jit(solution)/shard_map/ppermute | solution.py:397
  42.0 15.9 %collective-permute-start.7 = (bf16[96,256]{1,0:T(8,128)(2,1)S(1)}, bf16[96,256]{1,0:T(8,128)(2,1)S(1)}, u32[]{:S(2)}, u32[]{:S(2)}) collective-permute-start(bf16[96,256]{1,0:T(8,128)(2,1)S(1)} %get-tuple-element.29), channel_id=1, source_target_pairs={{0,4},{1,20},{4,0},{5,16},{8,12},{9,28},{12,8},{13,24},{16,5},{17,... | collective-permute-start | bytes 147464 | tf_op jit(solution)/shard_map/ppermute | solution.py:397
  42.1 15.8 %collective-permute-start.8 = (bf16[96,256]{1,0:T(8,128)(2,1)S(1)}, bf16[96,256]{1,0:T(8,128)(2,1)S(1)}, u32[]{:S(2)}, u32[]{:S(2)}) collective-permute-start(bf16[96,256]{1,0:T(8,128)(2,1)S(1)} %get-tuple-element.28), channel_id=1, source_target_pairs={{0,8},{1,24},{4,12},{5,28},{8,0},{9,16},{12,4},{13,20},{16,9},{17,... | collective-permute-start | bytes 147464 | tf_op jit(solution)/shard_map/ppermute | solution.py:397
  45.0 12.9 %collective-permute-start.9 = (bf16[96,256]{1,0:T(8,128)(2,1)S(1)}, bf16[96,256]{1,0:T(8,128)(2,1)S(1)}, u32[]{:S(2)}, u32[]{:S(2)}) collective-permute-start(bf16[96,256]{1,0:T(8,128)(2,1)S(1)} %get-tuple-element.27), channel_id=1, source_target_pairs={{0,12},{1,28},{4,8},{5,24},{8,4},{9,20},{12,0},{13,16},{16,13},{17... | collective-permute-start | bytes 147464 | tf_op jit(solution)/shard_map/ppermute | solution.py:397
  64.1 107.5 %all-to-all-start.1 = ((bf16[4,512,1024]{2,1,0:T(8,128)(2,1)}), bf16[4,512,1024]{2,1,0:T(8,128)(2,1)}, u32[]{:S(2)}, u32[]{:S(2)}) async-start(bf16[4,512,1024]{2,1,0:T(8,128)(2,1)} %bitcast.63), calls=%async_computation.1 | async-start | bytes 8388608 | tf_op jit(solution)/shard_map/all_to_all | solution.py:453
  68.9 51.9 %copy-start.7 = (bf16[512,1024]{1,0:T(8,128)(2,1)S(1)}, bf16[512,1024]{1,0:T(8,128)(2,1)}, u32[]{:S(2)}) copy-start(bf16[512,1024]{1,0:T(8,128)(2,1)} %param.18) | copy-start | bytes 3145732
  68.9 52.5 %copy-start.9 = (s32[128,1]{0,1:T(1,128)S(1)}, s32[128,1]{0,1:T(1,128)}, u32[]{:S(2)}) copy-start(s32[128,1]{0,1:T(1,128)} %param.28) | copy-start | bytes 1540
  68.9 102.6 %all-gather.2.cloned.1.call-start = ((), (), s32[]{:S(2)}) async-start(), calls=%async_computation.4 | async-start | bytes 1966080 | tf_op jit(solution)/shard_map/all_gather | solution.py:404
  69.0 51.0 %collective-permute-start.10 = (bf16[384,256]{1,0:T(8,128)(2,1)S(1)}, bf16[384,256]{1,0:T(8,128)(2,1)S(1)}, u32[]{:S(2)}, u32[]{:S(2)}) collective-permute-start(bf16[384,256]{1,0:T(8,128)(2,1)S(1)} %pad_maximum_fusion.3), channel_id=1, source_target_pairs={{0,128},{128,0},{1,129},{129,1},{2,130},{130,2},{3,131},{131,3},{4... | collective-permute-start | bytes 589832 | tf_op jit(solution)/shard_map/ppermute | solution.py:306
  124.6 26.9 %collective-permute-start = (bf16[512,384]{1,0:T(8,128)(2,1)S(1)}, bf16[512,384]{1,0:T(8,128)(2,1)S(1)}, u32[]{:S(2)}, u32[]{:S(2)}) collective-permute-start(bf16[512,384]{1,0:T(8,128)(2,1)S(1)} %get-tuple-element.17), channel_id=1, source_target_pairs={{0,0},{1,16},{4,4},{5,20},{8,8},{9,24},{12,12},{13,28},{16,1},{17,... | collective-permute-start | bytes 1179656 | tf_op jit(solution)/shard_map/ppermute | solution.py:397
  134.8 32.0 %collective-permute-start.1 = (bf16[512,384]{1,0:T(8,128)(2,1)S(1)}, bf16[512,384]{1,0:T(8,128)(2,1)S(1)}, u32[]{:S(2)}, u32[]{:S(2)}) collective-permute-start(bf16[512,384]{1,0:T(8,128)(2,1)S(1)} %get-tuple-element.16), channel_id=1, source_target_pairs={{0,4},{1,20},{4,0},{5,16},{8,12},{9,28},{12,8},{13,24},{16,5},{17,... | collective-permute-start | bytes 1179656 | tf_op jit(solution)/shard_map/ppermute | solution.py:397
  134.9 31.9 %collective-permute-start.2 = (bf16[512,384]{1,0:T(8,128)(2,1)S(1)}, bf16[512,384]{1,0:T(8,128)(2,1)S(1)}, u32[]{:S(2)}, u32[]{:S(2)}) collective-permute-start(bf16[512,384]{1,0:T(8,128)(2,1)S(1)} %get-tuple-element.15), channel_id=1, source_target_pairs={{0,8},{1,24},{4,12},{5,28},{8,0},{9,16},{12,4},{13,20},{16,9},{17,... | collective-permute-start | bytes 1179656 | tf_op jit(solution)/shard_map/ppermute | solution.py:397
  137.9 33.6 %collective-permute-start.3 = (bf16[512,384]{1,0:T(8,128)(2,1)S(1)}, bf16[512,384]{1,0:T(8,128)(2,1)S(1)}, u32[]{:S(2)}, u32[]{:S(2)}) collective-permute-start(bf16[512,384]{1,0:T(8,128)(2,1)S(1)} %get-tuple-element.14), channel_id=1, source_target_pairs={{0,12},{1,28},{4,8},{5,24},{8,4},{9,20},{12,0},{13,16},{16,13},{17... | collective-permute-start | bytes 1179656 | tf_op jit(solution)/shard_map/ppermute | solution.py:397
  171.5 11.2 %copy-start.1 = (bf16[3072,256]{1,0:T(8,128)(2,1)S(1)}, bf16[3072,256]{1,0:T(8,128)(2,1)}, u32[]{:S(2)}) copy-start(bf16[3072,256]{1,0:T(8,128)(2,1)} %all-gather.2.cloned.1.call-done.refs_7_) | copy-start | bytes 4718596
  171.5 51.1 %all-to-all-start.2 = ((bf16[64,96,128]{2,1,0:T(8,128)(2,1)}), bf16[64,96,128]{2,1,0:T(8,128)(2,1)}, u32[]{:S(2)}, u32[]{:S(2)}) async-start(bf16[64,96,128]{2,1,0:T(8,128)(2,1)} %reshape.300), calls=%async_computation.2 | async-start | bytes 3145728 | tf_op jit(solution)/shard_map/all_to_all | solution.py:462
  182.7 9.7 %collective-permute-start.11 = (bf16[3072,256]{1,0:T(8,128)(2,1)S(1)}, bf16[3072,256]{1,0:T(8,128)(2,1)S(1)}, u32[]{:S(2)}, u32[]{:S(2)}) collective-permute-start(bf16[3072,256]{1,0:T(8,128)(2,1)S(1)} %copy-done.1), channel_id=1, source_target_pairs={{0,1},{1,0},{2,3},{3,2},{4,5},{5,4},{6,7},{7,6},{8,9},{9,8},{10,11... | collective-permute-start | bytes 4718600 | tf_op jit(solution)/shard_map/ppermute | solution.py:306
  184.6 7.6 %collective-permute-start.5 = (bf16[208,256]{1,0:T(8,128)(2,1)S(1)}, bf16[208,256]{1,0:T(8,128)(2,1)S(1)}, u32[]{:S(2)}, u32[]{:S(2)}) collective-permute-start(bf16[208,256]{1,0:T(8,128)(2,1)S(1)} %fusion.3), channel_id=1, source_target_pairs={{1,0},{32,1},{33,32},{64,33},{65,64},{96,65},{97,96},{128,97},{129... | collective-permute-start | bytes 319496 | tf_op jit(solution)/shard_map/ppermute | solution.py:431
  186.7 5.8 %collective-permute-start.4 = (bf16[208,256]{1,0:T(8,128)(2,1)S(1)}, bf16[208,256]{1,0:T(8,128)(2,1)S(1)}, u32[]{:S(2)}, u32[]{:S(2)}) collective-permute-start(bf16[208,256]{1,0:T(8,128)(2,1)S(1)} %fusion.7), channel_id=1, source_target_pairs={{0,1},{1,32},{32,33},{33,64},{64,65},{65,96},{96,97},{97,128},{128... | collective-permute-start | bytes 319496 | tf_op jit(solution)/shard_map/ppermute | solution.py:426
  225.2 54.0 %copy-start.3 = (f32[1024]{0:T(1024)S(1)}, f32[1024]{0:T(1024)}, u32[]{:S(2)}) copy-start(f32[1024]{0:T(1024)} %param.19) | copy-start | bytes 12292
  257.1 12.0 %collective-permute-start.13 = (bf16[3072,128]{1,0:T(8,128)(2,1)S(1)}, bf16[3072,128]{1,0:T(8,128)(2,1)S(1)}, u32[]{:S(2)}, u32[]{:S(2)}) collective-permute-start(bf16[3072,128]{1,0:T(8,128)(2,1)S(1)} %bitcast.57), channel_id=1, source_target_pairs={{0,2},{1,3},{2,0},{3,1},{4,6},{5,7},{6,4},{7,5},{8,10},{9,11},{10,... | collective-permute-start | bytes 2359304 | tf_op jit(solution)/shard_map/ppermute | solution.py:306
  258.5 18.7 %collective-permute-start.12 = (bf16[3072,128]{1,0:T(8,128)(2,1)S(1)}, bf16[3072,128]{1,0:T(8,128)(2,1)}, u32[]{:S(2)}, u32[]{:S(2)}) collective-permute-start(bf16[3072,128]{1,0:T(8,128)(2,1)S(1)} %bitcast.58), channel_id=1, source_target_pairs={{0,1},{1,0},{2,3},{3,2},{4,5},{5,4},{6,7},{7,6},{8,9},{9,8},{10,11... | collective-permute-start | bytes 2359304 | tf_op jit(solution)/shard_map/ppermute | solution.py:306
  269.0 10.2 %collective-permute-start.14 = (bf16[3072,128]{1,0:T(8,128)(2,1)S(1)}, bf16[3072,128]{1,0:T(8,128)(2,1)}, u32[]{:S(2)}, u32[]{:S(2)}) collective-permute-start(bf16[3072,128]{1,0:T(8,128)(2,1)S(1)} %collective-permute-done.13.a2), channel_id=1, source_target_pairs={{0,1},{1,0},{2,3},{3,2},{4,5},{5,4},{6,7},{7,6},{8,9},{9,8},{10,11... | collective-permute-start | bytes 2359304 | tf_op jit(solution)/shard_map/ppermute | solution.py:306
  (5 other events, 17.3 us)
Sparse Core Ops, SparseCore 0:
  120.9 30.9 all-gather.1

commit v3 on v2

--- a/solution.py
+++ b/solution.py
@@ -232,23 +232,20 @@
     )(off, tgt, zp, *ys, left, right, ids, *pieces)
 
 
-def project_kernel(core, a0, a1, a2, a3, weights, res, scale, mix, out, att, pick):
+def project_kernel(core, a0, a1, a2, a3, w0, w1, w2, w3, res, scale, mix, out, att, res32, proj):
     b = pl.program_id(0)
-    c = core[1]
+    c = core[0]
     groups = a0.shape[0] // (8 * 48)
 
     @pl.when(b == 0)
     def _():
-        slot = lax.broadcasted_iota(jnp.int32, pick.shape, 0)
-        row = lax.broadcasted_iota(jnp.int32, pick.shape, 1)
-        slots = out.shape[0]
-        pick[...] = (row == (slot % slots) * 4 + slot // slots).astype(bf16)
+        res32[...] = res[...].astype(f32)
         for k, a in enumerate((a0, a1, a2, a3)):
 
             def move(g, carry):
                 to = pl.ds(pl.multiple_of((g * 2 + (c ^ (k % 2))) * 48, 16), 48)
                 for p in range(8):
-                    block = (core[0] ^ (k // 2)) * 2 + p // 4
+                    block = (k // 2) * 2 + (c ^ (p // 4))
                     src = pl.ds(pl.multiple_of(g * 384 + p * 48, 16), 48)
                     att[block, to, (p % 4) * HD : (p % 4 + 1) * HD] = a[src, :]
                 return carry
@@ -256,22 +253,28 @@
             lax.fori_loop(0, groups, move, 0)
 
     total = None
-    for k in range(4):
-        part = jnp.dot(att[k], weights[k], preferred_element_type=f32)
+    for k, w in enumerate((w0, w1, w2, w3)):
+        part = jnp.dot(att[k], w[...], preferred_element_type=f32)
         total = part if total is None else total + part
-    layer = (res[...].astype(f32) + total * scale[...]).astype(bf16)
-    turns = jnp.dot(pick[...], layer, preferred_element_type=f32).astype(bf16)
+    total = total * scale[...]
     slots = out.shape[0]
-    for d in range(weights.shape[2] // HD):
-        cols = slice(d * HD, (d + 1) * HD)
-        rows = jnp.concatenate([turns[t * slots : (t + 1) * slots, cols] for t in range(4)], axis=1)
+    per = w0.shape[1] // HD
+    for d in range(per):
+        proj[d * 4 * slots : (d + 1) * 4 * slots, :] = total[:, d * HD : (d + 1) * HD]
+    for d in range(per):
+        parts = []
+        for t in range(4):
+            new = proj[pl.ds(d * 4 * slots + t, slots, stride=4), :]
+            old = res32[pl.ds(t * 8 + b * per + d, slots, stride=32), :]
+            parts.append((old + new).astype(bf16))
+        rows = jnp.concatenate(parts, axis=1)
         out[:, d * 4 * HD : (d + 1) * 4 * HD] = jnp.dot(
             rows, mix[...], preferred_element_type=f32
         ).astype(bf16)
 
 
 def project(core, atts, weights, res, scale, slots):
-    width = weights.shape[2]
+    width = weights[0].shape[1]
     part = 256
     whole = pl.BlockSpec(memory_space=pltpu.VMEM)
     source = np.arange(4 * HD)
@@ -284,12 +287,13 @@
             num_scalar_prefetch=1,
             grid=(width // part,),
             in_specs=[whole] * 4
-            + [pl.BlockSpec((*weights.shape[:2], part), lambda b, *_: (0, 0, b))]
-            + [pl.BlockSpec((slots * 4, part), lambda b, *_: (0, b)), pl.BlockSpec((1, part), lambda b, *_: (0, b)), whole],
+            + [pl.BlockSpec((weights[0].shape[0], part), lambda b, *_: (0, b))] * 4
+            + [whole, pl.BlockSpec((1, part), lambda b, *_: (0, b)), whole],
             out_specs=pl.BlockSpec((slots, 4 * part), lambda b, *_: (0, b)),
             scratch_shapes=[
                 pltpu.VMEM((4, slots * 4, 4 * HD), bf16),
-                pltpu.VMEM((slots * 4, slots * 4), bf16),
+                pltpu.VMEM((slots * 32, HD), f32),
+                pltpu.VMEM((slots * 4 * part // HD, HD), f32),
             ],
         ),
         compiler_params=pltpu.CompilerParams(
@@ -298,7 +302,7 @@
         cost_estimate=pl.CostEstimate(
             flops=2 * 768 * 2048 * 1024, bytes_accessed=16 << 20, transcendentals=0
         ),
-    )(core, *atts, weights, res, scale, jnp.asarray(mix, bf16))
+    )(core, *atts, *weights, res, scale, jnp.asarray(mix, bf16))
 
 
 def swap(x, axis, k):
@@ -328,10 +332,9 @@
 ):
     tokens, columns = queries.shape
     heads = columns // HD
-    n_head = lax.axis_size(HEAD)
     n_seq = lax.axis_size(SEQ)
     seq = lax.axis_index(SEQ)
-    xh, y, zp, xl, c = (lax.axis_index(n) for n in ("xh", "y", "zp", "xl", "c"))
+    xh, y, zp, c = (lax.axis_index(n) for n in ("xh", "y", "zp", "c"))
     head = lax.axis_index(HEAD)
     merged_rows = tokens // 4
     group = (xh * 4 + y) * 2 + c
@@ -449,8 +452,11 @@
     tgt = (group_owners * (heads * CAP) + peer * CAP + slots_of(group_owners)).reshape(-1)
 
     width = residual.shape[1]
-    weights = out_weight.reshape(columns, n_head, width).transpose(1, 0, 2)
-    weights = lax.all_to_all(tie(weights, kv4), HEAD, split_axis=0, concat_axis=0, tiled=True)
+    out_weight = tie(out_weight, kv8)
+    weights = []
+    for j in range(lax.axis_size(HEAD)):
+        part = lax.dynamic_slice(out_weight, (0, (head ^ j) * width), (columns, width))
+        weights.append(part if j == 0 else swap(part, HEAD, j))
 
     own_target = owners[:, 0] * CAP + slots_of(owners[:, 0][None, :])[0]
     choose = (jnp.arange(n_seq * CAP, dtype=jnp.int32)[:, None] == own_target[None, :]).astype(bf16)
@@ -459,20 +465,20 @@
         choose, residual.reshape(merged_rows, 4 * width), preferred_element_type=f32
     ).astype(bf16)
     res = res.reshape(n_seq, CAP * 4 * width // HD, HD)
-    res = lax.all_to_all(tie(res, kv32, weights, *ys), SEQ, split_axis=0, concat_axis=0, tiled=True)
-    res = res.reshape(n_seq * CAP * 4, width)
+    res = lax.all_to_all(tie(res, kv32, weights[2], *ys), SEQ, split_axis=0, concat_axis=0, tiled=True)
 
     one = zp[None].astype(jnp.int32)
     sent = attend(off, tgt, one, ys, left, right, ids, pieces, n_seq * heads * CAP)
-    sent, res, weights = lax.optimization_barrier((sent, res, weights))
+    sent, res, *weights = lax.optimization_barrier((sent, res, *weights))
     got = lax.all_to_all(
         sent.reshape(n_seq, heads * CAP * 4, HD), SEQ, split_axis=0, concat_axis=0, tiled=True
     ).reshape(n_seq * heads * CAP * 4, HD)
+    res = res.reshape(n_seq * CAP * 4 * width // HD, HD)
     got_c = swap(got, HEAD, 1)
     got_x = swap(got, HEAD, 2)
     got_xc = swap(got_x, HEAD, 1)
     delivered = project(
-        jnp.stack([xl, c]).astype(jnp.int32),
+        c[None].astype(jnp.int32),
         (got, got_c, got_x, got_xc),
         weights,
         res,

time: 301 us -> 271 us (0.900)
  waiting for transfers between devices: 86.9 us -> 46.2 us
  blocking collectives: 31.9 us -> 63.5 us
  starting transfers between devices: 79 us -> 69.6 us
  local copies, waits for them, and re-layouts: 24.6 us -> 16.9 us
  other arithmetic: 10.5 us -> 6.94 us
    ppermute x5 -> x8, waiting for transfers between devices: 53 us -> 17.7 us  [swap(): return lax.ppermute(x, axis, [(i, i ^ k) for i in range(n)])]
    all_to_all x1, blocking collectives: 31.9 us -> 63.5 us  [shards(): lax.all_to_all(sent.reshape(n_seq, heads * CAP * 4, HD), SEQ, split_axis=...]
    reshape x2 -> x0, local copies, waits for them, and re-layouts: 8.86 us -> none  [the longest x1 6.31 us: shards(): weights = out_weight.reshape(columns, n_head, width).transpose(1, 0, 2)]
    ppermute x5 -> x8, starting transfers between devices: 21.5 us -> 13.3 us  [swap(): return lax.ppermute(x, axis, [(i, i ^ k) for i in range(n)])]
    ppermute x8, waiting for transfers between devices: 31.8 us -> 25.9 us  [spread(): return lax.ppermute(part, ('zh', 'zp', 'c'), pairs)]
    unnamed x23 -> x25, local copies, waits for them, and re-layouts: 8.54 us -> 2.76 us
    dynamic_slice x0 -> x1, local copies, waits for them, and re-layouts: none -> 4.03 us  [shards(): lax.dynamic_slice(out_weight, (0, (head ^ j) * width), (columns, width))]
    pallas_call x1, Pallas kernels: 14.4 us -> 11.4 us  [project(): pl.pallas_call(project_kernel, out_shape=jax.ShapeDtypeStruct((slots, 4 *...]
  transfers between devices with their start and end apart: 19 -> 21, of which waited for: 8 -> 9; matrix products, arithmetic and copies ran while one was open for 10% -> 8% of each run, Pallas kernels for 11% -> 12%
where the time goes in v3:
time: 271 us; the launch traced here: 270 us
  starting transfers between devices  69.6 us (26%)
  blocking collectives  63.5 us (23%)
  Pallas kernels  47.1 us (17%)
  waiting for transfers between devices  46.2 us (17%)
  local copies, waits for them, and re-layouts  16.9 us (6%)
  between operations  15.2 us (6%)
  other arithmetic  6.94 us (3%)
  matrix products  4.54 us (2%)
    all_to_all x1, blocking collectives, shards(): lax.all_to_all(sent.reshape(n_seq, heads * CAP * 4, HD), SEQ, split_axis=...  63.5 us
    pallas_call x1, Pallas kernels, attend(): pl.pallas_call(attention_kernel, out_shape=jax.ShapeDtypeStruct((slots *...  30.2 us
    ppermute x8, waiting for transfers between devices, spread(): return lax.ppermute(part, ('zh', 'zp', 'c'), pairs)  25.9 us
    ppermute x8, starting transfers between devices, spread(): return lax.ppermute(part, ('zh', 'zp', 'c'), pairs)  22.6 us
    ppermute x8, waiting for transfers between devices, swap(): return lax.ppermute(x, axis, [(i, i ^ k) for i in range(n)])  17.7 us
    all_to_all x1, starting transfers between devices, shards(): lax.all_to_all(meta, SEQ, split_axis=0, concat_axis=0, tiled=True)[:, 0, :]  15.1 us
    ppermute x8, starting transfers between devices, swap(): return lax.ppermute(x, axis, [(i, i ^ k) for i in range(n)])  13.3 us
    all_to_all x1, starting transfers between devices, shards(): lax.all_to_all(tie(res, kv32, weights[2], *ys), SEQ, split_axis=0, concat...  13 us
  transfers between devices with their start and end apart: 21, of which 9 were waited for; matrix products, arithmetic and copies ran while one was open for 8% of the time, Pallas kernels for 12%

profile of v3, /device:TPU:1, one launch (start us, length us, event | category | flops | bytes accessed | tf_op | source)
XLA Modules:
  0.0 269.9 jit_solution(13161832705632441219)
XLA Ops:
  10.3 15.1 %all-to-all-start = ((s32[64,1,768]{2,1,0:T(1,128)}), s32[64,1,768]{2,1,0:T(1,128)S(1)}, u32[]{:S(2)}, u32[]{:S(2)}) async-start(s32[64,1,768]{2,1,0:T(1,128)} %broadcast_in_dim.74), calls=%async_computation | async-start | bytes 393216 | tf_op jit(solution)/shard_map/all_to_all | solution.py:350
  27.0 2.8 %fusion.15 = f32[16,512]{1,0:T(8,128)S(1)} fusion(bf16[16,4096]{1,0:T(8,128)(2,1)S(1)} %copy-done, bf16[4096,512]{1,0:T(8,128)(2,1)} %param.27), kind=kOutput, calls=%fused_computation.92 | convolution fusion | flops 67108864 | bytes 4358144 | tf_op jit(solution)/shard_map/dot_general | solution.py:374
  34.1 7.9 %collective-permute-start.6 = (bf16[96,256]{1,0:T(8,128)(2,1)S(1)}, bf16[96,256]{1,0:T(8,128)(2,1)S(1)}, u32[]{:S(2)}, u32[]{:S(2)}) collective-permute-start(bf16[96,256]{1,0:T(8,128)(2,1)S(1)} %get-tuple-element.36), channel_id=1, source_target_pairs={{0,0},{1,16},{4,4},{5,20},{8,8},{9,24},{12,12},{13,28},{16,1},{17,... | collective-permute-start | bytes 147464 | tf_op jit(solution)/shard_map/ppermute | solution.py:400
  42.2 3.8 %collective-permute-start.8 = (bf16[96,256]{1,0:T(8,128)(2,1)S(1)}, bf16[96,256]{1,0:T(8,128)(2,1)S(1)}, u32[]{:S(2)}, u32[]{:S(2)}) collective-permute-start(bf16[96,256]{1,0:T(8,128)(2,1)S(1)} %get-tuple-element.38), channel_id=1, source_target_pairs={{0,8},{1,24},{4,12},{5,28},{8,0},{9,16},{12,4},{13,20},{16,9},{17,... | collective-permute-start | bytes 147464 | tf_op jit(solution)/shard_map/ppermute | solution.py:400
  48.4 4.3 %collective-permute-done.7 = bf16[96,256]{1,0:T(8,128)(2,1)S(1)} collective-permute-done((bf16[96,256]{1,0:T(8,128)(2,1)S(1)}, bf16[96,256]{1,0:T(8,128)(2,1)S(1)}, u32[]{:S(2)}, u32[]{:S(2)}) %collective-permute-start.7) | collective-permute-done | bytes 49184 | tf_op jit(solution)/shard_map/ppermute | solution.py:400
  55.6 3.2 %shard_map.158 = bf16[4,512,384]{2,1,0:T(8,128)(2,1)} custom-call(bf16[512,512]{1,0:T(8,128)(2,1)} %q_ref.1, bf16[512,512]{1,0:T(8,128)(2,1)} %k_ref.1, bf16[512,512]{1,0:T(8,128)(2,1)} %v_ref.2, f32[512,128]{1,0:T(8,128)} %get-tuple-element.47.c_ref, f32[512,128]{1,0:T(8,128)} %get-tuple-element.48.s_ref), custom_call_target="tpu_custom_call" | custom-call | tf_op jit(solution)/shard_map/pallas_call | solution.py:359
  58.8 2.8 %collective-permute-start.10 = (bf16[384,256]{1,0:T(8,128)(2,1)S(1)}, bf16[384,256]{1,0:T(8,128)(2,1)S(1)}, u32[]{:S(2)}, u32[]{:S(2)}) collective-permute-start(bf16[384,256]{1,0:T(8,128)(2,1)S(1)} %pad_maximum_fusion.2), channel_id=1, source_target_pairs={{0,128},{128,0},{1,129},{129,1},{2,130},{130,2},{3,131},{131,3},{4... | collective-permute-start | bytes 589832 | tf_op jit(solution)/shard_map/ppermute | solution.py:310
  61.7 3.2 %collective-permute-done.10 = bf16[384,256]{1,0:T(8,128)(2,1)S(1)} collective-permute-done((bf16[384,256]{1,0:T(8,128)(2,1)S(1)}, bf16[384,256]{1,0:T(8,128)(2,1)S(1)}, u32[]{:S(2)}, u32[]{:S(2)}) %collective-permute-start.10) | collective-permute-done | bytes 196640 | tf_op jit(solution)/shard_map/ppermute | solution.py:310
  65.8 4.0 %constant_dynamic-slice_fusion = (bf16[512,1024]{1,0:T(8,128)(2,1)}, bf16[512,1024]{1,0:T(8,128)(2,1)}, bf16[512,1024]{1,0:T(8,128)(2,1)S(1)}, bf16[512,1024]{1,0:T(8,128)(2,1)}) fusion(bf16[512,4096]{1,0:T(8,128)(2,1)} %param.20, s32[]{:T(128)S(6)} %select_n.93, s32[]{:T(128)S(6)} %select_n.92, s32[]{:T(128)S(6)} %select_n.91, s32[]{:T(128)S(6)} %select_n.90), kind=kLoop, calls=%fused_computation.63 | loop fusion | bytes 8388624 | tf_op jit(solution)/shard_map/dynamic_slice | solution.py:458
  70.4 2.5 reshape.296
  75.1 2.8 %collective-permute-start.2 = (bf16[512,384]{1,0:T(8,128)(2,1)}, bf16[512,384]{1,0:T(8,128)(2,1)S(1)}, u32[]{:S(2)}, u32[]{:S(2)}) collective-permute-start(bf16[512,384]{1,0:T(8,128)(2,1)} %get-tuple-element.25), channel_id=1, source_target_pairs={{0,8},{1,24},{4,12},{5,28},{8,0},{9,16},{12,4},{13,20},{16,9},{17,... | collective-permute-start | bytes 1179656 | tf_op jit(solution)/shard_map/ppermute | solution.py:400
  79.1 5.9 %collective-permute-start = (bf16[512,384]{1,0:T(8,128)(2,1)}, bf16[512,384]{1,0:T(8,128)(2,1)S(1)}, u32[]{:S(2)}, u32[]{:S(2)}) collective-permute-start(bf16[512,384]{1,0:T(8,128)(2,1)} %get-tuple-element.27), channel_id=1, source_target_pairs={{0,0},{1,16},{4,4},{5,20},{8,8},{9,24},{12,12},{13,28},{16,1},{17,... | collective-permute-start | bytes 1179656 | tf_op jit(solution)/shard_map/ppermute | solution.py:400
  86.7 3.8 %reshape.297 = bf16[64,96,128]{2,1,0:T(8,128)(2,1)} reshape(bf16[192,4096]{1,0:T(8,128)(2,1)} %convolution_convert_fusion) | data formatting | bytes 3145728 | tf_op jit(solution)/shard_map/reshape | solution.py:467
  90.5 10.1 %collective-permute-done.2.refs_2_ = bf16[512,384]{1,0:T(8,128)(2,1)S(1)} collective-permute-done((bf16[512,384]{1,0:T(8,128)(2,1)}, bf16[512,384]{1,0:T(8,128)(2,1)S(1)}, u32[]{:S(2)}, u32[]{:S(2)}) %collective-permute-start.2) | collective-permute-done | bytes 393248 | tf_op jit(solution)/shard_map/ppermute | solution.py:400
  100.6 9.0 %collective-permute-done.1.refs_1_ = bf16[512,384]{1,0:T(8,128)(2,1)S(1)} collective-permute-done((bf16[512,384]{1,0:T(8,128)(2,1)}, bf16[512,384]{1,0:T(8,128)(2,1)S(1)}, u32[]{:S(2)}, u32[]{:S(2)}) %collective-permute-start.1) | collective-permute-done | bytes 393248 | tf_op jit(solution)/shard_map/ppermute | solution.py:400
  109.7 13.0 %all-to-all-start.1 = ((bf16[64,96,128]{2,1,0:T(8,128)(2,1)}), bf16[64,96,128]{2,1,0:T(8,128)(2,1)}, u32[]{:S(2)}, u32[]{:S(2)}) async-start(bf16[64,96,128]{2,1,0:T(8,128)(2,1)} %reshape.297), calls=%async_computation.1 | async-start | bytes 3145728 | tf_op jit(solution)/shard_map/all_to_all | solution.py:468
  128.8 3.6 %collective-permute-start.4 = (bf16[208,256]{1,0:T(8,128)(2,1)S(1)}, bf16[208,256]{1,0:T(8,128)(2,1)S(1)}, u32[]{:S(2)}, u32[]{:S(2)}) collective-permute-start(bf16[208,256]{1,0:T(8,128)(2,1)S(1)} %fusion.7), channel_id=1, source_target_pairs={{0,1},{1,32},{32,33},{33,64},{64,65},{65,96},{96,97},{97,128},{128... | collective-permute-start | bytes 319496 | tf_op jit(solution)/shard_map/ppermute | solution.py:429
  132.6 2.6 collective-permute-done.5.refs_5_
  135.1 30.2 %shard_map.160 = bf16[3072,128]{1,0:T(8,128)(2,1)S(1)} custom-call(s32[65]{0:T(128)S(1)} %select_reduce_fusion.1.off, s32[512]{0:T(512)S(1)} %bitcast.59, s32[1]{0:T(128)} %bitcast.4.zp, bf16[512,384]{1,0:T(8,128)(2,1)S(1)} %collective-permute-done.refs_0_, bf16[512,384]{1,0:T(8,128)(2,1)S(1)} %collective-permute-done.1.refs_1_, ...), custom_call_target="tpu_custom_call" | custom-call | flops 7516192768 | bytes 8388608 | tf_op jit(solution)/shard_map/pallas_call | solution.py:202
  166.3 63.5 %all_to_all.15 = bf16[64,48,128]{2,1,0:T(8,128)(2,1)S(1)} all-to-all(bf16[64,48,128]{2,1,0:T(8,128)(2,1)S(1)} %bitcast.58), channel_id=1, replica_groups=mesh['xh'=2,'y'=4,'zh'=2,'zp'=4,'xl'=2,'c'=2] {'xh','y','zh','zp'}, dimensions={0} | all-to-all | bytes 1572864 | tf_op jit(solution)/shard_map/all_to_all | solution.py:473
  229.9 3.4 %collective-permute-start.15 = (bf16[3072,128]{1,0:T(8,128)(2,1)S(1)}, bf16[3072,128]{1,0:T(8,128)(2,1)S(1)}, u32[]{:S(2)}, u32[]{:S(2)}) collective-permute-start(bf16[3072,128]{1,0:T(8,128)(2,1)S(1)} %bitcast.56), channel_id=1, source_target_pairs={{0,1},{1,0},{2,3},{3,2},{4,5},{5,4},{6,7},{7,6},{8,9},{9,8},{10,11... | collective-permute-start | bytes 2359304 | tf_op jit(solution)/shard_map/ppermute | solution.py:310
  233.3 12.6 %collective-permute-done.16.a2 = bf16[3072,128]{1,0:T(8,128)(2,1)S(1)} collective-permute-done((bf16[3072,128]{1,0:T(8,128)(2,1)S(1)}, bf16[3072,128]{1,0:T(8,128)(2,1)S(1)}, u32[]{:S(2)}, u32[]{:S(2)}) %collective-permute-start.16) | collective-permute-done | bytes 786464 | tf_op jit(solution)/shard_map/ppermute | solution.py:310
  245.9 3.9 %collective-permute-start.17 = (bf16[3072,128]{1,0:T(8,128)(2,1)S(1)}, bf16[3072,128]{1,0:T(8,128)(2,1)S(1)}, u32[]{:S(2)}, u32[]{:S(2)}) collective-permute-start(bf16[3072,128]{1,0:T(8,128)(2,1)S(1)} %collective-permute-done.16.a2), channel_id=1, source_target_pairs={{0,1},{1,0},{2,3},{3,2},{4,5},{5,4},{6,7},{7,6},{8,9},{9,8},{10,11... | collective-permute-start | bytes 2359304 | tf_op jit(solution)/shard_map/ppermute | solution.py:310
  251.7 11.4 %shard_map.161 = bf16[192,4096]{1,0:T(8,128)(2,1)} custom-call(s32[1]{0:T(128)} %bitcast.core, bf16[3072,128]{1,0:T(8,128)(2,1)S(1)} %bitcast.57, bf16[3072,128]{1,0:T(8,128)(2,1)S(1)} %collective-permute-done.15.a1, bf16[3072,128]{1,0:T(8,128)(2,1)S(1)} %collective-permute-done.16.a2, bf16[3072,128]{1,0:T(8,128)(2,1)S(1)} %collective-permute-done.17.a3, ...), custom_call_target="tpu_custom_call" | custom-call | flops 3221225472 | bytes 16777216 | tf_op jit(solution)/shard_map/pallas_call | solution.py:283
  (110 shorter events, 29.1 us)
Async XLA Ops:
  10.3 42.4 %all-to-all-start = ((s32[64,1,768]{2,1,0:T(1,128)}), s32[64,1,768]{2,1,0:T(1,128)S(1)}, u32[]{:S(2)}, u32[]{:S(2)}) async-start(s32[64,1,768]{2,1,0:T(1,128)} %broadcast_in_dim.74), calls=%async_computation | async-start | bytes 393216 | tf_op jit(solution)/shard_map/all_to_all | solution.py:350
  25.5 84.2 %all-gather.2.cloned.1.call-start = ((), (), s32[]{:S(2)}) async-start(), calls=%async_computation.3 | async-start | bytes 1966080 | tf_op jit(solution)/shard_map/all_gather | solution.py:407
  34.1 11.9 %collective-permute-start.6 = (bf16[96,256]{1,0:T(8,128)(2,1)S(1)}, bf16[96,256]{1,0:T(8,128)(2,1)S(1)}, u32[]{:S(2)}, u32[]{:S(2)}) collective-permute-start(bf16[96,256]{1,0:T(8,128)(2,1)S(1)} %get-tuple-element.36), channel_id=1, source_target_pairs={{0,0},{1,16},{4,4},{5,20},{8,8},{9,24},{12,12},{13,28},{16,1},{17,... | collective-permute-start | bytes 147464 | tf_op jit(solution)/shard_map/ppermute | solution.py:400
  42.1 4.8 %collective-permute-start.9 = (bf16[96,256]{1,0:T(8,128)(2,1)S(1)}, bf16[96,256]{1,0:T(8,128)(2,1)S(1)}, u32[]{:S(2)}, u32[]{:S(2)}) collective-permute-start(bf16[96,256]{1,0:T(8,128)(2,1)S(1)} %get-tuple-element.37), channel_id=1, source_target_pairs={{0,12},{1,28},{4,8},{5,24},{8,4},{9,20},{12,0},{13,16},{16,13},{17... | collective-permute-start | bytes 147464 | tf_op jit(solution)/shard_map/ppermute | solution.py:400
  42.2 6.2 %collective-permute-start.8 = (bf16[96,256]{1,0:T(8,128)(2,1)S(1)}, bf16[96,256]{1,0:T(8,128)(2,1)S(1)}, u32[]{:S(2)}, u32[]{:S(2)}) collective-permute-start(bf16[96,256]{1,0:T(8,128)(2,1)S(1)} %get-tuple-element.38), channel_id=1, source_target_pairs={{0,8},{1,24},{4,12},{5,28},{8,0},{9,16},{12,4},{13,20},{16,9},{17,... | collective-permute-start | bytes 147464 | tf_op jit(solution)/shard_map/ppermute | solution.py:400
  46.0 6.7 %collective-permute-start.7 = (bf16[96,256]{1,0:T(8,128)(2,1)S(1)}, bf16[96,256]{1,0:T(8,128)(2,1)S(1)}, u32[]{:S(2)}, u32[]{:S(2)}) collective-permute-start(bf16[96,256]{1,0:T(8,128)(2,1)S(1)} %get-tuple-element.39), channel_id=1, source_target_pairs={{0,4},{1,20},{4,0},{5,16},{8,12},{9,28},{12,8},{13,24},{16,5},{17,... | collective-permute-start | bytes 147464 | tf_op jit(solution)/shard_map/ppermute | solution.py:400
  58.8 6.0 %collective-permute-start.10 = (bf16[384,256]{1,0:T(8,128)(2,1)S(1)}, bf16[384,256]{1,0:T(8,128)(2,1)S(1)}, u32[]{:S(2)}, u32[]{:S(2)}) collective-permute-start(bf16[384,256]{1,0:T(8,128)(2,1)S(1)} %pad_maximum_fusion.2), channel_id=1, source_target_pairs={{0,128},{128,0},{1,129},{129,1},{2,130},{130,2},{3,131},{131,3},{4... | collective-permute-start | bytes 589832 | tf_op jit(solution)/shard_map/ppermute | solution.py:310
  69.9 39.8 %collective-permute-start.12 = (bf16[512,1024]{1,0:T(8,128)(2,1)}, bf16[512,1024]{1,0:T(8,128)(2,1)}, u32[]{:S(2)}, u32[]{:S(2)}) collective-permute-start(bf16[512,1024]{1,0:T(8,128)(2,1)} %get-tuple-element.23), channel_id=1, source_target_pairs={{0,2},{1,3},{2,0},{3,1},{4,6},{5,7},{6,4},{7,5},{8,10},{9,11},{10,... | collective-permute-start | bytes 3145736 | tf_op jit(solution)/shard_map/ppermute | solution.py:310
  74.3 16.2 %collective-permute-start.3 = (bf16[512,384]{1,0:T(8,128)(2,1)}, bf16[512,384]{1,0:T(8,128)(2,1)S(1)}, u32[]{:S(2)}, u32[]{:S(2)}) collective-permute-start(bf16[512,384]{1,0:T(8,128)(2,1)} %get-tuple-element.24), channel_id=1, source_target_pairs={{0,12},{1,28},{4,8},{5,24},{8,4},{9,20},{12,0},{13,16},{16,13},{17... | collective-permute-start | bytes 1179656 | tf_op jit(solution)/shard_map/ppermute | solution.py:400
  75.1 25.5 %collective-permute-start.2 = (bf16[512,384]{1,0:T(8,128)(2,1)}, bf16[512,384]{1,0:T(8,128)(2,1)S(1)}, u32[]{:S(2)}, u32[]{:S(2)}) collective-permute-start(bf16[512,384]{1,0:T(8,128)(2,1)} %get-tuple-element.25), channel_id=1, source_target_pairs={{0,8},{1,24},{4,12},{5,28},{8,0},{9,16},{12,4},{13,20},{16,9},{17,... | collective-permute-start | bytes 1179656 | tf_op jit(solution)/shard_map/ppermute | solution.py:400
  78.0 31.7 %collective-permute-start.1 = (bf16[512,384]{1,0:T(8,128)(2,1)}, bf16[512,384]{1,0:T(8,128)(2,1)S(1)}, u32[]{:S(2)}, u32[]{:S(2)}) collective-permute-start(bf16[512,384]{1,0:T(8,128)(2,1)} %get-tuple-element.26), channel_id=1, source_target_pairs={{0,4},{1,20},{4,0},{5,16},{8,12},{9,28},{12,8},{13,24},{16,5},{17,... | collective-permute-start | bytes 1179656 | tf_op jit(solution)/shard_map/ppermute | solution.py:400
  79.1 30.6 %collective-permute-start = (bf16[512,384]{1,0:T(8,128)(2,1)}, bf16[512,384]{1,0:T(8,128)(2,1)S(1)}, u32[]{:S(2)}, u32[]{:S(2)}) collective-permute-start(bf16[512,384]{1,0:T(8,128)(2,1)} %get-tuple-element.27), channel_id=1, source_target_pairs={{0,0},{1,16},{4,4},{5,20},{8,8},{9,24},{12,12},{13,28},{16,1},{17,... | collective-permute-start | bytes 1179656 | tf_op jit(solution)/shard_map/ppermute | solution.py:400
  109.7 56.6 %all-to-all-start.1 = ((bf16[64,96,128]{2,1,0:T(8,128)(2,1)}), bf16[64,96,128]{2,1,0:T(8,128)(2,1)}, u32[]{:S(2)}, u32[]{:S(2)}) async-start(bf16[64,96,128]{2,1,0:T(8,128)(2,1)} %reshape.297), calls=%async_computation.1 | async-start | bytes 3145728 | tf_op jit(solution)/shard_map/all_to_all | solution.py:468
  123.6 11.5 %collective-permute-start.11 = (bf16[3072,256]{1,0:T(8,128)(2,1)}, bf16[3072,256]{1,0:T(8,128)(2,1)S(1)}, u32[]{:S(2)}, u32[]{:S(2)}) collective-permute-start(bf16[3072,256]{1,0:T(8,128)(2,1)} %all-gather.2.cloned.1.call-done.refs_7_), channel_id=1, source_target_pairs={{0,1},{1,0},{2,3},{3,2},{4,5},{5,4},{6,7},{7,6},{8,9},{9,8},{10,11... | collective-permute-start | bytes 4718600 | tf_op jit(solution)/shard_map/ppermute | solution.py:310
  125.3 40.1 %collective-permute-start.14 = (bf16[512,1024]{1,0:T(8,128)(2,1)}, bf16[512,1024]{1,0:T(8,128)(2,1)}, u32[]{:S(2)}, u32[]{:S(2)}) collective-permute-start(bf16[512,1024]{1,0:T(8,128)(2,1)} %get-tuple-element.20), channel_id=1, source_target_pairs={{0,3},{1,2},{2,1},{3,0},{4,7},{5,6},{6,5},{7,4},{8,11},{9,10},{10,... | collective-permute-start | bytes 3145736 | tf_op jit(solution)/shard_map/ppermute | solution.py:310
  126.1 39.3 %collective-permute-start.13 = (bf16[512,1024]{1,0:T(8,128)(2,1)}, bf16[512,1024]{1,0:T(8,128)(2,1)S(1)}, u32[]{:S(2)}, u32[]{:S(2)}) collective-permute-start(bf16[512,1024]{1,0:T(8,128)(2,1)} %get-tuple-element.21), channel_id=1, source_target_pairs={{0,1},{1,0},{2,3},{3,2},{4,5},{5,4},{6,7},{7,6},{8,9},{9,8},{10,11... | collective-permute-start | bytes 3145736 | tf_op jit(solution)/shard_map/ppermute | solution.py:310
  126.8 8.4 %collective-permute-start.5 = (bf16[208,256]{1,0:T(8,128)(2,1)S(1)}, bf16[208,256]{1,0:T(8,128)(2,1)S(1)}, u32[]{:S(2)}, u32[]{:S(2)}) collective-permute-start(bf16[208,256]{1,0:T(8,128)(2,1)S(1)} %fusion.3), channel_id=1, source_target_pairs={{1,0},{32,1},{33,32},{64,33},{65,64},{96,65},{97,96},{128,97},{129... | collective-permute-start | bytes 319496 | tf_op jit(solution)/shard_map/ppermute | solution.py:434
  128.8 6.3 %collective-permute-start.4 = (bf16[208,256]{1,0:T(8,128)(2,1)S(1)}, bf16[208,256]{1,0:T(8,128)(2,1)S(1)}, u32[]{:S(2)}, u32[]{:S(2)}) collective-permute-start(bf16[208,256]{1,0:T(8,128)(2,1)S(1)} %fusion.7), channel_id=1, source_target_pairs={{0,1},{1,32},{32,33},{33,64},{64,65},{65,96},{96,97},{97,128},{128... | collective-permute-start | bytes 319496 | tf_op jit(solution)/shard_map/ppermute | solution.py:429
  165.3 86.4 %copy-start.4 = (f32[1024]{0:T(1024)S(1)}, f32[1024]{0:T(1024)}, u32[]{:S(2)}) copy-start(f32[1024]{0:T(1024)} %param.19) | copy-start | bytes 12292
  165.3 86.4 %copy-start.5 = (bf16[512,512]{1,0:T(8,128)(2,1)S(1)}, bf16[512,512]{1,0:T(8,128)(2,1)}, u32[]{:S(2)}) copy-start(bf16[512,512]{1,0:T(8,128)(2,1)} %constant.119.clone.mix) | copy-start | bytes 1572868
  166.3 85.4 %copy-start.3 = (bf16[512,1024]{1,0:T(8,128)(2,1)S(1)}, bf16[512,1024]{1,0:T(8,128)(2,1)}, u32[]{:S(2)}) copy-start(bf16[512,1024]{1,0:T(8,128)(2,1)} %copy-done.2) | copy-start | bytes 3145732
  229.9 16.0 %collective-permute-start.16 = (bf16[3072,128]{1,0:T(8,128)(2,1)S(1)}, bf16[3072,128]{1,0:T(8,128)(2,1)S(1)}, u32[]{:S(2)}, u32[]{:S(2)}) collective-permute-start(bf16[3072,128]{1,0:T(8,128)(2,1)S(1)} %bitcast.55), channel_id=1, source_target_pairs={{0,2},{1,3},{2,0},{3,1},{4,6},{5,7},{6,4},{7,5},{8,10},{9,11},{10,... | collective-permute-start | bytes 2359304 | tf_op jit(solution)/shard_map/ppermute | solution.py:310
  229.9 20.0 %collective-permute-start.15 = (bf16[3072,128]{1,0:T(8,128)(2,1)S(1)}, bf16[3072,128]{1,0:T(8,128)(2,1)S(1)}, u32[]{:S(2)}, u32[]{:S(2)}) collective-permute-start(bf16[3072,128]{1,0:T(8,128)(2,1)S(1)} %bitcast.56), channel_id=1, source_target_pairs={{0,1},{1,0},{2,3},{3,2},{4,5},{5,4},{6,7},{7,6},{8,9},{9,8},{10,11... | collective-permute-start | bytes 2359304 | tf_op jit(solution)/shard_map/ppermute | solution.py:310
  245.9 5.8 %collective-permute-start.17 = (bf16[3072,128]{1,0:T(8,128)(2,1)S(1)}, bf16[3072,128]{1,0:T(8,128)(2,1)S(1)}, u32[]{:S(2)}, u32[]{:S(2)}) collective-permute-start(bf16[3072,128]{1,0:T(8,128)(2,1)S(1)} %collective-permute-done.16.a2), channel_id=1, source_target_pairs={{0,1},{1,0},{2,3},{3,2},{4,5},{5,4},{6,7},{7,6},{8,9},{9,8},{10,11... | collective-permute-start | bytes 2359304 | tf_op jit(solution)/shard_map/ppermute | solution.py:310
  (8 other events, 52.0 us)
Sparse Core Ops, SparseCore 0:
  65.8 29.1 all-gather.1

commit v4 on v3

--- a/solution.py
+++ b/solution.py
@@ -332,6 +332,7 @@
 ):
     tokens, columns = queries.shape
     heads = columns // HD
+    n_head = lax.axis_size(HEAD)
     n_seq = lax.axis_size(SEQ)
     seq = lax.axis_index(SEQ)
     xh, y, zp, c = (lax.axis_index(n) for n in ("xh", "y", "zp", "c"))
@@ -342,15 +343,8 @@
     whole = pl.BlockSpec(memory_space=pltpu.VMEM)
 
     marks = segment_ids + 1
-    n_blocks = block_live.shape[0]
-    meta = jnp.concatenate(
-        [marks, owners[:, 0], block_live, jnp.zeros((128 - n_blocks,), jnp.int32)]
-    )
-    meta = jnp.broadcast_to(meta[None, None, :], (n_seq, 1, meta.shape[0]))
-    meta = lax.all_to_all(meta, SEQ, split_axis=0, concat_axis=0, tiled=True)[:, 0, :]
-    marks_all = jnp.pad(meta[:, :tokens].reshape(-1), (PAD, PAD))
-
-    near = lax.dynamic_slice(marks_all, (seq * tokens,), (PAD + tokens,))
+    before = lax.ppermute(marks[tokens - PAD :], SEQ, [(i, i + 1) for i in range(n_seq - 1)])
+    near = jnp.concatenate([before, marks])
     same = marks[:, None] == near[None, :]
     index = jnp.arange(PAD + tokens, dtype=jnp.int32)
     first = jnp.min(jnp.where(same, index[None, :], PAD + tokens), axis=1)
@@ -378,6 +372,7 @@
     refreshed = lax.dynamic_update_slice(cache_keys, fresh, (block * BLK, 0))
 
     live = block_live > 0
+    n_blocks = block_live.shape[0]
     blocks = jnp.arange(n_blocks, dtype=jnp.int32)
     rank = jnp.sum(jnp.where(blocks[None, :] < blocks[:, None], live[None, :], False), axis=1)
     hit = live[None, :] & (rank[None, :] == jnp.arange(LIVE_MOST, dtype=jnp.int32)[:, None])
@@ -399,13 +394,23 @@
         part = lax.dynamic_index_in_dim(x, zp ^ j, 0, keepdims=False)
         return lax.ppermute(part, ("zh", "zp", "c"), pairs)
 
-    kv4 = jnp.concatenate([spread(kv, j) for j in range(heads)], axis=0)
+    kv = tie(kv, before)
+    cached = [spread(kv, j) for j in range(heads)]
+    kv4 = jnp.concatenate(cached, axis=0)
+
     ys = [spread(qkv, j) for j in range(heads)]
 
     kv4 = tie(kv4, qkv)
     kv8 = jnp.concatenate([kv4, swap(kv4, "xh", 1)], axis=0)
     kv32 = lax.all_gather(kv8, "y", axis=0, tiled=True)
-    pieces = [kv32, swap(kv32, "c", 1)]
+    pieces = [kv32, swap(tie(kv32, *ys), "c", 1)]
+
+    meta = jnp.concatenate(
+        [marks, owners[:, 0], block_live, jnp.zeros((128 - n_blocks,), jnp.int32)]
+    )
+    meta = jnp.broadcast_to(tie(meta, kv8, qkv)[None, None, :], (n_seq, 1, meta.shape[0]))
+    meta = lax.all_to_all(meta, SEQ, split_axis=0, concat_axis=0, tiled=True)[:, 0, :]
+    marks_all = jnp.pad(meta[:, :tokens].reshape(-1), (PAD, PAD))
 
     owners_all = meta[:, tokens : tokens + merged_rows]
     live_all = meta[:, tokens + merged_rows : tokens + merged_rows + n_blocks]
@@ -423,8 +428,17 @@
     ends = jnp.arange(n_seq + 1, dtype=jnp.int32)
     off = jnp.sum(jnp.where(every[None, :] < ends[:, None], counts[None, :] * BLK, 0), axis=1)
 
-    tails = jnp.stack([t[tokens - HALO :, HD:] for t in ys])
-    starts = jnp.stack([t[:HALO, HD:] for t in ys])
+    width = residual.shape[1]
+    out_weight = tie(out_weight, kv8)
+    blocks_w = [
+        lax.dynamic_slice(out_weight, (0, (head ^ j) * width), (columns, width))
+        for j in range(n_head)
+    ]
+    weight_x = swap(blocks_w[2], HEAD, 2)
+
+    ends_of = tie(tuple(ys), weight_x, meta)
+    tails = jnp.stack([t[tokens - HALO :, HD:] for t in ends_of])
+    starts = jnp.stack([t[:HALO, HD:] for t in ends_of])
     ahead = [(i, i + 1) for i in range(n_group - 1)]
     left = lax.ppermute(
         lax.dynamic_index_in_dim(tails, zp ^ (heads - 1), 0, keepdims=False),
@@ -451,21 +465,22 @@
     peer = jnp.arange(heads, dtype=jnp.int32)[:, None]
     tgt = (group_owners * (heads * CAP) + peer * CAP + slots_of(group_owners)).reshape(-1)
 
-    width = residual.shape[1]
-    out_weight = tie(out_weight, kv8)
-    weights = []
-    for j in range(lax.axis_size(HEAD)):
-        part = lax.dynamic_slice(out_weight, (0, (head ^ j) * width), (columns, width))
-        weights.append(part if j == 0 else swap(part, HEAD, j))
+    weights = [
+        blocks_w[0],
+        swap(tie(blocks_w[1], left, right), HEAD, 1),
+        weight_x,
+        swap(tie(blocks_w[3], left, right), HEAD, 3),
+    ]
 
     own_target = owners[:, 0] * CAP + slots_of(owners[:, 0][None, :])[0]
     choose = (jnp.arange(n_seq * CAP, dtype=jnp.int32)[:, None] == own_target[None, :]).astype(bf16)
     width = residual.shape[1]
+    residual = tie(residual, kv32)
     res = jnp.dot(
         choose, residual.reshape(merged_rows, 4 * width), preferred_element_type=f32
     ).astype(bf16)
     res = res.reshape(n_seq, CAP * 4 * width // HD, HD)
-    res = lax.all_to_all(tie(res, kv32, weights[2], *ys), SEQ, split_axis=0, concat_axis=0, tiled=True)
+    res = lax.all_to_all(tie(res, pieces[1], left, right), SEQ, split_axis=0, concat_axis=0, tiled=True)
 
     one = zp[None].astype(jnp.int32)
     sent = attend(off, tgt, one, ys, left, right, ids, pieces, n_seq * heads * CAP)

time: 271 us -> 253 us (0.934)
  blocking collectives: 63.5 us -> 35 us
  local copies, waits for them, and re-layouts: 16.9 us -> 21.9 us
    all_to_all x1, blocking collectives: 63.5 us -> 35 us  [shards(): lax.all_to_all(sent.reshape(n_seq, heads * CAP * 4, HD), SEQ, split_axis=...]
    all_to_all x1, starting transfers between devices: 13 us -> 7.3 us  [shards(): lax.all_to_all(tie(res, pieces[1], left, right), SEQ, split_axis=0, conca...]
    all_to_all x1, starting transfers between devices: 15.1 us -> 9.57 us  [shards(): lax.all_to_all(meta, SEQ, split_axis=0, concat_axis=0, tiled=True)[:, 0, :]]
    ppermute x1, starting transfers between devices: 3.64 us -> 8.33 us  [shards(): lax.ppermute(lax.dynamic_index_in_dim(tails, zp ^ heads - 1, 0, keepdims=...]
    ppermute x0 -> x1, starting transfers between devices: none -> 4.36 us  [shards(): lax.ppermute(marks[tokens - PAD:], SEQ, [(i, i + 1) for i in range(n_seq...]
    ppermute x8, starting transfers between devices: 22.6 us -> 26.3 us  [spread(): return lax.ppermute(part, ('zh', 'zp', 'c'), pairs)]
    unnamed x25 -> x29, local copies, waits for them, and re-layouts: 2.76 us -> 6.3 us
    ppermute x8, waiting for transfers between devices: 17.7 us -> 21.2 us  [swap(): return lax.ppermute(x, axis, [(i, i ^ k) for i in range(n)])]
  transfers between devices with their start and end apart: 21 -> 22, of which waited for: 9 -> 8; matrix products, arithmetic and copies ran while one was open for 8% -> 11% of each run, Pallas kernels for 12% -> 15%
where the time goes in v4:
time: 253 us; the launch traced here: 252 us
  starting transfers between devices  71.9 us (28%)
  Pallas kernels  48.2 us (19%)
  waiting for transfers between devices  46.7 us (18%)
  blocking collectives  35 us (14%)
  local copies, waits for them, and re-layouts  21.9 us (9%)
  between operations  15.2 us (6%)
  other arithmetic  6.89 us (3%)
  matrix products  5.77 us (2%)
    all_to_all x1, blocking collectives, shards(): lax.all_to_all(sent.reshape(n_seq, heads * CAP * 4, HD), SEQ, split_axis=...  35 us
    pallas_call x1, Pallas kernels, attend(): pl.pallas_call(attention_kernel, out_shape=jax.ShapeDtypeStruct((slots *...  31.3 us
    ppermute x8, starting transfers between devices, spread(): return lax.ppermute(part, ('zh', 'zp', 'c'), pairs)  26.3 us
    ppermute x8, waiting for transfers between devices, spread(): return lax.ppermute(part, ('zh', 'zp', 'c'), pairs)  25.5 us
    ppermute x8, waiting for transfers between devices, swap(): return lax.ppermute(x, axis, [(i, i ^ k) for i in range(n)])  21.2 us
    ppermute x8, starting transfers between devices, swap(): return lax.ppermute(x, axis, [(i, i ^ k) for i in range(n)])  14.1 us
    pallas_call x1, Pallas kernels, project(): pl.pallas_call(project_kernel, out_shape=jax.ShapeDtypeStruct((slots, 4 *...  11.3 us
    all_to_all x1, starting transfers between devices, shards(): lax.all_to_all(meta, SEQ, split_axis=0, concat_axis=0, tiled=True)[:, 0, :]  9.57 us
  transfers between devices with their start and end apart: 22, of which 8 were waited for; matrix products, arithmetic and copies ran while one was open for 11% of the time, Pallas kernels for 15%

profile of v4, /device:TPU:1, one launch (start us, length us, event | category | flops | bytes accessed | tf_op | source)
XLA Modules:
  0.0 251.6 jit_solution(1956294948967378984)
XLA Ops:
  8.9 4.4 %collective-permute-start = (s32[256]{0:T(256)S(1)}, s32[256]{0:T(256)S(1)}, u32[]{:S(2)}, u32[]{:S(2)}) collective-permute-start(s32[256]{0:T(256)S(1)} %slice.44), channel_id=1, source_target_pairs={{0,4},{4,8},{8,12},{12,16},{16,20},{20,24},{24,28},{28,32},{32,36}... | collective-permute-start | bytes 3080 | tf_op jit(solution)/shard_map/ppermute | solution.py:346
  15.4 2.8 %fusion.15 = f32[16,512]{1,0:T(8,128)S(1)} fusion(bf16[16,4096]{1,0:T(8,128)(2,1)S(1)} %copy-done, bf16[4096,512]{1,0:T(8,128)(2,1)} %param.27), kind=kOutput, calls=%fused_computation.92 | convolution fusion | flops 67108864 | bytes 4358144 | tf_op jit(solution)/shard_map/dot_general | solution.py:368
  22.5 4.6 %collective-permute-start.4 = (bf16[96,256]{1,0:T(8,128)(2,1)S(1)}, bf16[96,256]{1,0:T(8,128)(2,1)S(1)}, u32[]{:S(2)}, u32[]{:S(2)}) collective-permute-start(bf16[96,256]{1,0:T(8,128)(2,1)S(1)} %get-tuple-element.57), channel_id=1, source_target_pairs={{0,12},{1,28},{4,8},{5,24},{8,4},{9,20},{12,0},{13,16},{16,13},{17... | collective-permute-start | bytes 147464 | tf_op jit(solution)/shard_map/ppermute | solution.py:395
  28.7 3.7 %collective-permute-start.2 = (bf16[96,256]{1,0:T(8,128)(2,1)S(1)}, bf16[96,256]{1,0:T(8,128)(2,1)S(1)}, u32[]{:S(2)}, u32[]{:S(2)}) collective-permute-start(bf16[96,256]{1,0:T(8,128)(2,1)S(1)} %get-tuple-element.59), channel_id=1, source_target_pairs={{0,4},{1,20},{4,0},{5,16},{8,12},{9,28},{12,8},{13,24},{16,5},{17,... | collective-permute-start | bytes 147464 | tf_op jit(solution)/shard_map/ppermute | solution.py:395
  32.4 3.7 %collective-permute-start.1 = (bf16[96,256]{1,0:T(8,128)(2,1)S(1)}, bf16[96,256]{1,0:T(8,128)(2,1)S(1)}, u32[]{:S(2)}, u32[]{:S(2)}) collective-permute-start(bf16[96,256]{1,0:T(8,128)(2,1)S(1)} %get-tuple-element.56), channel_id=1, source_target_pairs={{0,0},{1,16},{4,4},{5,20},{8,8},{9,24},{12,12},{13,28},{16,1},{17,... | collective-permute-start | bytes 147464 | tf_op jit(solution)/shard_map/ppermute | solution.py:395
  38.6 3.2 %shard_map.159 = bf16[4,512,384]{2,1,0:T(8,128)(2,1)} custom-call(bf16[512,512]{1,0:T(8,128)(2,1)} %q_ref.1, bf16[512,512]{1,0:T(8,128)(2,1)} %k_ref.1, bf16[512,512]{1,0:T(8,128)(2,1)} %v_ref.3, f32[512,128]{1,0:T(8,128)} %get-tuple-element.69.c_ref, f32[512,128]{1,0:T(8,128)} %get-tuple-element.70.s_ref), custom_call_target="tpu_custom_call" | custom-call | tf_op jit(solution)/shard_map/pallas_call | solution.py:353
  45.0 3.3 %collective-permute-done.5 = bf16[384,256]{1,0:T(8,128)(2,1)S(1)} collective-permute-done((bf16[384,256]{1,0:T(8,128)(2,1)S(1)}, bf16[384,256]{1,0:T(8,128)(2,1)S(1)}, u32[]{:S(2)}, u32[]{:S(2)}) %collective-permute-start.5) | collective-permute-done | bytes 196640 | tf_op jit(solution)/shard_map/ppermute | solution.py:310
  49.1 4.1 %constant_dynamic-slice_fusion = (bf16[512,1024]{1,0:T(8,128)(2,1)}, bf16[512,1024]{1,0:T(8,128)(2,1)}, bf16[512,1024]{1,0:T(8,128)(2,1)S(1)}, bf16[512,1024]{1,0:T(8,128)(2,1)}) fusion(bf16[512,4096]{1,0:T(8,128)(2,1)} %param.20, s32[]{:T(128)S(6)} %select_n.89, s32[]{:T(128)S(6)} %select_n.88, s32[]{:T(128)S(6)} %select_n.87, s32[]{:T(128)S(6)} %select_n.85), kind=kLoop, calls=%fused_computation.62 | loop fusion | bytes 8388624 | tf_op jit(solution)/shard_map/dynamic_slice | solution.py:434
  55.5 6.9 %collective-permute-start.6 = (bf16[512,384]{1,0:T(8,128)(2,1)}, bf16[512,384]{1,0:T(8,128)(2,1)S(1)}, u32[]{:S(2)}, u32[]{:S(2)}) collective-permute-start(bf16[512,384]{1,0:T(8,128)(2,1)} %get-tuple-element.47), channel_id=1, source_target_pairs={{0,0},{1,16},{4,4},{5,20},{8,8},{9,24},{12,12},{13,28},{16,1},{17,... | collective-permute-start | bytes 1179656 | tf_op jit(solution)/shard_map/ppermute | solution.py:395
  69.1 9.6 %all-to-all-start = ((s32[64,1,768]{2,1,0:T(1,128)}), s32[64,1,768]{2,1,0:T(1,128)S(1)}, u32[]{:S(2)}, u32[]{:S(2)}) async-start(s32[64,1,768]{2,1,0:T(1,128)} %broadcast_in_dim.80), calls=%async_computation | async-start | bytes 393216 | tf_op jit(solution)/shard_map/all_to_all | solution.py:412
  78.8 11.9 %collective-permute-done.7.refs_1_ = bf16[512,384]{1,0:T(8,128)(2,1)S(1)} collective-permute-done((bf16[512,384]{1,0:T(8,128)(2,1)}, bf16[512,384]{1,0:T(8,128)(2,1)S(1)}, u32[]{:S(2)}, u32[]{:S(2)}) %collective-permute-start.7) | collective-permute-done | bytes 393248 | tf_op jit(solution)/shard_map/ppermute | solution.py:395
  90.7 6.4 %collective-permute-done.8.refs_2_ = bf16[512,384]{1,0:T(8,128)(2,1)S(1)} collective-permute-done((bf16[512,384]{1,0:T(8,128)(2,1)}, bf16[512,384]{1,0:T(8,128)(2,1)S(1)}, u32[]{:S(2)}, u32[]{:S(2)}) %collective-permute-start.8) | collective-permute-done | bytes 393248 | tf_op jit(solution)/shard_map/ppermute | solution.py:395
  97.1 7.0 %collective-permute-done.9.refs_3_ = bf16[512,384]{1,0:T(8,128)(2,1)S(1)} collective-permute-done((bf16[512,384]{1,0:T(8,128)(2,1)S(1)}, bf16[512,384]{1,0:T(8,128)(2,1)S(1)}, u32[]{:S(2)}, u32[]{:S(2)}) %collective-permute-start.9) | collective-permute-done | bytes 393248 | tf_op jit(solution)/shard_map/ppermute | solution.py:395
  104.5 8.3 %collective-permute-start.11 = (bf16[208,256]{1,0:T(8,128)(2,1)S(1)}, bf16[208,256]{1,0:T(8,128)(2,1)S(1)}, u32[]{:S(2)}, u32[]{:S(2)}) collective-permute-start(bf16[208,256]{1,0:T(8,128)(2,1)S(1)} %fusion.7), channel_id=1, source_target_pairs={{0,1},{1,32},{32,33},{33,64},{64,65},{65,96},{96,97},{97,128},{128... | collective-permute-start | bytes 319496 | tf_op jit(solution)/shard_map/ppermute | solution.py:443
  118.0 2.9 %convolution_convert_fusion = bf16[192,4096]{1,0:T(8,128)(2,1)} fusion(bf16[128,4096]{1,0:T(8,128)(2,1)} %reshape.296, s32[128]{0:T(128)S(1)} %multiply_add_fusion), kind=kOutput, calls=%fused_computation | convolution fusion | flops 202137600 | bytes 2621952 | tf_op jit(solution)/shard_map/dot_general | solution.py:479
  120.9 3.7 %reshape.297 = bf16[64,96,128]{2,1,0:T(8,128)(2,1)} reshape(bf16[192,4096]{1,0:T(8,128)(2,1)} %convolution_convert_fusion) | data formatting | bytes 3145728 | tf_op jit(solution)/shard_map/reshape | solution.py:482
  125.4 7.3 %all-to-all-start.1 = ((bf16[64,96,128]{2,1,0:T(8,128)(2,1)}), bf16[64,96,128]{2,1,0:T(8,128)(2,1)}, u32[]{:S(2)}, u32[]{:S(2)}) async-start(bf16[64,96,128]{2,1,0:T(8,128)(2,1)} %reshape.297), calls=%async_computation.1 | async-start | bytes 3145728 | tf_op jit(solution)/shard_map/all_to_all | solution.py:483
  135.7 3.4 %collective-permute-start.14 = (bf16[512,1024]{1,0:T(8,128)(2,1)}, bf16[512,1024]{1,0:T(8,128)(2,1)}, u32[]{:S(2)}, u32[]{:S(2)}) collective-permute-start(bf16[512,1024]{1,0:T(8,128)(2,1)} %get-tuple-element.32), channel_id=1, source_target_pairs={{0,1},{1,0},{2,3},{3,2},{4,5},{5,4},{6,7},{7,6},{8,9},{9,8},{10,11... | collective-permute-start | bytes 3145736 | tf_op jit(solution)/shard_map/ppermute | solution.py:310
  142.6 31.3 %shard_map.160 = bf16[3072,128]{1,0:T(8,128)(2,1)S(1)} custom-call(s32[65]{0:T(128)S(1)} %select_reduce_fusion.1.off, s32[512]{0:T(512)S(1)} %bitcast.59, s32[1]{0:T(128)} %bitcast.9.zp, bf16[512,384]{1,0:T(8,128)(2,1)S(1)} %collective-permute-done.6.refs_0_, bf16[512,384]{1,0:T(8,128)(2,1)S(1)} %collective-permute-done.7.refs_1_, ...), custom_call_target="tpu_custom_call" | custom-call | flops 7516192768 | bytes 8388608 | tf_op jit(solution)/shard_map/pallas_call | solution.py:202
  176.6 35.0 %all_to_all.15 = bf16[64,48,128]{2,1,0:T(8,128)(2,1)S(1)} all-to-all(bf16[64,48,128]{2,1,0:T(8,128)(2,1)S(1)} %bitcast.58), channel_id=1, replica_groups=mesh['xh'=2,'y'=4,'zh'=2,'zp'=4,'xl'=2,'c'=2] {'xh','y','zh','zp'}, dimensions={0} | all-to-all | bytes 1572864 | tf_op jit(solution)/shard_map/all_to_all | solution.py:488
  211.5 3.0 %collective-permute-start.16 = (bf16[3072,128]{1,0:T(8,128)(2,1)S(1)}, bf16[3072,128]{1,0:T(8,128)(2,1)S(1)}, u32[]{:S(2)}, u32[]{:S(2)}) collective-permute-start(bf16[3072,128]{1,0:T(8,128)(2,1)S(1)} %bitcast.56), channel_id=1, source_target_pairs={{0,1},{1,0},{2,3},{3,2},{4,5},{5,4},{6,7},{7,6},{8,9},{9,8},{10,11... | collective-permute-start | bytes 2359304 | tf_op jit(solution)/shard_map/ppermute | solution.py:310
  214.5 13.3 %collective-permute-done.17.a2 = bf16[3072,128]{1,0:T(8,128)(2,1)S(1)} collective-permute-done((bf16[3072,128]{1,0:T(8,128)(2,1)S(1)}, bf16[3072,128]{1,0:T(8,128)(2,1)S(1)}, u32[]{:S(2)}, u32[]{:S(2)}) %collective-permute-start.17) | collective-permute-done | bytes 786464 | tf_op jit(solution)/shard_map/ppermute | solution.py:310
  227.8 3.7 %collective-permute-start.18 = (bf16[3072,128]{1,0:T(8,128)(2,1)S(1)}, bf16[3072,128]{1,0:T(8,128)(2,1)S(1)}, u32[]{:S(2)}, u32[]{:S(2)}) collective-permute-start(bf16[3072,128]{1,0:T(8,128)(2,1)S(1)} %collective-permute-done.17.a2), channel_id=1, source_target_pairs={{0,1},{1,0},{2,3},{3,2},{4,5},{5,4},{6,7},{7,6},{8,9},{9,8},{10,11... | collective-permute-start | bytes 2359304 | tf_op jit(solution)/shard_map/ppermute | solution.py:310
  233.4 11.3 %shard_map.161 = bf16[192,4096]{1,0:T(8,128)(2,1)} custom-call(s32[1]{0:T(128)} %bitcast.core, bf16[3072,128]{1,0:T(8,128)(2,1)S(1)} %bitcast.57, bf16[3072,128]{1,0:T(8,128)(2,1)S(1)} %collective-permute-done.16.a1, bf16[3072,128]{1,0:T(8,128)(2,1)S(1)} %collective-permute-done.17.a2, bf16[3072,128]{1,0:T(8,128)(2,1)S(1)} %collective-permute-done.18.a3, ...), custom_call_target="tpu_custom_call" | custom-call | flops 3221225472 | bytes 16777216 | tf_op jit(solution)/shard_map/pallas_call | solution.py:283
  (116 shorter events, 41.5 us)
Async XLA Ops:
  7.2 96.9 %all-gather.2.cloned.1.call-start = ((), (), s32[]{:S(2)}) async-start(), calls=%async_computation.3 | async-start | bytes 1966080 | tf_op jit(solution)/shard_map/all_gather | solution.py:405
  8.9 12.8 %collective-permute-start = (s32[256]{0:T(256)S(1)}, s32[256]{0:T(256)S(1)}, u32[]{:S(2)}, u32[]{:S(2)}) collective-permute-start(s32[256]{0:T(256)S(1)} %slice.44), channel_id=1, source_target_pairs={{0,4},{4,8},{8,12},{12,16},{16,20},{20,24},{24,28},{28,32},{32,36}... | collective-permute-start | bytes 3080 | tf_op jit(solution)/shard_map/ppermute | solution.py:346
  22.5 19.3 %collective-permute-start.4 = (bf16[96,256]{1,0:T(8,128)(2,1)S(1)}, bf16[96,256]{1,0:T(8,128)(2,1)S(1)}, u32[]{:S(2)}, u32[]{:S(2)}) collective-permute-start(bf16[96,256]{1,0:T(8,128)(2,1)S(1)} %get-tuple-element.57), channel_id=1, source_target_pairs={{0,12},{1,28},{4,8},{5,24},{8,4},{9,20},{12,0},{13,16},{16,13},{17... | collective-permute-start | bytes 147464 | tf_op jit(solution)/shard_map/ppermute | solution.py:395
  27.1 14.7 %collective-permute-start.3 = (bf16[96,256]{1,0:T(8,128)(2,1)S(1)}, bf16[96,256]{1,0:T(8,128)(2,1)S(1)}, u32[]{:S(2)}, u32[]{:S(2)}) collective-permute-start(bf16[96,256]{1,0:T(8,128)(2,1)S(1)} %get-tuple-element.58), channel_id=1, source_target_pairs={{0,8},{1,24},{4,12},{5,28},{8,0},{9,16},{12,4},{13,20},{16,9},{17,... | collective-permute-start | bytes 147464 | tf_op jit(solution)/shard_map/ppermute | solution.py:395
  28.7 13.2 %collective-permute-start.2 = (bf16[96,256]{1,0:T(8,128)(2,1)S(1)}, bf16[96,256]{1,0:T(8,128)(2,1)S(1)}, u32[]{:S(2)}, u32[]{:S(2)}) collective-permute-start(bf16[96,256]{1,0:T(8,128)(2,1)S(1)} %get-tuple-element.59), channel_id=1, source_target_pairs={{0,4},{1,20},{4,0},{5,16},{8,12},{9,28},{12,8},{13,24},{16,5},{17,... | collective-permute-start | bytes 147464 | tf_op jit(solution)/shard_map/ppermute | solution.py:395
  32.4 9.7 %collective-permute-start.1 = (bf16[96,256]{1,0:T(8,128)(2,1)S(1)}, bf16[96,256]{1,0:T(8,128)(2,1)S(1)}, u32[]{:S(2)}, u32[]{:S(2)}) collective-permute-start(bf16[96,256]{1,0:T(8,128)(2,1)S(1)} %get-tuple-element.56), channel_id=1, source_target_pairs={{0,0},{1,16},{4,4},{5,20},{8,8},{9,24},{12,12},{13,28},{16,1},{17,... | collective-permute-start | bytes 147464 | tf_op jit(solution)/shard_map/ppermute | solution.py:395
  42.1 6.1 %collective-permute-start.5 = (bf16[384,256]{1,0:T(8,128)(2,1)S(1)}, bf16[384,256]{1,0:T(8,128)(2,1)S(1)}, u32[]{:S(2)}, u32[]{:S(2)}) collective-permute-start(bf16[384,256]{1,0:T(8,128)(2,1)S(1)} %pad_maximum_fusion.2), channel_id=1, source_target_pairs={{0,128},{128,0},{1,129},{129,1},{2,130},{130,2},{3,131},{131,3},{4... | collective-permute-start | bytes 589832 | tf_op jit(solution)/shard_map/ppermute | solution.py:310
  53.3 51.1 %collective-permute-start.10 = (bf16[512,1024]{1,0:T(8,128)(2,1)}, bf16[512,1024]{1,0:T(8,128)(2,1)}, u32[]{:S(2)}, u32[]{:S(2)}) collective-permute-start(bf16[512,1024]{1,0:T(8,128)(2,1)} %get-tuple-element.43), channel_id=1, source_target_pairs={{0,2},{1,3},{2,0},{3,1},{4,6},{5,7},{6,4},{7,5},{8,10},{9,11},{10,... | collective-permute-start | bytes 3145736 | tf_op jit(solution)/shard_map/ppermute | solution.py:310
  55.5 23.3 %collective-permute-start.6 = (bf16[512,384]{1,0:T(8,128)(2,1)}, bf16[512,384]{1,0:T(8,128)(2,1)S(1)}, u32[]{:S(2)}, u32[]{:S(2)}) collective-permute-start(bf16[512,384]{1,0:T(8,128)(2,1)} %get-tuple-element.47), channel_id=1, source_target_pairs={{0,0},{1,16},{4,4},{5,20},{8,8},{9,24},{12,12},{13,28},{16,1},{17,... | collective-permute-start | bytes 1179656 | tf_op jit(solution)/shard_map/ppermute | solution.py:395
  62.5 28.2 %collective-permute-start.7 = (bf16[512,384]{1,0:T(8,128)(2,1)}, bf16[512,384]{1,0:T(8,128)(2,1)S(1)}, u32[]{:S(2)}, u32[]{:S(2)}) collective-permute-start(bf16[512,384]{1,0:T(8,128)(2,1)} %get-tuple-element.46), channel_id=1, source_target_pairs={{0,4},{1,20},{4,0},{5,16},{8,12},{9,28},{12,8},{13,24},{16,5},{17,... | collective-permute-start | bytes 1179656 | tf_op jit(solution)/shard_map/ppermute | solution.py:395
  63.8 33.3 %collective-permute-start.8 = (bf16[512,384]{1,0:T(8,128)(2,1)}, bf16[512,384]{1,0:T(8,128)(2,1)S(1)}, u32[]{:S(2)}, u32[]{:S(2)}) collective-permute-start(bf16[512,384]{1,0:T(8,128)(2,1)} %get-tuple-element.45), channel_id=1, source_target_pairs={{0,8},{1,24},{4,12},{5,28},{8,0},{9,16},{12,4},{13,20},{16,9},{17,... | collective-permute-start | bytes 1179656 | tf_op jit(solution)/shard_map/ppermute | solution.py:395
  65.9 38.2 %collective-permute-start.9 = (bf16[512,384]{1,0:T(8,128)(2,1)S(1)}, bf16[512,384]{1,0:T(8,128)(2,1)S(1)}, u32[]{:S(2)}, u32[]{:S(2)}) collective-permute-start(bf16[512,384]{1,0:T(8,128)(2,1)S(1)} %get-tuple-element.44), channel_id=1, source_target_pairs={{0,12},{1,28},{4,8},{5,24},{8,4},{9,20},{12,0},{13,16},{16,13},{17... | collective-permute-start | bytes 1179656 | tf_op jit(solution)/shard_map/ppermute | solution.py:395
  69.1 35.0 %all-to-all-start = ((s32[64,1,768]{2,1,0:T(1,128)}), s32[64,1,768]{2,1,0:T(1,128)S(1)}, u32[]{:S(2)}, u32[]{:S(2)}) async-start(s32[64,1,768]{2,1,0:T(1,128)} %broadcast_in_dim.80), calls=%async_computation | async-start | bytes 393216 | tf_op jit(solution)/shard_map/all_to_all | solution.py:412
  104.1 20.6 %collective-permute-start.13 = (bf16[3072,256]{1,0:T(8,128)(2,1)}, bf16[3072,256]{1,0:T(8,128)(2,1)}, u32[]{:S(2)}, u32[]{:S(2)}) collective-permute-start(bf16[3072,256]{1,0:T(8,128)(2,1)} %all-gather.2.cloned.1.call-done.refs_7_), channel_id=1, source_target_pairs={{0,1},{1,0},{2,3},{3,2},{4,5},{5,4},{6,7},{7,6},{8,9},{9,8},{10,11... | collective-permute-start | bytes 4718600 | tf_op jit(solution)/shard_map/ppermute | solution.py:310
  104.5 20.1 %collective-permute-start.11 = (bf16[208,256]{1,0:T(8,128)(2,1)S(1)}, bf16[208,256]{1,0:T(8,128)(2,1)S(1)}, u32[]{:S(2)}, u32[]{:S(2)}) collective-permute-start(bf16[208,256]{1,0:T(8,128)(2,1)S(1)} %fusion.7), channel_id=1, source_target_pairs={{0,1},{1,32},{32,33},{33,64},{64,65},{65,96},{96,97},{97,128},{128... | collective-permute-start | bytes 319496 | tf_op jit(solution)/shard_map/ppermute | solution.py:443
  113.6 11.1 %collective-permute-start.12 = (bf16[208,256]{1,0:T(8,128)(2,1)}, bf16[208,256]{1,0:T(8,128)(2,1)S(1)}, u32[]{:S(2)}, u32[]{:S(2)}) collective-permute-start(bf16[208,256]{1,0:T(8,128)(2,1)} %fusion.3), channel_id=1, source_target_pairs={{1,0},{32,1},{33,32},{64,33},{65,64},{96,65},{97,96},{128,97},{129... | collective-permute-start | bytes 319496 | tf_op jit(solution)/shard_map/ppermute | solution.py:448
  125.4 51.2 %all-to-all-start.1 = ((bf16[64,96,128]{2,1,0:T(8,128)(2,1)}), bf16[64,96,128]{2,1,0:T(8,128)(2,1)}, u32[]{:S(2)}, u32[]{:S(2)}) async-start(bf16[64,96,128]{2,1,0:T(8,128)(2,1)} %reshape.297), calls=%async_computation.1 | async-start | bytes 3145728 | tf_op jit(solution)/shard_map/all_to_all | solution.py:483
  135.7 38.2 %collective-permute-start.14 = (bf16[512,1024]{1,0:T(8,128)(2,1)}, bf16[512,1024]{1,0:T(8,128)(2,1)}, u32[]{:S(2)}, u32[]{:S(2)}) collective-permute-start(bf16[512,1024]{1,0:T(8,128)(2,1)} %get-tuple-element.32), channel_id=1, source_target_pairs={{0,1},{1,0},{2,3},{3,2},{4,5},{5,4},{6,7},{7,6},{8,9},{9,8},{10,11... | collective-permute-start | bytes 3145736 | tf_op jit(solution)/shard_map/ppermute | solution.py:310
  139.1 37.5 %collective-permute-start.15 = (bf16[512,1024]{1,0:T(8,128)(2,1)}, bf16[512,1024]{1,0:T(8,128)(2,1)}, u32[]{:S(2)}, u32[]{:S(2)}) collective-permute-start(bf16[512,1024]{1,0:T(8,128)(2,1)} %get-tuple-element.33), channel_id=1, source_target_pairs={{0,3},{1,2},{2,1},{3,0},{4,7},{5,6},{6,5},{7,4},{8,11},{9,10},{10,... | collective-permute-start | bytes 3145736 | tf_op jit(solution)/shard_map/ppermute | solution.py:310
  173.9 59.5 %copy-start.6 = (f32[1024]{0:T(1024)S(1)}, f32[1024]{0:T(1024)}, u32[]{:S(2)}) copy-start(f32[1024]{0:T(1024)} %param.19) | copy-start | bytes 12292
  173.9 59.5 %copy-start.7 = (bf16[512,512]{1,0:T(8,128)(2,1)S(1)}, bf16[512,512]{1,0:T(8,128)(2,1)}, u32[]{:S(2)}) copy-start(bf16[512,512]{1,0:T(8,128)(2,1)} %constant.117.clone.mix) | copy-start | bytes 1572868
  211.5 16.3 %collective-permute-start.17 = (bf16[3072,128]{1,0:T(8,128)(2,1)S(1)}, bf16[3072,128]{1,0:T(8,128)(2,1)S(1)}, u32[]{:S(2)}, u32[]{:S(2)}) collective-permute-start(bf16[3072,128]{1,0:T(8,128)(2,1)S(1)} %bitcast.55), channel_id=1, source_target_pairs={{0,2},{1,3},{2,0},{3,1},{4,6},{5,7},{6,4},{7,5},{8,10},{9,11},{10,... | collective-permute-start | bytes 2359304 | tf_op jit(solution)/shard_map/ppermute | solution.py:310
  211.5 20.0 %collective-permute-start.16 = (bf16[3072,128]{1,0:T(8,128)(2,1)S(1)}, bf16[3072,128]{1,0:T(8,128)(2,1)S(1)}, u32[]{:S(2)}, u32[]{:S(2)}) collective-permute-start(bf16[3072,128]{1,0:T(8,128)(2,1)S(1)} %bitcast.56), channel_id=1, source_target_pairs={{0,1},{1,0},{2,3},{3,2},{4,5},{5,4},{6,7},{7,6},{8,9},{9,8},{10,11... | collective-permute-start | bytes 2359304 | tf_op jit(solution)/shard_map/ppermute | solution.py:310
  227.8 5.6 %collective-permute-start.18 = (bf16[3072,128]{1,0:T(8,128)(2,1)S(1)}, bf16[3072,128]{1,0:T(8,128)(2,1)S(1)}, u32[]{:S(2)}, u32[]{:S(2)}) collective-permute-start(bf16[3072,128]{1,0:T(8,128)(2,1)S(1)} %collective-permute-done.17.a2), channel_id=1, source_target_pairs={{0,1},{1,0},{2,3},{3,2},{4,5},{5,4},{6,7},{7,6},{8,9},{9,8},{10,11... | collective-permute-start | bytes 2359304 | tf_op jit(solution)/shard_map/ppermute | solution.py:310
  (11 other events, 61.1 us)
Sparse Core Ops, SparseCore 0:
  49.2 31.6 all-gather.1

commit v5 on v4

--- a/solution.py
+++ b/solution.py
@@ -42,14 +42,15 @@
     heads = out_ref.shape[0]
     for j in range(LIVE_MOST):
         rows = pl.ds(pl.multiple_of(idx[j] * BLK, BLK), BLK)
-        k = k_ref[rows, :]
+        k = jnp.where(j < idx[LIVE_MOST], k_ref[rows, :], jnp.inf).astype(bf16)
         v = v_ref[rows, :]
         for p in range(heads):
             out_ref[p, j * BLK : (j + 1) * BLK, :HD] = k[:, p * HD : (p + 1) * HD]
             out_ref[p, j * BLK : (j + 1) * BLK, HD:] = v[:, p * HD : (p + 1) * HD]
 
 
-def rope_kernel(q_ref, k_ref, v_ref, c_ref, s_ref, out_ref):
+def rope_kernel(q_ref, k_ref, v_ref, c_ref, s_ref, extra_ref, out_ref):
+    tokens = q_ref.shape[0]
     c = c_ref[...]
     s = s_ref[...]
     for h in range(out_ref.shape[0]):
@@ -57,16 +58,17 @@
         for j, ref in enumerate((q_ref, k_ref)):
             x = ref[:, cols].astype(f32)
             turned = x * c + pltpu.roll(x, HD // 2, 1) * s
-            out_ref[h, :, j * HD : (j + 1) * HD] = turned.astype(bf16)
-        out_ref[h, :, 2 * HD :] = v_ref[:, cols]
+            out_ref[h, :tokens, j * HD : (j + 1) * HD] = turned.astype(bf16)
+        out_ref[h, :tokens, 2 * HD :] = v_ref[:, cols]
+        out_ref[h, tokens:, :] = extra_ref[...]
 
 
 def attention_kernel(off, tgt, zp, *refs):
     chunks = 4
     ys = refs[:chunks]
-    left, right, ids = refs[chunks : chunks + 3]
-    pieces = refs[chunks + 3 : -13]
-    out, kc, vc, qs, kw, vw, ob, send, mx, ac, idcol, gathered, sems = refs[-13:]
+    left, right = refs[chunks : chunks + 2]
+    pieces = refs[chunks + 2 : -14]
+    out, kc, vc, qs, kw, vw, ob, send, mx, ac, idcol, gathered, ids, sems = refs[-14:]
     i = pl.program_id(0)
     sources = off.shape[0] - 1
     slot_rows = LIVE_MOST * BLK
@@ -88,18 +90,25 @@
         for k, y in enumerate(ys):
             chunk = zp[0] ^ k
             dst = pl.ds(pl.multiple_of(chunk * TOK, TOK), TOK)
-            qs[dst, :] = y[:, :HD]
+            qs[dst, :] = y[:TOK, :HD]
             dst = pl.ds(pl.multiple_of(PAD + chunk * TOK, PAD), TOK)
-            kw[dst, :] = y[:, HD : 2 * HD]
-            vw[dst, :HD] = y[:, 2 * HD :]
+            kw[dst, :] = y[:TOK, HD : 2 * HD]
+            vw[dst, :HD] = y[:TOK, 2 * HD :]
+            line = y[TOK:, :].astype(f32)
+            at = pl.multiple_of(PAD + chunk * TOK, PAD)
+            ids[:, pl.ds(at, 3 * HD)] = line[0:1, :]
+            at = pl.multiple_of(PAD + chunk * TOK + 3 * HD, HD)
+            ids[:, pl.ds(at, HD)] = line[1:2, :HD]
         end = PAD + chunks * TOK
         gap = PAD - HALO
         kw[:gap, :] = jnp.zeros((gap, HD), bf16)
         vw[:gap, :HD] = jnp.zeros((gap, HD), bf16)
-        kw[gap:PAD, :] = left[:, :HD]
-        vw[gap:PAD, :HD] = left[:, HD:]
-        kw[end : end + HALO, :] = right[:, :HD]
-        vw[end : end + HALO, :HD] = right[:, HD:]
+        kw[gap:PAD, :] = left[:HALO, :HD]
+        vw[gap:PAD, :HD] = left[:HALO, HD:]
+        kw[end : end + HALO, :] = right[:HALO, :HD]
+        vw[end : end + HALO, :HD] = right[:HALO, HD:]
+        ids[:, :PAD] = left[HALO:, :].astype(f32)[0:1, :]
+        ids[:, end:] = right[HALO:, :].astype(f32)[0:1, :]
         kw[end + HALO :, :] = jnp.zeros((gap, HD), bf16)
         vw[end + HALO :, :HD] = jnp.zeros((gap, HD), bf16)
         send[...] = jnp.zeros(send.shape, f32)
@@ -183,7 +192,7 @@
     ob[...] = ac[:, :HD] / ac[:, HD:]
 
     def place(r, carry):
-        dst = tgt[i * (TOK // 4) + r] * 4
+        dst = tgt[(i ^ zp[0]) * (TOK // 4) + r] * 4
         send[pl.ds(pl.multiple_of(dst, 4), 4), :] = ob[pl.ds(pl.multiple_of(r * 4, 4), 4), :]
         return carry
 
@@ -194,7 +203,7 @@
         out[...] = send[...].astype(bf16)
 
 
-def attend(off, tgt, zp, ys, left, right, ids, pieces, slots):
+def attend(off, tgt, zp, ys, left, right, pieces, slots):
     chunks = len(ys)
     sources = off.shape[0] - 1
     cache_most = sources * LIVE_MOST * BLK
@@ -205,7 +214,7 @@
         grid_spec=pltpu.PrefetchScalarGridSpec(
             num_scalar_prefetch=3,
             grid=(chunks,),
-            in_specs=[whole] * (chunks + 3)
+            in_specs=[whole] * (chunks + 2)
             + [pl.BlockSpec(memory_space=pl.ANY)] * len(pieces),
             out_specs=whole,
             scratch_shapes=[
@@ -220,6 +229,7 @@
                 pltpu.VMEM((TOK, 2 * HD), f32),
                 pltpu.VMEM((TOK, 128), f32),
                 pltpu.VMEM((cache_most, 2 * HD), bf16),
+                pltpu.VMEM((1, chunks * TOK + 2 * PAD), f32),
                 pltpu.SemaphoreType.DMA((len(pieces),)),
             ],
         ),
@@ -229,7 +239,7 @@
         cost_estimate=pl.CostEstimate(
             flops=4 * 2048 * 7168 * 128, bytes_accessed=8 << 20, transcendentals=2048 * 7168
         ),
-    )(off, tgt, zp, *ys, left, right, ids, *pieces)
+    )(off, tgt, zp, *ys, left, right, *pieces)
 
 
 def project_kernel(core, a0, a1, a2, a3, w0, w1, w2, w3, res, scale, mix, out, att, res32, proj):
@@ -335,10 +345,9 @@
     n_head = lax.axis_size(HEAD)
     n_seq = lax.axis_size(SEQ)
     seq = lax.axis_index(SEQ)
-    xh, y, zp, c = (lax.axis_index(n) for n in ("xh", "y", "zp", "c"))
+    zp, c = (lax.axis_index(n) for n in ("zp", "c"))
     head = lax.axis_index(HEAD)
     merged_rows = tokens // 4
-    group = (xh * 4 + y) * 2 + c
     n_group = n_seq // heads
     whole = pl.BlockSpec(memory_space=pltpu.VMEM)
 
@@ -350,10 +359,12 @@
     first = jnp.min(jnp.where(same, index[None, :], PAD + tokens), axis=1)
     cosine, sine = rope_parts(PAD + jnp.arange(tokens, dtype=jnp.int32) - first)
 
+    extra = jnp.concatenate([marks, owners[:, 0]])
+    extra = jnp.pad(extra, (0, BLK * 3 * HD - extra.shape[0])).astype(bf16).reshape(BLK, 3 * HD)
     qkv = pl.pallas_call(
         rope_kernel,
-        out_shape=jax.ShapeDtypeStruct((heads, tokens, 3 * HD), bf16),
-        in_specs=[whole] * 5,
+        out_shape=jax.ShapeDtypeStruct((heads, tokens + BLK, 3 * HD), bf16),
+        in_specs=[whole] * 6,
         out_specs=whole,
     )(
         queries,
@@ -361,6 +372,7 @@
         values_new,
         jnp.concatenate([cosine, cosine], axis=1),
         jnp.concatenate([-sine, sine], axis=1),
+        extra,
     )
 
     cache_rows = cache_keys.shape[0]
@@ -377,6 +389,7 @@
     rank = jnp.sum(jnp.where(blocks[None, :] < blocks[:, None], live[None, :], False), axis=1)
     hit = live[None, :] & (rank[None, :] == jnp.arange(LIVE_MOST, dtype=jnp.int32)[:, None])
     order = jnp.sum(jnp.where(hit, blocks[None, :], 0), axis=1)
+    order = jnp.concatenate([order, jnp.sum(live.astype(jnp.int32), keepdims=True)])
     kv = pl.pallas_call(
         pack_kernel,
         out_shape=jax.ShapeDtypeStruct((heads, LIVE_MOST * BLK, 2 * HD), bf16),
@@ -403,30 +416,6 @@
     kv4 = tie(kv4, qkv)
     kv8 = jnp.concatenate([kv4, swap(kv4, "xh", 1)], axis=0)
     kv32 = lax.all_gather(kv8, "y", axis=0, tiled=True)
-    pieces = [kv32, swap(tie(kv32, *ys), "c", 1)]
-
-    meta = jnp.concatenate(
-        [marks, owners[:, 0], block_live, jnp.zeros((128 - n_blocks,), jnp.int32)]
-    )
-    meta = jnp.broadcast_to(tie(meta, kv8, qkv)[None, None, :], (n_seq, 1, meta.shape[0]))
-    meta = lax.all_to_all(meta, SEQ, split_axis=0, concat_axis=0, tiled=True)[:, 0, :]
-    marks_all = jnp.pad(meta[:, :tokens].reshape(-1), (PAD, PAD))
-
-    owners_all = meta[:, tokens : tokens + merged_rows]
-    live_all = meta[:, tokens + merged_rows : tokens + merged_rows + n_blocks]
-    counts = jnp.sum((live_all > 0).astype(jnp.int32), axis=1)
-    j4 = jnp.arange(heads, dtype=jnp.int32) ^ zp
-    x2 = jnp.arange(2, dtype=jnp.int32) ^ xh
-    y4 = jnp.arange(4, dtype=jnp.int32)
-    c2 = jnp.arange(2, dtype=jnp.int32) ^ c
-    arrival = (
-        (x2[None, None, :, None] * 4 + y4[None, :, None, None]) * 2 + c2[:, None, None, None]
-    ) * heads + j4[None, None, None, :]
-    arrival = arrival.reshape(-1)
-    every = jnp.arange(n_seq, dtype=jnp.int32)
-    counts = jnp.sum(jnp.where(arrival[:, None] == every[None, :], counts[None, :], 0), axis=1)
-    ends = jnp.arange(n_seq + 1, dtype=jnp.int32)
-    off = jnp.sum(jnp.where(every[None, :] < ends[:, None], counts[None, :] * BLK, 0), axis=1)
 
     width = residual.shape[1]
     out_weight = tie(out_weight, kv8)
@@ -436,33 +425,51 @@
     ]
     weight_x = swap(blocks_w[2], HEAD, 2)
 
-    ends_of = tie(tuple(ys), weight_x, meta)
-    tails = jnp.stack([t[tokens - HALO :, HD:] for t in ends_of])
-    starts = jnp.stack([t[:HALO, HD:] for t in ends_of])
-    ahead = [(i, i + 1) for i in range(n_group - 1)]
-    left = lax.ppermute(
-        lax.dynamic_index_in_dim(tails, zp ^ (heads - 1), 0, keepdims=False),
-        ("xh", "y", "c"),
-        ahead,
-    )
-    right = lax.ppermute(
-        lax.dynamic_index_in_dim(starts, zp, 0, keepdims=False),
-        ("xh", "y", "c"),
-        [(j, i) for i, j in ahead],
-    )
-    span = heads * tokens
-    ids = lax.dynamic_slice(
-        marks_all, (group * span,), (span + 2 * PAD,)
-    )
-    ids = ids.astype(f32)[None, :]
-
     def slots_of(owner_rows):
         r = jnp.arange(merged_rows, dtype=jnp.int32)
         equal = owner_rows[:, :, None] == owner_rows[:, None, :]
         return jnp.sum((equal & (r[None, None, :] < r[None, :, None])).astype(jnp.int32), axis=2)
 
-    group_owners = lax.dynamic_slice(owners_all, (group * heads, 0), (heads, merged_rows))
-    peer = jnp.arange(heads, dtype=jnp.int32)[:, None]
+    own_target = owners[:, 0] * CAP + slots_of(owners[:, 0][None, :])[0]
+    choose = (jnp.arange(n_seq * CAP, dtype=jnp.int32)[:, None] == own_target[None, :]).astype(bf16)
+    residual = tie(residual, kv8, qkv)
+    res = jnp.dot(
+        choose, residual.reshape(merged_rows, 4 * width), preferred_element_type=f32
+    ).astype(bf16)
+    res = res.reshape(n_seq, CAP * 4 * width // HD, HD)
+
+    edges = tie(tuple(ys), weight_x, res)
+
+    def edge(low, j, line, pairs):
+        part = jnp.stack([t[low : low + HALO, HD:] for t in edges])
+        part = lax.dynamic_index_in_dim(part, j, 0, keepdims=False)
+        line = lax.dynamic_index_in_dim(jnp.stack([line(t[tokens : tokens + 2]) for t in edges]), j, 0)
+        part = jnp.concatenate([part, jnp.pad(line, ((0, BLK - 1), (0, 0)))], axis=0)
+        return lax.ppermute(part, ("xh", "y", "c"), pairs)
+
+    ahead = [(i, i + 1) for i in range(n_group - 1)]
+    none = jnp.zeros((PAD - HALO,), bf16)
+    lead = tokens - HALO
+    left = edge(
+        lead,
+        zp ^ (heads - 1),
+        lambda t: jnp.concatenate([none, t[0, lead:], t[1, : tokens - 3 * HD]]),
+        ahead,
+    )
+    right = edge(
+        0, zp, lambda t: jnp.concatenate([t[0, :HALO], none]), [(j, i) for i, j in ahead]
+    )
+
+    pieces = [kv32, swap(tie(kv32, left, right), "c", 1)]
+
+    firsts = jnp.stack([p.reshape(-1, LIVE_MOST, BLK, 2 * HD)[:, :, 0, 0] for p in pieces])
+    counts = jnp.sum(jnp.isfinite(firsts).astype(jnp.int32), axis=2).reshape(-1)
+    every = jnp.arange(n_seq, dtype=jnp.int32)
+    ends = jnp.arange(n_seq + 1, dtype=jnp.int32)
+    off = jnp.sum(jnp.where(every[None, :] < ends[:, None], counts[None, :] * BLK, 0), axis=1)
+
+    group_owners = jnp.stack([t[tokens + 1, HD : HD + merged_rows] for t in ys]).astype(jnp.int32)
+    peer = (jnp.arange(heads, dtype=jnp.int32) ^ zp)[:, None]
     tgt = (group_owners * (heads * CAP) + peer * CAP + slots_of(group_owners)).reshape(-1)
 
     weights = [
@@ -472,18 +479,10 @@
         swap(tie(blocks_w[3], left, right), HEAD, 3),
     ]
 
-    own_target = owners[:, 0] * CAP + slots_of(owners[:, 0][None, :])[0]
-    choose = (jnp.arange(n_seq * CAP, dtype=jnp.int32)[:, None] == own_target[None, :]).astype(bf16)
-    width = residual.shape[1]
-    residual = tie(residual, kv32)
-    res = jnp.dot(
-        choose, residual.reshape(merged_rows, 4 * width), preferred_element_type=f32
-    ).astype(bf16)
-    res = res.reshape(n_seq, CAP * 4 * width // HD, HD)
-    res = lax.all_to_all(tie(res, pieces[1], left, right), SEQ, split_axis=0, concat_axis=0, tiled=True)
+    res = lax.all_to_all(tie(res, pieces[1], weight_x, left, right), SEQ, split_axis=0, concat_axis=0, tiled=True)
 
     one = zp[None].astype(jnp.int32)
-    sent = attend(off, tgt, one, ys, left, right, ids, pieces, n_seq * heads * CAP)
+    sent = attend(off, tgt, one, ys, left, right, pieces, n_seq * heads * CAP)
     sent, res, *weights = lax.optimization_barrier((sent, res, *weights))
     got = lax.all_to_all(
         sent.reshape(n_seq, heads * CAP * 4, HD), SEQ, split_axis=0, concat_axis=0, tiled=True

time: 253 us -> 247 us (0.976)
  starting transfers between devices: 71.9 us -> 61.2 us
  waiting for transfers between devices: 46.7 us -> 52.8 us
    ppermute x2, starting transfers between devices: 10.2 us -> 4.33 us  [edge(): return lax.ppermute(part, ('xh', 'y', 'c'), pairs)]
    ppermute x8, waiting for transfers between devices: 21.2 us -> 25 us  [swap(): return lax.ppermute(x, axis, [(i, i ^ k) for i in range(n)])]
    ppermute x2, waiting for transfers between devices: 0.01 us -> 3.69 us  [edge(): return lax.ppermute(part, ('xh', 'y', 'c'), pairs)]
    all_to_all x2 -> x1, starting transfers between devices: 16.9 us -> 14 us  [shards(): lax.all_to_all(tie(res, pieces[1], weight_x, left, right), SEQ, split_axi...]
    ppermute x8, starting transfers between devices: 14.1 us -> 11.4 us  [swap(): return lax.ppermute(x, axis, [(i, i ^ k) for i in range(n)])]
    unnamed x29 -> x24, local copies, waits for them, and re-layouts: 6.3 us -> 3.66 us
  transfers between devices with their start and end apart: 22 -> 21, of which waited for: 8 -> 10; matrix products, arithmetic and copies ran while one was open for 11% -> 10% of each run, Pallas kernels for 15% -> 15%
where the time goes in v5:
time: 247 us; the launch traced here: 246 us
  starting transfers between devices  61.2 us (25%)
  waiting for transfers between devices  52.8 us (21%)
  Pallas kernels  48.5 us (20%)
  blocking collectives  35 us (14%)
  local copies, waits for them, and re-layouts  19.5 us (8%)
  between operations  15.2 us (6%)
  other arithmetic  7.92 us (3%)
  matrix products  5.76 us (2%)
    all_to_all x1, blocking collectives, shards(): lax.all_to_all(sent.reshape(n_seq, heads * CAP * 4, HD), SEQ, split_axis=...  35 us
    pallas_call x1, Pallas kernels, attend(): pl.pallas_call(attention_kernel, out_shape=jax.ShapeDtypeStruct((slots *...  31.6 us
    ppermute x8, starting transfers between devices, spread(): return lax.ppermute(part, ('zh', 'zp', 'c'), pairs)  27.2 us
    ppermute x8, waiting for transfers between devices, swap(): return lax.ppermute(x, axis, [(i, i ^ k) for i in range(n)])  25 us
    ppermute x8, waiting for transfers between devices, spread(): return lax.ppermute(part, ('zh', 'zp', 'c'), pairs)  24.1 us
    all_to_all x1, starting transfers between devices, shards(): lax.all_to_all(tie(res, pieces[1], weight_x, left, right), SEQ, split_axi...  14 us
    pallas_call x1, Pallas kernels, project(): pl.pallas_call(project_kernel, out_shape=jax.ShapeDtypeStruct((slots, 4 *...  11.4 us
    ppermute x8, starting transfers between devices, swap(): return lax.ppermute(x, axis, [(i, i ^ k) for i in range(n)])  11.4 us
  transfers between devices with their start and end apart: 21, of which 10 were waited for; matrix products, arithmetic and copies ran while one was open for 10% of the time, Pallas kernels for 15%

profile of v5, /device:TPU:1, one launch (start us, length us, event | category | flops | bytes accessed | tf_op | source)
XLA Modules:
  0.0 246.0 jit_solution(11724123222123823004)
XLA Ops:
  8.9 4.4 %collective-permute-start = (s32[256]{0:T(256)S(1)}, s32[256]{0:T(256)S(1)}, u32[]{:S(2)}, u32[]{:S(2)}) collective-permute-start(s32[256]{0:T(256)S(1)} %slice.109), channel_id=1, source_target_pairs={{0,4},{4,8},{8,12},{12,16},{16,20},{20,24},{24,28},{28,32},{32,36}... | collective-permute-start | bytes 3080 | tf_op jit(solution)/shard_map/ppermute | solution.py:355
  24.6 4.6 %collective-permute-start.4 = (bf16[96,256]{1,0:T(8,128)(2,1)S(1)}, bf16[96,256]{1,0:T(8,128)(2,1)S(1)}, u32[]{:S(2)}, u32[]{:S(2)}) collective-permute-start(bf16[96,256]{1,0:T(8,128)(2,1)S(1)} %get-tuple-element.55), channel_id=1, source_target_pairs={{0,12},{1,28},{4,8},{5,24},{8,4},{9,20},{12,0},{13,16},{16,13},{17... | collective-permute-start | bytes 147464 | tf_op jit(solution)/shard_map/ppermute | solution.py:408
  30.7 3.7 %collective-permute-start.2 = (bf16[96,256]{1,0:T(8,128)(2,1)S(1)}, bf16[96,256]{1,0:T(8,128)(2,1)S(1)}, u32[]{:S(2)}, u32[]{:S(2)}) collective-permute-start(bf16[96,256]{1,0:T(8,128)(2,1)S(1)} %get-tuple-element.57), channel_id=1, source_target_pairs={{0,4},{1,20},{4,0},{5,16},{8,12},{9,28},{12,8},{13,24},{16,5},{17,... | collective-permute-start | bytes 147464 | tf_op jit(solution)/shard_map/ppermute | solution.py:408
  34.5 3.7 %collective-permute-start.1 = (bf16[96,256]{1,0:T(8,128)(2,1)S(1)}, bf16[96,256]{1,0:T(8,128)(2,1)S(1)}, u32[]{:S(2)}, u32[]{:S(2)}) collective-permute-start(bf16[96,256]{1,0:T(8,128)(2,1)S(1)} %get-tuple-element.54), channel_id=1, source_target_pairs={{0,0},{1,16},{4,4},{5,20},{8,8},{9,24},{12,12},{13,28},{16,1},{17,... | collective-permute-start | bytes 147464 | tf_op jit(solution)/shard_map/ppermute | solution.py:408
  40.6 3.3 %shard_map.159 = bf16[4,528,384]{2,1,0:T(8,128)(2,1)} custom-call(bf16[512,512]{1,0:T(8,128)(2,1)} %q_ref.1, bf16[512,512]{1,0:T(8,128)(2,1)} %k_ref.1, bf16[512,512]{1,0:T(8,128)(2,1)} %v_ref.3, f32[512,128]{1,0:T(8,128)} %get-tuple-element.71.c_ref, f32[512,128]{1,0:T(8,128)} %get-tuple-element.72.s_ref, bf16[16,384]{1,0:T(8,128)(2,1)} %reshape.300.extra_ref), custom_call_target="tpu_custom_call" | custom-call | tf_op jit(solution)/shard_map/pallas_call | solution.py:364
  47.0 3.3 %collective-permute-done.5 = bf16[384,256]{1,0:T(8,128)(2,1)S(1)} collective-permute-done((bf16[384,256]{1,0:T(8,128)(2,1)S(1)}, bf16[384,256]{1,0:T(8,128)(2,1)S(1)}, u32[]{:S(2)}, u32[]{:S(2)}) %collective-permute-start.5) | collective-permute-done | bytes 196640 | tf_op jit(solution)/shard_map/ppermute | solution.py:320
  50.3 4.2 %constant_dynamic-slice_fusion.4 = (bf16[512,1024]{1,0:T(8,128)(2,1)}, bf16[512,1024]{1,0:T(8,128)(2,1)}, bf16[512,1024]{1,0:T(8,128)(2,1)S(1)}, bf16[512,1024]{1,0:T(8,128)(2,1)}) fusion(bf16[512,4096]{1,0:T(8,128)(2,1)} %param.20, s32[]{:T(128)S(6)} %select_n.79, s32[]{:T(128)S(6)} %select_n.78, s32[]{:T(128)S(6)} %select_n.77, s32[]{:T(128)S(6)} %select_n.75), kind=kLoop, calls=%fused_computation.69 | loop fusion | bytes 8388624 | tf_op jit(solution)/shard_map/dynamic_slice | solution.py:423
  57.0 6.9 %collective-permute-start.6 = (bf16[528,384]{1,0:T(8,128)(2,1)}, bf16[528,384]{1,0:T(8,128)(2,1)S(1)}, u32[]{:S(2)}, u32[]{:S(2)}) collective-permute-start(bf16[528,384]{1,0:T(8,128)(2,1)} %get-tuple-element.45), channel_id=1, source_target_pairs={{0,0},{1,16},{4,4},{5,20},{8,8},{9,24},{12,12},{13,28},{16,1},{17,... | collective-permute-start | bytes 1216520 | tf_op jit(solution)/shard_map/ppermute | solution.py:408
  67.3 3.3 %collective-permute-start.9 = (bf16[528,384]{1,0:T(8,128)(2,1)S(1)}, bf16[528,384]{1,0:T(8,128)(2,1)S(1)}, u32[]{:S(2)}, u32[]{:S(2)}) collective-permute-start(bf16[528,384]{1,0:T(8,128)(2,1)S(1)} %get-tuple-element.42), channel_id=1, source_target_pairs={{0,12},{1,28},{4,8},{5,24},{8,4},{9,20},{12,0},{13,16},{16,13},{17... | collective-permute-start | bytes 1216520 | tf_op jit(solution)/shard_map/ppermute | solution.py:408
  73.1 2.9 %convolution_convert_fusion = bf16[192,4096]{1,0:T(8,128)(2,1)} fusion(bf16[128,4096]{1,0:T(8,128)(2,1)} %reshape.302, s32[128]{0:T(128)S(1)} %multiply_add_fusion), kind=kOutput, calls=%fused_computation | convolution fusion | flops 202137600 | bytes 2621952 | tf_op jit(solution)/shard_map/dot_general | solution.py:436
  76.0 3.8 %reshape.303 = bf16[64,96,128]{2,1,0:T(8,128)(2,1)} reshape(bf16[192,4096]{1,0:T(8,128)(2,1)} %convolution_convert_fusion) | data formatting | bytes 3145728 | tf_op jit(solution)/shard_map/reshape | solution.py:439
  79.8 11.4 %collective-permute-done.7.refs_1_ = bf16[528,384]{1,0:T(8,128)(2,1)S(1)} collective-permute-done((bf16[528,384]{1,0:T(8,128)(2,1)}, bf16[528,384]{1,0:T(8,128)(2,1)S(1)}, u32[]{:S(2)}, u32[]{:S(2)}) %collective-permute-start.7) | collective-permute-done | bytes 405536 | tf_op jit(solution)/shard_map/ppermute | solution.py:408
  91.2 5.3 %collective-permute-done.8.refs_2_ = bf16[528,384]{1,0:T(8,128)(2,1)S(1)} collective-permute-done((bf16[528,384]{1,0:T(8,128)(2,1)}, bf16[528,384]{1,0:T(8,128)(2,1)S(1)}, u32[]{:S(2)}, u32[]{:S(2)}) %collective-permute-start.8) | collective-permute-done | bytes 405536 | tf_op jit(solution)/shard_map/ppermute | solution.py:408
  96.5 7.1 %collective-permute-done.9.refs_3_ = bf16[528,384]{1,0:T(8,128)(2,1)S(1)} collective-permute-done((bf16[528,384]{1,0:T(8,128)(2,1)S(1)}, bf16[528,384]{1,0:T(8,128)(2,1)S(1)}, u32[]{:S(2)}, u32[]{:S(2)}) %collective-permute-start.9) | collective-permute-done | bytes 405536 | tf_op jit(solution)/shard_map/ppermute | solution.py:408
  109.0 3.7 %collective-permute-done.12.refs_5_ = bf16[224,256]{1,0:T(8,128)(2,1)S(1)} collective-permute-done((bf16[224,256]{1,0:T(8,128)(2,1)S(1)}, bf16[224,256]{1,0:T(8,128)(2,1)S(1)}, u32[]{:S(2)}, u32[]{:S(2)}) %collective-permute-start.12) | collective-permute-done | bytes 114720 | tf_op jit(solution)/shard_map/ppermute | solution.py:448
  112.7 3.8 %collective-permute-done.13.refs_7_ = bf16[3072,256]{1,0:T(8,128)(2,1)} collective-permute-done((bf16[3072,256]{1,0:T(8,128)(2,1)}, bf16[3072,256]{1,0:T(8,128)(2,1)}, u32[]{:S(2)}, u32[]{:S(2)}) %collective-permute-start.13) | collective-permute-done | bytes 1572896 | tf_op jit(solution)/shard_map/ppermute | solution.py:320
  116.5 14.0 %all-to-all-start = ((bf16[64,96,128]{2,1,0:T(8,128)(2,1)}), bf16[64,96,128]{2,1,0:T(8,128)(2,1)}, u32[]{:S(2)}, u32[]{:S(2)}) async-start(bf16[64,96,128]{2,1,0:T(8,128)(2,1)} %reshape.303), calls=%async_computation | async-start | bytes 3145728 | tf_op jit(solution)/shard_map/all_to_all | solution.py:482
  136.4 31.6 %shard_map.160 = bf16[3072,128]{1,0:T(8,128)(2,1)S(1)} custom-call(s32[65]{0:T(128)S(1)} %select_reduce_fusion.1.off, s32[512]{0:T(512)S(1)} %add_bitcast_fusion.tgt, s32[1]{0:T(128)} %bitcast.35.zp, bf16[528,384]{1,0:T(8,128)(2,1)S(1)} %collective-permute-done.6.refs_0_, bf16[528,384]{1,0:T(8,128)(2,1)S(1)} %collective-permute-done.7.refs_1_, ...), custom_call_target="tpu_custom_call" | custom-call | flops 7516192768 | bytes 8388608 | tf_op jit(solution)/shard_map/pallas_call | solution.py:211
  168.0 2.9 %collective-permute-done.15.w3 = bf16[512,1024]{1,0:T(8,128)(2,1)} collective-permute-done((bf16[512,1024]{1,0:T(8,128)(2,1)}, bf16[512,1024]{1,0:T(8,128)(2,1)}, u32[]{:S(2)}, u32[]{:S(2)}) %collective-permute-start.15) | collective-permute-done | bytes 1048608 | tf_op jit(solution)/shard_map/ppermute | solution.py:320
  170.9 35.0 %all_to_all.10 = bf16[64,48,128]{2,1,0:T(8,128)(2,1)S(1)} all-to-all(bf16[64,48,128]{2,1,0:T(8,128)(2,1)S(1)} %bitcast.78), channel_id=1, replica_groups=mesh['xh'=2,'y'=4,'zh'=2,'zp'=4,'xl'=2,'c'=2] {'xh','y','zh','zp'}, dimensions={0} | all-to-all | bytes 1572864 | tf_op jit(solution)/shard_map/all_to_all | solution.py:487
  206.2 2.9 %collective-permute-start.16 = (bf16[3072,128]{1,0:T(8,128)(2,1)S(1)}, bf16[3072,128]{1,0:T(8,128)(2,1)S(1)}, u32[]{:S(2)}, u32[]{:S(2)}) collective-permute-start(bf16[3072,128]{1,0:T(8,128)(2,1)S(1)} %bitcast.76), channel_id=1, source_target_pairs={{0,1},{1,0},{2,3},{3,2},{4,5},{5,4},{6,7},{7,6},{8,9},{9,8},{10,11... | collective-permute-start | bytes 2359304 | tf_op jit(solution)/shard_map/ppermute | solution.py:320
  209.1 13.1 %collective-permute-done.17.a2 = bf16[3072,128]{1,0:T(8,128)(2,1)S(1)} collective-permute-done((bf16[3072,128]{1,0:T(8,128)(2,1)S(1)}, bf16[3072,128]{1,0:T(8,128)(2,1)S(1)}, u32[]{:S(2)}, u32[]{:S(2)}) %collective-permute-start.17) | collective-permute-done | bytes 786464 | tf_op jit(solution)/shard_map/ppermute | solution.py:320
  222.2 3.6 %collective-permute-start.18 = (bf16[3072,128]{1,0:T(8,128)(2,1)S(1)}, bf16[3072,128]{1,0:T(8,128)(2,1)S(1)}, u32[]{:S(2)}, u32[]{:S(2)}) collective-permute-start(bf16[3072,128]{1,0:T(8,128)(2,1)S(1)} %collective-permute-done.17.a2), channel_id=1, source_target_pairs={{0,1},{1,0},{2,3},{3,2},{4,5},{5,4},{6,7},{7,6},{8,9},{9,8},{10,11... | collective-permute-start | bytes 2359304 | tf_op jit(solution)/shard_map/ppermute | solution.py:320
  227.8 11.4 %shard_map.161 = bf16[192,4096]{1,0:T(8,128)(2,1)} custom-call(s32[1]{0:T(128)} %bitcast.core, bf16[3072,128]{1,0:T(8,128)(2,1)S(1)} %bitcast.77, bf16[3072,128]{1,0:T(8,128)(2,1)S(1)} %collective-permute-done.16.a1, bf16[3072,128]{1,0:T(8,128)(2,1)S(1)} %collective-permute-done.17.a2, bf16[3072,128]{1,0:T(8,128)(2,1)S(1)} %collective-permute-done.18.a3, ...), custom_call_target="tpu_custom_call" | custom-call | flops 3221225472 | bytes 16777216 | tf_op jit(solution)/shard_map/pallas_call | solution.py:293
  (132 shorter events, 41.0 us)
Async XLA Ops:
  7.2 105.5 %all-gather.2.cloned.1.call-start = ((), (), s32[]{:S(2)}) async-start(), calls=%async_computation.2 | async-start | bytes 1966080 | tf_op jit(solution)/shard_map/all_gather | solution.py:418
  8.9 14.8 %collective-permute-start = (s32[256]{0:T(256)S(1)}, s32[256]{0:T(256)S(1)}, u32[]{:S(2)}, u32[]{:S(2)}) collective-permute-start(s32[256]{0:T(256)S(1)} %slice.109), channel_id=1, source_target_pairs={{0,4},{4,8},{8,12},{12,16},{16,20},{20,24},{24,28},{28,32},{32,36}... | collective-permute-start | bytes 3080 | tf_op jit(solution)/shard_map/ppermute | solution.py:355
  24.6 19.3 %collective-permute-start.4 = (bf16[96,256]{1,0:T(8,128)(2,1)S(1)}, bf16[96,256]{1,0:T(8,128)(2,1)S(1)}, u32[]{:S(2)}, u32[]{:S(2)}) collective-permute-start(bf16[96,256]{1,0:T(8,128)(2,1)S(1)} %get-tuple-element.55), channel_id=1, source_target_pairs={{0,12},{1,28},{4,8},{5,24},{8,4},{9,20},{12,0},{13,16},{16,13},{17... | collective-permute-start | bytes 147464 | tf_op jit(solution)/shard_map/ppermute | solution.py:408
  29.2 14.7 %collective-permute-start.3 = (bf16[96,256]{1,0:T(8,128)(2,1)S(1)}, bf16[96,256]{1,0:T(8,128)(2,1)S(1)}, u32[]{:S(2)}, u32[]{:S(2)}) collective-permute-start(bf16[96,256]{1,0:T(8,128)(2,1)S(1)} %get-tuple-element.56), channel_id=1, source_target_pairs={{0,8},{1,24},{4,12},{5,28},{8,0},{9,16},{12,4},{13,20},{16,9},{17,... | collective-permute-start | bytes 147464 | tf_op jit(solution)/shard_map/ppermute | solution.py:408
  30.7 13.1 %collective-permute-start.2 = (bf16[96,256]{1,0:T(8,128)(2,1)S(1)}, bf16[96,256]{1,0:T(8,128)(2,1)S(1)}, u32[]{:S(2)}, u32[]{:S(2)}) collective-permute-start(bf16[96,256]{1,0:T(8,128)(2,1)S(1)} %get-tuple-element.57), channel_id=1, source_target_pairs={{0,4},{1,20},{4,0},{5,16},{8,12},{9,28},{12,8},{13,24},{16,5},{17,... | collective-permute-start | bytes 147464 | tf_op jit(solution)/shard_map/ppermute | solution.py:408
  34.5 9.7 %collective-permute-start.1 = (bf16[96,256]{1,0:T(8,128)(2,1)S(1)}, bf16[96,256]{1,0:T(8,128)(2,1)S(1)}, u32[]{:S(2)}, u32[]{:S(2)}) collective-permute-start(bf16[96,256]{1,0:T(8,128)(2,1)S(1)} %get-tuple-element.54), channel_id=1, source_target_pairs={{0,0},{1,16},{4,4},{5,20},{8,8},{9,24},{12,12},{13,28},{16,1},{17,... | collective-permute-start | bytes 147464 | tf_op jit(solution)/shard_map/ppermute | solution.py:408
  44.2 6.1 %collective-permute-start.5 = (bf16[384,256]{1,0:T(8,128)(2,1)S(1)}, bf16[384,256]{1,0:T(8,128)(2,1)S(1)}, u32[]{:S(2)}, u32[]{:S(2)}) collective-permute-start(bf16[384,256]{1,0:T(8,128)(2,1)S(1)} %pad_maximum_fusion.2), channel_id=1, source_target_pairs={{0,128},{128,0},{1,129},{129,1},{2,130},{130,2},{3,131},{131,3},{4... | collective-permute-start | bytes 589832 | tf_op jit(solution)/shard_map/ppermute | solution.py:320
  54.5 49.1 %collective-permute-start.10 = (bf16[512,1024]{1,0:T(8,128)(2,1)}, bf16[512,1024]{1,0:T(8,128)(2,1)}, u32[]{:S(2)}, u32[]{:S(2)}) collective-permute-start(bf16[512,1024]{1,0:T(8,128)(2,1)} %get-tuple-element.41), channel_id=1, source_target_pairs={{0,2},{1,3},{2,0},{3,1},{4,6},{5,7},{6,4},{7,5},{8,10},{9,11},{10,... | collective-permute-start | bytes 3145736 | tf_op jit(solution)/shard_map/ppermute | solution.py:320
  57.0 22.8 %collective-permute-start.6 = (bf16[528,384]{1,0:T(8,128)(2,1)}, bf16[528,384]{1,0:T(8,128)(2,1)S(1)}, u32[]{:S(2)}, u32[]{:S(2)}) collective-permute-start(bf16[528,384]{1,0:T(8,128)(2,1)} %get-tuple-element.45), channel_id=1, source_target_pairs={{0,0},{1,16},{4,4},{5,20},{8,8},{9,24},{12,12},{13,28},{16,1},{17,... | collective-permute-start | bytes 1216520 | tf_op jit(solution)/shard_map/ppermute | solution.py:408
  63.9 27.3 %collective-permute-start.7 = (bf16[528,384]{1,0:T(8,128)(2,1)}, bf16[528,384]{1,0:T(8,128)(2,1)S(1)}, u32[]{:S(2)}, u32[]{:S(2)}) collective-permute-start(bf16[528,384]{1,0:T(8,128)(2,1)} %get-tuple-element.44), channel_id=1, source_target_pairs={{0,4},{1,20},{4,0},{5,16},{8,12},{9,28},{12,8},{13,24},{16,5},{17,... | collective-permute-start | bytes 1216520 | tf_op jit(solution)/shard_map/ppermute | solution.py:408
  66.1 30.4 %collective-permute-start.8 = (bf16[528,384]{1,0:T(8,128)(2,1)}, bf16[528,384]{1,0:T(8,128)(2,1)S(1)}, u32[]{:S(2)}, u32[]{:S(2)}) collective-permute-start(bf16[528,384]{1,0:T(8,128)(2,1)} %get-tuple-element.43), channel_id=1, source_target_pairs={{0,8},{1,24},{4,12},{5,28},{8,0},{9,16},{12,4},{13,20},{16,9},{17,... | collective-permute-start | bytes 1216520 | tf_op jit(solution)/shard_map/ppermute | solution.py:408
  67.3 36.3 %collective-permute-start.9 = (bf16[528,384]{1,0:T(8,128)(2,1)S(1)}, bf16[528,384]{1,0:T(8,128)(2,1)S(1)}, u32[]{:S(2)}, u32[]{:S(2)}) collective-permute-start(bf16[528,384]{1,0:T(8,128)(2,1)S(1)} %get-tuple-element.42), channel_id=1, source_target_pairs={{0,12},{1,28},{4,8},{5,24},{8,4},{9,20},{12,0},{13,16},{16,13},{17... | collective-permute-start | bytes 1216520 | tf_op jit(solution)/shard_map/ppermute | solution.py:408
  103.6 26.9 %copy-start.1 = (bf16[528,384]{1,0:T(8,128)(2,1)}, bf16[528,384]{1,0:T(8,128)(2,1)S(1)}, u32[]{:S(2)}) copy-start(bf16[528,384]{1,0:T(8,128)(2,1)S(1)} %collective-permute-done.9.refs_3_) | copy-start | bytes 1216516
  104.3 4.7 %collective-permute-start.11 = (bf16[224,256]{1,0:T(8,128)(2,1)S(1)}, bf16[224,256]{1,0:T(8,128)(2,1)S(1)}, u32[]{:S(2)}, u32[]{:S(2)}) collective-permute-start(bf16[224,256]{1,0:T(8,128)(2,1)S(1)} %fusion.2), channel_id=1, source_target_pairs={{0,1},{1,32},{32,33},{33,64},{64,65},{65,96},{96,97},{97,128},{128... | collective-permute-start | bytes 344072 | tf_op jit(solution)/shard_map/ppermute | solution.py:448
  106.6 6.1 %collective-permute-start.12 = (bf16[224,256]{1,0:T(8,128)(2,1)S(1)}, bf16[224,256]{1,0:T(8,128)(2,1)S(1)}, u32[]{:S(2)}, u32[]{:S(2)}) collective-permute-start(bf16[224,256]{1,0:T(8,128)(2,1)S(1)} %fusion.3), channel_id=1, source_target_pairs={{1,0},{32,1},{33,32},{64,33},{65,64},{96,65},{97,96},{128,97},{129... | collective-permute-start | bytes 344072 | tf_op jit(solution)/shard_map/ppermute | solution.py:448
  112.7 3.8 %collective-permute-start.13 = (bf16[3072,256]{1,0:T(8,128)(2,1)}, bf16[3072,256]{1,0:T(8,128)(2,1)}, u32[]{:S(2)}, u32[]{:S(2)}) collective-permute-start(bf16[3072,256]{1,0:T(8,128)(2,1)} %all-gather.2.cloned.1.call-done.refs_6_), channel_id=1, source_target_pairs={{0,1},{1,0},{2,3},{3,2},{4,5},{5,4},{6,7},{7,6},{8,9},{9,8},{10,11... | collective-permute-start | bytes 4718600 | tf_op jit(solution)/shard_map/ppermute | solution.py:320
  116.5 54.4 %all-to-all-start = ((bf16[64,96,128]{2,1,0:T(8,128)(2,1)}), bf16[64,96,128]{2,1,0:T(8,128)(2,1)}, u32[]{:S(2)}, u32[]{:S(2)}) async-start(bf16[64,96,128]{2,1,0:T(8,128)(2,1)} %reshape.303), calls=%async_computation | async-start | bytes 3145728 | tf_op jit(solution)/shard_map/all_to_all | solution.py:482
  130.8 37.2 %collective-permute-start.14 = (bf16[512,1024]{1,0:T(8,128)(2,1)}, bf16[512,1024]{1,0:T(8,128)(2,1)}, u32[]{:S(2)}, u32[]{:S(2)}) collective-permute-start(bf16[512,1024]{1,0:T(8,128)(2,1)} %get-tuple-element.30), channel_id=1, source_target_pairs={{0,1},{1,0},{2,3},{3,2},{4,5},{5,4},{6,7},{7,6},{8,9},{9,8},{10,11... | collective-permute-start | bytes 3145736 | tf_op jit(solution)/shard_map/ppermute | solution.py:320
  131.3 39.6 %collective-permute-start.15 = (bf16[512,1024]{1,0:T(8,128)(2,1)}, bf16[512,1024]{1,0:T(8,128)(2,1)}, u32[]{:S(2)}, u32[]{:S(2)}) collective-permute-start(bf16[512,1024]{1,0:T(8,128)(2,1)} %get-tuple-element.31), channel_id=1, source_target_pairs={{0,3},{1,2},{2,1},{3,0},{4,7},{5,6},{6,5},{7,4},{8,11},{9,10},{10,... | collective-permute-start | bytes 3145736 | tf_op jit(solution)/shard_map/ppermute | solution.py:320
  168.0 59.8 %copy-start.4 = (f32[1024]{0:T(1024)S(1)}, f32[1024]{0:T(1024)}, u32[]{:S(2)}) copy-start(f32[1024]{0:T(1024)} %param.19) | copy-start | bytes 12292
  168.0 59.8 %copy-start.5 = (bf16[512,512]{1,0:T(8,128)(2,1)S(1)}, bf16[512,512]{1,0:T(8,128)(2,1)}, u32[]{:S(2)}) copy-start(bf16[512,512]{1,0:T(8,128)(2,1)} %constant.116.clone.mix) | copy-start | bytes 1572868
  205.9 16.3 %collective-permute-start.17 = (bf16[3072,128]{1,0:T(8,128)(2,1)S(1)}, bf16[3072,128]{1,0:T(8,128)(2,1)S(1)}, u32[]{:S(2)}, u32[]{:S(2)}) collective-permute-start(bf16[3072,128]{1,0:T(8,128)(2,1)S(1)} %bitcast.75), channel_id=1, source_target_pairs={{0,2},{1,3},{2,0},{3,1},{4,6},{5,7},{6,4},{7,5},{8,10},{9,11},{10,... | collective-permute-start | bytes 2359304 | tf_op jit(solution)/shard_map/ppermute | solution.py:320
  206.2 19.7 %collective-permute-start.16 = (bf16[3072,128]{1,0:T(8,128)(2,1)S(1)}, bf16[3072,128]{1,0:T(8,128)(2,1)S(1)}, u32[]{:S(2)}, u32[]{:S(2)}) collective-permute-start(bf16[3072,128]{1,0:T(8,128)(2,1)S(1)} %bitcast.76), channel_id=1, source_target_pairs={{0,1},{1,0},{2,3},{3,2},{4,5},{5,4},{6,7},{7,6},{8,9},{9,8},{10,11... | collective-permute-start | bytes 2359304 | tf_op jit(solution)/shard_map/ppermute | solution.py:320
  222.2 5.5 %collective-permute-start.18 = (bf16[3072,128]{1,0:T(8,128)(2,1)S(1)}, bf16[3072,128]{1,0:T(8,128)(2,1)S(1)}, u32[]{:S(2)}, u32[]{:S(2)}) collective-permute-start(bf16[3072,128]{1,0:T(8,128)(2,1)S(1)} %collective-permute-done.17.a2), channel_id=1, source_target_pairs={{0,1},{1,0},{2,3},{3,2},{4,5},{5,4},{6,7},{7,6},{8,9},{9,8},{10,11... | collective-permute-start | bytes 2359304 | tf_op jit(solution)/shard_map/ppermute | solution.py:320
  (7 other events, 24.7 us)
Sparse Core Ops, SparseCore 0:
  70.7 29.7 all-gather.1

commit v6 on v5

--- a/solution.py
+++ b/solution.py
@@ -181,13 +181,12 @@
     rest = total - full * KT
     lax.fori_loop(0, full, loop, 0)
 
-    @pl.when(rest > KT // 2)
-    def _():
-        visit(full * KT, KT, True)
-
-    @pl.when((rest > 0) & (rest <= KT // 2))
-    def _():
-        visit(full * KT, KT // 2, True)
+    for size in (KT, KT // 2, KT // 4):
+        least = size // 2 if size > KT // 4 else 0
+
+        @pl.when((rest > least) & (rest <= size))
+        def _():
+            visit(full * KT, size, True)
 
     ob[...] = ac[:, :HD] / ac[:, HD:]
 
@@ -351,6 +350,13 @@
     n_group = n_seq // heads
     whole = pl.BlockSpec(memory_space=pltpu.VMEM)
 
+    width = residual.shape[1]
+
+    def weight_rows(j):
+        return lax.dynamic_slice(out_weight, (0, (head ^ j) * width), (columns, width))
+
+    weight_x = swap(weight_rows(2), HEAD, 2)
+
     marks = segment_ids + 1
     before = lax.ppermute(marks[tokens - PAD :], SEQ, [(i, i + 1) for i in range(n_seq - 1)])
     near = jnp.concatenate([before, marks])
@@ -413,17 +419,9 @@
 
     ys = [spread(qkv, j) for j in range(heads)]
 
-    kv4 = tie(kv4, qkv)
+    kv4 = tie(kv4, qkv, weight_x)
     kv8 = jnp.concatenate([kv4, swap(kv4, "xh", 1)], axis=0)
     kv32 = lax.all_gather(kv8, "y", axis=0, tiled=True)
-
-    width = residual.shape[1]
-    out_weight = tie(out_weight, kv8)
-    blocks_w = [
-        lax.dynamic_slice(out_weight, (0, (head ^ j) * width), (columns, width))
-        for j in range(n_head)
-    ]
-    weight_x = swap(blocks_w[2], HEAD, 2)
 
     def slots_of(owner_rows):
         r = jnp.arange(merged_rows, dtype=jnp.int32)
@@ -438,7 +436,7 @@
     ).astype(bf16)
     res = res.reshape(n_seq, CAP * 4 * width // HD, HD)
 
-    edges = tie(tuple(ys), weight_x, res)
+    edges = tie(tuple(ys), res)
 
     def edge(low, j, line, pairs):
         part = jnp.stack([t[low : low + HALO, HD:] for t in edges])
@@ -462,8 +460,12 @@
 
     pieces = [kv32, swap(tie(kv32, left, right), "c", 1)]
 
-    firsts = jnp.stack([p.reshape(-1, LIVE_MOST, BLK, 2 * HD)[:, :, 0, 0] for p in pieces])
-    counts = jnp.sum(jnp.isfinite(firsts).astype(jnp.int32), axis=2).reshape(-1)
+    def live_blocks(piece):
+        firsts = piece.reshape(-1, LIVE_MOST, BLK, 2 * HD)[:, :, 0, 0]
+        return jnp.sum(jnp.isfinite(firsts).astype(jnp.int32), axis=1)
+
+    live_near = live_blocks(pieces[0])
+    counts = jnp.concatenate([live_near, live_blocks(pieces[1])])
     every = jnp.arange(n_seq, dtype=jnp.int32)
     ends = jnp.arange(n_seq + 1, dtype=jnp.int32)
     off = jnp.sum(jnp.where(every[None, :] < ends[:, None], counts[None, :] * BLK, 0), axis=1)
@@ -472,14 +474,15 @@
     peer = (jnp.arange(heads, dtype=jnp.int32) ^ zp)[:, None]
     tgt = (group_owners * (heads * CAP) + peer * CAP + slots_of(group_owners)).reshape(-1)
 
+    out_weight = tie(out_weight, left, right)
     weights = [
-        blocks_w[0],
-        swap(tie(blocks_w[1], left, right), HEAD, 1),
+        weight_rows(0),
+        swap(weight_rows(1), HEAD, 1),
         weight_x,
-        swap(tie(blocks_w[3], left, right), HEAD, 3),
+        swap(weight_rows(3), HEAD, 3),
     ]
 
-    res = lax.all_to_all(tie(res, pieces[1], weight_x, left, right), SEQ, split_axis=0, concat_axis=0, tiled=True)
+    res = lax.all_to_all(tie(res, pieces[1], live_near), SEQ, split_axis=0, concat_axis=0, tiled=True)
 
     one = zp[None].astype(jnp.int32)
     sent = attend(off, tgt, one, ys, left, right, pieces, n_seq * heads * CAP)

time: 247 us -> 236 us (0.955)
  local copies, waits for them, and re-layouts: 19.5 us -> 15.6 us
  Pallas kernels: 48.5 us -> 44.6 us
  waiting for transfers between devices: 52.8 us -> 49.5 us
    pallas_call x1, Pallas kernels: 31.6 us -> 27.6 us  [attend(): pl.pallas_call(attention_kernel, out_shape=jax.ShapeDtypeStruct((slots *...]
    ppermute x8, waiting for transfers between devices: 24.1 us -> 20.5 us  [spread(): return lax.ppermute(part, ('zh', 'zp', 'c'), pairs)]
    reduce_sum x1 -> x2, other arithmetic: 0.03 us -> 3.34 us  [live_blocks(): return jnp.sum(jnp.isfinite(firsts).astype(jnp.int32), axis=1)]
    ppermute x8, starting transfers between devices: 27.2 us -> 24.7 us  [spread(): return lax.ppermute(part, ('zh', 'zp', 'c'), pairs)]
  transfers between devices with their start and end apart: 21 -> 21, of which waited for: 10 -> 8; matrix products, arithmetic and copies ran while one was open for 10% -> 11% of each run, Pallas kernels for 15% -> 14%
where the time goes in v6:
time: 236 us; the launch traced here: 235 us
  starting transfers between devices  60.2 us (26%)
  waiting for transfers between devices  49.5 us (21%)
  Pallas kernels  44.6 us (19%)
  blocking collectives  35.1 us (15%)
  local copies, waits for them, and re-layouts  15.6 us (7%)
  between operations  15.3 us (6%)
  other arithmetic  9.93 us (4%)
  matrix products  4.61 us (2%)
    all_to_all x1, blocking collectives, shards(): lax.all_to_all(sent.reshape(n_seq, heads * CAP * 4, HD), SEQ, split_axis=...  35.1 us
    pallas_call x1, Pallas kernels, attend(): pl.pallas_call(attention_kernel, out_shape=jax.ShapeDtypeStruct((slots *...  27.6 us
    ppermute x8, waiting for transfers between devices, swap(): return lax.ppermute(x, axis, [(i, i ^ k) for i in range(n)])  25.3 us
    ppermute x8, starting transfers between devices, spread(): return lax.ppermute(part, ('zh', 'zp', 'c'), pairs)  24.7 us
    ppermute x8, waiting for transfers between devices, spread(): return lax.ppermute(part, ('zh', 'zp', 'c'), pairs)  20.5 us
    all_to_all x1, starting transfers between devices, shards(): lax.all_to_all(tie(res, pieces[1], live_near), SEQ, split_axis=0, concat_...  14.6 us
    ppermute x8, starting transfers between devices, swap(): return lax.ppermute(x, axis, [(i, i ^ k) for i in range(n)])  12.2 us
    pallas_call x1, Pallas kernels, project(): pl.pallas_call(project_kernel, out_shape=jax.ShapeDtypeStruct((slots, 4 *...  11.4 us
  transfers between devices with their start and end apart: 21, of which 8 were waited for; matrix products, arithmetic and copies ran while one was open for 11% of the time, Pallas kernels for 14%

profile of v6, /device:TPU:1, one launch (start us, length us, event | category | flops | bytes accessed | tf_op | source)
XLA Modules:
  0.0 234.8 jit_solution(17768363279166385237)
XLA Ops:
  8.9 4.4 %collective-permute-start = (s32[256]{0:T(256)S(1)}, s32[256]{0:T(256)S(1)}, u32[]{:S(2)}, u32[]{:S(2)}) collective-permute-start(s32[256]{0:T(256)S(1)} %slice.109), channel_id=1, source_target_pairs={{0,4},{4,8},{8,12},{12,16},{16,20},{20,24},{24,28},{28,32},{32,36}... | collective-permute-start | bytes 3080 | tf_op jit(solution)/shard_map/ppermute | solution.py:361
  17.6 2.8 %fusion.34 = f32[16,512]{1,0:T(8,128)S(1)} fusion(bf16[16,4096]{1,0:T(8,128)(2,1)S(1)} %copy-done, bf16[4096,512]{1,0:T(8,128)(2,1)} %param.27), kind=kOutput, calls=%fused_computation.130 | convolution fusion | flops 67108864 | bytes 4358144 | tf_op jit(solution)/shard_map/dot_general | solution.py:386
  22.7 2.3 shard_map.158
  26.0 9.0 %collective-permute-start.1 = (bf16[96,256]{1,0:T(8,128)(2,1)S(1)}, bf16[96,256]{1,0:T(8,128)(2,1)S(1)}, u32[]{:S(2)}, u32[]{:S(2)}) collective-permute-start(bf16[96,256]{1,0:T(8,128)(2,1)S(1)} %get-tuple-element.49), channel_id=1, source_target_pairs={{0,0},{1,16},{4,4},{5,20},{8,8},{9,24},{12,12},{13,28},{16,1},{17,... | collective-permute-start | bytes 147464 | tf_op jit(solution)/shard_map/ppermute | solution.py:414
  36.2 3.2 %collective-permute-start.3 = (bf16[96,256]{1,0:T(8,128)(2,1)S(1)}, bf16[96,256]{1,0:T(8,128)(2,1)S(1)}, u32[]{:S(2)}, u32[]{:S(2)}) collective-permute-start(bf16[96,256]{1,0:T(8,128)(2,1)S(1)} %get-tuple-element.51), channel_id=1, source_target_pairs={{0,8},{1,24},{4,12},{5,28},{8,0},{9,16},{12,4},{13,20},{16,9},{17,... | collective-permute-start | bytes 147464 | tf_op jit(solution)/shard_map/ppermute | solution.py:414
  42.3 3.3 %shard_map.159 = bf16[4,528,384]{2,1,0:T(8,128)(2,1)} custom-call(bf16[512,512]{1,0:T(8,128)(2,1)} %q_ref.1, bf16[512,512]{1,0:T(8,128)(2,1)} %k_ref.1, bf16[512,512]{1,0:T(8,128)(2,1)} %v_ref.3, f32[512,128]{1,0:T(8,128)} %get-tuple-element.66.c_ref, f32[512,128]{1,0:T(8,128)} %get-tuple-element.67.s_ref, bf16[16,384]{1,0:T(8,128)(2,1)} %reshape.311.extra_ref), custom_call_target="tpu_custom_call" | custom-call | tf_op jit(solution)/shard_map/pallas_call | solution.py:370
  46.5 2.5 %collective-permute-start.6 = (bf16[384,256]{1,0:T(8,128)(2,1)S(1)}, bf16[384,256]{1,0:T(8,128)(2,1)S(1)}, u32[]{:S(2)}, u32[]{:S(2)}) collective-permute-start(bf16[384,256]{1,0:T(8,128)(2,1)S(1)} %pad_maximum_fusion.2), channel_id=1, source_target_pairs={{0,128},{128,0},{1,129},{129,1},{2,130},{130,2},{3,131},{131,3},{4... | collective-permute-start | bytes 589832 | tf_op jit(solution)/shard_map/ppermute | solution.py:319
  49.0 2.6 %dynamic-slice_bitcast_fusion = (bf16[528,384]{1,0:T(8,128)(2,1)}, bf16[528,384]{1,0:T(8,128)(2,1)}, bf16[528,384]{1,0:T(8,128)(2,1)}, bf16[528,384]{1,0:T(8,128)(2,1)}) fusion(bf16[4,528,384]{2,1,0:T(8,128)(2,1)} %shard_map.159, s32[]{:T(128)S(6)} %select_n.73, s32[]{:T(128)S(6)} %select_n.72, s32[]{:T(128)S(6)} %select_n.71, s32[]{:T(128)S(6)} %select_n.70), kind=kLoop, calls=%fused_computation.10 | loop fusion | bytes 3244048 | tf_op jit(solution)/shard_map/jit(dynamic_index_in_dim)/squeeze | solution.py:413
  52.5 2.4 %collective-permute-start.9 = (bf16[528,384]{1,0:T(8,128)(2,1)}, bf16[528,384]{1,0:T(8,128)(2,1)S(1)}, u32[]{:S(2)}, u32[]{:S(2)}) collective-permute-start(bf16[528,384]{1,0:T(8,128)(2,1)} %get-tuple-element.38), channel_id=1, source_target_pairs={{0,8},{1,24},{4,12},{5,28},{8,0},{9,16},{12,4},{13,20},{16,9},{17,... | collective-permute-start | bytes 1216520 | tf_op jit(solution)/shard_map/ppermute | solution.py:414
  54.8 2.9 %collective-permute-start.8 = (bf16[528,384]{1,0:T(8,128)(2,1)}, bf16[528,384]{1,0:T(8,128)(2,1)S(1)}, u32[]{:S(2)}, u32[]{:S(2)}) collective-permute-start(bf16[528,384]{1,0:T(8,128)(2,1)} %get-tuple-element.39), channel_id=1, source_target_pairs={{0,4},{1,20},{4,0},{5,16},{8,12},{9,28},{12,8},{13,24},{16,5},{17,... | collective-permute-start | bytes 1216520 | tf_op jit(solution)/shard_map/ppermute | solution.py:414
  57.8 4.6 %collective-permute-start.7 = (bf16[528,384]{1,0:T(8,128)(2,1)}, bf16[528,384]{1,0:T(8,128)(2,1)S(1)}, u32[]{:S(2)}, u32[]{:S(2)}) collective-permute-start(bf16[528,384]{1,0:T(8,128)(2,1)} %get-tuple-element.40), channel_id=1, source_target_pairs={{0,0},{1,16},{4,4},{5,20},{8,8},{9,24},{12,12},{13,28},{16,1},{17,... | collective-permute-start | bytes 1216520 | tf_op jit(solution)/shard_map/ppermute | solution.py:414
  68.6 14.1 %collective-permute-done.9.refs_2_ = bf16[528,384]{1,0:T(8,128)(2,1)S(1)} collective-permute-done((bf16[528,384]{1,0:T(8,128)(2,1)}, bf16[528,384]{1,0:T(8,128)(2,1)S(1)}, u32[]{:S(2)}, u32[]{:S(2)}) %collective-permute-start.9) | collective-permute-done | bytes 405536 | tf_op jit(solution)/shard_map/ppermute | solution.py:414
  82.7 5.4 %collective-permute-done.8.refs_1_ = bf16[528,384]{1,0:T(8,128)(2,1)S(1)} collective-permute-done((bf16[528,384]{1,0:T(8,128)(2,1)}, bf16[528,384]{1,0:T(8,128)(2,1)S(1)}, u32[]{:S(2)}, u32[]{:S(2)}) %collective-permute-start.8) | collective-permute-done | bytes 405536 | tf_op jit(solution)/shard_map/ppermute | solution.py:414
  91.1 2.4 %collective-permute-start.12 = (bf16[224,256]{1,0:T(8,128)(2,1)S(1)}, bf16[224,256]{1,0:T(8,128)(2,1)S(1)}, u32[]{:S(2)}, u32[]{:S(2)}) collective-permute-start(bf16[224,256]{1,0:T(8,128)(2,1)S(1)} %fusion.3), channel_id=1, source_target_pairs={{1,0},{32,1},{33,32},{64,33},{65,64},{96,65},{97,96},{128,97},{129... | collective-permute-start | bytes 344072 | tf_op jit(solution)/shard_map/ppermute | solution.py:446
  93.6 3.7 %collective-permute-done.12.refs_5_ = bf16[224,256]{1,0:T(8,128)(2,1)S(1)} collective-permute-done((bf16[224,256]{1,0:T(8,128)(2,1)S(1)}, bf16[224,256]{1,0:T(8,128)(2,1)S(1)}, u32[]{:S(2)}, u32[]{:S(2)}) %collective-permute-start.12) | collective-permute-done | bytes 114720 | tf_op jit(solution)/shard_map/ppermute | solution.py:446
  101.0 14.6 %all-to-all-start = ((bf16[64,96,128]{2,1,0:T(8,128)(2,1)}), bf16[64,96,128]{2,1,0:T(8,128)(2,1)}, u32[]{:S(2)}, u32[]{:S(2)}) async-start(bf16[64,96,128]{2,1,0:T(8,128)(2,1)} %reshape.314), calls=%async_computation | async-start | bytes 3145728 | tf_op jit(solution)/shard_map/all_to_all | solution.py:485
  116.1 2.3 constant_dynamic-slice_fusion.4
  121.5 27.6 %shard_map.160 = bf16[3072,128]{1,0:T(8,128)(2,1)S(1)} custom-call(s32[65]{0:T(128)S(1)} %select_reduce_fusion.1.off, s32[512]{0:T(512)S(1)} %add_bitcast_fusion.tgt, s32[1]{0:T(128)} %bitcast.33.zp, bf16[528,384]{1,0:T(8,128)(2,1)S(1)} %copy-done.2, bf16[528,384]{1,0:T(8,128)(2,1)S(1)} %collective-permute-done.8.refs_1_, ...), custom_call_target="tpu_custom_call" | custom-call | flops 7516192768 | bytes 8388608 | tf_op jit(solution)/shard_map/pallas_call | solution.py:210
  149.1 8.5 %collective-permute-done.15.w3 = bf16[512,1024]{1,0:T(8,128)(2,1)S(1)} collective-permute-done((bf16[512,1024]{1,0:T(8,128)(2,1)S(1)}, bf16[512,1024]{1,0:T(8,128)(2,1)S(1)}, u32[]{:S(2)}, u32[]{:S(2)}) %collective-permute-start.15) | collective-permute-done | bytes 1048608 | tf_op jit(solution)/shard_map/ppermute | solution.py:319
  159.6 35.1 %all_to_all.10 = bf16[64,48,128]{2,1,0:T(8,128)(2,1)S(1)} all-to-all(bf16[64,48,128]{2,1,0:T(8,128)(2,1)S(1)} %bitcast.76), channel_id=1, replica_groups=mesh['xh'=2,'y'=4,'zh'=2,'zp'=4,'xl'=2,'c'=2] {'xh','y','zh','zp'}, dimensions={0} | all-to-all | bytes 1572864 | tf_op jit(solution)/shard_map/all_to_all | solution.py:490
  195.2 3.0 %collective-permute-start.16 = (bf16[3072,128]{1,0:T(8,128)(2,1)S(1)}, bf16[3072,128]{1,0:T(8,128)(2,1)S(1)}, u32[]{:S(2)}, u32[]{:S(2)}) collective-permute-start(bf16[3072,128]{1,0:T(8,128)(2,1)S(1)} %bitcast.74), channel_id=1, source_target_pairs={{0,1},{1,0},{2,3},{3,2},{4,5},{5,4},{6,7},{7,6},{8,9},{9,8},{10,11... | collective-permute-start | bytes 2359304 | tf_op jit(solution)/shard_map/ppermute | solution.py:319
  198.1 12.9 %collective-permute-done.17.a2 = bf16[3072,128]{1,0:T(8,128)(2,1)S(1)} collective-permute-done((bf16[3072,128]{1,0:T(8,128)(2,1)S(1)}, bf16[3072,128]{1,0:T(8,128)(2,1)S(1)}, u32[]{:S(2)}, u32[]{:S(2)}) %collective-permute-start.17) | collective-permute-done | bytes 786464 | tf_op jit(solution)/shard_map/ppermute | solution.py:319
  211.0 3.6 %collective-permute-start.18 = (bf16[3072,128]{1,0:T(8,128)(2,1)S(1)}, bf16[3072,128]{1,0:T(8,128)(2,1)S(1)}, u32[]{:S(2)}, u32[]{:S(2)}) collective-permute-start(bf16[3072,128]{1,0:T(8,128)(2,1)S(1)} %collective-permute-done.17.a2), channel_id=1, source_target_pairs={{0,1},{1,0},{2,3},{3,2},{4,5},{5,4},{6,7},{7,6},{8,9},{9,8},{10,11... | collective-permute-start | bytes 2359304 | tf_op jit(solution)/shard_map/ppermute | solution.py:319
  216.6 11.4 %shard_map.161 = bf16[192,4096]{1,0:T(8,128)(2,1)} custom-call(s32[1]{0:T(128)} %bitcast.core, bf16[3072,128]{1,0:T(8,128)(2,1)S(1)} %bitcast.75, bf16[3072,128]{1,0:T(8,128)(2,1)S(1)} %collective-permute-done.16.a1, bf16[3072,128]{1,0:T(8,128)(2,1)S(1)} %collective-permute-done.17.a2, bf16[3072,128]{1,0:T(8,128)(2,1)S(1)} %collective-permute-done.18.a3, ...), custom_call_target="tpu_custom_call" | custom-call | flops 3221225472 | bytes 16777216 | tf_op jit(solution)/shard_map/pallas_call | solution.py:292
  (137 shorter events, 34.9 us)
Async XLA Ops:
  7.2 90.1 %all-gather.2.cloned.1.call-start = ((), (), s32[]{:S(2)}) async-start(), calls=%async_computation.2 | async-start | bytes 1966080 | tf_op jit(solution)/shard_map/all_gather | solution.py:424
  8.9 16.2 %collective-permute-start = (s32[256]{0:T(256)S(1)}, s32[256]{0:T(256)S(1)}, u32[]{:S(2)}, u32[]{:S(2)}) collective-permute-start(s32[256]{0:T(256)S(1)} %slice.109), channel_id=1, source_target_pairs={{0,4},{4,8},{8,12},{12,16},{16,20},{20,24},{24,28},{28,32},{32,36}... | collective-permute-start | bytes 3080 | tf_op jit(solution)/shard_map/ppermute | solution.py:361
  14.6 31.9 %collective-permute-start.5 = (bf16[512,1024]{1,0:T(8,128)(2,1)S(1)}, bf16[512,1024]{1,0:T(8,128)(2,1)}, u32[]{:S(2)}, u32[]{:S(2)}) collective-permute-start(bf16[512,1024]{1,0:T(8,128)(2,1)S(1)} %constant_dynamic-slice_fusion.11), channel_id=1, source_target_pairs={{0,2},{1,3},{2,0},{3,1},{4,6},{5,7},{6,4},{7,5},{8,10},{9,11},{10,... | collective-permute-start | bytes 3145736 | tf_op jit(solution)/shard_map/ppermute | solution.py:319
  26.0 19.6 %collective-permute-start.1 = (bf16[96,256]{1,0:T(8,128)(2,1)S(1)}, bf16[96,256]{1,0:T(8,128)(2,1)S(1)}, u32[]{:S(2)}, u32[]{:S(2)}) collective-permute-start(bf16[96,256]{1,0:T(8,128)(2,1)S(1)} %get-tuple-element.49), channel_id=1, source_target_pairs={{0,0},{1,16},{4,4},{5,20},{8,8},{9,24},{12,12},{13,28},{16,1},{17,... | collective-permute-start | bytes 147464 | tf_op jit(solution)/shard_map/ppermute | solution.py:414
  35.0 10.5 %collective-permute-start.4 = (bf16[96,256]{1,0:T(8,128)(2,1)S(1)}, bf16[96,256]{1,0:T(8,128)(2,1)S(1)}, u32[]{:S(2)}, u32[]{:S(2)}) collective-permute-start(bf16[96,256]{1,0:T(8,128)(2,1)S(1)} %get-tuple-element.50), channel_id=1, source_target_pairs={{0,12},{1,28},{4,8},{5,24},{8,4},{9,20},{12,0},{13,16},{16,13},{17... | collective-permute-start | bytes 147464 | tf_op jit(solution)/shard_map/ppermute | solution.py:414
  36.2 9.3 %collective-permute-start.3 = (bf16[96,256]{1,0:T(8,128)(2,1)S(1)}, bf16[96,256]{1,0:T(8,128)(2,1)S(1)}, u32[]{:S(2)}, u32[]{:S(2)}) collective-permute-start(bf16[96,256]{1,0:T(8,128)(2,1)S(1)} %get-tuple-element.51), channel_id=1, source_target_pairs={{0,8},{1,24},{4,12},{5,28},{8,0},{9,16},{12,4},{13,20},{16,9},{17,... | collective-permute-start | bytes 147464 | tf_op jit(solution)/shard_map/ppermute | solution.py:414
  39.4 7.0 %collective-permute-start.2 = (bf16[96,256]{1,0:T(8,128)(2,1)S(1)}, bf16[96,256]{1,0:T(8,128)(2,1)S(1)}, u32[]{:S(2)}, u32[]{:S(2)}) collective-permute-start(bf16[96,256]{1,0:T(8,128)(2,1)S(1)} %get-tuple-element.52), channel_id=1, source_target_pairs={{0,4},{1,20},{4,0},{5,16},{8,12},{9,28},{12,8},{13,24},{16,5},{17,... | collective-permute-start | bytes 147464 | tf_op jit(solution)/shard_map/ppermute | solution.py:414
  46.5 15.9 %collective-permute-start.6 = (bf16[384,256]{1,0:T(8,128)(2,1)S(1)}, bf16[384,256]{1,0:T(8,128)(2,1)S(1)}, u32[]{:S(2)}, u32[]{:S(2)}) collective-permute-start(bf16[384,256]{1,0:T(8,128)(2,1)S(1)} %pad_maximum_fusion.2), channel_id=1, source_target_pairs={{0,128},{128,0},{1,129},{129,1},{2,130},{130,2},{3,131},{131,3},{4... | collective-permute-start | bytes 589832 | tf_op jit(solution)/shard_map/ppermute | solution.py:319
  51.6 17.0 %collective-permute-start.10 = (bf16[528,384]{1,0:T(8,128)(2,1)}, bf16[528,384]{1,0:T(8,128)(2,1)S(1)}, u32[]{:S(2)}, u32[]{:S(2)}) collective-permute-start(bf16[528,384]{1,0:T(8,128)(2,1)} %get-tuple-element.37), channel_id=1, source_target_pairs={{0,12},{1,28},{4,8},{5,24},{8,4},{9,20},{12,0},{13,16},{16,13},{17... | collective-permute-start | bytes 1216520 | tf_op jit(solution)/shard_map/ppermute | solution.py:414
  52.5 30.2 %collective-permute-start.9 = (bf16[528,384]{1,0:T(8,128)(2,1)}, bf16[528,384]{1,0:T(8,128)(2,1)S(1)}, u32[]{:S(2)}, u32[]{:S(2)}) collective-permute-start(bf16[528,384]{1,0:T(8,128)(2,1)} %get-tuple-element.38), channel_id=1, source_target_pairs={{0,8},{1,24},{4,12},{5,28},{8,0},{9,16},{12,4},{13,20},{16,9},{17,... | collective-permute-start | bytes 1216520 | tf_op jit(solution)/shard_map/ppermute | solution.py:414
  54.8 33.3 %collective-permute-start.8 = (bf16[528,384]{1,0:T(8,128)(2,1)}, bf16[528,384]{1,0:T(8,128)(2,1)S(1)}, u32[]{:S(2)}, u32[]{:S(2)}) collective-permute-start(bf16[528,384]{1,0:T(8,128)(2,1)} %get-tuple-element.39), channel_id=1, source_target_pairs={{0,4},{1,20},{4,0},{5,16},{8,12},{9,28},{12,8},{13,24},{16,5},{17,... | collective-permute-start | bytes 1216520 | tf_op jit(solution)/shard_map/ppermute | solution.py:414
  57.8 30.4 %collective-permute-start.7 = (bf16[528,384]{1,0:T(8,128)(2,1)}, bf16[528,384]{1,0:T(8,128)(2,1)S(1)}, u32[]{:S(2)}, u32[]{:S(2)}) collective-permute-start(bf16[528,384]{1,0:T(8,128)(2,1)} %get-tuple-element.40), channel_id=1, source_target_pairs={{0,0},{1,16},{4,4},{5,20},{8,8},{9,24},{12,12},{13,28},{16,1},{17,... | collective-permute-start | bytes 1216520 | tf_op jit(solution)/shard_map/ppermute | solution.py:414
  89.1 4.5 %collective-permute-start.11 = (bf16[224,256]{1,0:T(8,128)(2,1)S(1)}, bf16[224,256]{1,0:T(8,128)(2,1)S(1)}, u32[]{:S(2)}, u32[]{:S(2)}) collective-permute-start(bf16[224,256]{1,0:T(8,128)(2,1)S(1)} %fusion.2), channel_id=1, source_target_pairs={{0,1},{1,32},{32,33},{33,64},{64,65},{65,96},{96,97},{97,128},{128... | collective-permute-start | bytes 344072 | tf_op jit(solution)/shard_map/ppermute | solution.py:446
  91.1 6.1 %collective-permute-start.12 = (bf16[224,256]{1,0:T(8,128)(2,1)S(1)}, bf16[224,256]{1,0:T(8,128)(2,1)S(1)}, u32[]{:S(2)}, u32[]{:S(2)}) collective-permute-start(bf16[224,256]{1,0:T(8,128)(2,1)S(1)} %fusion.3), channel_id=1, source_target_pairs={{1,0},{32,1},{33,32},{64,33},{65,64},{96,65},{97,96},{128,97},{129... | collective-permute-start | bytes 344072 | tf_op jit(solution)/shard_map/ppermute | solution.py:446
  97.3 3.8 %collective-permute-start.13 = (bf16[3072,256]{1,0:T(8,128)(2,1)}, bf16[3072,256]{1,0:T(8,128)(2,1)}, u32[]{:S(2)}, u32[]{:S(2)}) collective-permute-start(bf16[3072,256]{1,0:T(8,128)(2,1)} %all-gather.2.cloned.1.call-done.refs_6_), channel_id=1, source_target_pairs={{0,1},{1,0},{2,3},{3,2},{4,5},{5,4},{6,7},{7,6},{8,9},{9,8},{10,11... | collective-permute-start | bytes 4718600 | tf_op jit(solution)/shard_map/ppermute | solution.py:319
  101.0 58.6 %all-to-all-start = ((bf16[64,96,128]{2,1,0:T(8,128)(2,1)}), bf16[64,96,128]{2,1,0:T(8,128)(2,1)}, u32[]{:S(2)}, u32[]{:S(2)}) async-start(bf16[64,96,128]{2,1,0:T(8,128)(2,1)} %reshape.314), calls=%async_computation | async-start | bytes 3145728 | tf_op jit(solution)/shard_map/all_to_all | solution.py:485
  118.4 39.2 %collective-permute-start.15 = (bf16[512,1024]{1,0:T(8,128)(2,1)S(1)}, bf16[512,1024]{1,0:T(8,128)(2,1)S(1)}, u32[]{:S(2)}, u32[]{:S(2)}) collective-permute-start(bf16[512,1024]{1,0:T(8,128)(2,1)S(1)} %get-tuple-element.34), channel_id=1, source_target_pairs={{0,3},{1,2},{2,1},{3,0},{4,7},{5,6},{6,5},{7,4},{8,11},{9,10},{10,... | collective-permute-start | bytes 3145736 | tf_op jit(solution)/shard_map/ppermute | solution.py:319
  119.6 39.0 %collective-permute-start.14 = (bf16[512,1024]{1,0:T(8,128)(2,1)S(1)}, bf16[512,1024]{1,0:T(8,128)(2,1)S(1)}, u32[]{:S(2)}, u32[]{:S(2)}) collective-permute-start(bf16[512,1024]{1,0:T(8,128)(2,1)S(1)} %get-tuple-element.35), channel_id=1, source_target_pairs={{0,1},{1,0},{2,3},{3,2},{4,5},{5,4},{6,7},{7,6},{8,9},{9,8},{10,11... | collective-permute-start | bytes 3145736 | tf_op jit(solution)/shard_map/ppermute | solution.py:319
  149.1 67.4 %copy-start.6 = (f32[1024]{0:T(1024)S(1)}, f32[1024]{0:T(1024)}, u32[]{:S(2)}) copy-start(f32[1024]{0:T(1024)} %param.19) | copy-start | bytes 12292
  149.1 67.4 %copy-start.7 = (bf16[512,512]{1,0:T(8,128)(2,1)S(1)}, bf16[512,512]{1,0:T(8,128)(2,1)}, u32[]{:S(2)}) copy-start(bf16[512,512]{1,0:T(8,128)(2,1)} %constant.116.clone.mix) | copy-start | bytes 1572868
  159.6 57.0 %copy-start.5 = (bf16[512,1024]{1,0:T(8,128)(2,1)S(1)}, bf16[512,1024]{1,0:T(8,128)(2,1)}, u32[]{:S(2)}) copy-start(bf16[512,1024]{1,0:T(8,128)(2,1)} %copy-done.4) | copy-start | bytes 3145732
  194.7 16.3 %collective-permute-start.17 = (bf16[3072,128]{1,0:T(8,128)(2,1)S(1)}, bf16[3072,128]{1,0:T(8,128)(2,1)S(1)}, u32[]{:S(2)}, u32[]{:S(2)}) collective-permute-start(bf16[3072,128]{1,0:T(8,128)(2,1)S(1)} %bitcast.73), channel_id=1, source_target_pairs={{0,2},{1,3},{2,0},{3,1},{4,6},{5,7},{6,4},{7,5},{8,10},{9,11},{10,... | collective-permute-start | bytes 2359304 | tf_op jit(solution)/shard_map/ppermute | solution.py:319
  195.2 19.5 %collective-permute-start.16 = (bf16[3072,128]{1,0:T(8,128)(2,1)S(1)}, bf16[3072,128]{1,0:T(8,128)(2,1)S(1)}, u32[]{:S(2)}, u32[]{:S(2)}) collective-permute-start(bf16[3072,128]{1,0:T(8,128)(2,1)S(1)} %bitcast.74), channel_id=1, source_target_pairs={{0,1},{1,0},{2,3},{3,2},{4,5},{5,4},{6,7},{7,6},{8,9},{9,8},{10,11... | collective-permute-start | bytes 2359304 | tf_op jit(solution)/shard_map/ppermute | solution.py:319
  211.0 5.5 %collective-permute-start.18 = (bf16[3072,128]{1,0:T(8,128)(2,1)S(1)}, bf16[3072,128]{1,0:T(8,128)(2,1)S(1)}, u32[]{:S(2)}, u32[]{:S(2)}) collective-permute-start(bf16[3072,128]{1,0:T(8,128)(2,1)S(1)} %collective-permute-done.17.a2), channel_id=1, source_target_pairs={{0,1},{1,0},{2,3},{3,2},{4,5},{5,4},{6,7},{7,6},{8,9},{9,8},{10,11... | collective-permute-start | bytes 2359304 | tf_op jit(solution)/shard_map/ppermute | solution.py:319
  (11 other events, 88.0 us)
Sparse Core Ops, SparseCore 0:
  63.3 26.6 all-gather.1

commit v7 on v6

--- a/solution.py
+++ b/solution.py
@@ -128,12 +128,12 @@
         vc[tail, :HD] = jnp.zeros((KT, HD), bf16)
 
     base = pl.multiple_of(i * TOK, TOK)
-    sub = 128
+    sub = 256
     parts = TOK // sub
     wide = sub + 2 * PAD
     for b in range(parts):
         line = ids[:, pl.ds(pl.multiple_of(base + PAD + b * sub, sub), sub)]
-        idcol[b * sub : (b + 1) * sub, :] = jnp.transpose(jnp.broadcast_to(line, (sub, sub)))
+        idcol[b * sub : (b + 1) * sub, :] = jnp.transpose(jnp.broadcast_to(line, (128, sub)))
 
     def scores(b, keys):
         q = qs[pl.ds(pl.multiple_of(base + b * sub, sub), sub), :]
@@ -158,20 +158,34 @@
         rows = pl.ds(pl.multiple_of(start, size // 2), size)
         keys, values = kc[rows, :], vc[rows, :]
 
-        def rows_of(b, carry):
-            s = scores(b, keys)
-            if masked:
-                col = lax.broadcasted_iota(jnp.int32, s.shape, 1)
-                s = jnp.where(col < total - start, s, NEG)
+        def mask(s):
+            if not masked:
+                return s
+            col = lax.broadcasted_iota(jnp.int32, s.shape, 1)
+            return jnp.where(col < total - start, s, NEG)
+
+        def absorb(b, s):
             here = pl.ds(pl.multiple_of(b * sub, sub), sub)
             m = mx[here, :]
             new, w = weigh(s, m)
             mx[here, :] = new
             part = jnp.dot(w, values, preferred_element_type=f32)
             ac[here, :] = ac[here, :] * jnp.exp2((m - new) * coef) + part
-            return carry
-
-        lax.fori_loop(0, parts, rows_of, 0, unroll=2 if masked else True)
+
+        if masked:
+
+            def rows_of(b, carry):
+                absorb(b, mask(scores(b, keys)))
+                return carry
+
+            lax.fori_loop(0, parts, rows_of, 0)
+        else:
+            ahead = scores(0, keys)
+            for b in range(parts):
+                s = ahead
+                if b + 1 < parts:
+                    ahead = scores(b + 1, keys)
+                absorb(b, s)
 
     def loop(j, carry):
         visit(j * KT, KT, False)
@@ -482,7 +496,7 @@
         swap(weight_rows(3), HEAD, 3),
     ]
 
-    res = lax.all_to_all(tie(res, pieces[1], live_near), SEQ, split_axis=0, concat_axis=0, tiled=True)
+    res = lax.all_to_all(tie(res, left, right), SEQ, split_axis=0, concat_axis=0, tiled=True)
 
     one = zp[None].astype(jnp.int32)
     sent = attend(off, tgt, one, ys, left, right, pieces, n_seq * heads * CAP)

time: 236 us -> 231 us (0.979)
  waiting for transfers between devices: 49.5 us -> 46.4 us
    ppermute x8, waiting for transfers between devices: 25.3 us -> 22.1 us  [swap(): return lax.ppermute(x, axis, [(i, i ^ k) for i in range(n)])]
  transfers between devices with their start and end apart: 21 -> 21, of which waited for: 8 -> 7; matrix products, arithmetic and copies ran while one was open for 11% -> 11% of each run, Pallas kernels for 14% -> 14%
where the time goes in v7:
time: 231 us; the launch traced here: 230 us
  starting transfers between devices  60.3 us (26%)
  waiting for transfers between devices  46.4 us (20%)
  Pallas kernels  44.5 us (19%)
  blocking collectives  34.5 us (15%)
  local copies, waits for them, and re-layouts  15.6 us (7%)
  between operations  15.3 us (7%)
  other arithmetic  8.94 us (4%)
  matrix products  4.61 us (2%)
    all_to_all x1, blocking collectives, shards(): lax.all_to_all(sent.reshape(n_seq, heads * CAP * 4, HD), SEQ, split_axis=...  34.5 us
    pallas_call x1, Pallas kernels, attend(): pl.pallas_call(attention_kernel, out_shape=jax.ShapeDtypeStruct((slots *...  27.5 us
    ppermute x8, starting transfers between devices, spread(): return lax.ppermute(part, ('zh', 'zp', 'c'), pairs)  24.7 us
    ppermute x8, waiting for transfers between devices, swap(): return lax.ppermute(x, axis, [(i, i ^ k) for i in range(n)])  22.1 us
    ppermute x8, waiting for transfers between devices, spread(): return lax.ppermute(part, ('zh', 'zp', 'c'), pairs)  20.5 us
    all_to_all x1, starting transfers between devices, shards(): lax.all_to_all(tie(res, left, right), SEQ, split_axis=0, concat_axis=0, t...  14.6 us
    ppermute x8, starting transfers between devices, swap(): return lax.ppermute(x, axis, [(i, i ^ k) for i in range(n)])  12.3 us
    pallas_call x1, Pallas kernels, project(): pl.pallas_call(project_kernel, out_shape=jax.ShapeDtypeStruct((slots, 4 *...  11.4 us
  transfers between devices with their start and end apart: 21, of which 7 were waited for; matrix products, arithmetic and copies ran while one was open for 11% of the time, Pallas kernels for 14%

profile of v7, /device:TPU:1, one launch (start us, length us, event | category | flops | bytes accessed | tf_op | source)
XLA Modules:
  0.0 230.1 jit_solution(18431529353180982620)
XLA Ops:
  8.9 4.4 %collective-permute-start = (s32[256]{0:T(256)S(1)}, s32[256]{0:T(256)S(1)}, u32[]{:S(2)}, u32[]{:S(2)}) collective-permute-start(s32[256]{0:T(256)S(1)} %slice.109), channel_id=1, source_target_pairs={{0,4},{4,8},{8,12},{12,16},{16,20},{20,24},{24,28},{28,32},{32,36}... | collective-permute-start | bytes 3080 | tf_op jit(solution)/shard_map/ppermute | solution.py:375
  17.6 2.8 %fusion.34 = f32[16,512]{1,0:T(8,128)S(1)} fusion(bf16[16,4096]{1,0:T(8,128)(2,1)S(1)} %copy-done, bf16[4096,512]{1,0:T(8,128)(2,1)} %param.27), kind=kOutput, calls=%fused_computation.130 | convolution fusion | flops 67108864 | bytes 4358144 | tf_op jit(solution)/shard_map/dot_general | solution.py:400
  22.7 2.3 %shard_map.158 = bf16[4,96,256]{2,1,0:T(8,128)(2,1)} custom-call(s32[7]{0:T(128)} %pad_add_fusion.1.idx, bf16[128,512]{1,0:T(8,128)(2,1)} %copy-done.10, bf16[128,512]{1,0:T(8,128)(2,1)} %v_ref.2), custom_call_target="tpu_custom_call" | custom-call | tf_op jit(solution)/shard_map/pallas_call | solution.py:413
  26.0 9.0 %collective-permute-start.1 = (bf16[96,256]{1,0:T(8,128)(2,1)S(1)}, bf16[96,256]{1,0:T(8,128)(2,1)S(1)}, u32[]{:S(2)}, u32[]{:S(2)}) collective-permute-start(bf16[96,256]{1,0:T(8,128)(2,1)S(1)} %get-tuple-element.49), channel_id=1, source_target_pairs={{0,0},{1,16},{4,4},{5,20},{8,8},{9,24},{12,12},{13,28},{16,1},{17,... | collective-permute-start | bytes 147464 | tf_op jit(solution)/shard_map/ppermute | solution.py:428
  36.2 3.2 %collective-permute-start.3 = (bf16[96,256]{1,0:T(8,128)(2,1)S(1)}, bf16[96,256]{1,0:T(8,128)(2,1)S(1)}, u32[]{:S(2)}, u32[]{:S(2)}) collective-permute-start(bf16[96,256]{1,0:T(8,128)(2,1)S(1)} %get-tuple-element.51), channel_id=1, source_target_pairs={{0,8},{1,24},{4,12},{5,28},{8,0},{9,16},{12,4},{13,20},{16,9},{17,... | collective-permute-start | bytes 147464 | tf_op jit(solution)/shard_map/ppermute | solution.py:428
  42.3 3.3 %shard_map.159 = bf16[4,528,384]{2,1,0:T(8,128)(2,1)} custom-call(bf16[512,512]{1,0:T(8,128)(2,1)} %q_ref.1, bf16[512,512]{1,0:T(8,128)(2,1)} %k_ref.1, bf16[512,512]{1,0:T(8,128)(2,1)} %v_ref.3, f32[512,128]{1,0:T(8,128)} %get-tuple-element.66.c_ref, f32[512,128]{1,0:T(8,128)} %get-tuple-element.67.s_ref, bf16[16,384]{1,0:T(8,128)(2,1)} %reshape.311.extra_ref), custom_call_target="tpu_custom_call" | custom-call | tf_op jit(solution)/shard_map/pallas_call | solution.py:384
  46.5 2.5 %collective-permute-start.6 = (bf16[384,256]{1,0:T(8,128)(2,1)S(1)}, bf16[384,256]{1,0:T(8,128)(2,1)S(1)}, u32[]{:S(2)}, u32[]{:S(2)}) collective-permute-start(bf16[384,256]{1,0:T(8,128)(2,1)S(1)} %pad_maximum_fusion.2), channel_id=1, source_target_pairs={{0,128},{128,0},{1,129},{129,1},{2,130},{130,2},{3,131},{131,3},{4... | collective-permute-start | bytes 589832 | tf_op jit(solution)/shard_map/ppermute | solution.py:333
  49.0 2.6 %dynamic-slice_bitcast_fusion = (bf16[528,384]{1,0:T(8,128)(2,1)}, bf16[528,384]{1,0:T(8,128)(2,1)}, bf16[528,384]{1,0:T(8,128)(2,1)}, bf16[528,384]{1,0:T(8,128)(2,1)}) fusion(bf16[4,528,384]{2,1,0:T(8,128)(2,1)} %shard_map.159, s32[]{:T(128)S(6)} %select_n.73, s32[]{:T(128)S(6)} %select_n.72, s32[]{:T(128)S(6)} %select_n.71, s32[]{:T(128)S(6)} %select_n.70), kind=kLoop, calls=%fused_computation.10 | loop fusion | bytes 3244048 | tf_op jit(solution)/shard_map/jit(dynamic_index_in_dim)/squeeze | solution.py:427
  52.5 2.4 %collective-permute-start.9 = (bf16[528,384]{1,0:T(8,128)(2,1)}, bf16[528,384]{1,0:T(8,128)(2,1)S(1)}, u32[]{:S(2)}, u32[]{:S(2)}) collective-permute-start(bf16[528,384]{1,0:T(8,128)(2,1)} %get-tuple-element.38), channel_id=1, source_target_pairs={{0,8},{1,24},{4,12},{5,28},{8,0},{9,16},{12,4},{13,20},{16,9},{17,... | collective-permute-start | bytes 1216520 | tf_op jit(solution)/shard_map/ppermute | solution.py:428
  54.8 2.9 %collective-permute-start.8 = (bf16[528,384]{1,0:T(8,128)(2,1)}, bf16[528,384]{1,0:T(8,128)(2,1)S(1)}, u32[]{:S(2)}, u32[]{:S(2)}) collective-permute-start(bf16[528,384]{1,0:T(8,128)(2,1)} %get-tuple-element.39), channel_id=1, source_target_pairs={{0,4},{1,20},{4,0},{5,16},{8,12},{9,28},{12,8},{13,24},{16,5},{17,... | collective-permute-start | bytes 1216520 | tf_op jit(solution)/shard_map/ppermute | solution.py:428
  57.8 4.6 %collective-permute-start.7 = (bf16[528,384]{1,0:T(8,128)(2,1)}, bf16[528,384]{1,0:T(8,128)(2,1)S(1)}, u32[]{:S(2)}, u32[]{:S(2)}) collective-permute-start(bf16[528,384]{1,0:T(8,128)(2,1)} %get-tuple-element.40), channel_id=1, source_target_pairs={{0,0},{1,16},{4,4},{5,20},{8,8},{9,24},{12,12},{13,28},{16,1},{17,... | collective-permute-start | bytes 1216520 | tf_op jit(solution)/shard_map/ppermute | solution.py:428
  68.6 14.1 %collective-permute-done.9.refs_2_ = bf16[528,384]{1,0:T(8,128)(2,1)S(1)} collective-permute-done((bf16[528,384]{1,0:T(8,128)(2,1)}, bf16[528,384]{1,0:T(8,128)(2,1)S(1)}, u32[]{:S(2)}, u32[]{:S(2)}) %collective-permute-start.9) | collective-permute-done | bytes 405536 | tf_op jit(solution)/shard_map/ppermute | solution.py:428
  82.7 5.4 %collective-permute-done.8.refs_1_ = bf16[528,384]{1,0:T(8,128)(2,1)S(1)} collective-permute-done((bf16[528,384]{1,0:T(8,128)(2,1)}, bf16[528,384]{1,0:T(8,128)(2,1)S(1)}, u32[]{:S(2)}, u32[]{:S(2)}) %collective-permute-start.8) | collective-permute-done | bytes 405536 | tf_op jit(solution)/shard_map/ppermute | solution.py:428
  91.1 2.4 %collective-permute-start.12 = (bf16[224,256]{1,0:T(8,128)(2,1)S(1)}, bf16[224,256]{1,0:T(8,128)(2,1)S(1)}, u32[]{:S(2)}, u32[]{:S(2)}) collective-permute-start(bf16[224,256]{1,0:T(8,128)(2,1)S(1)} %fusion.3), channel_id=1, source_target_pairs={{1,0},{32,1},{33,32},{64,33},{65,64},{96,65},{97,96},{128,97},{129... | collective-permute-start | bytes 344072 | tf_op jit(solution)/shard_map/ppermute | solution.py:460
  93.6 3.7 %collective-permute-done.12.refs_5_ = bf16[224,256]{1,0:T(8,128)(2,1)S(1)} collective-permute-done((bf16[224,256]{1,0:T(8,128)(2,1)S(1)}, bf16[224,256]{1,0:T(8,128)(2,1)S(1)}, u32[]{:S(2)}, u32[]{:S(2)}) %collective-permute-start.12) | collective-permute-done | bytes 114720 | tf_op jit(solution)/shard_map/ppermute | solution.py:460
  97.2 14.6 %all-to-all-start = ((bf16[64,96,128]{2,1,0:T(8,128)(2,1)}), bf16[64,96,128]{2,1,0:T(8,128)(2,1)}, u32[]{:S(2)}, u32[]{:S(2)}) async-start(bf16[64,96,128]{2,1,0:T(8,128)(2,1)} %reshape.314), calls=%async_computation | async-start | bytes 3145728 | tf_op jit(solution)/shard_map/all_to_all | solution.py:499
  112.6 2.3 %constant_dynamic-slice_fusion.4 = (bf16[512,1024]{1,0:T(8,128)(2,1)S(1)}, bf16[512,1024]{1,0:T(8,128)(2,1)S(1)}, bf16[512,1024]{1,0:T(8,128)(2,1)S(1)}) fusion(bf16[512,4096]{1,0:T(8,128)(2,1)} %param.20, s32[]{:T(128)S(6)} %select_n.79, s32[]{:T(128)S(6)} %select_n.78, s32[]{:T(128)S(6)} %select_n.77), kind=kLoop, calls=%fused_computation.72 | loop fusion | bytes 6291468 | tf_op jit(solution)/shard_map/dynamic_slice | solution.py:370
  118.8 27.5 %shard_map.160 = bf16[3072,128]{1,0:T(8,128)(2,1)S(1)} custom-call(s32[65]{0:T(128)S(1)} %select_reduce_fusion.1.off, s32[512]{0:T(512)S(1)} %add_bitcast_fusion.tgt, s32[1]{0:T(128)} %bitcast.33.zp, bf16[528,384]{1,0:T(8,128)(2,1)S(1)} %copy-done.2, bf16[528,384]{1,0:T(8,128)(2,1)S(1)} %collective-permute-done.8.refs_1_, ...), custom_call_target="tpu_custom_call" | custom-call | flops 7516192768 | bytes 8388608 | tf_op jit(solution)/shard_map/pallas_call | solution.py:224
  146.3 7.1 %collective-permute-done.15.w3 = bf16[512,1024]{1,0:T(8,128)(2,1)S(1)} collective-permute-done((bf16[512,1024]{1,0:T(8,128)(2,1)S(1)}, bf16[512,1024]{1,0:T(8,128)(2,1)S(1)}, u32[]{:S(2)}, u32[]{:S(2)}) %collective-permute-start.15) | collective-permute-done | bytes 1048608 | tf_op jit(solution)/shard_map/ppermute | solution.py:333
  155.4 34.5 %all_to_all.10 = bf16[64,48,128]{2,1,0:T(8,128)(2,1)S(1)} all-to-all(bf16[64,48,128]{2,1,0:T(8,128)(2,1)S(1)} %bitcast.76), channel_id=1, replica_groups=mesh['xh'=2,'y'=4,'zh'=2,'zp'=4,'xl'=2,'c'=2] {'xh','y','zh','zp'}, dimensions={0} | all-to-all | bytes 1572864 | tf_op jit(solution)/shard_map/all_to_all | solution.py:504
  190.2 3.0 %collective-permute-start.16 = (bf16[3072,128]{1,0:T(8,128)(2,1)S(1)}, bf16[3072,128]{1,0:T(8,128)(2,1)S(1)}, u32[]{:S(2)}, u32[]{:S(2)}) collective-permute-start(bf16[3072,128]{1,0:T(8,128)(2,1)S(1)} %bitcast.74), channel_id=1, source_target_pairs={{0,1},{1,0},{2,3},{3,2},{4,5},{5,4},{6,7},{7,6},{8,9},{9,8},{10,11... | collective-permute-start | bytes 2359304 | tf_op jit(solution)/shard_map/ppermute | solution.py:333
  193.2 13.1 %collective-permute-done.17.a2 = bf16[3072,128]{1,0:T(8,128)(2,1)S(1)} collective-permute-done((bf16[3072,128]{1,0:T(8,128)(2,1)S(1)}, bf16[3072,128]{1,0:T(8,128)(2,1)S(1)}, u32[]{:S(2)}, u32[]{:S(2)}) %collective-permute-start.17) | collective-permute-done | bytes 786464 | tf_op jit(solution)/shard_map/ppermute | solution.py:333
  206.3 3.6 %collective-permute-start.18 = (bf16[3072,128]{1,0:T(8,128)(2,1)S(1)}, bf16[3072,128]{1,0:T(8,128)(2,1)S(1)}, u32[]{:S(2)}, u32[]{:S(2)}) collective-permute-start(bf16[3072,128]{1,0:T(8,128)(2,1)S(1)} %collective-permute-done.17.a2), channel_id=1, source_target_pairs={{0,1},{1,0},{2,3},{3,2},{4,5},{5,4},{6,7},{7,6},{8,9},{9,8},{10,11... | collective-permute-start | bytes 2359304 | tf_op jit(solution)/shard_map/ppermute | solution.py:333
  211.8 11.4 %shard_map.161 = bf16[192,4096]{1,0:T(8,128)(2,1)} custom-call(s32[1]{0:T(128)} %bitcast.core, bf16[3072,128]{1,0:T(8,128)(2,1)S(1)} %bitcast.75, bf16[3072,128]{1,0:T(8,128)(2,1)S(1)} %collective-permute-done.16.a1, bf16[3072,128]{1,0:T(8,128)(2,1)S(1)} %collective-permute-done.17.a2, bf16[3072,128]{1,0:T(8,128)(2,1)S(1)} %collective-permute-done.18.a3, ...), custom_call_target="tpu_custom_call" | custom-call | flops 3221225472 | bytes 16777216 | tf_op jit(solution)/shard_map/pallas_call | solution.py:306
  (137 shorter events, 31.9 us)
Async XLA Ops:
  7.2 104.7 %all-gather.2.cloned.1.call-start = ((), (), s32[]{:S(2)}) async-start(), calls=%async_computation.2 | async-start | bytes 1966080 | tf_op jit(solution)/shard_map/all_gather | solution.py:438
  8.9 16.2 %collective-permute-start = (s32[256]{0:T(256)S(1)}, s32[256]{0:T(256)S(1)}, u32[]{:S(2)}, u32[]{:S(2)}) collective-permute-start(s32[256]{0:T(256)S(1)} %slice.109), channel_id=1, source_target_pairs={{0,4},{4,8},{8,12},{12,16},{16,20},{20,24},{24,28},{28,32},{32,36}... | collective-permute-start | bytes 3080 | tf_op jit(solution)/shard_map/ppermute | solution.py:375
  14.6 31.9 %collective-permute-start.5 = (bf16[512,1024]{1,0:T(8,128)(2,1)S(1)}, bf16[512,1024]{1,0:T(8,128)(2,1)}, u32[]{:S(2)}, u32[]{:S(2)}) collective-permute-start(bf16[512,1024]{1,0:T(8,128)(2,1)S(1)} %constant_dynamic-slice_fusion.11), channel_id=1, source_target_pairs={{0,2},{1,3},{2,0},{3,1},{4,6},{5,7},{6,4},{7,5},{8,10},{9,11},{10,... | collective-permute-start | bytes 3145736 | tf_op jit(solution)/shard_map/ppermute | solution.py:333
  26.0 19.6 %collective-permute-start.1 = (bf16[96,256]{1,0:T(8,128)(2,1)S(1)}, bf16[96,256]{1,0:T(8,128)(2,1)S(1)}, u32[]{:S(2)}, u32[]{:S(2)}) collective-permute-start(bf16[96,256]{1,0:T(8,128)(2,1)S(1)} %get-tuple-element.49), channel_id=1, source_target_pairs={{0,0},{1,16},{4,4},{5,20},{8,8},{9,24},{12,12},{13,28},{16,1},{17,... | collective-permute-start | bytes 147464 | tf_op jit(solution)/shard_map/ppermute | solution.py:428
  35.0 10.5 %collective-permute-start.4 = (bf16[96,256]{1,0:T(8,128)(2,1)S(1)}, bf16[96,256]{1,0:T(8,128)(2,1)S(1)}, u32[]{:S(2)}, u32[]{:S(2)}) collective-permute-start(bf16[96,256]{1,0:T(8,128)(2,1)S(1)} %get-tuple-element.50), channel_id=1, source_target_pairs={{0,12},{1,28},{4,8},{5,24},{8,4},{9,20},{12,0},{13,16},{16,13},{17... | collective-permute-start | bytes 147464 | tf_op jit(solution)/shard_map/ppermute | solution.py:428
  36.2 9.3 %collective-permute-start.3 = (bf16[96,256]{1,0:T(8,128)(2,1)S(1)}, bf16[96,256]{1,0:T(8,128)(2,1)S(1)}, u32[]{:S(2)}, u32[]{:S(2)}) collective-permute-start(bf16[96,256]{1,0:T(8,128)(2,1)S(1)} %get-tuple-element.51), channel_id=1, source_target_pairs={{0,8},{1,24},{4,12},{5,28},{8,0},{9,16},{12,4},{13,20},{16,9},{17,... | collective-permute-start | bytes 147464 | tf_op jit(solution)/shard_map/ppermute | solution.py:428
  39.4 7.0 %collective-permute-start.2 = (bf16[96,256]{1,0:T(8,128)(2,1)S(1)}, bf16[96,256]{1,0:T(8,128)(2,1)S(1)}, u32[]{:S(2)}, u32[]{:S(2)}) collective-permute-start(bf16[96,256]{1,0:T(8,128)(2,1)S(1)} %get-tuple-element.52), channel_id=1, source_target_pairs={{0,4},{1,20},{4,0},{5,16},{8,12},{9,28},{12,8},{13,24},{16,5},{17,... | collective-permute-start | bytes 147464 | tf_op jit(solution)/shard_map/ppermute | solution.py:428
  46.5 15.9 %collective-permute-start.6 = (bf16[384,256]{1,0:T(8,128)(2,1)S(1)}, bf16[384,256]{1,0:T(8,128)(2,1)S(1)}, u32[]{:S(2)}, u32[]{:S(2)}) collective-permute-start(bf16[384,256]{1,0:T(8,128)(2,1)S(1)} %pad_maximum_fusion.2), channel_id=1, source_target_pairs={{0,128},{128,0},{1,129},{129,1},{2,130},{130,2},{3,131},{131,3},{4... | collective-permute-start | bytes 589832 | tf_op jit(solution)/shard_map/ppermute | solution.py:333
  51.6 17.0 %collective-permute-start.10 = (bf16[528,384]{1,0:T(8,128)(2,1)}, bf16[528,384]{1,0:T(8,128)(2,1)S(1)}, u32[]{:S(2)}, u32[]{:S(2)}) collective-permute-start(bf16[528,384]{1,0:T(8,128)(2,1)} %get-tuple-element.37), channel_id=1, source_target_pairs={{0,12},{1,28},{4,8},{5,24},{8,4},{9,20},{12,0},{13,16},{16,13},{17... | collective-permute-start | bytes 1216520 | tf_op jit(solution)/shard_map/ppermute | solution.py:428
  52.5 30.2 %collective-permute-start.9 = (bf16[528,384]{1,0:T(8,128)(2,1)}, bf16[528,384]{1,0:T(8,128)(2,1)S(1)}, u32[]{:S(2)}, u32[]{:S(2)}) collective-permute-start(bf16[528,384]{1,0:T(8,128)(2,1)} %get-tuple-element.38), channel_id=1, source_target_pairs={{0,8},{1,24},{4,12},{5,28},{8,0},{9,16},{12,4},{13,20},{16,9},{17,... | collective-permute-start | bytes 1216520 | tf_op jit(solution)/shard_map/ppermute | solution.py:428
  54.8 33.3 %collective-permute-start.8 = (bf16[528,384]{1,0:T(8,128)(2,1)}, bf16[528,384]{1,0:T(8,128)(2,1)S(1)}, u32[]{:S(2)}, u32[]{:S(2)}) collective-permute-start(bf16[528,384]{1,0:T(8,128)(2,1)} %get-tuple-element.39), channel_id=1, source_target_pairs={{0,4},{1,20},{4,0},{5,16},{8,12},{9,28},{12,8},{13,24},{16,5},{17,... | collective-permute-start | bytes 1216520 | tf_op jit(solution)/shard_map/ppermute | solution.py:428
  57.8 30.4 %collective-permute-start.7 = (bf16[528,384]{1,0:T(8,128)(2,1)}, bf16[528,384]{1,0:T(8,128)(2,1)S(1)}, u32[]{:S(2)}, u32[]{:S(2)}) collective-permute-start(bf16[528,384]{1,0:T(8,128)(2,1)} %get-tuple-element.40), channel_id=1, source_target_pairs={{0,0},{1,16},{4,4},{5,20},{8,8},{9,24},{12,12},{13,28},{16,1},{17,... | collective-permute-start | bytes 1216520 | tf_op jit(solution)/shard_map/ppermute | solution.py:428
  89.0 4.5 %collective-permute-start.11 = (bf16[224,256]{1,0:T(8,128)(2,1)S(1)}, bf16[224,256]{1,0:T(8,128)(2,1)S(1)}, u32[]{:S(2)}, u32[]{:S(2)}) collective-permute-start(bf16[224,256]{1,0:T(8,128)(2,1)S(1)} %fusion.2), channel_id=1, source_target_pairs={{0,1},{1,32},{32,33},{33,64},{64,65},{65,96},{96,97},{97,128},{128... | collective-permute-start | bytes 344072 | tf_op jit(solution)/shard_map/ppermute | solution.py:460
  91.1 6.1 %collective-permute-start.12 = (bf16[224,256]{1,0:T(8,128)(2,1)S(1)}, bf16[224,256]{1,0:T(8,128)(2,1)S(1)}, u32[]{:S(2)}, u32[]{:S(2)}) collective-permute-start(bf16[224,256]{1,0:T(8,128)(2,1)S(1)} %fusion.3), channel_id=1, source_target_pairs={{1,0},{32,1},{33,32},{64,33},{65,64},{96,65},{97,96},{128,97},{129... | collective-permute-start | bytes 344072 | tf_op jit(solution)/shard_map/ppermute | solution.py:460
  97.2 58.2 %all-to-all-start = ((bf16[64,96,128]{2,1,0:T(8,128)(2,1)}), bf16[64,96,128]{2,1,0:T(8,128)(2,1)}, u32[]{:S(2)}, u32[]{:S(2)}) async-start(bf16[64,96,128]{2,1,0:T(8,128)(2,1)} %reshape.314), calls=%async_computation | async-start | bytes 3145728 | tf_op jit(solution)/shard_map/all_to_all | solution.py:499
  111.9 5.0 %collective-permute-start.13 = (bf16[3072,256]{1,0:T(8,128)(2,1)}, bf16[3072,256]{1,0:T(8,128)(2,1)}, u32[]{:S(2)}, u32[]{:S(2)}) collective-permute-start(bf16[3072,256]{1,0:T(8,128)(2,1)} %all-gather.2.cloned.1.call-done.refs_6_), channel_id=1, source_target_pairs={{0,1},{1,0},{2,3},{3,2},{4,5},{5,4},{6,7},{7,6},{8,9},{9,8},{10,11... | collective-permute-start | bytes 4718600 | tf_op jit(solution)/shard_map/ppermute | solution.py:333
  114.9 38.5 %collective-permute-start.15 = (bf16[512,1024]{1,0:T(8,128)(2,1)S(1)}, bf16[512,1024]{1,0:T(8,128)(2,1)S(1)}, u32[]{:S(2)}, u32[]{:S(2)}) collective-permute-start(bf16[512,1024]{1,0:T(8,128)(2,1)S(1)} %get-tuple-element.34), channel_id=1, source_target_pairs={{0,3},{1,2},{2,1},{3,0},{4,7},{5,6},{6,5},{7,4},{8,11},{9,10},{10,... | collective-permute-start | bytes 3145736 | tf_op jit(solution)/shard_map/ppermute | solution.py:333
  116.2 38.2 %collective-permute-start.14 = (bf16[512,1024]{1,0:T(8,128)(2,1)S(1)}, bf16[512,1024]{1,0:T(8,128)(2,1)S(1)}, u32[]{:S(2)}, u32[]{:S(2)}) collective-permute-start(bf16[512,1024]{1,0:T(8,128)(2,1)S(1)} %get-tuple-element.35), channel_id=1, source_target_pairs={{0,1},{1,0},{2,3},{3,2},{4,5},{5,4},{6,7},{7,6},{8,9},{9,8},{10,11... | collective-permute-start | bytes 3145736 | tf_op jit(solution)/shard_map/ppermute | solution.py:333
  146.3 65.6 %copy-start.6 = (f32[1024]{0:T(1024)S(1)}, f32[1024]{0:T(1024)}, u32[]{:S(2)}) copy-start(f32[1024]{0:T(1024)} %param.19) | copy-start | bytes 12292
  146.3 65.5 %copy-start.7 = (bf16[512,512]{1,0:T(8,128)(2,1)S(1)}, bf16[512,512]{1,0:T(8,128)(2,1)}, u32[]{:S(2)}) copy-start(bf16[512,512]{1,0:T(8,128)(2,1)} %constant.116.clone.mix) | copy-start | bytes 1572868
  155.4 56.4 %copy-start.5 = (bf16[512,1024]{1,0:T(8,128)(2,1)S(1)}, bf16[512,1024]{1,0:T(8,128)(2,1)}, u32[]{:S(2)}) copy-start(bf16[512,1024]{1,0:T(8,128)(2,1)} %copy-done.4) | copy-start | bytes 3145732
  189.9 16.3 %collective-permute-start.17 = (bf16[3072,128]{1,0:T(8,128)(2,1)S(1)}, bf16[3072,128]{1,0:T(8,128)(2,1)S(1)}, u32[]{:S(2)}, u32[]{:S(2)}) collective-permute-start(bf16[3072,128]{1,0:T(8,128)(2,1)S(1)} %bitcast.73), channel_id=1, source_target_pairs={{0,2},{1,3},{2,0},{3,1},{4,6},{5,7},{6,4},{7,5},{8,10},{9,11},{10,... | collective-permute-start | bytes 2359304 | tf_op jit(solution)/shard_map/ppermute | solution.py:333
  190.2 19.7 %collective-permute-start.16 = (bf16[3072,128]{1,0:T(8,128)(2,1)S(1)}, bf16[3072,128]{1,0:T(8,128)(2,1)S(1)}, u32[]{:S(2)}, u32[]{:S(2)}) collective-permute-start(bf16[3072,128]{1,0:T(8,128)(2,1)S(1)} %bitcast.74), channel_id=1, source_target_pairs={{0,1},{1,0},{2,3},{3,2},{4,5},{5,4},{6,7},{7,6},{8,9},{9,8},{10,11... | collective-permute-start | bytes 2359304 | tf_op jit(solution)/shard_map/ppermute | solution.py:333
  206.3 5.5 %collective-permute-start.18 = (bf16[3072,128]{1,0:T(8,128)(2,1)S(1)}, bf16[3072,128]{1,0:T(8,128)(2,1)S(1)}, u32[]{:S(2)}, u32[]{:S(2)}) collective-permute-start(bf16[3072,128]{1,0:T(8,128)(2,1)S(1)} %collective-permute-done.17.a2), channel_id=1, source_target_pairs={{0,1},{1,0},{2,3},{3,2},{4,5},{5,4},{6,7},{7,6},{8,9},{9,8},{10,11... | collective-permute-start | bytes 2359304 | tf_op jit(solution)/shard_map/ppermute | solution.py:333
  (11 other events, 83.4 us)
Sparse Core Ops, SparseCore 0:
  63.3 26.6 all-gather.1

commit v8 on v7

--- a/solution.py
+++ b/solution.py
@@ -195,8 +195,7 @@
     rest = total - full * KT
     lax.fori_loop(0, full, loop, 0)
 
-    for size in (KT, KT // 2, KT // 4):
-        least = size // 2 if size > KT // 4 else 0
+    for least, size in ((0, KT // 4), (KT // 4, KT)):
 
         @pl.when((rest > least) & (rest <= size))
         def _():
@@ -255,40 +254,56 @@
     )(off, tgt, zp, *ys, left, right, *pieces)
 
 
-def project_kernel(core, a0, a1, a2, a3, w0, w1, w2, w3, res, scale, mix, out, att, res32, proj):
+def project_half(core, halves, weights, scale, att, proj):
+    c = core[0]
+    groups = halves[0].shape[0] // (8 * 48)
+
+    @pl.when(pl.program_id(0) == 0)
+    def _():
+        for k, a in enumerate(halves):
+
+            def move(g, carry):
+                to = pl.ds(pl.multiple_of((g * 2 + (c ^ k)) * 48, 16), 48)
+                for p in range(8):
+                    src = pl.ds(pl.multiple_of(g * 384 + p * 48, 16), 48)
+                    att[c ^ (p // 4), to, (p % 4) * HD : (p % 4 + 1) * HD] = a[src, :]
+                return carry
+
+            lax.fori_loop(0, groups, move, 0)
+
+    total = jnp.dot(att[0], weights[0][...], preferred_element_type=f32)
+    total = total + jnp.dot(att[1], weights[1][...], preferred_element_type=f32)
+    total = total * scale[...]
+    rows = total.shape[0]
+    for d in range(total.shape[1] // HD):
+        proj[d * rows : (d + 1) * rows, :] = total[:, d * HD : (d + 1) * HD]
+
+
+def near_kernel(core, a0, a1, w0, w1, res, scale, out, att, proj, res32):
     b = pl.program_id(0)
-    c = core[0]
-    groups = a0.shape[0] // (8 * 48)
 
     @pl.when(b == 0)
     def _():
         res32[...] = res[...].astype(f32)
-        for k, a in enumerate((a0, a1, a2, a3)):
-
-            def move(g, carry):
-                to = pl.ds(pl.multiple_of((g * 2 + (c ^ (k % 2))) * 48, 16), 48)
-                for p in range(8):
-                    block = (k // 2) * 2 + (c ^ (p // 4))
-                    src = pl.ds(pl.multiple_of(g * 384 + p * 48, 16), 48)
-                    att[block, to, (p % 4) * HD : (p % 4 + 1) * HD] = a[src, :]
-                return carry
-
-            lax.fori_loop(0, groups, move, 0)
-
-    total = None
-    for k, w in enumerate((w0, w1, w2, w3)):
-        part = jnp.dot(att[k], w[...], preferred_element_type=f32)
-        total = part if total is None else total + part
-    total = total * scale[...]
+
+    project_half(core, (a0, a1), (w0, w1), scale, att, proj)
+    slots = out.shape[0] // 4
+    per = out.shape[1] // HD
+    for d in range(per):
+        for t in range(4):
+            new = proj[pl.ds(d * 4 * slots + t, slots, stride=4), :]
+            old = res32[pl.ds(t * 8 + b * per + d, slots, stride=32), :]
+            out[t * slots : (t + 1) * slots, d * HD : (d + 1) * HD] = old + new
+
+
+def far_kernel(core, a0, a1, w0, w1, base, scale, mix, out, att, proj):
+    project_half(core, (a0, a1), (w0, w1), scale, att, proj)
     slots = out.shape[0]
-    per = w0.shape[1] // HD
-    for d in range(per):
-        proj[d * 4 * slots : (d + 1) * 4 * slots, :] = total[:, d * HD : (d + 1) * HD]
-    for d in range(per):
+    for d in range(base.shape[1] // HD):
         parts = []
         for t in range(4):
             new = proj[pl.ds(d * 4 * slots + t, slots, stride=4), :]
-            old = res32[pl.ds(t * 8 + b * per + d, slots, stride=32), :]
+            old = base[t * slots : (t + 1) * slots, d * HD : (d + 1) * HD]
             parts.append((old + new).astype(bf16))
         rows = jnp.concatenate(parts, axis=1)
         out[:, d * 4 * HD : (d + 1) * 4 * HD] = jnp.dot(
@@ -296,36 +311,47 @@
         ).astype(bf16)
 
 
-def project(core, atts, weights, res, scale, slots):
+def project(core, atts, weights, rest, scale, slots, near):
     width = weights[0].shape[1]
     part = 256
     whole = pl.BlockSpec(memory_space=pltpu.VMEM)
-    source = np.arange(4 * HD)
-    mix = np.zeros((4 * HD, 4 * HD), np.float32)
-    mix[source, (source % HD) * 4 + source // HD] = 1.0
+    blocks = lambda rows, columns: pl.BlockSpec((rows, columns), lambda b, *_: (0, b))
+    specs = [whole] * 2 + [blocks(weights[0].shape[0], part)] * 2
+    scratch = [
+        pltpu.VMEM((2, slots * 4, 4 * HD), bf16),
+        pltpu.VMEM((slots * 4 * part // HD, HD), f32),
+    ]
+    if near:
+        specs += [whole, blocks(1, part)]
+        scratch.append(pltpu.VMEM((slots * 32, HD), f32))
+        out_shape = jax.ShapeDtypeStruct((slots * 4, width), f32)
+        out_specs = blocks(slots * 4, part)
+        given = (rest, scale)
+    else:
+        source = np.arange(4 * HD)
+        mix = np.zeros((4 * HD, 4 * HD), np.float32)
+        mix[source, (source % HD) * 4 + source // HD] = 1.0
+        specs += [blocks(slots * 4, part), blocks(1, part), whole]
+        out_shape = jax.ShapeDtypeStruct((slots, 4 * width), bf16)
+        out_specs = blocks(slots, 4 * part)
+        given = (rest, scale, jnp.asarray(mix, bf16))
     return pl.pallas_call(
-        project_kernel,
-        out_shape=jax.ShapeDtypeStruct((slots, 4 * width), bf16),
+        near_kernel if near else far_kernel,
+        out_shape=out_shape,
         grid_spec=pltpu.PrefetchScalarGridSpec(
             num_scalar_prefetch=1,
             grid=(width // part,),
-            in_specs=[whole] * 4
-            + [pl.BlockSpec((weights[0].shape[0], part), lambda b, *_: (0, b))] * 4
-            + [whole, pl.BlockSpec((1, part), lambda b, *_: (0, b)), whole],
-            out_specs=pl.BlockSpec((slots, 4 * part), lambda b, *_: (0, b)),
-            scratch_shapes=[
-                pltpu.VMEM((4, slots * 4, 4 * HD), bf16),
-                pltpu.VMEM((slots * 32, HD), f32),
-                pltpu.VMEM((slots * 4 * part // HD, HD), f32),
-            ],
+            in_specs=specs,
+            out_specs=out_specs,
+            scratch_shapes=scratch,
         ),
         compiler_params=pltpu.CompilerParams(
-            dimension_semantics=("arbitrary",), vmem_limit_bytes=48 << 20
+            dimension_semantics=("arbitrary",), vmem_limit_bytes=40 << 20
         ),
         cost_estimate=pl.CostEstimate(
-            flops=2 * 768 * 2048 * 1024, bytes_accessed=16 << 20, transcendentals=0
-        ),
-    )(core, *atts, *weights, res, scale, jnp.asarray(mix, bf16))
+            flops=2 * 768 * 1024 * 1024, bytes_accessed=10 << 20, transcendentals=0
+        ),
+    )(core, *atts, *weights, *given)
 
 
 def swap(x, axis, k):
@@ -507,15 +533,12 @@
     res = res.reshape(n_seq * CAP * 4 * width // HD, HD)
     got_c = swap(got, HEAD, 1)
     got_x = swap(got, HEAD, 2)
-    got_xc = swap(got_x, HEAD, 1)
-    delivered = project(
-        c[None].astype(jnp.int32),
-        (got, got_c, got_x, got_xc),
-        weights,
-        res,
-        layer_scale[None, :],
-        n_seq * CAP,
-    )
+    core = c[None].astype(jnp.int32)
+    gain = layer_scale[None, :]
+    slots = n_seq * CAP
+    base = project(core, (got, got_c), weights[:2], res, gain, slots, True)
+    got_xc = swap(tie(got_x, base), HEAD, 1)
+    delivered = project(core, (got_x, got_xc), weights[2:], base, gain, slots, False)
     return (delivered, refreshed)
 
 

time: 231 us -> 230 us (level)
  starting transfers between devices: 60.3 us -> 56.9 us
  local copies, waits for them, and re-layouts: 15.6 us -> 18 us
    ppermute x8, starting transfers between devices: 12.3 us -> 9.09 us  [swap(): return lax.ppermute(x, axis, [(i, i ^ k) for i in range(n)])]
    unnamed x30 -> x54, local copies, waits for them, and re-layouts: 3.73 us -> 5.05 us
    pallas_call x1 -> x2, Pallas kernels: 11.4 us -> 11.9 us  [project(): pl.pallas_call(near_kernel if near else far_kernel, out_shape=out_shape,...]
  transfers between devices with their start and end apart: 21 -> 21, of which waited for: 7 -> 8; matrix products, arithmetic and copies ran while one was open for 11% -> 11% of each run, Pallas kernels for 14% -> 17%
where the time goes in v8:
time: 230 us; the launch traced here: 229 us
  starting transfers between devices  56.9 us (25%)
  Pallas kernels  45.4 us (20%)
  waiting for transfers between devices  45.2 us (20%)
  blocking collectives  34.7 us (15%)
  local copies, waits for them, and re-layouts  18 us (8%)
  between operations  15.4 us (7%)
  other arithmetic  8.95 us (4%)
  matrix products  4.61 us (2%)
    all_to_all x1, blocking collectives, shards(): lax.all_to_all(sent.reshape(n_seq, heads * CAP * 4, HD), SEQ, split_axis=...  34.7 us
    pallas_call x1, Pallas kernels, attend(): pl.pallas_call(attention_kernel, out_shape=jax.ShapeDtypeStruct((slots *...  27.8 us
    ppermute x8, starting transfers between devices, spread(): return lax.ppermute(part, ('zh', 'zp', 'c'), pairs)  24.7 us
    ppermute x8, waiting for transfers between devices, swap(): return lax.ppermute(x, axis, [(i, i ^ k) for i in range(n)])  22.6 us
    ppermute x8, waiting for transfers between devices, spread(): return lax.ppermute(part, ('zh', 'zp', 'c'), pairs)  19.4 us
    all_to_all x1, starting transfers between devices, shards(): lax.all_to_all(tie(res, left, right), SEQ, split_axis=0, concat_axis=0, t...  14.4 us
    pallas_call x2, Pallas kernels, project(): pl.pallas_call(near_kernel if near else far_kernel, out_shape=out_shape,...  11.9 us
    ppermute x8, starting transfers between devices, swap(): return lax.ppermute(x, axis, [(i, i ^ k) for i in range(n)])  9.09 us
  transfers between devices with their start and end apart: 21, of which 8 were waited for; matrix products, arithmetic and copies ran while one was open for 11% of the time, Pallas kernels for 17%

profile of v8, /device:TPU:1, one launch (start us, length us, event | category | flops | bytes accessed | tf_op | source)
XLA Modules:
  0.0 229.0 jit_solution(4575762366883229569)
XLA Ops:
  8.9 4.4 %collective-permute-start = (s32[256]{0:T(256)S(1)}, s32[256]{0:T(256)S(1)}, u32[]{:S(2)}, u32[]{:S(2)}) collective-permute-start(s32[256]{0:T(256)S(1)} %slice.109), channel_id=1, source_target_pairs={{0,4},{4,8},{8,12},{12,16},{16,20},{20,24},{24,28},{28,32},{32,36}... | collective-permute-start | bytes 3080 | tf_op jit(solution)/shard_map/ppermute | solution.py:401
  17.6 2.8 %fusion.34 = f32[16,512]{1,0:T(8,128)S(1)} fusion(bf16[16,4096]{1,0:T(8,128)(2,1)S(1)} %copy-done, bf16[4096,512]{1,0:T(8,128)(2,1)} %param.27), kind=kOutput, calls=%fused_computation.130 | convolution fusion | flops 67108864 | bytes 4358144 | tf_op jit(solution)/shard_map/dot_general | solution.py:426
  26.0 9.0 %collective-permute-start.1 = (bf16[96,256]{1,0:T(8,128)(2,1)S(1)}, bf16[96,256]{1,0:T(8,128)(2,1)S(1)}, u32[]{:S(2)}, u32[]{:S(2)}) collective-permute-start(bf16[96,256]{1,0:T(8,128)(2,1)S(1)} %get-tuple-element.51), channel_id=1, source_target_pairs={{0,0},{1,16},{4,4},{5,20},{8,8},{9,24},{12,12},{13,28},{16,1},{17,... | collective-permute-start | bytes 147464 | tf_op jit(solution)/shard_map/ppermute | solution.py:454
  36.2 3.2 %collective-permute-start.3 = (bf16[96,256]{1,0:T(8,128)(2,1)S(1)}, bf16[96,256]{1,0:T(8,128)(2,1)S(1)}, u32[]{:S(2)}, u32[]{:S(2)}) collective-permute-start(bf16[96,256]{1,0:T(8,128)(2,1)S(1)} %get-tuple-element.53), channel_id=1, source_target_pairs={{0,8},{1,24},{4,12},{5,28},{8,0},{9,16},{12,4},{13,20},{16,9},{17,... | collective-permute-start | bytes 147464 | tf_op jit(solution)/shard_map/ppermute | solution.py:454
  42.3 3.3 %shard_map.159 = bf16[4,528,384]{2,1,0:T(8,128)(2,1)} custom-call(bf16[512,512]{1,0:T(8,128)(2,1)} %q_ref.1, bf16[512,512]{1,0:T(8,128)(2,1)} %k_ref.1, bf16[512,512]{1,0:T(8,128)(2,1)} %v_ref.3, f32[512,128]{1,0:T(8,128)} %get-tuple-element.68.c_ref, f32[512,128]{1,0:T(8,128)} %get-tuple-element.69.s_ref, bf16[16,384]{1,0:T(8,128)(2,1)} %reshape.311.extra_ref), custom_call_target="tpu_custom_call" | custom-call | tf_op jit(solution)/shard_map/pallas_call | solution.py:410
  46.5 2.5 %collective-permute-start.6 = (bf16[384,256]{1,0:T(8,128)(2,1)S(1)}, bf16[384,256]{1,0:T(8,128)(2,1)S(1)}, u32[]{:S(2)}, u32[]{:S(2)}) collective-permute-start(bf16[384,256]{1,0:T(8,128)(2,1)S(1)} %pad_maximum_fusion.2), channel_id=1, source_target_pairs={{0,128},{128,0},{1,129},{129,1},{2,130},{130,2},{3,131},{131,3},{4... | collective-permute-start | bytes 589832 | tf_op jit(solution)/shard_map/ppermute | solution.py:359
  49.0 2.6 %dynamic-slice_bitcast_fusion = (bf16[528,384]{1,0:T(8,128)(2,1)}, bf16[528,384]{1,0:T(8,128)(2,1)}, bf16[528,384]{1,0:T(8,128)(2,1)}, bf16[528,384]{1,0:T(8,128)(2,1)}) fusion(bf16[4,528,384]{2,1,0:T(8,128)(2,1)} %shard_map.159, s32[]{:T(128)S(6)} %select_n.73, s32[]{:T(128)S(6)} %select_n.72, s32[]{:T(128)S(6)} %select_n.71, s32[]{:T(128)S(6)} %select_n.70), kind=kLoop, calls=%fused_computation.10 | loop fusion | bytes 3244048 | tf_op jit(solution)/shard_map/jit(dynamic_index_in_dim)/squeeze | solution.py:453
  52.5 2.4 %collective-permute-start.9 = (bf16[528,384]{1,0:T(8,128)(2,1)}, bf16[528,384]{1,0:T(8,128)(2,1)S(1)}, u32[]{:S(2)}, u32[]{:S(2)}) collective-permute-start(bf16[528,384]{1,0:T(8,128)(2,1)} %get-tuple-element.40), channel_id=1, source_target_pairs={{0,8},{1,24},{4,12},{5,28},{8,0},{9,16},{12,4},{13,20},{16,9},{17,... | collective-permute-start | bytes 1216520 | tf_op jit(solution)/shard_map/ppermute | solution.py:454
  55.0 2.9 %collective-permute-start.8 = (bf16[528,384]{1,0:T(8,128)(2,1)}, bf16[528,384]{1,0:T(8,128)(2,1)S(1)}, u32[]{:S(2)}, u32[]{:S(2)}) collective-permute-start(bf16[528,384]{1,0:T(8,128)(2,1)} %get-tuple-element.41), channel_id=1, source_target_pairs={{0,4},{1,20},{4,0},{5,16},{8,12},{9,28},{12,8},{13,24},{16,5},{17,... | collective-permute-start | bytes 1216520 | tf_op jit(solution)/shard_map/ppermute | solution.py:454
  57.8 4.6 %collective-permute-start.7 = (bf16[528,384]{1,0:T(8,128)(2,1)}, bf16[528,384]{1,0:T(8,128)(2,1)S(1)}, u32[]{:S(2)}, u32[]{:S(2)}) collective-permute-start(bf16[528,384]{1,0:T(8,128)(2,1)} %get-tuple-element.42), channel_id=1, source_target_pairs={{0,0},{1,16},{4,4},{5,20},{8,8},{9,24},{12,12},{13,28},{16,1},{17,... | collective-permute-start | bytes 1216520 | tf_op jit(solution)/shard_map/ppermute | solution.py:454
  63.3 2.5 %reshape.313 = bf16[128,4096]{1,0:T(8,128)(2,1)} reshape(bf16[512,1024]{1,0:T(8,128)(2,1)} %param.18) | data formatting | bytes 2097152 | tf_op jit(solution)/shard_map/reshape | solution.py:475
  69.7 13.0 %collective-permute-done.9.refs_2_ = bf16[528,384]{1,0:T(8,128)(2,1)S(1)} collective-permute-done((bf16[528,384]{1,0:T(8,128)(2,1)}, bf16[528,384]{1,0:T(8,128)(2,1)S(1)}, u32[]{:S(2)}, u32[]{:S(2)}) %collective-permute-start.9) | collective-permute-done | bytes 405536 | tf_op jit(solution)/shard_map/ppermute | solution.py:454
  82.6 5.6 %collective-permute-done.8.refs_1_ = bf16[528,384]{1,0:T(8,128)(2,1)S(1)} collective-permute-done((bf16[528,384]{1,0:T(8,128)(2,1)}, bf16[528,384]{1,0:T(8,128)(2,1)S(1)}, u32[]{:S(2)}, u32[]{:S(2)}) %collective-permute-start.8) | collective-permute-done | bytes 405536 | tf_op jit(solution)/shard_map/ppermute | solution.py:454
  91.2 2.4 %collective-permute-start.12 = (bf16[224,256]{1,0:T(8,128)(2,1)S(1)}, bf16[224,256]{1,0:T(8,128)(2,1)S(1)}, u32[]{:S(2)}, u32[]{:S(2)}) collective-permute-start(bf16[224,256]{1,0:T(8,128)(2,1)S(1)} %fusion.3), channel_id=1, source_target_pairs={{1,0},{32,1},{33,32},{64,33},{65,64},{96,65},{97,96},{128,97},{129... | collective-permute-start | bytes 344072 | tf_op jit(solution)/shard_map/ppermute | solution.py:486
  94.3 3.0 %collective-permute-done.12.refs_5_ = bf16[224,256]{1,0:T(8,128)(2,1)S(1)} collective-permute-done((bf16[224,256]{1,0:T(8,128)(2,1)S(1)}, bf16[224,256]{1,0:T(8,128)(2,1)S(1)}, u32[]{:S(2)}, u32[]{:S(2)}) %collective-permute-start.12) | collective-permute-done | bytes 114720 | tf_op jit(solution)/shard_map/ppermute | solution.py:486
  97.9 14.4 %all-to-all-start = ((bf16[64,96,128]{2,1,0:T(8,128)(2,1)}), bf16[64,96,128]{2,1,0:T(8,128)(2,1)S(1)}, u32[]{:S(2)}, u32[]{:S(2)}) async-start(bf16[64,96,128]{2,1,0:T(8,128)(2,1)} %reshape.314), calls=%async_computation | async-start | bytes 3145728 | tf_op jit(solution)/shard_map/all_to_all | solution.py:525
  113.1 2.4 %constant_dynamic-slice_fusion.4 = (bf16[512,1024]{1,0:T(8,128)(2,1)S(1)}, bf16[512,1024]{1,0:T(8,128)(2,1)S(1)}, bf16[512,1024]{1,0:T(8,128)(2,1)S(1)}) fusion(bf16[512,4096]{1,0:T(8,128)(2,1)} %param.20, s32[]{:T(128)S(6)} %select_n.79, s32[]{:T(128)S(6)} %select_n.78, s32[]{:T(128)S(6)} %select_n.77), kind=kLoop, calls=%fused_computation.72 | loop fusion | bytes 6291468 | tf_op jit(solution)/shard_map/dynamic_slice | solution.py:396
  119.3 27.8 %shard_map.160 = bf16[3072,128]{1,0:T(8,128)(2,1)S(1)} custom-call(s32[65]{0:T(128)S(1)} %select_reduce_fusion.1.off, s32[512]{0:T(512)S(1)} %add_bitcast_fusion.tgt, s32[1]{0:T(128)} %bitcast.33.zp, bf16[528,384]{1,0:T(8,128)(2,1)S(1)} %copy-done.15, bf16[528,384]{1,0:T(8,128)(2,1)S(1)} %copy-done.13, bf16[528,384]{1,0:T(8,128)(2,1)S(1)} %copy-done.11, ...), custom_call_target="tpu_custom_call" | custom-call | flops 7516192768 | bytes 8388608 | tf_op jit(solution)/shard_map/pallas_call | solution.py:223
  147.1 6.8 %collective-permute-done.15.w1 = bf16[512,1024]{1,0:T(8,128)(2,1)S(1)} collective-permute-done((bf16[512,1024]{1,0:T(8,128)(2,1)S(1)}, bf16[512,1024]{1,0:T(8,128)(2,1)S(1)}, u32[]{:S(2)}, u32[]{:S(2)}) %collective-permute-start.15) | collective-permute-done | bytes 1048608 | tf_op jit(solution)/shard_map/ppermute | solution.py:359
  155.9 34.7 %all_to_all.10 = bf16[64,48,128]{2,1,0:T(8,128)(2,1)S(1)} all-to-all(bf16[64,48,128]{2,1,0:T(8,128)(2,1)S(1)} %bitcast.77), channel_id=1, replica_groups=mesh['xh'=2,'y'=4,'zh'=2,'zp'=4,'xl'=2,'c'=2] {'xh','y','zh','zp'}, dimensions={0} | all-to-all | bytes 1572864 | tf_op jit(solution)/shard_map/all_to_all | solution.py:530
  190.6 2.7 %collective-permute-start.17 = (bf16[3072,128]{1,0:T(8,128)(2,1)S(1)}, bf16[3072,128]{1,0:T(8,128)(2,1)S(1)}, u32[]{:S(2)}, u32[]{:S(2)}) collective-permute-start(bf16[3072,128]{1,0:T(8,128)(2,1)S(1)} %bitcast.74), channel_id=1, source_target_pairs={{0,1},{1,0},{2,3},{3,2},{4,5},{5,4},{6,7},{7,6},{8,9},{9,8},{10,11... | collective-permute-start | bytes 2359304 | tf_op jit(solution)/shard_map/ppermute | solution.py:359
  195.2 4.9 %shard_map.161.base = f32[768,1024]{1,0:T(8,128)S(1)} custom-call(s32[1]{0:T(128)} %bitcast.core, bf16[3072,128]{1,0:T(8,128)(2,1)S(1)} %bitcast.76, bf16[3072,128]{1,0:T(8,128)(2,1)S(1)} %collective-permute-done.17.a1, bf16[512,1024]{1,0:T(8,128)(2,1)S(1)} %get-tuple-element.30.w0, bf16[512,1024]{1,0:T(8,128)(2,1)S(1)} %copy-done.6, ...), custom_call_target="tpu_custom_call" | custom-call | flops 1610612736 | bytes 10485760 | tf_op jit(solution)/shard_map/pallas_call | solution.py:338
  200.2 12.3 %collective-permute-done.16.a0 = bf16[3072,128]{1,0:T(8,128)(2,1)S(1)} collective-permute-done((bf16[3072,128]{1,0:T(8,128)(2,1)S(1)}, bf16[3072,128]{1,0:T(8,128)(2,1)S(1)}, u32[]{:S(2)}, u32[]{:S(2)}) %collective-permute-start.16) | collective-permute-done | bytes 786464 | tf_op jit(solution)/shard_map/ppermute | solution.py:359
  215.2 7.0 %shard_map.162 = bf16[192,4096]{1,0:T(8,128)(2,1)} custom-call(s32[1]{0:T(128)} %bitcast.core, bf16[3072,128]{1,0:T(8,128)(2,1)S(1)} %collective-permute-done.16.a0, bf16[3072,128]{1,0:T(8,128)(2,1)S(1)} %collective-permute-done.18.a1, bf16[512,1024]{1,0:T(8,128)(2,1)S(1)} %copy-done.2, bf16[512,1024]{1,0:T(8,128)(2,1)S(1)} %copy-done.4, ...), custom_call_target="tpu_custom_call" | custom-call | flops 1610612736 | bytes 10485760 | tf_op jit(solution)/shard_map/pallas_call | solution.py:338
  (162 shorter events, 36.4 us)
Async XLA Ops:
  7.2 105.1 %all-gather.2.cloned.1.call-start = ((), (), s32[]{:S(2)}) async-start(), calls=%async_computation.2 | async-start | bytes 1966080 | tf_op jit(solution)/shard_map/all_gather | solution.py:464
  8.9 16.2 %collective-permute-start = (s32[256]{0:T(256)S(1)}, s32[256]{0:T(256)S(1)}, u32[]{:S(2)}, u32[]{:S(2)}) collective-permute-start(s32[256]{0:T(256)S(1)} %slice.109), channel_id=1, source_target_pairs={{0,4},{4,8},{8,12},{12,16},{16,20},{20,24},{24,28},{28,32},{32,36}... | collective-permute-start | bytes 3080 | tf_op jit(solution)/shard_map/ppermute | solution.py:401
  14.6 31.9 %collective-permute-start.5 = (bf16[512,1024]{1,0:T(8,128)(2,1)S(1)}, bf16[512,1024]{1,0:T(8,128)(2,1)S(1)}, u32[]{:S(2)}, u32[]{:S(2)}) collective-permute-start(bf16[512,1024]{1,0:T(8,128)(2,1)S(1)} %constant_dynamic-slice_fusion.11), channel_id=1, source_target_pairs={{0,2},{1,3},{2,0},{3,1},{4,6},{5,7},{6,4},{7,5},{8,10},{9,11},{10,... | collective-permute-start | bytes 3145736 | tf_op jit(solution)/shard_map/ppermute | solution.py:359
  26.0 19.6 %collective-permute-start.1 = (bf16[96,256]{1,0:T(8,128)(2,1)S(1)}, bf16[96,256]{1,0:T(8,128)(2,1)S(1)}, u32[]{:S(2)}, u32[]{:S(2)}) collective-permute-start(bf16[96,256]{1,0:T(8,128)(2,1)S(1)} %get-tuple-element.51), channel_id=1, source_target_pairs={{0,0},{1,16},{4,4},{5,20},{8,8},{9,24},{12,12},{13,28},{16,1},{17,... | collective-permute-start | bytes 147464 | tf_op jit(solution)/shard_map/ppermute | solution.py:454
  35.0 10.5 %collective-permute-start.4 = (bf16[96,256]{1,0:T(8,128)(2,1)S(1)}, bf16[96,256]{1,0:T(8,128)(2,1)S(1)}, u32[]{:S(2)}, u32[]{:S(2)}) collective-permute-start(bf16[96,256]{1,0:T(8,128)(2,1)S(1)} %get-tuple-element.52), channel_id=1, source_target_pairs={{0,12},{1,28},{4,8},{5,24},{8,4},{9,20},{12,0},{13,16},{16,13},{17... | collective-permute-start | bytes 147464 | tf_op jit(solution)/shard_map/ppermute | solution.py:454
  36.2 9.3 %collective-permute-start.3 = (bf16[96,256]{1,0:T(8,128)(2,1)S(1)}, bf16[96,256]{1,0:T(8,128)(2,1)S(1)}, u32[]{:S(2)}, u32[]{:S(2)}) collective-permute-start(bf16[96,256]{1,0:T(8,128)(2,1)S(1)} %get-tuple-element.53), channel_id=1, source_target_pairs={{0,8},{1,24},{4,12},{5,28},{8,0},{9,16},{12,4},{13,20},{16,9},{17,... | collective-permute-start | bytes 147464 | tf_op jit(solution)/shard_map/ppermute | solution.py:454
  39.4 7.0 %collective-permute-start.2 = (bf16[96,256]{1,0:T(8,128)(2,1)S(1)}, bf16[96,256]{1,0:T(8,128)(2,1)S(1)}, u32[]{:S(2)}, u32[]{:S(2)}) collective-permute-start(bf16[96,256]{1,0:T(8,128)(2,1)S(1)} %get-tuple-element.54), channel_id=1, source_target_pairs={{0,4},{1,20},{4,0},{5,16},{8,12},{9,28},{12,8},{13,24},{16,5},{17,... | collective-permute-start | bytes 147464 | tf_op jit(solution)/shard_map/ppermute | solution.py:454
  46.5 16.0 %collective-permute-start.6 = (bf16[384,256]{1,0:T(8,128)(2,1)S(1)}, bf16[384,256]{1,0:T(8,128)(2,1)S(1)}, u32[]{:S(2)}, u32[]{:S(2)}) collective-permute-start(bf16[384,256]{1,0:T(8,128)(2,1)S(1)} %pad_maximum_fusion.2), channel_id=1, source_target_pairs={{0,128},{128,0},{1,129},{129,1},{2,130},{130,2},{3,131},{131,3},{4... | collective-permute-start | bytes 589832 | tf_op jit(solution)/shard_map/ppermute | solution.py:359
  51.6 18.0 %collective-permute-start.10 = (bf16[528,384]{1,0:T(8,128)(2,1)}, bf16[528,384]{1,0:T(8,128)(2,1)S(1)}, u32[]{:S(2)}, u32[]{:S(2)}) collective-permute-start(bf16[528,384]{1,0:T(8,128)(2,1)} %get-tuple-element.39), channel_id=1, source_target_pairs={{0,12},{1,28},{4,8},{5,24},{8,4},{9,20},{12,0},{13,16},{16,13},{17... | collective-permute-start | bytes 1216520 | tf_op jit(solution)/shard_map/ppermute | solution.py:454
  52.5 30.1 %collective-permute-start.9 = (bf16[528,384]{1,0:T(8,128)(2,1)}, bf16[528,384]{1,0:T(8,128)(2,1)S(1)}, u32[]{:S(2)}, u32[]{:S(2)}) collective-permute-start(bf16[528,384]{1,0:T(8,128)(2,1)} %get-tuple-element.40), channel_id=1, source_target_pairs={{0,8},{1,24},{4,12},{5,28},{8,0},{9,16},{12,4},{13,20},{16,9},{17,... | collective-permute-start | bytes 1216520 | tf_op jit(solution)/shard_map/ppermute | solution.py:454
  55.0 33.2 %collective-permute-start.8 = (bf16[528,384]{1,0:T(8,128)(2,1)}, bf16[528,384]{1,0:T(8,128)(2,1)S(1)}, u32[]{:S(2)}, u32[]{:S(2)}) collective-permute-start(bf16[528,384]{1,0:T(8,128)(2,1)} %get-tuple-element.41), channel_id=1, source_target_pairs={{0,4},{1,20},{4,0},{5,16},{8,12},{9,28},{12,8},{13,24},{16,5},{17,... | collective-permute-start | bytes 1216520 | tf_op jit(solution)/shard_map/ppermute | solution.py:454
  57.8 30.4 %collective-permute-start.7 = (bf16[528,384]{1,0:T(8,128)(2,1)}, bf16[528,384]{1,0:T(8,128)(2,1)S(1)}, u32[]{:S(2)}, u32[]{:S(2)}) collective-permute-start(bf16[528,384]{1,0:T(8,128)(2,1)} %get-tuple-element.42), channel_id=1, source_target_pairs={{0,0},{1,16},{4,4},{5,20},{8,8},{9,24},{12,12},{13,28},{16,1},{17,... | collective-permute-start | bytes 1216520 | tf_op jit(solution)/shard_map/ppermute | solution.py:454
  69.6 43.0 %copy-start.8 = (bf16[528,384]{1,0:T(8,128)(2,1)}, bf16[528,384]{1,0:T(8,128)(2,1)S(1)}, u32[]{:S(2)}) copy-start(bf16[528,384]{1,0:T(8,128)(2,1)S(1)} %collective-permute-done.10.refs_3_) | copy-start | bytes 1216516
  89.1 4.5 %collective-permute-start.11 = (bf16[224,256]{1,0:T(8,128)(2,1)S(1)}, bf16[224,256]{1,0:T(8,128)(2,1)S(1)}, u32[]{:S(2)}, u32[]{:S(2)}) collective-permute-start(bf16[224,256]{1,0:T(8,128)(2,1)S(1)} %fusion.2), channel_id=1, source_target_pairs={{0,1},{1,32},{32,33},{33,64},{64,65},{65,96},{96,97},{97,128},{128... | collective-permute-start | bytes 344072 | tf_op jit(solution)/shard_map/ppermute | solution.py:486
  91.2 6.1 %collective-permute-start.12 = (bf16[224,256]{1,0:T(8,128)(2,1)S(1)}, bf16[224,256]{1,0:T(8,128)(2,1)S(1)}, u32[]{:S(2)}, u32[]{:S(2)}) collective-permute-start(bf16[224,256]{1,0:T(8,128)(2,1)S(1)} %fusion.3), channel_id=1, source_target_pairs={{1,0},{32,1},{33,32},{64,33},{65,64},{96,65},{97,96},{128,97},{129... | collective-permute-start | bytes 344072 | tf_op jit(solution)/shard_map/ppermute | solution.py:486
  97.9 58.0 %all-to-all-start = ((bf16[64,96,128]{2,1,0:T(8,128)(2,1)}), bf16[64,96,128]{2,1,0:T(8,128)(2,1)S(1)}, u32[]{:S(2)}, u32[]{:S(2)}) async-start(bf16[64,96,128]{2,1,0:T(8,128)(2,1)} %reshape.314), calls=%async_computation | async-start | bytes 3145728 | tf_op jit(solution)/shard_map/all_to_all | solution.py:525
  112.3 5.0 %collective-permute-start.13 = (bf16[3072,256]{1,0:T(8,128)(2,1)}, bf16[3072,256]{1,0:T(8,128)(2,1)}, u32[]{:S(2)}, u32[]{:S(2)}) collective-permute-start(bf16[3072,256]{1,0:T(8,128)(2,1)} %all-gather.2.cloned.1.call-done.refs_6_), channel_id=1, source_target_pairs={{0,1},{1,0},{2,3},{3,2},{4,5},{5,4},{6,7},{7,6},{8,9},{9,8},{10,11... | collective-permute-start | bytes 4718600 | tf_op jit(solution)/shard_map/ppermute | solution.py:359
  115.5 38.4 %collective-permute-start.15 = (bf16[512,1024]{1,0:T(8,128)(2,1)S(1)}, bf16[512,1024]{1,0:T(8,128)(2,1)S(1)}, u32[]{:S(2)}, u32[]{:S(2)}) collective-permute-start(bf16[512,1024]{1,0:T(8,128)(2,1)S(1)} %get-tuple-element.36), channel_id=1, source_target_pairs={{0,3},{1,2},{2,1},{3,0},{4,7},{5,6},{6,5},{7,4},{8,11},{9,10},{10,... | collective-permute-start | bytes 3145736 | tf_op jit(solution)/shard_map/ppermute | solution.py:359
  116.6 38.3 %collective-permute-start.14 = (bf16[512,1024]{1,0:T(8,128)(2,1)S(1)}, bf16[512,1024]{1,0:T(8,128)(2,1)S(1)}, u32[]{:S(2)}, u32[]{:S(2)}) collective-permute-start(bf16[512,1024]{1,0:T(8,128)(2,1)S(1)} %get-tuple-element.37), channel_id=1, source_target_pairs={{0,1},{1,0},{2,3},{3,2},{4,5},{5,4},{6,7},{7,6},{8,9},{9,8},{10,11... | collective-permute-start | bytes 3145736 | tf_op jit(solution)/shard_map/ppermute | solution.py:359
  147.1 48.1 %copy-start.16 = (f32[1024]{0:T(1024)S(1)}, f32[1024]{0:T(1024)}, u32[]{:S(2)}) copy-start(f32[1024]{0:T(1024)} %param.19) | copy-start | bytes 12292
  155.9 39.3 %copy-start.6 = (bf16[512,1024]{1,0:T(8,128)(2,1)S(1)}, bf16[512,1024]{1,0:T(8,128)(2,1)}, u32[]{:S(2)}) copy-start(bf16[512,1024]{1,0:T(8,128)(2,1)} %copy-done.5) | copy-start | bytes 3145732
  190.6 4.6 %collective-permute-start.17 = (bf16[3072,128]{1,0:T(8,128)(2,1)S(1)}, bf16[3072,128]{1,0:T(8,128)(2,1)S(1)}, u32[]{:S(2)}, u32[]{:S(2)}) collective-permute-start(bf16[3072,128]{1,0:T(8,128)(2,1)S(1)} %bitcast.74), channel_id=1, source_target_pairs={{0,1},{1,0},{2,3},{3,2},{4,5},{5,4},{6,7},{7,6},{8,9},{9,8},{10,11... | collective-permute-start | bytes 2359304 | tf_op jit(solution)/shard_map/ppermute | solution.py:359
  193.3 19.2 %collective-permute-start.16 = (bf16[3072,128]{1,0:T(8,128)(2,1)S(1)}, bf16[3072,128]{1,0:T(8,128)(2,1)S(1)}, u32[]{:S(2)}, u32[]{:S(2)}) collective-permute-start(bf16[3072,128]{1,0:T(8,128)(2,1)S(1)} %bitcast.75), channel_id=1, source_target_pairs={{0,2},{1,3},{2,0},{3,1},{4,6},{5,7},{6,4},{7,5},{8,10},{9,11},{10,... | collective-permute-start | bytes 2359304 | tf_op jit(solution)/shard_map/ppermute | solution.py:359
  212.5 2.7 %collective-permute-start.18 = (bf16[3072,128]{1,0:T(8,128)(2,1)S(1)}, bf16[3072,128]{1,0:T(8,128)(2,1)S(1)}, u32[]{:S(2)}, u32[]{:S(2)}) collective-permute-start(bf16[3072,128]{1,0:T(8,128)(2,1)S(1)} %collective-permute-done.16.a0), channel_id=1, source_target_pairs={{0,1},{1,0},{2,3},{3,2},{4,5},{5,4},{6,7},{7,6},{8,9},{9,8},{10,11... | collective-permute-start | bytes 2359304 | tf_op jit(solution)/shard_map/ppermute | solution.py:359
  (23 other events, 218.6 us)
Sparse Core Ops, SparseCore 0:
  63.4 26.6 all-gather.1

commit v9 on v8

--- a/solution.py
+++ b/solution.py
@@ -476,7 +476,9 @@
     ).astype(bf16)
     res = res.reshape(n_seq, CAP * 4 * width // HD, HD)
 
-    edges = tie(tuple(ys), res)
+    out_weight = tie(out_weight, kv8, qkv)
+    rows_c, rows_xc = weight_rows(1), weight_rows(3)
+    edges = tie(tuple(ys), res, rows_c, rows_xc)
 
     def edge(low, j, line, pairs):
         part = jnp.stack([t[low : low + HALO, HD:] for t in edges])
@@ -514,12 +516,12 @@
     peer = (jnp.arange(heads, dtype=jnp.int32) ^ zp)[:, None]
     tgt = (group_owners * (heads * CAP) + peer * CAP + slots_of(group_owners)).reshape(-1)
 
-    out_weight = tie(out_weight, left, right)
+    rows_c, rows_xc = tie((rows_c, rows_xc), left, right)
     weights = [
         weight_rows(0),
-        swap(weight_rows(1), HEAD, 1),
+        swap(rows_c, HEAD, 1),
         weight_x,
-        swap(weight_rows(3), HEAD, 3),
+        swap(rows_xc, HEAD, 3),
     ]
 
     res = lax.all_to_all(tie(res, left, right), SEQ, split_axis=0, concat_axis=0, tiled=True)

time: 230 us -> 230 us (level)
  local copies, waits for them, and re-layouts: 18 us -> 29.2 us
  waiting for transfers between devices: 45.2 us -> 34.8 us
    unnamed x54, local copies, waits for them, and re-layouts: 5.05 us -> 12.2 us
    ppermute x8, waiting for transfers between devices: 22.6 us -> 16.6 us  [swap(): return lax.ppermute(x, axis, [(i, i ^ k) for i in range(n)])]
    ppermute x8, waiting for transfers between devices: 19.4 us -> 15.1 us  [spread(): return lax.ppermute(part, ('zh', 'zp', 'c'), pairs)]
  transfers between devices with their start and end apart: 21 -> 21, of which waited for: 8 -> 8; matrix products, arithmetic and copies ran while one was open for 11% -> 13% of each run, Pallas kernels for 17% -> 16%
where the time goes in v9:
time: 230 us; the launch traced here: 228 us
  starting transfers between devices  56.6 us (25%)
  Pallas kernels  43.8 us (19%)
  blocking collectives  35.2 us (15%)
  waiting for transfers between devices  34.8 us (15%)
  local copies, waits for them, and re-layouts  29.2 us (13%)
  between operations  15.3 us (7%)
  other arithmetic  8.95 us (4%)
  matrix products  4.53 us (2%)
    all_to_all x1, blocking collectives, shards(): lax.all_to_all(sent.reshape(n_seq, heads * CAP * 4, HD), SEQ, split_axis=...  35.2 us
    pallas_call x1, Pallas kernels, attend(): pl.pallas_call(attention_kernel, out_shape=jax.ShapeDtypeStruct((slots *...  26.3 us
    ppermute x8, starting transfers between devices, spread(): return lax.ppermute(part, ('zh', 'zp', 'c'), pairs)  24.7 us
    ppermute x8, waiting for transfers between devices, swap(): return lax.ppermute(x, axis, [(i, i ^ k) for i in range(n)])  16.6 us
    ppermute x8, waiting for transfers between devices, spread(): return lax.ppermute(part, ('zh', 'zp', 'c'), pairs)  15.1 us
    all_to_all x1, starting transfers between devices, shards(): lax.all_to_all(tie(res, left, right), SEQ, split_axis=0, concat_axis=0, t...  14.4 us
    unnamed x54, local copies, waits for them, and re-layouts  12.2 us
    pallas_call x2, Pallas kernels, project(): pl.pallas_call(near_kernel if near else far_kernel, out_shape=out_shape,...  11.9 us
  transfers between devices with their start and end apart: 21, of which 8 were waited for; matrix products, arithmetic and copies ran while one was open for 13% of the time, Pallas kernels for 16%

profile of v9, /device:TPU:1, one launch (start us, length us, event | category | flops | bytes accessed | tf_op | source)
XLA Modules:
  0.0 228.4 jit_solution(6839456755947122368)
XLA Ops:
  8.9 4.4 %collective-permute-start = (s32[256]{0:T(256)S(1)}, s32[256]{0:T(256)S(1)}, u32[]{:S(2)}, u32[]{:S(2)}) collective-permute-start(s32[256]{0:T(256)S(1)} %slice.109), channel_id=1, source_target_pairs={{0,4},{4,8},{8,12},{12,16},{16,20},{20,24},{24,28},{28,32},{32,36}... | collective-permute-start | bytes 3080 | tf_op jit(solution)/shard_map/ppermute | solution.py:401
  17.6 2.8 %fusion.34 = f32[16,512]{1,0:T(8,128)S(1)} fusion(bf16[16,4096]{1,0:T(8,128)(2,1)S(1)} %copy-done, bf16[4096,512]{1,0:T(8,128)(2,1)} %param.27), kind=kOutput, calls=%fused_computation.130 | convolution fusion | flops 67108864 | bytes 4358144 | tf_op jit(solution)/shard_map/dot_general | solution.py:426
  22.7 2.3 %shard_map.158 = bf16[4,96,256]{2,1,0:T(8,128)(2,1)} custom-call(s32[7]{0:T(128)} %pad_add_fusion.1.idx, bf16[128,512]{1,0:T(8,128)(2,1)} %copy-done.23, bf16[128,512]{1,0:T(8,128)(2,1)} %v_ref.2), custom_call_target="tpu_custom_call" | custom-call | tf_op jit(solution)/shard_map/pallas_call | solution.py:439
  26.0 9.0 %collective-permute-start.1 = (bf16[96,256]{1,0:T(8,128)(2,1)S(1)}, bf16[96,256]{1,0:T(8,128)(2,1)S(1)}, u32[]{:S(2)}, u32[]{:S(2)}) collective-permute-start(bf16[96,256]{1,0:T(8,128)(2,1)S(1)} %get-tuple-element.55), channel_id=1, source_target_pairs={{0,0},{1,16},{4,4},{5,20},{8,8},{9,24},{12,12},{13,28},{16,1},{17,... | collective-permute-start | bytes 147464 | tf_op jit(solution)/shard_map/ppermute | solution.py:454
  36.2 3.2 %collective-permute-start.3 = (bf16[96,256]{1,0:T(8,128)(2,1)S(1)}, bf16[96,256]{1,0:T(8,128)(2,1)S(1)}, u32[]{:S(2)}, u32[]{:S(2)}) collective-permute-start(bf16[96,256]{1,0:T(8,128)(2,1)S(1)} %get-tuple-element.57), channel_id=1, source_target_pairs={{0,8},{1,24},{4,12},{5,28},{8,0},{9,16},{12,4},{13,20},{16,9},{17,... | collective-permute-start | bytes 147464 | tf_op jit(solution)/shard_map/ppermute | solution.py:454
  42.3 3.3 %shard_map.159 = bf16[4,528,384]{2,1,0:T(8,128)(2,1)} custom-call(bf16[512,512]{1,0:T(8,128)(2,1)} %q_ref.1, bf16[512,512]{1,0:T(8,128)(2,1)} %k_ref.1, bf16[512,512]{1,0:T(8,128)(2,1)} %v_ref.3, f32[512,128]{1,0:T(8,128)} %get-tuple-element.72.c_ref, f32[512,128]{1,0:T(8,128)} %get-tuple-element.73.s_ref, bf16[16,384]{1,0:T(8,128)(2,1)} %reshape.311.extra_ref), custom_call_target="tpu_custom_call" | custom-call | tf_op jit(solution)/shard_map/pallas_call | solution.py:410
  46.5 2.5 %collective-permute-start.6 = (bf16[384,256]{1,0:T(8,128)(2,1)S(1)}, bf16[384,256]{1,0:T(8,128)(2,1)S(1)}, u32[]{:S(2)}, u32[]{:S(2)}) collective-permute-start(bf16[384,256]{1,0:T(8,128)(2,1)S(1)} %pad_maximum_fusion.2), channel_id=1, source_target_pairs={{0,128},{128,0},{1,129},{129,1},{2,130},{130,2},{3,131},{131,3},{4... | collective-permute-start | bytes 589832 | tf_op jit(solution)/shard_map/ppermute | solution.py:359
  49.0 2.6 %dynamic-slice_bitcast_fusion = (bf16[528,384]{1,0:T(8,128)(2,1)}, bf16[528,384]{1,0:T(8,128)(2,1)}, bf16[528,384]{1,0:T(8,128)(2,1)}, bf16[528,384]{1,0:T(8,128)(2,1)}) fusion(bf16[4,528,384]{2,1,0:T(8,128)(2,1)} %shard_map.159, s32[]{:T(128)S(6)} %select_n.73, s32[]{:T(128)S(6)} %select_n.72, s32[]{:T(128)S(6)} %select_n.71, s32[]{:T(128)S(6)} %select_n.70), kind=kLoop, calls=%fused_computation.10 | loop fusion | bytes 3244048 | tf_op jit(solution)/shard_map/jit(dynamic_index_in_dim)/squeeze | solution.py:453
  52.5 2.4 %collective-permute-start.9 = (bf16[528,384]{1,0:T(8,128)(2,1)}, bf16[528,384]{1,0:T(8,128)(2,1)S(1)}, u32[]{:S(2)}, u32[]{:S(2)}) collective-permute-start(bf16[528,384]{1,0:T(8,128)(2,1)} %get-tuple-element.44), channel_id=1, source_target_pairs={{0,8},{1,24},{4,12},{5,28},{8,0},{9,16},{12,4},{13,20},{16,9},{17,... | collective-permute-start | bytes 1216520 | tf_op jit(solution)/shard_map/ppermute | solution.py:454
  55.0 2.9 %collective-permute-start.8 = (bf16[528,384]{1,0:T(8,128)(2,1)}, bf16[528,384]{1,0:T(8,128)(2,1)S(1)}, u32[]{:S(2)}, u32[]{:S(2)}) collective-permute-start(bf16[528,384]{1,0:T(8,128)(2,1)} %get-tuple-element.45), channel_id=1, source_target_pairs={{0,4},{1,20},{4,0},{5,16},{8,12},{9,28},{12,8},{13,24},{16,5},{17,... | collective-permute-start | bytes 1216520 | tf_op jit(solution)/shard_map/ppermute | solution.py:454
  57.8 4.6 %collective-permute-start.7 = (bf16[528,384]{1,0:T(8,128)(2,1)}, bf16[528,384]{1,0:T(8,128)(2,1)S(1)}, u32[]{:S(2)}, u32[]{:S(2)}) collective-permute-start(bf16[528,384]{1,0:T(8,128)(2,1)} %get-tuple-element.46), channel_id=1, source_target_pairs={{0,0},{1,16},{4,4},{5,20},{8,8},{9,24},{12,12},{13,28},{16,1},{17,... | collective-permute-start | bytes 1216520 | tf_op jit(solution)/shard_map/ppermute | solution.py:454
  66.7 3.7 %reshape.314 = bf16[64,96,128]{2,1,0:T(8,128)(2,1)} reshape(bf16[192,4096]{1,0:T(8,128)(2,1)} %convolution_convert_fusion) | data formatting | bytes 3145728 | tf_op jit(solution)/shard_map/reshape | solution.py:477
  70.5 3.5 %constant_dynamic-slice_fusion.4 = (bf16[512,1024]{1,0:T(8,128)(2,1)S(1)}, bf16[512,1024]{1,0:T(8,128)(2,1)}, bf16[512,1024]{1,0:T(8,128)(2,1)}) fusion(bf16[512,4096]{1,0:T(8,128)(2,1)} %param.20, s32[]{:T(128)S(6)} %select_n.79, s32[]{:T(128)S(6)} %select_n.77, s32[]{:T(128)S(6)} %select_n.76), kind=kLoop, calls=%fused_computation.72 | loop fusion | bytes 6291468 | tf_op jit(solution)/shard_map/dynamic_slice | solution.py:396
  74.0 8.7 %collective-permute-done.9.refs_2_ = bf16[528,384]{1,0:T(8,128)(2,1)S(1)} collective-permute-done((bf16[528,384]{1,0:T(8,128)(2,1)}, bf16[528,384]{1,0:T(8,128)(2,1)S(1)}, u32[]{:S(2)}, u32[]{:S(2)}) %collective-permute-start.9) | collective-permute-done | bytes 405536 | tf_op jit(solution)/shard_map/ppermute | solution.py:454
  82.6 5.6 %collective-permute-done.8.refs_1_ = bf16[528,384]{1,0:T(8,128)(2,1)S(1)} collective-permute-done((bf16[528,384]{1,0:T(8,128)(2,1)}, bf16[528,384]{1,0:T(8,128)(2,1)S(1)}, u32[]{:S(2)}, u32[]{:S(2)}) %collective-permute-start.8) | collective-permute-done | bytes 405536 | tf_op jit(solution)/shard_map/ppermute | solution.py:454
  91.2 2.4 %collective-permute-start.12 = (bf16[224,256]{1,0:T(8,128)(2,1)S(1)}, bf16[224,256]{1,0:T(8,128)(2,1)S(1)}, u32[]{:S(2)}, u32[]{:S(2)}) collective-permute-start(bf16[224,256]{1,0:T(8,128)(2,1)S(1)} %fusion.3), channel_id=1, source_target_pairs={{1,0},{32,1},{33,32},{64,33},{65,64},{96,65},{97,96},{128,97},{129... | collective-permute-start | bytes 344072 | tf_op jit(solution)/shard_map/ppermute | solution.py:488
  94.3 3.0 %collective-permute-done.12.refs_5_ = bf16[224,256]{1,0:T(8,128)(2,1)S(1)} collective-permute-done((bf16[224,256]{1,0:T(8,128)(2,1)S(1)}, bf16[224,256]{1,0:T(8,128)(2,1)S(1)}, u32[]{:S(2)}, u32[]{:S(2)}) %collective-permute-start.12) | collective-permute-done | bytes 114720 | tf_op jit(solution)/shard_map/ppermute | solution.py:488
  97.9 14.4 %all-to-all-start = ((bf16[64,96,128]{2,1,0:T(8,128)(2,1)}), bf16[64,96,128]{2,1,0:T(8,128)(2,1)S(1)}, u32[]{:S(2)}, u32[]{:S(2)}) async-start(bf16[64,96,128]{2,1,0:T(8,128)(2,1)} %reshape.314), calls=%async_computation | async-start | bytes 3145728 | tf_op jit(solution)/shard_map/all_to_all | solution.py:527
  126.0 26.3 %shard_map.160 = bf16[3072,128]{1,0:T(8,128)(2,1)S(1)} custom-call(s32[65]{0:T(128)S(1)} %select_reduce_fusion.1.off, s32[512]{0:T(512)S(1)} %add_bitcast_fusion.tgt, s32[1]{0:T(128)} %bitcast.33.zp, bf16[528,384]{1,0:T(8,128)(2,1)S(1)} %copy-done.15, bf16[528,384]{1,0:T(8,128)(2,1)S(1)} %copy-done.13, bf16[528,384]{1,0:T(8,128)(2,1)S(1)} %copy-done.11, ...), custom_call_target="tpu_custom_call" | custom-call | flops 7516192768 | bytes 8388608 | tf_op jit(solution)/shard_map/pallas_call | solution.py:223
  154.8 35.2 %all_to_all.10 = bf16[64,48,128]{2,1,0:T(8,128)(2,1)S(1)} all-to-all(bf16[64,48,128]{2,1,0:T(8,128)(2,1)S(1)} %bitcast.77), channel_id=1, replica_groups=mesh['xh'=2,'y'=4,'zh'=2,'zp'=4,'xl'=2,'c'=2] {'xh','y','zh','zp'}, dimensions={0} | all-to-all | bytes 1572864 | tf_op jit(solution)/shard_map/all_to_all | solution.py:532
  190.0 2.7 %collective-permute-start.17 = (bf16[3072,128]{1,0:T(8,128)(2,1)S(1)}, bf16[3072,128]{1,0:T(8,128)(2,1)S(1)}, u32[]{:S(2)}, u32[]{:S(2)}) collective-permute-start(bf16[3072,128]{1,0:T(8,128)(2,1)S(1)} %bitcast.74), channel_id=1, source_target_pairs={{0,1},{1,0},{2,3},{3,2},{4,5},{5,4},{6,7},{7,6},{8,9},{9,8},{10,11... | collective-permute-start | bytes 2359304 | tf_op jit(solution)/shard_map/ppermute | solution.py:359
  194.6 4.9 %shard_map.161.base = f32[768,1024]{1,0:T(8,128)S(1)} custom-call(s32[1]{0:T(128)} %bitcast.core, bf16[3072,128]{1,0:T(8,128)(2,1)S(1)} %bitcast.76, bf16[3072,128]{1,0:T(8,128)(2,1)S(1)} %collective-permute-done.17.a1, bf16[512,1024]{1,0:T(8,128)(2,1)S(1)} %get-tuple-element.34.w0, bf16[512,1024]{1,0:T(8,128)(2,1)S(1)} %copy-done.6, ...), custom_call_target="tpu_custom_call" | custom-call | flops 1610612736 | bytes 10485760 | tf_op jit(solution)/shard_map/pallas_call | solution.py:338
  199.5 12.3 %collective-permute-done.16.a0 = bf16[3072,128]{1,0:T(8,128)(2,1)S(1)} collective-permute-done((bf16[3072,128]{1,0:T(8,128)(2,1)S(1)}, bf16[3072,128]{1,0:T(8,128)(2,1)S(1)}, u32[]{:S(2)}, u32[]{:S(2)}) %collective-permute-start.16) | collective-permute-done | bytes 786464 | tf_op jit(solution)/shard_map/ppermute | solution.py:359
  214.6 7.0 %shard_map.162 = bf16[192,4096]{1,0:T(8,128)(2,1)} custom-call(s32[1]{0:T(128)} %bitcast.core, bf16[3072,128]{1,0:T(8,128)(2,1)S(1)} %collective-permute-done.16.a0, bf16[3072,128]{1,0:T(8,128)(2,1)S(1)} %collective-permute-done.18.a1, bf16[512,1024]{1,0:T(8,128)(2,1)S(1)} %copy-done.2, bf16[512,1024]{1,0:T(8,128)(2,1)S(1)} %copy-done.4, ...), custom_call_target="tpu_custom_call" | custom-call | flops 1610612736 | bytes 10485760 | tf_op jit(solution)/shard_map/pallas_call | solution.py:338
  (162 shorter events, 43.3 us)
Async XLA Ops:
  7.2 105.2 %all-gather.2.cloned.1.call-start = ((), (), s32[]{:S(2)}) async-start(), calls=%async_computation.2 | async-start | bytes 1966080 | tf_op jit(solution)/shard_map/all_gather | solution.py:464
  8.9 16.2 %collective-permute-start = (s32[256]{0:T(256)S(1)}, s32[256]{0:T(256)S(1)}, u32[]{:S(2)}, u32[]{:S(2)}) collective-permute-start(s32[256]{0:T(256)S(1)} %slice.109), channel_id=1, source_target_pairs={{0,4},{4,8},{8,12},{12,16},{16,20},{20,24},{24,28},{28,32},{32,36}... | collective-permute-start | bytes 3080 | tf_op jit(solution)/shard_map/ppermute | solution.py:401
  14.6 31.9 %collective-permute-start.5 = (bf16[512,1024]{1,0:T(8,128)(2,1)S(1)}, bf16[512,1024]{1,0:T(8,128)(2,1)S(1)}, u32[]{:S(2)}, u32[]{:S(2)}) collective-permute-start(bf16[512,1024]{1,0:T(8,128)(2,1)S(1)} %constant_dynamic-slice_fusion.11), channel_id=1, source_target_pairs={{0,2},{1,3},{2,0},{3,1},{4,6},{5,7},{6,4},{7,5},{8,10},{9,11},{10,... | collective-permute-start | bytes 3145736 | tf_op jit(solution)/shard_map/ppermute | solution.py:359
  26.0 19.6 %collective-permute-start.1 = (bf16[96,256]{1,0:T(8,128)(2,1)S(1)}, bf16[96,256]{1,0:T(8,128)(2,1)S(1)}, u32[]{:S(2)}, u32[]{:S(2)}) collective-permute-start(bf16[96,256]{1,0:T(8,128)(2,1)S(1)} %get-tuple-element.55), channel_id=1, source_target_pairs={{0,0},{1,16},{4,4},{5,20},{8,8},{9,24},{12,12},{13,28},{16,1},{17,... | collective-permute-start | bytes 147464 | tf_op jit(solution)/shard_map/ppermute | solution.py:454
  35.0 10.5 %collective-permute-start.4 = (bf16[96,256]{1,0:T(8,128)(2,1)S(1)}, bf16[96,256]{1,0:T(8,128)(2,1)S(1)}, u32[]{:S(2)}, u32[]{:S(2)}) collective-permute-start(bf16[96,256]{1,0:T(8,128)(2,1)S(1)} %get-tuple-element.56), channel_id=1, source_target_pairs={{0,12},{1,28},{4,8},{5,24},{8,4},{9,20},{12,0},{13,16},{16,13},{17... | collective-permute-start | bytes 147464 | tf_op jit(solution)/shard_map/ppermute | solution.py:454
  36.2 9.3 %collective-permute-start.3 = (bf16[96,256]{1,0:T(8,128)(2,1)S(1)}, bf16[96,256]{1,0:T(8,128)(2,1)S(1)}, u32[]{:S(2)}, u32[]{:S(2)}) collective-permute-start(bf16[96,256]{1,0:T(8,128)(2,1)S(1)} %get-tuple-element.57), channel_id=1, source_target_pairs={{0,8},{1,24},{4,12},{5,28},{8,0},{9,16},{12,4},{13,20},{16,9},{17,... | collective-permute-start | bytes 147464 | tf_op jit(solution)/shard_map/ppermute | solution.py:454
  39.4 7.0 %collective-permute-start.2 = (bf16[96,256]{1,0:T(8,128)(2,1)S(1)}, bf16[96,256]{1,0:T(8,128)(2,1)S(1)}, u32[]{:S(2)}, u32[]{:S(2)}) collective-permute-start(bf16[96,256]{1,0:T(8,128)(2,1)S(1)} %get-tuple-element.58), channel_id=1, source_target_pairs={{0,4},{1,20},{4,0},{5,16},{8,12},{9,28},{12,8},{13,24},{16,5},{17,... | collective-permute-start | bytes 147464 | tf_op jit(solution)/shard_map/ppermute | solution.py:454
  46.5 16.0 %collective-permute-start.6 = (bf16[384,256]{1,0:T(8,128)(2,1)S(1)}, bf16[384,256]{1,0:T(8,128)(2,1)S(1)}, u32[]{:S(2)}, u32[]{:S(2)}) collective-permute-start(bf16[384,256]{1,0:T(8,128)(2,1)S(1)} %pad_maximum_fusion.2), channel_id=1, source_target_pairs={{0,128},{128,0},{1,129},{129,1},{2,130},{130,2},{3,131},{131,3},{4... | collective-permute-start | bytes 589832 | tf_op jit(solution)/shard_map/ppermute | solution.py:359
  51.6 22.4 %collective-permute-start.10 = (bf16[528,384]{1,0:T(8,128)(2,1)}, bf16[528,384]{1,0:T(8,128)(2,1)S(1)}, u32[]{:S(2)}, u32[]{:S(2)}) collective-permute-start(bf16[528,384]{1,0:T(8,128)(2,1)} %get-tuple-element.43), channel_id=1, source_target_pairs={{0,12},{1,28},{4,8},{5,24},{8,4},{9,20},{12,0},{13,16},{16,13},{17... | collective-permute-start | bytes 1216520 | tf_op jit(solution)/shard_map/ppermute | solution.py:454
  52.5 30.1 %collective-permute-start.9 = (bf16[528,384]{1,0:T(8,128)(2,1)}, bf16[528,384]{1,0:T(8,128)(2,1)S(1)}, u32[]{:S(2)}, u32[]{:S(2)}) collective-permute-start(bf16[528,384]{1,0:T(8,128)(2,1)} %get-tuple-element.44), channel_id=1, source_target_pairs={{0,8},{1,24},{4,12},{5,28},{8,0},{9,16},{12,4},{13,20},{16,9},{17,... | collective-permute-start | bytes 1216520 | tf_op jit(solution)/shard_map/ppermute | solution.py:454
  55.0 33.2 %collective-permute-start.8 = (bf16[528,384]{1,0:T(8,128)(2,1)}, bf16[528,384]{1,0:T(8,128)(2,1)S(1)}, u32[]{:S(2)}, u32[]{:S(2)}) collective-permute-start(bf16[528,384]{1,0:T(8,128)(2,1)} %get-tuple-element.45), channel_id=1, source_target_pairs={{0,4},{1,20},{4,0},{5,16},{8,12},{9,28},{12,8},{13,24},{16,5},{17,... | collective-permute-start | bytes 1216520 | tf_op jit(solution)/shard_map/ppermute | solution.py:454
  57.8 30.4 %collective-permute-start.7 = (bf16[528,384]{1,0:T(8,128)(2,1)}, bf16[528,384]{1,0:T(8,128)(2,1)S(1)}, u32[]{:S(2)}, u32[]{:S(2)}) collective-permute-start(bf16[528,384]{1,0:T(8,128)(2,1)} %get-tuple-element.46), channel_id=1, source_target_pairs={{0,0},{1,16},{4,4},{5,20},{8,8},{9,24},{12,12},{13,28},{16,1},{17,... | collective-permute-start | bytes 1216520 | tf_op jit(solution)/shard_map/ppermute | solution.py:454
  74.0 38.7 %copy-start.8 = (bf16[528,384]{1,0:T(8,128)(2,1)}, bf16[528,384]{1,0:T(8,128)(2,1)S(1)}, u32[]{:S(2)}) copy-start(bf16[528,384]{1,0:T(8,128)(2,1)S(1)} %collective-permute-done.10.refs_3_) | copy-start | bytes 1216516
  89.1 4.5 %collective-permute-start.11 = (bf16[224,256]{1,0:T(8,128)(2,1)S(1)}, bf16[224,256]{1,0:T(8,128)(2,1)S(1)}, u32[]{:S(2)}, u32[]{:S(2)}) collective-permute-start(bf16[224,256]{1,0:T(8,128)(2,1)S(1)} %fusion.2), channel_id=1, source_target_pairs={{0,1},{1,32},{32,33},{33,64},{64,65},{65,96},{96,97},{97,128},{128... | collective-permute-start | bytes 344072 | tf_op jit(solution)/shard_map/ppermute | solution.py:488
  91.2 6.1 %collective-permute-start.12 = (bf16[224,256]{1,0:T(8,128)(2,1)S(1)}, bf16[224,256]{1,0:T(8,128)(2,1)S(1)}, u32[]{:S(2)}, u32[]{:S(2)}) collective-permute-start(bf16[224,256]{1,0:T(8,128)(2,1)S(1)} %fusion.3), channel_id=1, source_target_pairs={{1,0},{32,1},{33,32},{64,33},{65,64},{96,65},{97,96},{128,97},{129... | collective-permute-start | bytes 344072 | tf_op jit(solution)/shard_map/ppermute | solution.py:488
  97.9 56.8 %all-to-all-start = ((bf16[64,96,128]{2,1,0:T(8,128)(2,1)}), bf16[64,96,128]{2,1,0:T(8,128)(2,1)S(1)}, u32[]{:S(2)}, u32[]{:S(2)}) async-start(bf16[64,96,128]{2,1,0:T(8,128)(2,1)} %reshape.314), calls=%async_computation | async-start | bytes 3145728 | tf_op jit(solution)/shard_map/all_to_all | solution.py:527
  112.4 5.6 %collective-permute-start.13 = (bf16[3072,256]{1,0:T(8,128)(2,1)}, bf16[3072,256]{1,0:T(8,128)(2,1)S(1)}, u32[]{:S(2)}, u32[]{:S(2)}) collective-permute-start(bf16[3072,256]{1,0:T(8,128)(2,1)} %all-gather.2.cloned.1.call-done.refs_6_), channel_id=1, source_target_pairs={{0,1},{1,0},{2,3},{3,2},{4,5},{5,4},{6,7},{7,6},{8,9},{9,8},{10,11... | collective-permute-start | bytes 4718600 | tf_op jit(solution)/shard_map/ppermute | solution.py:359
  115.1 37.3 %collective-permute-start.14 = (bf16[512,1024]{1,0:T(8,128)(2,1)}, bf16[512,1024]{1,0:T(8,128)(2,1)S(1)}, u32[]{:S(2)}, u32[]{:S(2)}) collective-permute-start(bf16[512,1024]{1,0:T(8,128)(2,1)} %get-tuple-element.31), channel_id=1, source_target_pairs={{0,1},{1,0},{2,3},{3,2},{4,5},{5,4},{6,7},{7,6},{8,9},{9,8},{10,11... | collective-permute-start | bytes 3145736 | tf_op jit(solution)/shard_map/ppermute | solution.py:359
  115.6 38.2 %collective-permute-start.15 = (bf16[512,1024]{1,0:T(8,128)(2,1)}, bf16[512,1024]{1,0:T(8,128)(2,1)S(1)}, u32[]{:S(2)}, u32[]{:S(2)}) collective-permute-start(bf16[512,1024]{1,0:T(8,128)(2,1)} %get-tuple-element.32), channel_id=1, source_target_pairs={{0,3},{1,2},{2,1},{3,0},{4,7},{5,6},{6,5},{7,4},{8,11},{9,10},{10,... | collective-permute-start | bytes 3145736 | tf_op jit(solution)/shard_map/ppermute | solution.py:359
  152.4 42.2 %copy-start.16 = (f32[1024]{0:T(1024)S(1)}, f32[1024]{0:T(1024)}, u32[]{:S(2)}) copy-start(f32[1024]{0:T(1024)} %param.19) | copy-start | bytes 12292
  154.8 39.8 %copy-start.6 = (bf16[512,1024]{1,0:T(8,128)(2,1)S(1)}, bf16[512,1024]{1,0:T(8,128)(2,1)}, u32[]{:S(2)}) copy-start(bf16[512,1024]{1,0:T(8,128)(2,1)} %copy-done.5) | copy-start | bytes 3145732
  190.0 4.6 %collective-permute-start.17 = (bf16[3072,128]{1,0:T(8,128)(2,1)S(1)}, bf16[3072,128]{1,0:T(8,128)(2,1)S(1)}, u32[]{:S(2)}, u32[]{:S(2)}) collective-permute-start(bf16[3072,128]{1,0:T(8,128)(2,1)S(1)} %bitcast.74), channel_id=1, source_target_pairs={{0,1},{1,0},{2,3},{3,2},{4,5},{5,4},{6,7},{7,6},{8,9},{9,8},{10,11... | collective-permute-start | bytes 2359304 | tf_op jit(solution)/shard_map/ppermute | solution.py:359
  192.7 19.2 %collective-permute-start.16 = (bf16[3072,128]{1,0:T(8,128)(2,1)S(1)}, bf16[3072,128]{1,0:T(8,128)(2,1)S(1)}, u32[]{:S(2)}, u32[]{:S(2)}) collective-permute-start(bf16[3072,128]{1,0:T(8,128)(2,1)S(1)} %bitcast.75), channel_id=1, source_target_pairs={{0,2},{1,3},{2,0},{3,1},{4,6},{5,7},{6,4},{7,5},{8,10},{9,11},{10,... | collective-permute-start | bytes 2359304 | tf_op jit(solution)/shard_map/ppermute | solution.py:359
  211.9 2.7 %collective-permute-start.18 = (bf16[3072,128]{1,0:T(8,128)(2,1)S(1)}, bf16[3072,128]{1,0:T(8,128)(2,1)S(1)}, u32[]{:S(2)}, u32[]{:S(2)}) collective-permute-start(bf16[3072,128]{1,0:T(8,128)(2,1)S(1)} %collective-permute-done.16.a0), channel_id=1, source_target_pairs={{0,1},{1,0},{2,3},{3,2},{4,5},{5,4},{6,7},{7,6},{8,9},{9,8},{10,11... | collective-permute-start | bytes 2359304 | tf_op jit(solution)/shard_map/ppermute | solution.py:359
  (23 other events, 141.0 us)
Sparse Core Ops, SparseCore 0:
  63.4 26.6 all-gather.1

commit v10 on v9

--- a/solution.py
+++ b/solution.py
@@ -65,10 +65,10 @@
 
 def attention_kernel(off, tgt, zp, *refs):
     chunks = 4
-    ys = refs[:chunks]
+    given = refs[:chunks]
     left, right = refs[chunks : chunks + 2]
-    pieces = refs[chunks + 2 : -14]
-    out, kc, vc, qs, kw, vw, ob, send, mx, ac, idcol, gathered, ids, sems = refs[-14:]
+    pieces = refs[chunks + 2 : -15]
+    out, kc, vc, qs, kw, vw, ob, send, mx, ac, idcol, gathered, ids, ybuf, sems = refs[-15:]
     i = pl.program_id(0)
     sources = off.shape[0] - 1
     slot_rows = LIVE_MOST * BLK
@@ -83,11 +83,17 @@
             to = gathered.at[pl.ds(row, piece.shape[0])]
             copies.append(pltpu.make_async_copy(piece, to, sems.at[n]))
             row += piece.shape[0]
-        for copy in copies:
+        loads = []
+        for n, y in enumerate(given):
+            loads.append(pltpu.make_async_copy(y, ybuf.at[n], sems.at[len(pieces) + n]))
+        for copy in loads + copies:
             copy.start()
         vc[:, HD:] = jnp.ones((vc.shape[0], HD), bf16)
         vw[:, HD:] = jnp.ones((vw.shape[0], HD), bf16)
-        for k, y in enumerate(ys):
+        for copy in loads:
+            copy.wait()
+        for k in range(chunks):
+            y = ybuf.at[k]
             chunk = zp[0] ^ k
             dst = pl.ds(pl.multiple_of(chunk * TOK, TOK), TOK)
             qs[dst, :] = y[:TOK, :HD]
@@ -226,7 +232,8 @@
         grid_spec=pltpu.PrefetchScalarGridSpec(
             num_scalar_prefetch=3,
             grid=(chunks,),
-            in_specs=[whole] * (chunks + 2)
+            in_specs=[pl.BlockSpec(memory_space=pl.ANY)] * chunks
+            + [whole] * 2
             + [pl.BlockSpec(memory_space=pl.ANY)] * len(pieces),
             out_specs=whole,
             scratch_shapes=[
@@ -242,7 +249,8 @@
                 pltpu.VMEM((TOK, 128), f32),
                 pltpu.VMEM((cache_most, 2 * HD), bf16),
                 pltpu.VMEM((1, chunks * TOK + 2 * PAD), f32),
-                pltpu.SemaphoreType.DMA((len(pieces),)),
+                pltpu.VMEM((chunks, *ys[0].shape), bf16),
+                pltpu.SemaphoreType.DMA((len(pieces) + chunks,)),
             ],
         ),
         compiler_params=pltpu.CompilerParams(

time: 230 us -> 231 us (level)
  transfers between devices with their start and end apart: 21 -> 21, of which waited for: 8 -> 7; matrix products, arithmetic and copies ran while one was open for 13% -> 13% of each run, Pallas kernels for 16% -> 16%
where the time goes in v10:
time: 231 us; the launch traced here: 229 us
  starting transfers between devices  56.6 us (25%)
  Pallas kernels  44.8 us (19%)
  blocking collectives  35.7 us (15%)
  waiting for transfers between devices  34.4 us (15%)
  local copies, waits for them, and re-layouts  29.2 us (13%)
  between operations  15.3 us (7%)
  other arithmetic  8.95 us (4%)
  matrix products  4.53 us (2%)
    all_to_all x1, blocking collectives, shards(): lax.all_to_all(sent.reshape(n_seq, heads * CAP * 4, HD), SEQ, split_axis=...  35.7 us
    pallas_call x1, Pallas kernels, attend(): pl.pallas_call(attention_kernel, out_shape=jax.ShapeDtypeStruct((slots *...  27.3 us
    ppermute x8, starting transfers between devices, spread(): return lax.ppermute(part, ('zh', 'zp', 'c'), pairs)  24.7 us
    ppermute x8, waiting for transfers between devices, swap(): return lax.ppermute(x, axis, [(i, i ^ k) for i in range(n)])  16.2 us
    ppermute x8, waiting for transfers between devices, spread(): return lax.ppermute(part, ('zh', 'zp', 'c'), pairs)  15.1 us
    all_to_all x1, starting transfers between devices, shards(): lax.all_to_all(tie(res, left, right), SEQ, split_axis=0, concat_axis=0, t...  14.4 us
    unnamed x54, local copies, waits for them, and re-layouts  12.2 us
    pallas_call x2, Pallas kernels, project(): pl.pallas_call(near_kernel if near else far_kernel, out_shape=out_shape,...  11.9 us
  transfers between devices with their start and end apart: 21, of which 7 were waited for; matrix products, arithmetic and copies ran while one was open for 13% of the time, Pallas kernels for 16%

profile of v10, /device:TPU:1, one launch (start us, length us, event | category | flops | bytes accessed | tf_op | source)
XLA Modules:
  0.0 229.4 jit_solution(1977289073205995796)
XLA Ops:
  8.9 4.4 %collective-permute-start = (s32[256]{0:T(256)S(1)}, s32[256]{0:T(256)S(1)}, u32[]{:S(2)}, u32[]{:S(2)}) collective-permute-start(s32[256]{0:T(256)S(1)} %slice.109), channel_id=1, source_target_pairs={{0,4},{4,8},{8,12},{12,16},{16,20},{20,24},{24,28},{28,32},{32,36}... | collective-permute-start | bytes 3080 | tf_op jit(solution)/shard_map/ppermute | solution.py:409
  17.6 2.8 %fusion.34 = f32[16,512]{1,0:T(8,128)S(1)} fusion(bf16[16,4096]{1,0:T(8,128)(2,1)S(1)} %copy-done, bf16[4096,512]{1,0:T(8,128)(2,1)} %param.27), kind=kOutput, calls=%fused_computation.130 | convolution fusion | flops 67108864 | bytes 4358144 | tf_op jit(solution)/shard_map/dot_general | solution.py:434
  22.7 2.3 %shard_map.158 = bf16[4,96,256]{2,1,0:T(8,128)(2,1)} custom-call(s32[7]{0:T(128)} %pad_add_fusion.1.idx, bf16[128,512]{1,0:T(8,128)(2,1)} %copy-done.23, bf16[128,512]{1,0:T(8,128)(2,1)} %v_ref.2), custom_call_target="tpu_custom_call" | custom-call | tf_op jit(solution)/shard_map/pallas_call | solution.py:447
  26.0 9.0 %collective-permute-start.1 = (bf16[96,256]{1,0:T(8,128)(2,1)S(1)}, bf16[96,256]{1,0:T(8,128)(2,1)S(1)}, u32[]{:S(2)}, u32[]{:S(2)}) collective-permute-start(bf16[96,256]{1,0:T(8,128)(2,1)S(1)} %get-tuple-element.55), channel_id=1, source_target_pairs={{0,0},{1,16},{4,4},{5,20},{8,8},{9,24},{12,12},{13,28},{16,1},{17,... | collective-permute-start | bytes 147464 | tf_op jit(solution)/shard_map/ppermute | solution.py:462
  36.2 3.2 %collective-permute-start.3 = (bf16[96,256]{1,0:T(8,128)(2,1)S(1)}, bf16[96,256]{1,0:T(8,128)(2,1)S(1)}, u32[]{:S(2)}, u32[]{:S(2)}) collective-permute-start(bf16[96,256]{1,0:T(8,128)(2,1)S(1)} %get-tuple-element.57), channel_id=1, source_target_pairs={{0,8},{1,24},{4,12},{5,28},{8,0},{9,16},{12,4},{13,20},{16,9},{17,... | collective-permute-start | bytes 147464 | tf_op jit(solution)/shard_map/ppermute | solution.py:462
  42.3 3.3 %shard_map.159 = bf16[4,528,384]{2,1,0:T(8,128)(2,1)} custom-call(bf16[512,512]{1,0:T(8,128)(2,1)} %q_ref.1, bf16[512,512]{1,0:T(8,128)(2,1)} %k_ref.1, bf16[512,512]{1,0:T(8,128)(2,1)} %v_ref.3, f32[512,128]{1,0:T(8,128)} %get-tuple-element.72.c_ref, f32[512,128]{1,0:T(8,128)} %get-tuple-element.73.s_ref, bf16[16,384]{1,0:T(8,128)(2,1)} %reshape.311.extra_ref), custom_call_target="tpu_custom_call" | custom-call | tf_op jit(solution)/shard_map/pallas_call | solution.py:418
  46.5 2.5 %collective-permute-start.6 = (bf16[384,256]{1,0:T(8,128)(2,1)S(1)}, bf16[384,256]{1,0:T(8,128)(2,1)S(1)}, u32[]{:S(2)}, u32[]{:S(2)}) collective-permute-start(bf16[384,256]{1,0:T(8,128)(2,1)S(1)} %pad_maximum_fusion.2), channel_id=1, source_target_pairs={{0,128},{128,0},{1,129},{129,1},{2,130},{130,2},{3,131},{131,3},{4... | collective-permute-start | bytes 589832 | tf_op jit(solution)/shard_map/ppermute | solution.py:367
  49.0 2.6 %dynamic-slice_bitcast_fusion = (bf16[528,384]{1,0:T(8,128)(2,1)}, bf16[528,384]{1,0:T(8,128)(2,1)}, bf16[528,384]{1,0:T(8,128)(2,1)}, bf16[528,384]{1,0:T(8,128)(2,1)}) fusion(bf16[4,528,384]{2,1,0:T(8,128)(2,1)} %shard_map.159, s32[]{:T(128)S(6)} %select_n.73, s32[]{:T(128)S(6)} %select_n.72, s32[]{:T(128)S(6)} %select_n.71, s32[]{:T(128)S(6)} %select_n.70), kind=kLoop, calls=%fused_computation.10 | loop fusion | bytes 3244048 | tf_op jit(solution)/shard_map/jit(dynamic_index_in_dim)/squeeze | solution.py:461
  52.5 2.4 %collective-permute-start.9 = (bf16[528,384]{1,0:T(8,128)(2,1)}, bf16[528,384]{1,0:T(8,128)(2,1)S(1)}, u32[]{:S(2)}, u32[]{:S(2)}) collective-permute-start(bf16[528,384]{1,0:T(8,128)(2,1)} %get-tuple-element.44), channel_id=1, source_target_pairs={{0,8},{1,24},{4,12},{5,28},{8,0},{9,16},{12,4},{13,20},{16,9},{17,... | collective-permute-start | bytes 1216520 | tf_op jit(solution)/shard_map/ppermute | solution.py:462
  55.0 2.9 %collective-permute-start.8 = (bf16[528,384]{1,0:T(8,128)(2,1)}, bf16[528,384]{1,0:T(8,128)(2,1)S(1)}, u32[]{:S(2)}, u32[]{:S(2)}) collective-permute-start(bf16[528,384]{1,0:T(8,128)(2,1)} %get-tuple-element.45), channel_id=1, source_target_pairs={{0,4},{1,20},{4,0},{5,16},{8,12},{9,28},{12,8},{13,24},{16,5},{17,... | collective-permute-start | bytes 1216520 | tf_op jit(solution)/shard_map/ppermute | solution.py:462
  57.8 4.6 %collective-permute-start.7 = (bf16[528,384]{1,0:T(8,128)(2,1)}, bf16[528,384]{1,0:T(8,128)(2,1)S(1)}, u32[]{:S(2)}, u32[]{:S(2)}) collective-permute-start(bf16[528,384]{1,0:T(8,128)(2,1)} %get-tuple-element.46), channel_id=1, source_target_pairs={{0,0},{1,16},{4,4},{5,20},{8,8},{9,24},{12,12},{13,28},{16,1},{17,... | collective-permute-start | bytes 1216520 | tf_op jit(solution)/shard_map/ppermute | solution.py:462
  66.7 3.7 %reshape.314 = bf16[64,96,128]{2,1,0:T(8,128)(2,1)} reshape(bf16[192,4096]{1,0:T(8,128)(2,1)} %convolution_convert_fusion) | data formatting | bytes 3145728 | tf_op jit(solution)/shard_map/reshape | solution.py:485
  70.5 3.5 %constant_dynamic-slice_fusion.4 = (bf16[512,1024]{1,0:T(8,128)(2,1)S(1)}, bf16[512,1024]{1,0:T(8,128)(2,1)}, bf16[512,1024]{1,0:T(8,128)(2,1)}) fusion(bf16[512,4096]{1,0:T(8,128)(2,1)} %param.20, s32[]{:T(128)S(6)} %select_n.79, s32[]{:T(128)S(6)} %select_n.77, s32[]{:T(128)S(6)} %select_n.76), kind=kLoop, calls=%fused_computation.72 | loop fusion | bytes 6291468 | tf_op jit(solution)/shard_map/dynamic_slice | solution.py:404
  74.0 8.7 %collective-permute-done.9.refs_2_ = bf16[528,384]{1,0:T(8,128)(2,1)S(1)} collective-permute-done((bf16[528,384]{1,0:T(8,128)(2,1)}, bf16[528,384]{1,0:T(8,128)(2,1)S(1)}, u32[]{:S(2)}, u32[]{:S(2)}) %collective-permute-start.9) | collective-permute-done | bytes 405536 | tf_op jit(solution)/shard_map/ppermute | solution.py:462
  82.6 5.6 %collective-permute-done.8.refs_1_ = bf16[528,384]{1,0:T(8,128)(2,1)S(1)} collective-permute-done((bf16[528,384]{1,0:T(8,128)(2,1)}, bf16[528,384]{1,0:T(8,128)(2,1)S(1)}, u32[]{:S(2)}, u32[]{:S(2)}) %collective-permute-start.8) | collective-permute-done | bytes 405536 | tf_op jit(solution)/shard_map/ppermute | solution.py:462
  91.2 2.4 %collective-permute-start.12 = (bf16[224,256]{1,0:T(8,128)(2,1)S(1)}, bf16[224,256]{1,0:T(8,128)(2,1)S(1)}, u32[]{:S(2)}, u32[]{:S(2)}) collective-permute-start(bf16[224,256]{1,0:T(8,128)(2,1)S(1)} %fusion.3), channel_id=1, source_target_pairs={{1,0},{32,1},{33,32},{64,33},{65,64},{96,65},{97,96},{128,97},{129... | collective-permute-start | bytes 344072 | tf_op jit(solution)/shard_map/ppermute | solution.py:496
  94.3 3.0 %collective-permute-done.12.refs_5_ = bf16[224,256]{1,0:T(8,128)(2,1)S(1)} collective-permute-done((bf16[224,256]{1,0:T(8,128)(2,1)S(1)}, bf16[224,256]{1,0:T(8,128)(2,1)S(1)}, u32[]{:S(2)}, u32[]{:S(2)}) %collective-permute-start.12) | collective-permute-done | bytes 114720 | tf_op jit(solution)/shard_map/ppermute | solution.py:496
  97.9 14.4 %all-to-all-start = ((bf16[64,96,128]{2,1,0:T(8,128)(2,1)}), bf16[64,96,128]{2,1,0:T(8,128)(2,1)S(1)}, u32[]{:S(2)}, u32[]{:S(2)}) async-start(bf16[64,96,128]{2,1,0:T(8,128)(2,1)} %reshape.314), calls=%async_computation | async-start | bytes 3145728 | tf_op jit(solution)/shard_map/all_to_all | solution.py:535
  126.0 27.3 %shard_map.160 = bf16[3072,128]{1,0:T(8,128)(2,1)S(1)} custom-call(s32[65]{0:T(128)S(1)} %select_reduce_fusion.1.off, s32[512]{0:T(512)S(1)} %add_bitcast_fusion.tgt, s32[1]{0:T(128)} %bitcast.33.zp, bf16[528,384]{1,0:T(8,128)(2,1)S(1)} %copy-done.15, bf16[528,384]{1,0:T(8,128)(2,1)S(1)} %copy-done.13, bf16[528,384]{1,0:T(8,128)(2,1)S(1)} %copy-done.11, ...), custom_call_target="tpu_custom_call" | custom-call | flops 7516192768 | bytes 8388608 | tf_op jit(solution)/shard_map/pallas_call | solution.py:229
  155.3 35.7 %all_to_all.10 = bf16[64,48,128]{2,1,0:T(8,128)(2,1)S(1)} all-to-all(bf16[64,48,128]{2,1,0:T(8,128)(2,1)S(1)} %bitcast.77), channel_id=1, replica_groups=mesh['xh'=2,'y'=4,'zh'=2,'zp'=4,'xl'=2,'c'=2] {'xh','y','zh','zp'}, dimensions={0} | all-to-all | bytes 1572864 | tf_op jit(solution)/shard_map/all_to_all | solution.py:540
  191.0 2.7 %collective-permute-start.17 = (bf16[3072,128]{1,0:T(8,128)(2,1)S(1)}, bf16[3072,128]{1,0:T(8,128)(2,1)S(1)}, u32[]{:S(2)}, u32[]{:S(2)}) collective-permute-start(bf16[3072,128]{1,0:T(8,128)(2,1)S(1)} %bitcast.74), channel_id=1, source_target_pairs={{0,1},{1,0},{2,3},{3,2},{4,5},{5,4},{6,7},{7,6},{8,9},{9,8},{10,11... | collective-permute-start | bytes 2359304 | tf_op jit(solution)/shard_map/ppermute | solution.py:367
  195.6 4.9 %shard_map.161.base = f32[768,1024]{1,0:T(8,128)S(1)} custom-call(s32[1]{0:T(128)} %bitcast.core, bf16[3072,128]{1,0:T(8,128)(2,1)S(1)} %bitcast.76, bf16[3072,128]{1,0:T(8,128)(2,1)S(1)} %collective-permute-done.17.a1, bf16[512,1024]{1,0:T(8,128)(2,1)S(1)} %get-tuple-element.34.w0, bf16[512,1024]{1,0:T(8,128)(2,1)S(1)} %copy-done.6, ...), custom_call_target="tpu_custom_call" | custom-call | flops 1610612736 | bytes 10485760 | tf_op jit(solution)/shard_map/pallas_call | solution.py:346
  200.5 12.3 %collective-permute-done.16.a0 = bf16[3072,128]{1,0:T(8,128)(2,1)S(1)} collective-permute-done((bf16[3072,128]{1,0:T(8,128)(2,1)S(1)}, bf16[3072,128]{1,0:T(8,128)(2,1)S(1)}, u32[]{:S(2)}, u32[]{:S(2)}) %collective-permute-start.16) | collective-permute-done | bytes 786464 | tf_op jit(solution)/shard_map/ppermute | solution.py:367
  215.5 7.0 %shard_map.162 = bf16[192,4096]{1,0:T(8,128)(2,1)} custom-call(s32[1]{0:T(128)} %bitcast.core, bf16[3072,128]{1,0:T(8,128)(2,1)S(1)} %collective-permute-done.16.a0, bf16[3072,128]{1,0:T(8,128)(2,1)S(1)} %collective-permute-done.18.a1, bf16[512,1024]{1,0:T(8,128)(2,1)S(1)} %copy-done.2, bf16[512,1024]{1,0:T(8,128)(2,1)S(1)} %copy-done.4, ...), custom_call_target="tpu_custom_call" | custom-call | flops 1610612736 | bytes 10485760 | tf_op jit(solution)/shard_map/pallas_call | solution.py:346
  (162 shorter events, 42.8 us)
Async XLA Ops:
  7.2 105.2 %all-gather.2.cloned.1.call-start = ((), (), s32[]{:S(2)}) async-start(), calls=%async_computation.2 | async-start | bytes 1966080 | tf_op jit(solution)/shard_map/all_gather | solution.py:472
  8.9 16.2 %collective-permute-start = (s32[256]{0:T(256)S(1)}, s32[256]{0:T(256)S(1)}, u32[]{:S(2)}, u32[]{:S(2)}) collective-permute-start(s32[256]{0:T(256)S(1)} %slice.109), channel_id=1, source_target_pairs={{0,4},{4,8},{8,12},{12,16},{16,20},{20,24},{24,28},{28,32},{32,36}... | collective-permute-start | bytes 3080 | tf_op jit(solution)/shard_map/ppermute | solution.py:409
  14.6 31.9 %collective-permute-start.5 = (bf16[512,1024]{1,0:T(8,128)(2,1)S(1)}, bf16[512,1024]{1,0:T(8,128)(2,1)S(1)}, u32[]{:S(2)}, u32[]{:S(2)}) collective-permute-start(bf16[512,1024]{1,0:T(8,128)(2,1)S(1)} %constant_dynamic-slice_fusion.11), channel_id=1, source_target_pairs={{0,2},{1,3},{2,0},{3,1},{4,6},{5,7},{6,4},{7,5},{8,10},{9,11},{10,... | collective-permute-start | bytes 3145736 | tf_op jit(solution)/shard_map/ppermute | solution.py:367
  26.0 19.6 %collective-permute-start.1 = (bf16[96,256]{1,0:T(8,128)(2,1)S(1)}, bf16[96,256]{1,0:T(8,128)(2,1)S(1)}, u32[]{:S(2)}, u32[]{:S(2)}) collective-permute-start(bf16[96,256]{1,0:T(8,128)(2,1)S(1)} %get-tuple-element.55), channel_id=1, source_target_pairs={{0,0},{1,16},{4,4},{5,20},{8,8},{9,24},{12,12},{13,28},{16,1},{17,... | collective-permute-start | bytes 147464 | tf_op jit(solution)/shard_map/ppermute | solution.py:462
  35.0 10.5 %collective-permute-start.4 = (bf16[96,256]{1,0:T(8,128)(2,1)S(1)}, bf16[96,256]{1,0:T(8,128)(2,1)S(1)}, u32[]{:S(2)}, u32[]{:S(2)}) collective-permute-start(bf16[96,256]{1,0:T(8,128)(2,1)S(1)} %get-tuple-element.56), channel_id=1, source_target_pairs={{0,12},{1,28},{4,8},{5,24},{8,4},{9,20},{12,0},{13,16},{16,13},{17... | collective-permute-start | bytes 147464 | tf_op jit(solution)/shard_map/ppermute | solution.py:462
  36.2 9.3 %collective-permute-start.3 = (bf16[96,256]{1,0:T(8,128)(2,1)S(1)}, bf16[96,256]{1,0:T(8,128)(2,1)S(1)}, u32[]{:S(2)}, u32[]{:S(2)}) collective-permute-start(bf16[96,256]{1,0:T(8,128)(2,1)S(1)} %get-tuple-element.57), channel_id=1, source_target_pairs={{0,8},{1,24},{4,12},{5,28},{8,0},{9,16},{12,4},{13,20},{16,9},{17,... | collective-permute-start | bytes 147464 | tf_op jit(solution)/shard_map/ppermute | solution.py:462
  39.4 7.0 %collective-permute-start.2 = (bf16[96,256]{1,0:T(8,128)(2,1)S(1)}, bf16[96,256]{1,0:T(8,128)(2,1)S(1)}, u32[]{:S(2)}, u32[]{:S(2)}) collective-permute-start(bf16[96,256]{1,0:T(8,128)(2,1)S(1)} %get-tuple-element.58), channel_id=1, source_target_pairs={{0,4},{1,20},{4,0},{5,16},{8,12},{9,28},{12,8},{13,24},{16,5},{17,... | collective-permute-start | bytes 147464 | tf_op jit(solution)/shard_map/ppermute | solution.py:462
  46.5 16.0 %collective-permute-start.6 = (bf16[384,256]{1,0:T(8,128)(2,1)S(1)}, bf16[384,256]{1,0:T(8,128)(2,1)S(1)}, u32[]{:S(2)}, u32[]{:S(2)}) collective-permute-start(bf16[384,256]{1,0:T(8,128)(2,1)S(1)} %pad_maximum_fusion.2), channel_id=1, source_target_pairs={{0,128},{128,0},{1,129},{129,1},{2,130},{130,2},{3,131},{131,3},{4... | collective-permute-start | bytes 589832 | tf_op jit(solution)/shard_map/ppermute | solution.py:367
  51.6 22.4 %collective-permute-start.10 = (bf16[528,384]{1,0:T(8,128)(2,1)}, bf16[528,384]{1,0:T(8,128)(2,1)S(1)}, u32[]{:S(2)}, u32[]{:S(2)}) collective-permute-start(bf16[528,384]{1,0:T(8,128)(2,1)} %get-tuple-element.43), channel_id=1, source_target_pairs={{0,12},{1,28},{4,8},{5,24},{8,4},{9,20},{12,0},{13,16},{16,13},{17... | collective-permute-start | bytes 1216520 | tf_op jit(solution)/shard_map/ppermute | solution.py:462
  52.5 30.1 %collective-permute-start.9 = (bf16[528,384]{1,0:T(8,128)(2,1)}, bf16[528,384]{1,0:T(8,128)(2,1)S(1)}, u32[]{:S(2)}, u32[]{:S(2)}) collective-permute-start(bf16[528,384]{1,0:T(8,128)(2,1)} %get-tuple-element.44), channel_id=1, source_target_pairs={{0,8},{1,24},{4,12},{5,28},{8,0},{9,16},{12,4},{13,20},{16,9},{17,... | collective-permute-start | bytes 1216520 | tf_op jit(solution)/shard_map/ppermute | solution.py:462
  55.0 33.2 %collective-permute-start.8 = (bf16[528,384]{1,0:T(8,128)(2,1)}, bf16[528,384]{1,0:T(8,128)(2,1)S(1)}, u32[]{:S(2)}, u32[]{:S(2)}) collective-permute-start(bf16[528,384]{1,0:T(8,128)(2,1)} %get-tuple-element.45), channel_id=1, source_target_pairs={{0,4},{1,20},{4,0},{5,16},{8,12},{9,28},{12,8},{13,24},{16,5},{17,... | collective-permute-start | bytes 1216520 | tf_op jit(solution)/shard_map/ppermute | solution.py:462
  57.8 30.4 %collective-permute-start.7 = (bf16[528,384]{1,0:T(8,128)(2,1)}, bf16[528,384]{1,0:T(8,128)(2,1)S(1)}, u32[]{:S(2)}, u32[]{:S(2)}) collective-permute-start(bf16[528,384]{1,0:T(8,128)(2,1)} %get-tuple-element.46), channel_id=1, source_target_pairs={{0,0},{1,16},{4,4},{5,20},{8,8},{9,24},{12,12},{13,28},{16,1},{17,... | collective-permute-start | bytes 1216520 | tf_op jit(solution)/shard_map/ppermute | solution.py:462
  74.0 38.7 %copy-start.8 = (bf16[528,384]{1,0:T(8,128)(2,1)}, bf16[528,384]{1,0:T(8,128)(2,1)S(1)}, u32[]{:S(2)}) copy-start(bf16[528,384]{1,0:T(8,128)(2,1)S(1)} %collective-permute-done.10.refs_3_) | copy-start | bytes 1216516
  89.1 4.5 %collective-permute-start.11 = (bf16[224,256]{1,0:T(8,128)(2,1)S(1)}, bf16[224,256]{1,0:T(8,128)(2,1)S(1)}, u32[]{:S(2)}, u32[]{:S(2)}) collective-permute-start(bf16[224,256]{1,0:T(8,128)(2,1)S(1)} %fusion.2), channel_id=1, source_target_pairs={{0,1},{1,32},{32,33},{33,64},{64,65},{65,96},{96,97},{97,128},{128... | collective-permute-start | bytes 344072 | tf_op jit(solution)/shard_map/ppermute | solution.py:496
  91.2 6.1 %collective-permute-start.12 = (bf16[224,256]{1,0:T(8,128)(2,1)S(1)}, bf16[224,256]{1,0:T(8,128)(2,1)S(1)}, u32[]{:S(2)}, u32[]{:S(2)}) collective-permute-start(bf16[224,256]{1,0:T(8,128)(2,1)S(1)} %fusion.3), channel_id=1, source_target_pairs={{1,0},{32,1},{33,32},{64,33},{65,64},{96,65},{97,96},{128,97},{129... | collective-permute-start | bytes 344072 | tf_op jit(solution)/shard_map/ppermute | solution.py:496
  97.9 57.4 %all-to-all-start = ((bf16[64,96,128]{2,1,0:T(8,128)(2,1)}), bf16[64,96,128]{2,1,0:T(8,128)(2,1)S(1)}, u32[]{:S(2)}, u32[]{:S(2)}) async-start(bf16[64,96,128]{2,1,0:T(8,128)(2,1)} %reshape.314), calls=%async_computation | async-start | bytes 3145728 | tf_op jit(solution)/shard_map/all_to_all | solution.py:535
  112.4 5.6 %collective-permute-start.13 = (bf16[3072,256]{1,0:T(8,128)(2,1)}, bf16[3072,256]{1,0:T(8,128)(2,1)S(1)}, u32[]{:S(2)}, u32[]{:S(2)}) collective-permute-start(bf16[3072,256]{1,0:T(8,128)(2,1)} %all-gather.2.cloned.1.call-done.refs_6_), channel_id=1, source_target_pairs={{0,1},{1,0},{2,3},{3,2},{4,5},{5,4},{6,7},{7,6},{8,9},{9,8},{10,11... | collective-permute-start | bytes 4718600 | tf_op jit(solution)/shard_map/ppermute | solution.py:367
  115.1 38.3 %collective-permute-start.14 = (bf16[512,1024]{1,0:T(8,128)(2,1)}, bf16[512,1024]{1,0:T(8,128)(2,1)S(1)}, u32[]{:S(2)}, u32[]{:S(2)}) collective-permute-start(bf16[512,1024]{1,0:T(8,128)(2,1)} %get-tuple-element.31), channel_id=1, source_target_pairs={{0,1},{1,0},{2,3},{3,2},{4,5},{5,4},{6,7},{7,6},{8,9},{9,8},{10,11... | collective-permute-start | bytes 3145736 | tf_op jit(solution)/shard_map/ppermute | solution.py:367
  115.6 38.7 %collective-permute-start.15 = (bf16[512,1024]{1,0:T(8,128)(2,1)}, bf16[512,1024]{1,0:T(8,128)(2,1)S(1)}, u32[]{:S(2)}, u32[]{:S(2)}) collective-permute-start(bf16[512,1024]{1,0:T(8,128)(2,1)} %get-tuple-element.32), channel_id=1, source_target_pairs={{0,3},{1,2},{2,1},{3,0},{4,7},{5,6},{6,5},{7,4},{8,11},{9,10},{10,... | collective-permute-start | bytes 3145736 | tf_op jit(solution)/shard_map/ppermute | solution.py:367
  153.3 42.2 %copy-start.16 = (f32[1024]{0:T(1024)S(1)}, f32[1024]{0:T(1024)}, u32[]{:S(2)}) copy-start(f32[1024]{0:T(1024)} %param.19) | copy-start | bytes 12292
  155.3 40.3 %copy-start.6 = (bf16[512,1024]{1,0:T(8,128)(2,1)S(1)}, bf16[512,1024]{1,0:T(8,128)(2,1)}, u32[]{:S(2)}) copy-start(bf16[512,1024]{1,0:T(8,128)(2,1)} %copy-done.5) | copy-start | bytes 3145732
  191.0 4.6 %collective-permute-start.17 = (bf16[3072,128]{1,0:T(8,128)(2,1)S(1)}, bf16[3072,128]{1,0:T(8,128)(2,1)S(1)}, u32[]{:S(2)}, u32[]{:S(2)}) collective-permute-start(bf16[3072,128]{1,0:T(8,128)(2,1)S(1)} %bitcast.74), channel_id=1, source_target_pairs={{0,1},{1,0},{2,3},{3,2},{4,5},{5,4},{6,7},{7,6},{8,9},{9,8},{10,11... | collective-permute-start | bytes 2359304 | tf_op jit(solution)/shard_map/ppermute | solution.py:367
  193.6 19.2 %collective-permute-start.16 = (bf16[3072,128]{1,0:T(8,128)(2,1)S(1)}, bf16[3072,128]{1,0:T(8,128)(2,1)S(1)}, u32[]{:S(2)}, u32[]{:S(2)}) collective-permute-start(bf16[3072,128]{1,0:T(8,128)(2,1)S(1)} %bitcast.75), channel_id=1, source_target_pairs={{0,2},{1,3},{2,0},{3,1},{4,6},{5,7},{6,4},{7,5},{8,10},{9,11},{10,... | collective-permute-start | bytes 2359304 | tf_op jit(solution)/shard_map/ppermute | solution.py:367
  212.8 2.7 %collective-permute-start.18 = (bf16[3072,128]{1,0:T(8,128)(2,1)S(1)}, bf16[3072,128]{1,0:T(8,128)(2,1)S(1)}, u32[]{:S(2)}, u32[]{:S(2)}) collective-permute-start(bf16[3072,128]{1,0:T(8,128)(2,1)S(1)} %collective-permute-done.16.a0), channel_id=1, source_target_pairs={{0,1},{1,0},{2,3},{3,2},{4,5},{5,4},{6,7},{7,6},{8,9},{9,8},{10,11... | collective-permute-start | bytes 2359304 | tf_op jit(solution)/shard_map/ppermute | solution.py:367
  (23 other events, 141.0 us)
Sparse Core Ops, SparseCore 0:
  63.4 26.6 all-gather.1
